TPU v7x, 32 devices: a whole 2x2x4 slice. The times are simulated.
32 devices in a mesh: group: 2 (over y), seq: 16 (over z, x, core).
Axes of the slice: x: 2, y: 2, z: 4, core: 2. Of those that a mesh axis runs over, the one named last changes fastest.
Arguments:
- queries: bfloat16 [4096, 4096], P(('group', 'seq')), parts along dimension 0, may hold values from -64 to 64
- key_vectors: bfloat16 [4096, 1024], P(('group', 'seq')), parts along dimension 0, may hold values from -2 to 2
- value_vectors: bfloat16 [4096, 1024], P(('group', 'seq')), parts along dimension 0, may hold values from -6 to 6
- grad_output: bfloat16 [4096, 4096], P(('group', 'seq')), parts along dimension 0, may hold values from -6 to 6
- document_ids: int32 [4096], P('group'), parts along dimension 0, may hold values from 0 to 3, never falling along the last dimension, each value on 1 to 1024 neighbouring positions
Outputs:
- attention_out: bfloat16 [4096, 4096], P(('group', 'seq')), parts along dimension 0
- grad_queries: bfloat16 [4096, 4096], P(('group', 'seq')), parts along dimension 0
- grad_keys: bfloat16 [4096, 1024], P(('group', 'seq')), parts along dimension 0
- grad_values: bfloat16 [4096, 1024], P(('group', 'seq')), parts along dimension 0
There are 2 independent parts, one for each index of `group`. A program takes and returns all parts, laid end to end along the dimension named above; each array names one. Nothing has to cross between parts.
Inputs may be any that keep to these rules, and one draw needn't show every extreme that they name: `document_ids`: document numbers never fall along positions; each document covers 1 to 1024 consecutive positions and one covers exactly 1024.
All inputs are finite; a program needn't handle non-finite values.
Results may differ from a plain program's by a relative error of at most 0.015.
Values may be sent and summed in bfloat16 or wider, within the bound.
No kernel may reach another device: no remote copies, remote signals or barrier semaphores. Data moves between devices by JAX's collectives and lax.ppermute only.
A program may use at most 128 MiB of HBM per device.

v0:
```python
import math

import jax
import jax.numpy as jnp
from jax import lax
from jax.sharding import PartitionSpec as P

H = 32
KV = 8
HD = 128
MOST = 1024


def shifted(block, axis, distance):
    devices = range(lax.axis_size(axis))
    route = [(i - distance, i) for i in devices if i - distance in devices]
    return lax.ppermute(block, axis, route)


def attend_block(query_block, grad_block, key_block, value_block, allowed):
    score_scale = 1.0 / math.sqrt(query_block.shape[-1])
    scores = (
        jnp.einsum("qgd,kd->gqk", query_block, key_block, preferred_element_type=jnp.float32)
        * score_scale
    )
    scores = jnp.where(allowed[None], scores, -1e30)
    row_max = jnp.max(scores, axis=-1, keepdims=True)
    weights = jnp.exp(scores - row_max)
    softmax = weights / jnp.sum(weights, axis=-1, keepdims=True)
    probs_low = softmax.astype(jnp.bfloat16)
    output = jnp.einsum(
        "gqk,kd->qgd", probs_low, value_block, preferred_element_type=jnp.float32
    ).astype(jnp.bfloat16)
    row_delta = jnp.sum(grad_block.astype(jnp.float32) * output.astype(jnp.float32), axis=-1)
    grad_probs = jnp.einsum(
        "qgd,kd->gqk", grad_block, value_block, preferred_element_type=jnp.float32
    )
    grad_scores = (softmax * (grad_probs - jnp.transpose(row_delta)[:, :, None])).astype(
        jnp.bfloat16
    )
    grad_query = (
        jnp.einsum("gqk,kd->qgd", grad_scores, key_block, preferred_element_type=jnp.float32)
        * score_scale
    ).astype(jnp.bfloat16)
    grad_key = (
        jnp.einsum("gqk,qgd->kd", grad_scores, query_block, preferred_element_type=jnp.float32)
        * score_scale
    )
    grad_value = jnp.einsum(
        "gqk,qgd->kd", probs_low, grad_block, preferred_element_type=jnp.float32
    )
    return (output, grad_query, grad_key, grad_value)


def on_device(queries, key_vectors, value_vectors, grad_output, document_ids):
    devices = lax.axis_size("seq")
    position = lax.axis_index("seq")
    local_rows = queries.shape[0]
    group = H // KV
    ratio = devices // KV
    slot_rows = local_rows // ratio
    block_len = slot_rows * devices
    block_rows = min(512, block_len)

    def to_slots(tensor, columns):
        return (
            tensor.reshape(ratio, slot_rows, KV, columns)
            .transpose(1, 2, 0, 3)
            .reshape(slot_rows, devices, columns)
        )

    def from_slots(tensor, columns):
        height = tensor.shape[0]
        return tensor.reshape(height, KV, ratio, columns).transpose(2, 0, 1, 3)

    query_send = to_slots(queries, group * HD)
    grad_send = to_slots(grad_output, group * HD)
    key_send = to_slots(key_vectors, HD)
    value_send = to_slots(value_vectors, HD)
    query_in, grad_in, key_in, value_in = (
        lax.all_to_all(query_send, "seq", split_axis=1, concat_axis=1, tiled=True),
        lax.all_to_all(grad_send, "seq", split_axis=1, concat_axis=1, tiled=True),
        lax.all_to_all(key_send, "seq", split_axis=1, concat_axis=1, tiled=True),
        lax.all_to_all(value_send, "seq", split_axis=1, concat_axis=1, tiled=True),
    )
    query_head = query_in.reshape(block_len, group, HD)
    grad_head = grad_in.reshape(block_len, group, HD)
    key_flat = key_in.reshape(-1, HD)
    value_flat = value_in.reshape(-1, HD)
    stacked = jnp.stack([key_flat, value_flat])
    previous = shifted(stacked, "seq", 1)
    key_window = jnp.concatenate([previous[0], key_flat], axis=0)
    value_window = jnp.concatenate([previous[1], value_flat], axis=0)
    start = position % ratio * block_len
    padded_ids = jnp.concatenate([jnp.full((MOST,), -1, jnp.int32), document_ids])
    column_ids_all = lax.dynamic_slice_in_dim(padded_ids, start, MOST + block_len)
    row_ids_all = lax.dynamic_slice_in_dim(document_ids, start, block_len)
    column_index = jnp.arange(block_rows + MOST, dtype=jnp.int32)[None, :]
    row_index = jnp.arange(block_rows, dtype=jnp.int32)[:, None]

    def one_block(step_index, totals):
        out_all, dq_all, key_grad, value_grad = totals
        offset = step_index * block_rows
        query_block = lax.dynamic_slice_in_dim(query_head, offset, block_rows, 0)
        grad_block = lax.dynamic_slice_in_dim(grad_head, offset, block_rows, 0)
        key_block = lax.dynamic_slice_in_dim(key_window, offset, block_rows + MOST, 0)
        value_block = lax.dynamic_slice_in_dim(value_window, offset, block_rows + MOST, 0)
        row_ids = lax.dynamic_slice_in_dim(row_ids_all, offset, block_rows)
        column_ids = lax.dynamic_slice_in_dim(column_ids_all, offset, block_rows + MOST)
        allowed = (row_ids[:, None] == column_ids[None, :]) & (column_index <= row_index + MOST)
        output, grad_query, grad_key, grad_value = attend_block(
            query_block, grad_block, key_block, value_block, allowed
        )
        out_all = lax.dynamic_update_slice_in_dim(out_all, output, offset, 0)
        dq_all = lax.dynamic_update_slice_in_dim(dq_all, grad_query, offset, 0)
        key_grad = lax.dynamic_update_slice_in_dim(
            key_grad,
            lax.dynamic_slice_in_dim(key_grad, offset, block_rows + MOST, 0) + grad_key,
            offset,
            0,
        )
        value_grad = lax.dynamic_update_slice_in_dim(
            value_grad,
            lax.dynamic_slice_in_dim(value_grad, offset, block_rows + MOST, 0) + grad_value,
            offset,
            0,
        )
        return (out_all, dq_all, key_grad, value_grad)

    initial = (
        jnp.zeros((block_len, group, HD), jnp.bfloat16),
        jnp.zeros((block_len, group, HD), jnp.bfloat16),
        jnp.zeros((MOST + block_len, HD), jnp.float32),
        jnp.zeros((MOST + block_len, HD), jnp.float32),
    )
    out_all, dq_all, key_grad, value_grad = lax.fori_loop(
        0, block_len // block_rows, one_block, initial
    )
    out_send = out_all.reshape(slot_rows, devices, group * HD)
    dq_send = dq_all.reshape(slot_rows, devices, group * HD)
    returned = shifted(
        jnp.stack([key_grad[:MOST], value_grad[:MOST]]).astype(jnp.bfloat16), "seq", -1
    ).astype(jnp.float32)
    key_own = key_grad[MOST:].at[block_len - MOST :].add(returned[0]).astype(jnp.bfloat16)
    value_own = value_grad[MOST:].at[block_len - MOST :].add(returned[1]).astype(jnp.bfloat16)
    out_back, dq_back, key_back, value_back = (
        lax.all_to_all(out_send, "seq", split_axis=1, concat_axis=1, tiled=True),
        lax.all_to_all(dq_send, "seq", split_axis=1, concat_axis=1, tiled=True),
        lax.all_to_all(
            key_own.reshape(slot_rows, devices, HD), "seq", split_axis=1, concat_axis=1, tiled=True
        ),
        lax.all_to_all(
            value_own.reshape(slot_rows, devices, HD),
            "seq",
            split_axis=1,
            concat_axis=1,
            tiled=True,
        ),
    )
    grad_keys = from_slots(key_back, HD).reshape(local_rows, KV * HD)
    grad_values = from_slots(value_back, HD).reshape(local_rows, KV * HD)
    attention_out = from_slots(out_back, group * HD).reshape(local_rows, H * HD)
    grad_queries = from_slots(dq_back, group * HD).reshape(local_rows, H * HD)
    return (attention_out, grad_queries, grad_keys, grad_values)


def solution(mesh):
    placed = (
        P(("group", "seq"), None),
        P(("group", "seq"), None),
        P(("group", "seq"), None),
        P(("group", "seq"), None),
        P("group"),
    )
    return jax.shard_map(
        on_device,
        mesh=mesh,
        in_specs=placed,
        out_specs=(
            P(("group", "seq"), None),
            P(("group", "seq"), None),
            P(("group", "seq"), None),
            P(("group", "seq"), None),
        ),
        check_vma=False,
    )
```

profile of v0, /device:TPU:0, one launch (start us, length us, event | category | flops | bytes accessed | tf_op | source)
XLA Modules:
  0.0 311.4 jit_solution(9346794623854736078)
XLA Ops:
  2.4 7.4 %all-to-all-start = ((bf16[64,16,128]{2,0,1:T(8,128)(2,1)}), bf16[64,16,128]{2,0,1:T(8,128)(2,1)S(1)}, u32[]{:S(2)}, u32[]{:S(2)}) async-start(bf16[64,16,128]{2,0,1:T(8,128)(2,1)} %bitcast.1), calls=%async_computation | async-start | bytes 524288 | tf_op jit(solution)/shard_map/all_to_all | solution.py:83
  11.5 8.3 %all-to-all-done = bf16[64,16,128]{2,0,1:T(8,128)(2,1)S(1)} async-done(((bf16[64,16,128]{2,0,1:T(8,128)(2,1)}), bf16[64,16,128]{2,0,1:T(8,128)(2,1)S(1)}, u32[]{:S(2)}, u32[]{:S(2)}) %all-to-all-start) | async-done | bytes 262176 | tf_op jit(solution)/shard_map/all_to_all | solution.py:83
  19.8 3.5 %all-to-all-start.1 = ((bf16[64,16,128]{2,0,1:T(8,128)(2,1)}), bf16[64,16,128]{2,0,1:T(8,128)(2,1)S(1)}, u32[]{:S(2)}, u32[]{:S(2)}) async-start(bf16[64,16,128]{2,0,1:T(8,128)(2,1)} %bitcast.4), calls=%async_computation.1 | async-start | bytes 524288 | tf_op jit(solution)/shard_map/all_to_all | solution.py:84
  26.3 7.0 %all-to-all-done.1 = bf16[64,16,128]{2,0,1:T(8,128)(2,1)S(1)} async-done(((bf16[64,16,128]{2,0,1:T(8,128)(2,1)}), bf16[64,16,128]{2,0,1:T(8,128)(2,1)S(1)}, u32[]{:S(2)}, u32[]{:S(2)}) %all-to-all-start.1) | async-done | bytes 262176 | tf_op jit(solution)/shard_map/all_to_all | solution.py:84
  33.4 3.7 %all-to-all-start.2 = ((bf16[64,16,512]{2,0,1:T(8,128)(2,1)}), bf16[64,16,512]{2,0,1:T(8,128)(2,1)S(1)}, u32[]{:S(2)}, u32[]{:S(2)}) async-start(bf16[64,16,512]{2,0,1:T(8,128)(2,1)} %bitcast.11), calls=%async_computation.2 | async-start | bytes 2097152 | tf_op jit(solution)/shard_map/all_to_all | solution.py:81
  40.0 19.9 %all-to-all-done.2 = bf16[64,16,512]{2,0,1:T(8,128)(2,1)S(1)} async-done(((bf16[64,16,512]{2,0,1:T(8,128)(2,1)}), bf16[64,16,512]{2,0,1:T(8,128)(2,1)S(1)}, u32[]{:S(2)}, u32[]{:S(2)}) %all-to-all-start.2) | async-done | bytes 1048608 | tf_op jit(solution)/shard_map/all_to_all | solution.py:81
  59.9 6.8 %all-to-all-start.3 = ((bf16[64,16,512]{2,0,1:T(8,128)(2,1)}), bf16[64,16,512]{2,0,1:T(8,128)(2,1)S(1)}, u32[]{:S(2)}, u32[]{:S(2)}) async-start(bf16[64,16,512]{2,0,1:T(8,128)(2,1)} %bitcast.13), calls=%async_computation.3 | async-start | bytes 2097152 | tf_op jit(solution)/shard_map/all_to_all | solution.py:82
  76.6 13.1 %all-to-all-done.3 = bf16[64,16,512]{2,0,1:T(8,128)(2,1)S(1)} async-done(((bf16[64,16,512]{2,0,1:T(8,128)(2,1)}), bf16[64,16,512]{2,0,1:T(8,128)(2,1)S(1)}, u32[]{:S(2)}, u32[]{:S(2)}) %all-to-all-start.3) | async-done | bytes 1048608 | tf_op jit(solution)/shard_map/all_to_all | solution.py:82
  96.0 102.4 %while.24 = (s32[]{:T(128)}, bf16[1024,4,128]{2,1,0:T(4,128)(2,1)}, bf16[1024,4,128]{2,1,0:T(4,128)(2,1)}, f32[2048,128]{1,0:T(8,128)}, f32[2048,128]{1,0:T(8,12...) while((s32[]{:T(128)}, bf16[1024,4,128]{2,1,0:T(4,128)(2,1)}, ...), condition=%wide.region_4.5_spmd.clone, body=%wide.region_0.4_spmd.clone.sunk | while | flops 4874371072 | bytes 147394880 | solution.py:136
  100.8 10.0 %fusion.83 = (f32[4,512]{1,0:T(4,128)S(1)}, f32[4,512,1536]{1,2,0:T(8,128)}) fusion(f32[1536,512,4]{1,0,2:T(8,128)S(1)} %fusion.81, pred[512,1536]{0,1:T(8,128)(4,1)} %fusion.82), kind=kOutput, calls=%fused_computation.72.clone.1 | output fusion | flops 18875904 | bytes 25960448 | tf_op jit(solution)/shard_map/while/body/eval_jaxpr/sub | solution.py:28
  110.8 9.1 %fusion.84 = bf16[4,512,1536]{1,2,0:T(8,128)(2,1)} fusion(f32[4,512,1536]{1,2,0:T(8,128)} %get-tuple-element.452, f32[4,512]{1,0:T(4,128)S(1)} %get-tuple-element.453), kind=kLoop, calls=%fused_computation.13.clone.1 | loop fusion | flops 6291456 | bytes 18882560 | tf_op jit(solution)/shard_map/while/body/eval_jaxpr/convert_element_type | solution.py:30
  120.4 4.0 %multiply_reduce_fusion.2 = (f32[512,4]{0,1:T(4,128)S(1)}, bf16[512,4,128]{0,2,1:T(8,128)(2,1)S(1)}) fusion(bf16[512,4,128]{0,2,1:T(8,128)(2,1)S(1)} %copy.153, bf16[4,512,1536]{1,2,0:T(8,128)(2,1)} %fusion.84, bf16[2048,128]{1,0:T(8,128)(2,1)} %get-tuple-element.495, s32[]{:T(128)S(6)} %select_n.66), kind=kOutput, calls=%fused_computation.28.clone.1 | convolution fusion | flops 806615040 | bytes 7741444 | tf_op jit(solution)/shard_map/while/body/eval_jaxpr/gqk,kd->qgd/dot_general | solution.py:31
  124.3 5.9 %fusion.85 = bf16[4,512,1536]{1,2,0:T(8,128)(2,1)S(1)} fusion(bf16[512,4,128]{0,2,1:T(8,128)(2,1)S(1)} %copy.153, f32[4,512]{1,0:T(4,128)S(1)} %bitcast.201, f32[4,512,1536]{1,2,0:T(8,128)} %get-tuple-element.452, f32[4,512]{1,0:T(4,128)S(1)} %get-tuple-element.453, bf16[2048,128]{1,0:T(8,128)(2,1)} %get-tuple-element.495, s32[]{:T(128)S(6)} %select_n.66), kind=kOutput, calls=%fused_computation.5.clone.1 | convolution fusion | flops 817889280 | bytes 19808260 | tf_op jit(solution)/shard_map/while/body/eval_jaxpr/qgd,kd->gqk/dot_general | solution.py:35
  130.2 2.6 copy-done
  135.9 5.6 %fusion.87 = f32[2048,128]{1,0:T(8,128)} fusion(f32[2048,128]{1,0:T(8,128)} %get-tuple-element.477, s32[]{:T(128)S(6)} %select_n.66, bf16[4,512,1536]{1,2,0:T(8,128)(2,1)} %copy-done, bf16[512,4,128]{2,1,0:T(4,128)(2,1)S(1)} %constant_dynamic-slice_fusion.5), kind=kOutput, calls=%fused_computation.20.clone.1 | convolution fusion | flops 805699584 | bytes 8388612 | tf_op jit(solution)/shard_map/while/body/eval_jaxpr/gqk,qgd->kd/dot_general | solution.py:46
  141.5 5.6 %fusion.88 = f32[2048,128]{1,0:T(8,128)} fusion(f32[2048,128]{1,0:T(8,128)} %get-tuple-element.478, s32[]{:T(128)S(6)} %select_n.66, bf16[4,512,1536]{1,2,0:T(8,128)(2,1)} %fusion.84, bf16[512,4,128]{0,2,1:T(8,128)(2,1)S(1)} %copy.153), kind=kOutput, calls=%fused_computation.22.clone.1 | convolution fusion | flops 805502976 | bytes 8388612 | tf_op jit(solution)/shard_map/while/body/eval_jaxpr/gqk,qgd->kd/dot_general | solution.py:49
  151.9 10.0 %fusion.83 = (f32[4,512]{1,0:T(4,128)S(1)}, f32[4,512,1536]{1,2,0:T(8,128)}) fusion(f32[1536,512,4]{1,0,2:T(8,128)S(1)} %fusion.81, pred[512,1536]{0,1:T(8,128)(4,1)} %fusion.82), kind=kOutput, calls=%fused_computation.72.clone.1 | output fusion | flops 18875904 | bytes 25960448 | tf_op jit(solution)/shard_map/while/body/eval_jaxpr/sub | solution.py:28
  161.9 9.1 %fusion.84 = bf16[4,512,1536]{1,2,0:T(8,128)(2,1)} fusion(f32[4,512,1536]{1,2,0:T(8,128)} %get-tuple-element.452, f32[4,512]{1,0:T(4,128)S(1)} %get-tuple-element.453), kind=kLoop, calls=%fused_computation.13.clone.1 | loop fusion | flops 6291456 | bytes 18882560 | tf_op jit(solution)/shard_map/while/body/eval_jaxpr/convert_element_type | solution.py:30
  171.5 4.0 %multiply_reduce_fusion.2 = (f32[512,4]{0,1:T(4,128)S(1)}, bf16[512,4,128]{0,2,1:T(8,128)(2,1)S(1)}) fusion(bf16[512,4,128]{0,2,1:T(8,128)(2,1)S(1)} %copy.153, bf16[4,512,1536]{1,2,0:T(8,128)(2,1)} %fusion.84, bf16[2048,128]{1,0:T(8,128)(2,1)} %get-tuple-element.495, s32[]{:T(128)S(6)} %select_n.66), kind=kOutput, calls=%fused_computation.28.clone.1 | convolution fusion | flops 806615040 | bytes 7741444 | tf_op jit(solution)/shard_map/while/body/eval_jaxpr/gqk,kd->qgd/dot_general | solution.py:31
  175.5 5.9 %fusion.85 = bf16[4,512,1536]{1,2,0:T(8,128)(2,1)S(1)} fusion(bf16[512,4,128]{0,2,1:T(8,128)(2,1)S(1)} %copy.153, f32[4,512]{1,0:T(4,128)S(1)} %bitcast.201, f32[4,512,1536]{1,2,0:T(8,128)} %get-tuple-element.452, f32[4,512]{1,0:T(4,128)S(1)} %get-tuple-element.453, bf16[2048,128]{1,0:T(8,128)(2,1)} %get-tuple-element.495, s32[]{:T(128)S(6)} %select_n.66), kind=kOutput, calls=%fused_computation.5.clone.1 | convolution fusion | flops 817889280 | bytes 19808260 | tf_op jit(solution)/shard_map/while/body/eval_jaxpr/qgd,kd->gqk/dot_general | solution.py:35
  181.4 2.6 copy-done
  187.0 5.7 %fusion.87 = f32[2048,128]{1,0:T(8,128)} fusion(f32[2048,128]{1,0:T(8,128)} %get-tuple-element.477, s32[]{:T(128)S(6)} %select_n.66, bf16[4,512,1536]{1,2,0:T(8,128)(2,1)} %copy-done, bf16[512,4,128]{2,1,0:T(4,128)(2,1)S(1)} %constant_dynamic-slice_fusion.5), kind=kOutput, calls=%fused_computation.20.clone.1 | convolution fusion | flops 805699584 | bytes 8388612 | tf_op jit(solution)/shard_map/while/body/eval_jaxpr/gqk,qgd->kd/dot_general | solution.py:46
  192.7 5.7 %fusion.88 = f32[2048,128]{1,0:T(8,128)} fusion(f32[2048,128]{1,0:T(8,128)} %get-tuple-element.478, s32[]{:T(128)S(6)} %select_n.66, bf16[4,512,1536]{1,2,0:T(8,128)(2,1)} %fusion.84, bf16[512,4,128]{0,2,1:T(8,128)(2,1)S(1)} %copy.153), kind=kOutput, calls=%fused_computation.22.clone.1 | convolution fusion | flops 805502976 | bytes 8388612 | tf_op jit(solution)/shard_map/while/body/eval_jaxpr/gqk,qgd->kd/dot_general | solution.py:49
  201.9 2.6 collective-permute-done.1
  206.7 22.8 %all-to-all-start.7 = ((bf16[64,16,128]{2,0,1:T(8,128)(2,1)}), bf16[64,16,128]{2,0,1:T(8,128)(2,1)S(1)}, u32[]{:S(2)}, u32[]{:S(2)}) async-start(bf16[64,16,128]{2,0,1:T(8,128)(2,1)} %copy.113), calls=%async_computation.7 | async-start | bytes 524288 | tf_op jit(solution)/shard_map/all_to_all | solution.py:152
  230.3 9.3 %all-to-all-done.7 = bf16[64,16,128]{2,0,1:T(8,128)(2,1)S(1)} async-done(((bf16[64,16,128]{2,0,1:T(8,128)(2,1)}), bf16[64,16,128]{2,0,1:T(8,128)(2,1)S(1)}, u32[]{:S(2)}, u32[]{:S(2)}) %all-to-all-start.7) | async-done | bytes 262176 | tf_op jit(solution)/shard_map/all_to_all | solution.py:152
  239.5 3.5 %all-to-all-start.6 = ((bf16[64,16,128]{2,0,1:T(8,128)(2,1)}), bf16[64,16,128]{2,0,1:T(8,128)(2,1)S(1)}, u32[]{:S(2)}, u32[]{:S(2)}) async-start(bf16[64,16,128]{2,0,1:T(8,128)(2,1)} %copy.111), calls=%async_computation.6 | async-start | bytes 524288 | tf_op jit(solution)/shard_map/all_to_all | solution.py:149
  246.1 7.0 %all-to-all-done.6 = bf16[64,16,128]{2,0,1:T(8,128)(2,1)S(1)} async-done(((bf16[64,16,128]{2,0,1:T(8,128)(2,1)}), bf16[64,16,128]{2,0,1:T(8,128)(2,1)S(1)}, u32[]{:S(2)}, u32[]{:S(2)}) %all-to-all-start.6) | async-done | bytes 262176 | tf_op jit(solution)/shard_map/all_to_all | solution.py:149
  253.1 3.7 %all-to-all-start.4 = ((bf16[64,16,512]{2,0,1:T(8,128)(2,1)}), bf16[64,16,512]{2,0,1:T(8,128)(2,1)S(1)}, u32[]{:S(2)}, u32[]{:S(2)}) async-start(bf16[64,16,512]{2,0,1:T(8,128)(2,1)} %copy.106), calls=%async_computation.4 | async-start | bytes 2097152 | tf_op jit(solution)/shard_map/all_to_all | solution.py:147
  258.8 20.9 %all-to-all-done.4 = bf16[64,16,512]{2,0,1:T(8,128)(2,1)S(1)} async-done(((bf16[64,16,512]{2,0,1:T(8,128)(2,1)}), bf16[64,16,512]{2,0,1:T(8,128)(2,1)S(1)}, u32[]{:S(2)}, u32[]{:S(2)}) %all-to-all-start.4) | async-done | bytes 1048608 | tf_op jit(solution)/shard_map/all_to_all | solution.py:147
  279.7 6.8 %all-to-all-start.5 = ((bf16[64,16,512]{2,0,1:T(8,128)(2,1)}), bf16[64,16,512]{2,0,1:T(8,128)(2,1)S(1)}, u32[]{:S(2)}, u32[]{:S(2)}) async-start(bf16[64,16,512]{2,0,1:T(8,128)(2,1)} %copy.109), calls=%async_computation.5 | async-start | bytes 2097152 | tf_op jit(solution)/shard_map/all_to_all | solution.py:148
  291.2 18.2 %all-to-all-done.5 = bf16[64,16,512]{2,0,1:T(8,128)(2,1)S(1)} async-done(((bf16[64,16,512]{2,0,1:T(8,128)(2,1)}), bf16[64,16,512]{2,0,1:T(8,128)(2,1)S(1)}, u32[]{:S(2)}, u32[]{:S(2)}) %all-to-all-start.5) | async-done | bytes 1048608 | tf_op jit(solution)/shard_map/all_to_all | solution.py:148
  (84 shorter events, 60.3 us)
Async XLA Ops:
  0.6 69.7 %copy-start.4 = (s32[2048]{0:T(1024)S(1)}, s32[2048]{0:T(1024)}, u32[]{:S(2)}) copy-start(s32[2048]{0:T(1024)} %param.19) | copy-start | bytes 24580
  2.4 17.4 %all-to-all-start = ((bf16[64,16,128]{2,0,1:T(8,128)(2,1)}), bf16[64,16,128]{2,0,1:T(8,128)(2,1)S(1)}, u32[]{:S(2)}, u32[]{:S(2)}) async-start(bf16[64,16,128]{2,0,1:T(8,128)(2,1)} %bitcast.1), calls=%async_computation | async-start | bytes 524288 | tf_op jit(solution)/shard_map/all_to_all | solution.py:83
  19.8 13.5 %all-to-all-start.1 = ((bf16[64,16,128]{2,0,1:T(8,128)(2,1)}), bf16[64,16,128]{2,0,1:T(8,128)(2,1)S(1)}, u32[]{:S(2)}, u32[]{:S(2)}) async-start(bf16[64,16,128]{2,0,1:T(8,128)(2,1)} %bitcast.4), calls=%async_computation.1 | async-start | bytes 524288 | tf_op jit(solution)/shard_map/all_to_all | solution.py:84
  33.4 26.6 %all-to-all-start.2 = ((bf16[64,16,512]{2,0,1:T(8,128)(2,1)}), bf16[64,16,512]{2,0,1:T(8,128)(2,1)S(1)}, u32[]{:S(2)}, u32[]{:S(2)}) async-start(bf16[64,16,512]{2,0,1:T(8,128)(2,1)} %bitcast.11), calls=%async_computation.2 | async-start | bytes 2097152 | tf_op jit(solution)/shard_map/all_to_all | solution.py:81
  59.9 29.8 %all-to-all-start.3 = ((bf16[64,16,512]{2,0,1:T(8,128)(2,1)}), bf16[64,16,512]{2,0,1:T(8,128)(2,1)S(1)}, u32[]{:S(2)}, u32[]{:S(2)}) async-start(bf16[64,16,512]{2,0,1:T(8,128)(2,1)} %bitcast.13), calls=%async_computation.3 | async-start | bytes 2097152 | tf_op jit(solution)/shard_map/all_to_all | solution.py:82
  68.0 4.0 %collective-permute-start = (bf16[2,1024,128]{2,1,0:T(8,128)(2,1)}, bf16[2,1024,128]{2,1,0:T(8,128)(2,1)S(1)}, u32[]{:S(2)}, u32[]{:S(2)}) collective-permute-start(bf16[2,1024,128]{2,1,0:T(8,128)(2,1)} %pad_maximum_fusion), channel_id=1, source_target_pairs={{0,1},{1,2},{2,3},{3,4},{4,5},{5,6},{6,7},{7,8},{8,9},{9,10},{10,1... | collective-permute-start | bytes 1572872 | tf_op jit(solution)/shard_map/ppermute | solution.py:17
  70.3 25.7 %dynamic-slice-start = ((s32[2048]{0:T(1024)}, s32[]{:T(128)}), s32[1024]{0:T(1024)S(1)}, s32[]{:S(2)}) async-start(s32[2048]{0:T(1024)} %param.19, s32[]{:T(128)} %select_n.46), calls=%async_computation.8 | async-start | bytes 8704 | tf_op jit(solution)/shard_map/dynamic_slice | solution.py:97
  110.8 9.1 %copy-start.1 = (bf16[1024,4,128]{2,1,0:T(4,128)(2,1)S(1)}, bf16[1024,4,128]{2,1,0:T(4,128)(2,1)}, u32[]{:S(2)}) copy-start(bf16[1024,4,128]{2,1,0:T(4,128)(2,1)} %get-tuple-element.500) | copy-start | bytes 3145732 | tf_op jit(solution)/shard_map/while
  130.2 2.7 copy-start
  161.9 9.1 %copy-start.1 = (bf16[1024,4,128]{2,1,0:T(4,128)(2,1)S(1)}, bf16[1024,4,128]{2,1,0:T(4,128)(2,1)}, u32[]{:S(2)}) copy-start(bf16[1024,4,128]{2,1,0:T(4,128)(2,1)} %get-tuple-element.500) | copy-start | bytes 3145732 | tf_op jit(solution)/shard_map/while
  181.4 2.7 copy-start
  198.3 58.4 %copy-start.2 = (bf16[1024,4,128]{2,1,0:T(4,128)(2,1)S(1)}, bf16[1024,4,128]{2,1,0:T(4,128)(2,1)}, u32[]{:S(2)}) copy-start(bf16[1024,4,128]{2,1,0:T(4,128)(2,1)} %get-tuple-element.262) | copy-start | bytes 3145732
  200.6 3.9 %collective-permute-start.1 = (bf16[2,1024,128]{2,1,0:T(8,128)(2,1)S(1)}, bf16[2,1024,128]{2,1,0:T(8,128)(2,1)S(1)}, u32[]{:S(2)}, u32[]{:S(2)}) collective-permute-start(bf16[2,1024,128]{2,1,0:T(8,128)(2,1)S(1)} %pad_maximum_fusion.3), channel_id=1, source_target_pairs={{1,0},{2,1},{3,2},{4,3},{5,4},{6,5},{7,6},{8,7},{9,8},{10,9},{11,1... | collective-permute-start | bytes 1572872 | tf_op jit(solution)/shard_map/ppermute | solution.py:17
  206.7 32.8 %all-to-all-start.7 = ((bf16[64,16,128]{2,0,1:T(8,128)(2,1)}), bf16[64,16,128]{2,0,1:T(8,128)(2,1)S(1)}, u32[]{:S(2)}, u32[]{:S(2)}) async-start(bf16[64,16,128]{2,0,1:T(8,128)(2,1)} %copy.113), calls=%async_computation.7 | async-start | bytes 524288 | tf_op jit(solution)/shard_map/all_to_all | solution.py:152
  239.5 13.5 %all-to-all-start.6 = ((bf16[64,16,128]{2,0,1:T(8,128)(2,1)}), bf16[64,16,128]{2,0,1:T(8,128)(2,1)S(1)}, u32[]{:S(2)}, u32[]{:S(2)}) async-start(bf16[64,16,128]{2,0,1:T(8,128)(2,1)} %copy.111), calls=%async_computation.6 | async-start | bytes 524288 | tf_op jit(solution)/shard_map/all_to_all | solution.py:149
  253.1 3.7 %copy-start.3 = (bf16[64,16,128]{2,0,1:T(8,128)(2,1)}, bf16[64,16,128]{2,0,1:T(8,128)(2,1)S(1)}, u32[]{:S(2)}) copy-start(bf16[64,16,128]{2,0,1:T(8,128)(2,1)S(1)} %all-to-all-done.6) | copy-start | bytes 786436
  253.1 26.6 %all-to-all-start.4 = ((bf16[64,16,512]{2,0,1:T(8,128)(2,1)}), bf16[64,16,512]{2,0,1:T(8,128)(2,1)S(1)}, u32[]{:S(2)}, u32[]{:S(2)}) async-start(bf16[64,16,512]{2,0,1:T(8,128)(2,1)} %copy.106), calls=%async_computation.4 | async-start | bytes 2097152 | tf_op jit(solution)/shard_map/all_to_all | solution.py:147
  279.7 29.8 %all-to-all-start.5 = ((bf16[64,16,512]{2,0,1:T(8,128)(2,1)}), bf16[64,16,512]{2,0,1:T(8,128)(2,1)S(1)}, u32[]{:S(2)}, u32[]{:S(2)}) async-start(bf16[64,16,512]{2,0,1:T(8,128)(2,1)} %copy.109), calls=%async_computation.5 | async-start | bytes 2097152 | tf_op jit(solution)/shard_map/all_to_all | solution.py:148
where the time goes:
time: 314 us; the launch traced here: 311 us
  waiting for transfers between devices  108 us (34%)
  starting transfers between devices  61.8 us (20%)
  local copies, waits for them, and re-layouts  48.3 us (15%)
  matrix products  47.9 us (15%)
  other arithmetic  44.5 us (14%)
    all_to_all x1, starting transfers between devices, on_device(): lax.all_to_all(value_own.reshape(slot_rows, devices, HD), 'seq', split_ax...  22.8 us
    all_to_all x1, waiting for transfers between devices, on_device(): lax.all_to_all(out_send, 'seq', split_axis=1, concat_axis=1, tiled=True)  20.9 us
    sub x2, other arithmetic, attend_block(): weights = jnp.exp(scores - row_max)  20 us
    all_to_all x1, waiting for transfers between devices, on_device(): lax.all_to_all(query_send, 'seq', split_axis=1, concat_axis=1, tiled=True)  19.9 us
    all_to_all x1, waiting for transfers between devices, on_device(): lax.all_to_all(dq_send, 'seq', split_axis=1, concat_axis=1, tiled=True)  18.2 us
    convert_element_type x2, other arithmetic, attend_block(): probs_low = softmax.astype(jnp.bfloat16)  18.2 us
    all_to_all x1, waiting for transfers between devices, on_device(): lax.all_to_all(grad_send, 'seq', split_axis=1, concat_axis=1, tiled=True)  13.1 us
    dot_general x2, matrix products, attend_block(): jnp.einsum('qgd,kd->gqk', grad_block, value_block, preferred_element_type...  11.7 us
  transfers between devices with their start and end apart: 10, of which 10 were waited for; matrix products, arithmetic and copies ran while one was open for 8% of the time, Pallas kernels for 0%

commit v1 on v0

v1 whole, which is shorter than its diff:
```python
import functools
import math

import jax
import jax.numpy as jnp
from jax import lax
from jax.experimental import pallas as pl
from jax.experimental.pallas import tpu as pltpu
from jax.sharding import PartitionSpec as P

H = 32
KV = 8
HD = 128
MOST = 1024
GROUP = H // KV
QR = 16
KR = 16
F32 = jnp.float32
BF16 = jnp.bfloat16
SCALE = 1.0 / math.sqrt(HD)
EXP2_SCALE = SCALE * math.log2(math.e)


def attend_kernel(heads, lanes, depth, start_ref, begin_ref, place_ref, key_place_ref, *refs):
    refs = list(refs)
    take = lambda count: [refs.pop(0) for _ in range(count)]
    query_refs, kv_refs = take(lanes), take(depth)
    out_refs, grad_refs = take(lanes), take(depth)
    key_turned, value_turned, key_sum, value_sum, score_ref, out_sum, query_sum = refs
    rows = query_refs[0].shape[1]
    key_tiles, query_tiles = rows // KR, rows // QR
    tile = depth * lanes * KR
    span = lanes * GROUP * QR

    def keys_of(which, head, step):
        at = pl.ds(pl.multiple_of(step * KR, KR), KR)
        columns = slice(head * HD, (head + 1) * HD)
        return jnp.concatenate(
            [ref[:, which, at, columns].reshape(lanes * KR, HD) for ref in kv_refs], axis=0
        )

    def queries_of(which, head, step):
        at = pl.ds(pl.multiple_of(step * QR, QR), QR)
        return jnp.concatenate(
            [
                ref[which, at, (head * GROUP + j) * HD : (head * GROUP + j + 1) * HD]
                for j in range(GROUP)
                for ref in query_refs
            ],
            axis=0,
        )

    def put_queries(which, head, step, value):
        at = pl.ds(pl.multiple_of(step * QR, QR), QR)
        for j in range(GROUP):
            for lane, ref in enumerate(out_refs):
                low = (j * lanes + lane) * QR
                ref[which, at, (head * GROUP + j) * HD : (head * GROUP + j + 1) * HD] = value[
                    low : low + QR
                ]

    for head in range(heads):

        @pl.loop(0, key_tiles)
        def _(step):
            key_turned[step] = keys_of(0, head, step).T
            value_turned[step] = keys_of(1, head, step).T
            key_sum[step] = jnp.zeros((tile, HD), F32)
            value_sum[step] = jnp.zeros((tile, HD), F32)

        @pl.loop(0, query_tiles)
        def _(turn):
            query, grad = queries_of(0, head, turn), queries_of(1, head, turn)
            query_t, grad_t = query.T, grad.T
            first = start_ref[turn]
            last = (turn + 1) * (QR // KR)
            begin, place = begin_ref[turn], place_ref[turn]

            def score(step, top):
                base = step * (tile // depth // lanes) * depth * lanes
                value = jnp.dot(keys_of(0, head, step), query_t, preferred_element_type=F32)
                key_place = jnp.concatenate([key_place_ref[...]] * (span // 128), axis=1)
                allowed = (key_place <= place - base) & (key_place >= begin - base)
                value = jnp.where(allowed, value, -1e30)
                score_ref[step - first] = value
                return jnp.maximum(top, value.reshape(tile // 8, 8, span).max(axis=0))

            top = lax.fori_loop(first, last, score, jnp.full((8, span), -1e30, F32))
            top = jnp.max(top, axis=0, keepdims=True)
            out_sum[...] = jnp.zeros((HD, span), F32)

            def weigh(step, total):
                weight = jnp.exp2((score_ref[step - first] - top) * EXP2_SCALE)
                score_ref[step - first] = weight
                out_sum[...] += jnp.dot(
                    value_turned[step], weight.astype(BF16), preferred_element_type=F32
                )
                return total + weight.reshape(tile // 8, 8, span).sum(axis=0)

            total = lax.fori_loop(first, last, weigh, jnp.zeros((8, span), F32))
            inverse = 1.0 / jnp.sum(total, axis=0, keepdims=True)
            out_t = (out_sum[...] * inverse).astype(BF16).astype(F32)
            delta = jnp.sum(out_t * grad_t.astype(F32), axis=0, keepdims=True)
            put_queries(0, head, turn, out_t.T.astype(BF16))
            query_sum[...] = jnp.zeros((HD, span), F32)

            def back(step, carry):
                prob = score_ref[step - first] * inverse
                value_sum[step] += jnp.dot(prob.astype(BF16), grad, preferred_element_type=F32)
                grad_prob = jnp.dot(keys_of(1, head, step), grad_t, preferred_element_type=F32)
                grad_score = (prob * (grad_prob - delta)).astype(BF16)
                key_sum[step] += jnp.dot(grad_score, query, preferred_element_type=F32)
                query_sum[...] += jnp.dot(
                    key_turned[step], grad_score, preferred_element_type=F32
                )
                return carry

            lax.fori_loop(first, last, back, 0)
            put_queries(1, head, turn, (query_sum[...] * SCALE).T.astype(BF16))

        @pl.loop(0, key_tiles)
        def _(step):
            at = pl.ds(pl.multiple_of(step * KR, KR), KR)
            columns = slice(head * HD, (head + 1) * HD)
            for which, total, factor in ((0, key_sum, SCALE), (1, value_sum, 1.0)):
                for k, ref in enumerate(grad_refs):
                    low = k * lanes * KR
                    part = total[step, low : low + lanes * KR, :] * factor
                    ref[:, which, at, columns] = part.astype(ref.dtype).reshape(lanes, KR, HD)


def attend(query_parts, kv_parts, starts, begins, places, key_places):
    lanes, depth = len(query_parts), len(kv_parts)
    _, rows, columns = query_parts[0].shape
    heads = columns // (GROUP * HD)
    tile, span = depth * lanes * KR, lanes * GROUP * QR
    key_tiles = rows // KR
    reach = QR // KR + -(-(MOST - 1) // tile)
    vmem = pl.BlockSpec(memory_space=pltpu.VMEM)
    pairs = heads * GROUP * rows * lanes * 640
    return pl.pallas_call(
        functools.partial(attend_kernel, heads, lanes, depth),
        out_shape=[jax.ShapeDtypeStruct(part.shape, BF16) for part in query_parts]
        + [
            jax.ShapeDtypeStruct(part.shape, F32 if k == 0 else BF16)
            for k, part in enumerate(kv_parts)
        ],
        in_specs=[pl.BlockSpec(memory_space=pltpu.SMEM)] + [vmem] * (3 + lanes + depth),
        out_specs=[vmem] * (lanes + depth),
        scratch_shapes=[
            pltpu.VMEM((key_tiles, HD, tile), BF16),
            pltpu.VMEM((key_tiles, HD, tile), BF16),
            pltpu.VMEM((key_tiles, tile, HD), F32),
            pltpu.VMEM((key_tiles, tile, HD), F32),
            pltpu.VMEM((min(reach, key_tiles), tile, span), F32),
            pltpu.VMEM((HD, span), F32),
            pltpu.VMEM((HD, span), F32),
        ],
        compiler_params=pltpu.CompilerParams(vmem_limit_bytes=60 << 20),
        cost_estimate=pl.CostEstimate(
            flops=10 * HD * pairs, bytes_accessed=8 << 20, transcendentals=pairs
        ),
    )(starts, begins, places, key_places, *query_parts, *kv_parts)


def swapped(tensor, mask):
    devices = lax.axis_size("seq")
    return lax.ppermute(tensor, "seq", [(i, i ^ mask) for i in range(devices)])


def on_device(queries, key_vectors, value_vectors, grad_output, document_ids):
    devices = lax.axis_size("seq")
    position = lax.axis_index("seq")
    rows = queries.shape[0]
    lanes = min(KV, devices // 4)
    depth = devices // lanes
    lane = position % lanes
    above = position - lane
    wide, narrow = H * HD // lanes, KV * HD // lanes

    def cut(tensor, mask, width):
        return lax.dynamic_slice_in_dim(tensor, (lane ^ mask) * width, width, 1)

    def kv_cut(mask):
        return jnp.stack([cut(key_vectors, mask, narrow), cut(value_vectors, mask, narrow)])

    def query_cut(mask):
        return jnp.stack([cut(queries, mask, wide), cut(grad_output, mask, wide)])

    kv_own = jnp.stack(
        [kv_cut(0)] + [swapped(kv_cut(mask), mask) for mask in range(1, lanes)]
    )
    kv_parts = [kv_own] + [swapped(kv_own, k * lanes) for k in range(1, depth)]
    query_parts = [query_cut(0)] + [swapped(query_cut(mask), mask) for mask in range(1, lanes)]

    ids = document_ids.reshape(rows, devices)
    lane_masks = jnp.arange(lanes, dtype=jnp.int32)
    mine = above + (lane ^ lane_masks)
    column = jnp.arange(devices, dtype=jnp.int32)
    own_ids = jnp.sum(
        jnp.where(column[None, None, :] == mine[:, None, None], ids[None], 0), axis=-1
    )
    begin = jnp.sum(
        (document_ids[None, None, :] < own_ids[:, :, None]).astype(jnp.int32), axis=-1
    )
    place = jnp.arange(rows, dtype=jnp.int32)[None, :] * devices + mine[:, None]

    def tiled(values):
        parts = values.reshape(lanes, rows // QR, QR).transpose(1, 0, 2)
        parts = parts.reshape(rows // QR, 1, lanes * QR)
        return jnp.tile(parts, (1, 1, GROUP))

    begins, places = tiled(begin), tiled(place)
    starts = jnp.min(begins, axis=(1, 2)) // (KR * devices)
    chunk = (jnp.arange(depth, dtype=jnp.int32) * lanes) ^ above
    key_place = (
        jnp.arange(KR, dtype=jnp.int32)[None, None, :] * devices
        + chunk[:, None, None]
        + (lane ^ lane_masks)[None, :, None]
    ).reshape(depth * lanes * KR, 1)
    key_places = jnp.broadcast_to(key_place, (depth * lanes * KR, 128))

    results = attend(query_parts, kv_parts, starts, begins, places, key_places)
    out_parts, grad_parts = results[:lanes], results[lanes:]
    out_back = [out_parts[0]] + [swapped(out_parts[mask], mask) for mask in range(1, lanes)]
    total = grad_parts[0]
    for k in range(1, depth):
        total = total + swapped(grad_parts[k], k * lanes).astype(F32)
    total = total.astype(BF16)
    kv_back = [total[0]] + [swapped(total[mask], mask) for mask in range(1, lanes)]

    def joined(parts, which, width):
        whole = jnp.zeros((rows, lanes * width), BF16)
        for mask, part in enumerate(parts):
            whole = lax.dynamic_update_slice_in_dim(whole, part[which], (lane ^ mask) * width, 1)
        return whole

    return (
        joined(out_back, 0, wide),
        joined(out_back, 1, wide),
        joined(kv_back, 0, narrow),
        joined(kv_back, 1, narrow),
    )


def solution(mesh):
    placed = P(("group", "seq"), None)
    return jax.shard_map(
        on_device,
        mesh=mesh,
        in_specs=(placed, placed, placed, placed, P("group")),
        out_specs=(placed, placed, placed, placed),
        check_vma=False,
    )
```

time: 314 us -> 163 us (0.52)
  the two profiles are of different devices: /device:TPU:0 before, /device:TPU:17 now
where the time goes in v1:
time: 163 us; the launch traced here: 164 us
  waiting for transfers between devices  91.6 us (56%)
  Pallas kernels  44.4 us (27%)
  starting transfers between devices  17.6 us (11%)
  local copies, waits for them, and re-layouts  6.7 us (4%)
  other arithmetic  3.13 us (2%)
    ppermute x18, waiting for transfers between devices, swapped(): return lax.ppermute(tensor, 'seq', [(i, i ^ mask) for i in range(devices)])  91.6 us
    pallas_call x1, Pallas kernels, attend(): pl.pallas_call(functools.partial(attend_kernel, heads, lanes, depth), out...  44.4 us
    ppermute x18, starting transfers between devices, swapped(): return lax.ppermute(tensor, 'seq', [(i, i ^ mask) for i in range(devices)])  17.6 us
  transfers between devices with their start and end apart: 18, of which 11 were waited for; matrix products, arithmetic and copies ran while one was open for 4% of the time, Pallas kernels for 0%

profile of v1, /device:TPU:17, one launch (start us, length us, event | category | flops | bytes accessed | tf_op | source)
XLA Modules:
  0.0 164.5 jit_solution(4578427170287510388)
XLA Ops:
  0.7 1.2 dynamic-slice_bitcast_fusion.14
  1.9 0.7 collective-permute-start.3
  2.7 1.3 collective-permute-start.4
  4.5 1.4 dynamic-slice_bitcast_fusion
  6.0 1.4 collective-permute-start.2
  8.5 0.6 collective-permute-start
  9.2 2.4 %collective-permute-done.5 = bf16[2,128,256]{2,1,0:T(8,128)(2,1)S(1)} collective-permute-done((bf16[2,128,256]{2,1,0:T(8,128)(2,1)S(1)}, bf16[2,128,256]{2,1,0:T(8,128)(2,1)S(1)}, u32[]{:S(2)}, u32[]{:S(2)}) %collective-permute-start.5) | collective-permute-done | bytes 131104 | tf_op jit(solution)/shard_map/ppermute | solution.py:168
  11.6 1.4 collective-permute-start.6
  13.1 9.6 %collective-permute-done.2.refs_3_ = bf16[2,128,1024]{2,1,0:T(8,128)(2,1)} collective-permute-done((bf16[2,128,1024]{2,1,0:T(8,128)(2,1)S(1)}, bf16[2,128,1024]{2,1,0:T(8,128)(2,1)}, u32[]{:S(2)}, u32[]{:S(2)}) %collective-permute-start.2) | collective-permute-done | bytes 524320 | tf_op jit(solution)/shard_map/ppermute | solution.py:168
  22.9 0.6 convert_reduce_fusion
  23.7 0.7 tile.20.begin_ref
  24.4 0.7 tile.22.place_ref
  25.3 0.8 pad_maximum_fusion.refs_0_
  26.7 6.5 %collective-permute-done.1.refs_2_ = bf16[2,128,1024]{2,1,0:T(8,128)(2,1)} collective-permute-done((bf16[2,128,1024]{2,1,0:T(8,128)(2,1)S(1)}, bf16[2,128,1024]{2,1,0:T(8,128)(2,1)}, u32[]{:S(2)}, u32[]{:S(2)}) %collective-permute-start.1) | collective-permute-done | bytes 524320 | tf_op jit(solution)/shard_map/ppermute | solution.py:168
  33.2 1.5 collective-permute-done.6.refs_5_
  34.7 2.1 %collective-permute-done.7.refs_6_ = bf16[4,2,128,256]{3,2,1,0:T(8,128)(2,1)} collective-permute-done((bf16[4,2,128,256]{3,2,1,0:T(8,128)(2,1)S(1)}, bf16[4,2,128,256]{3,2,1,0:T(8,128)(2,1)}, u32[]{:S(2)}, u32[]{:S(2)}) %collective-permute-start.7) | collective-permute-done | bytes 524320 | tf_op jit(solution)/shard_map/ppermute | solution.py:168
  36.8 23.7 %collective-permute-done.8.refs_7_ = bf16[4,2,128,256]{3,2,1,0:T(8,128)(2,1)} collective-permute-done((bf16[4,2,128,256]{3,2,1,0:T(8,128)(2,1)S(1)}, bf16[4,2,128,256]{3,2,1,0:T(8,128)(2,1)}, u32[]{:S(2)}, u32[]{:S(2)}) %collective-permute-start.8) | collective-permute-done | bytes 524320 | tf_op jit(solution)/shard_map/ppermute | solution.py:168
  60.5 0.8 broadcast_in_dim.40.key_place_ref
  61.2 44.4 %shard_map.84 = (bf16[2,128,1024]{2,1,0:T(8,128)(2,1)}, bf16[2,128,1024]{2,1,0:T(8,128)(2,1)}, bf16[2,128,1024]{2,1,0:T(8,128)(2,1)}, bf16[2,128,1024]{2,1,0:T(8...) custom-call(s32[8]{0:T(128)} %and_select_fusion.start_ref, ...), custom_call_target="tpu_custom_call" | custom-call | flops 3355443200 | bytes 8388608 | tf_op jit(solution)/shard_map/pallas_call | solution.py:141
  105.7 1.3 collective-permute-start.13
  107.0 1.3 collective-permute-start.14
  108.3 1.5 collective-permute-start.9
  109.8 1.2 collective-permute-start.10
  111.3 15.6 %collective-permute-done.12 = bf16[4,2,128,256]{3,2,1,0:T(8,128)(2,1)S(1)} collective-permute-done((bf16[4,2,128,256]{3,2,1,0:T(8,128)(2,1)}, bf16[4,2,128,256]{3,2,1,0:T(8,128)(2,1)S(1)}, u32[]{:S(2)}, u32[]{:S(2)}) %collective-permute-start.12) | collective-permute-done | bytes 524320 | tf_op jit(solution)/shard_map/ppermute | solution.py:168
  126.9 2.3 %collective-permute-start.11 = (bf16[2,128,1024]{2,1,0:T(8,128)(2,1)S(1)}, bf16[2,128,1024]{2,1,0:T(8,128)(2,1)S(1)}, u32[]{:S(2)}, u32[]{:S(2)}) collective-permute-start(bf16[2,128,1024]{2,1,0:T(8,128)(2,1)S(1)} %copy-done.9), channel_id=1, source_target_pairs={{0,3},{1,2},{2,1},{3,0},{4,7},{5,6},{6,5},{7,4},{8,11},{9,10},{10,... | collective-permute-start | bytes 1572872 | tf_op jit(solution)/shard_map/ppermute | solution.py:168
  129.2 0.7 collective-permute-done.13
  129.9 23.5 %collective-permute-done.14 = bf16[4,2,128,256]{3,2,1,0:T(8,128)(2,1)S(1)} collective-permute-done((bf16[4,2,128,256]{3,2,1,0:T(8,128)(2,1)}, bf16[4,2,128,256]{3,2,1,0:T(8,128)(2,1)S(1)}, u32[]{:S(2)}, u32[]{:S(2)}) %collective-permute-start.14) | collective-permute-done | bytes 524320 | tf_op jit(solution)/shard_map/ppermute | solution.py:168
  153.8 1.8 %collective-permute-start.15 = (bf16[2,128,256]{2,1,0:T(8,128)(2,1)S(1)}, bf16[2,128,256]{2,1,0:T(8,128)(2,1)S(1)}, u32[]{:S(2)}, u32[]{:S(2)}) collective-permute-start(bf16[2,128,256]{2,1,0:T(8,128)(2,1)S(1)} %get-tuple-element.30), channel_id=1, source_target_pairs={{0,1},{1,0},{2,3},{3,2},{4,5},{5,4},{6,7},{7,6},{8,9},{9,8},{10,11... | collective-permute-start | bytes 393224 | tf_op jit(solution)/shard_map/ppermute | solution.py:168
  155.6 1.2 collective-permute-start.16
  157.6 3.1 %collective-permute-done.16 = bf16[2,128,256]{2,1,0:T(8,128)(2,1)S(1)} collective-permute-done((bf16[2,128,256]{2,1,0:T(8,128)(2,1)S(1)}, bf16[2,128,256]{2,1,0:T(8,128)(2,1)S(1)}, u32[]{:S(2)}, u32[]{:S(2)}) %collective-permute-start.16) | collective-permute-done | bytes 131104 | tf_op jit(solution)/shard_map/ppermute | solution.py:168
  160.7 3.0 %collective-permute-done.17 = bf16[2,128,256]{2,1,0:T(8,128)(2,1)S(1)} collective-permute-done((bf16[2,128,256]{2,1,0:T(8,128)(2,1)S(1)}, bf16[2,128,256]{2,1,0:T(8,128)(2,1)S(1)}, u32[]{:S(2)}, u32[]{:S(2)}) %collective-permute-start.17) | collective-permute-done | bytes 131104 | tf_op jit(solution)/shard_map/ppermute | solution.py:168
  163.7 0.7 copy-done.6
  (81 shorter events, 4.6 us)
Async XLA Ops:
  0.6 3.8 %copy-start.3 = (bf16[128,4096]{1,0:T(8,128)(2,1)S(1)}, bf16[128,4096]{1,0:T(8,128)(2,1)}, u32[]{:S(2)}) copy-start(bf16[128,4096]{1,0:T(8,128)(2,1)} %param.8) | copy-start | bytes 3145732
  1.9 6.6 %collective-permute-start.3 = (bf16[2,128,256]{2,1,0:T(8,128)(2,1)S(1)}, bf16[2,128,256]{2,1,0:T(8,128)(2,1)S(1)}, u32[]{:S(2)}, u32[]{:S(2)}) collective-permute-start(bf16[2,128,256]{2,1,0:T(8,128)(2,1)S(1)} %pad_maximum_fusion.5), channel_id=1, source_target_pairs={{0,1},{1,0},{2,3},{3,2},{4,5},{5,4},{6,7},{7,6},{8,9},{9,8},{10,11... | collective-permute-start | bytes 393224 | tf_op jit(solution)/shard_map/ppermute | solution.py:168
  2.7 6.5 %collective-permute-start.4 = (bf16[2,128,256]{2,1,0:T(8,128)(2,1)S(1)}, bf16[2,128,256]{2,1,0:T(8,128)(2,1)S(1)}, u32[]{:S(2)}, u32[]{:S(2)}) collective-permute-start(bf16[2,128,256]{2,1,0:T(8,128)(2,1)S(1)} %pad_maximum_fusion.6), channel_id=1, source_target_pairs={{0,2},{1,3},{2,0},{3,1},{4,6},{5,7},{6,4},{7,5},{8,10},{9,11},{10,... | collective-permute-start | bytes 393224 | tf_op jit(solution)/shard_map/ppermute | solution.py:168
  4.0 7.6 %collective-permute-start.5 = (bf16[2,128,256]{2,1,0:T(8,128)(2,1)S(1)}, bf16[2,128,256]{2,1,0:T(8,128)(2,1)S(1)}, u32[]{:S(2)}, u32[]{:S(2)}) collective-permute-start(bf16[2,128,256]{2,1,0:T(8,128)(2,1)S(1)} %pad_maximum_fusion.7), channel_id=1, source_target_pairs={{0,3},{1,2},{2,1},{3,0},{4,7},{5,6},{6,5},{7,4},{8,11},{9,10},{10,... | collective-permute-start | bytes 393224 | tf_op jit(solution)/shard_map/ppermute | solution.py:168
  5.9 2.3 %copy-start.8 = (s32[2048]{0:T(1024)S(1)}, s32[2048]{0:T(1024)}, u32[]{:S(2)}) copy-start(s32[2048]{0:T(1024)} %param.9) | copy-start | bytes 24580
  6.0 16.7 %collective-permute-start.2 = (bf16[2,128,1024]{2,1,0:T(8,128)(2,1)S(1)}, bf16[2,128,1024]{2,1,0:T(8,128)(2,1)}, u32[]{:S(2)}, u32[]{:S(2)}) collective-permute-start(bf16[2,128,1024]{2,1,0:T(8,128)(2,1)S(1)} %pad_maximum_fusion.3), channel_id=1, source_target_pairs={{0,3},{1,2},{2,1},{3,0},{4,7},{5,6},{6,5},{7,4},{8,11},{9,10},{10,... | collective-permute-start | bytes 1572872 | tf_op jit(solution)/shard_map/ppermute | solution.py:168
  7.4 25.8 %collective-permute-start.1 = (bf16[2,128,1024]{2,1,0:T(8,128)(2,1)S(1)}, bf16[2,128,1024]{2,1,0:T(8,128)(2,1)}, u32[]{:S(2)}, u32[]{:S(2)}) collective-permute-start(bf16[2,128,1024]{2,1,0:T(8,128)(2,1)S(1)} %pad_maximum_fusion.2), channel_id=1, source_target_pairs={{0,2},{1,3},{2,0},{3,1},{4,6},{5,7},{6,4},{7,5},{8,10},{9,11},{10,... | collective-permute-start | bytes 1572872 | tf_op jit(solution)/shard_map/ppermute | solution.py:168
  8.5 24.7 %collective-permute-start = (bf16[2,128,1024]{2,1,0:T(8,128)(2,1)S(1)}, bf16[2,128,1024]{2,1,0:T(8,128)(2,1)}, u32[]{:S(2)}, u32[]{:S(2)}) collective-permute-start(bf16[2,128,1024]{2,1,0:T(8,128)(2,1)S(1)} %pad_maximum_fusion.1), channel_id=1, source_target_pairs={{0,1},{1,0},{2,3},{3,2},{4,5},{5,4},{6,7},{7,6},{8,9},{9,8},{10,11... | collective-permute-start | bytes 1572872 | tf_op jit(solution)/shard_map/ppermute | solution.py:168
  11.6 49.6 %copy-start.5 = (bf16[4,2,128,256]{3,2,1,0:T(8,128)(2,1)}, bf16[4,2,128,256]{3,2,1,0:T(8,128)(2,1)S(1)}, u32[]{:S(2)}) copy-start(bf16[4,2,128,256]{3,2,1,0:T(8,128)(2,1)S(1)} %pad_maximum_fusion.4.refs_4_) | copy-start | bytes 1572868
  11.6 23.0 %collective-permute-start.6 = (bf16[4,2,128,256]{3,2,1,0:T(8,128)(2,1)S(1)}, bf16[4,2,128,256]{3,2,1,0:T(8,128)(2,1)S(1)}, u32[]{:S(2)}, u32[]{:S(2)}) collective-permute-start(bf16[4,2,128,256]{3,2,1,0:T(8,128)(2,1)S(1)} %pad_maximum_fusion.4.refs_4_), channel_id=1, source_target_pairs={{0,4},{1,5},{2,6},{3,7},{4,0},{5,1},{6,2},{7,3},{8,12},{9,13},{10,... | collective-permute-start | bytes 1572872 | tf_op jit(solution)/shard_map/ppermute | solution.py:168
  13.0 23.8 %collective-permute-start.7 = (bf16[4,2,128,256]{3,2,1,0:T(8,128)(2,1)S(1)}, bf16[4,2,128,256]{3,2,1,0:T(8,128)(2,1)}, u32[]{:S(2)}, u32[]{:S(2)}) collective-permute-start(bf16[4,2,128,256]{3,2,1,0:T(8,128)(2,1)S(1)} %pad_maximum_fusion.4.refs_4_), channel_id=1, source_target_pairs={{0,8},{1,9},{2,10},{3,11},{4,12},{5,13},{6,14},{7,15},{8,0},{9,1},... | collective-permute-start | bytes 1572872 | tf_op jit(solution)/shard_map/ppermute | solution.py:168
  22.7 37.8 %collective-permute-start.8 = (bf16[4,2,128,256]{3,2,1,0:T(8,128)(2,1)S(1)}, bf16[4,2,128,256]{3,2,1,0:T(8,128)(2,1)}, u32[]{:S(2)}, u32[]{:S(2)}) collective-permute-start(bf16[4,2,128,256]{3,2,1,0:T(8,128)(2,1)S(1)} %pad_maximum_fusion.4.refs_4_), channel_id=1, source_target_pairs={{0,12},{1,13},{2,14},{3,15},{4,8},{5,9},{6,10},{7,11},{8,4},{9,5},... | collective-permute-start | bytes 1572872 | tf_op jit(solution)/shard_map/ppermute | solution.py:168
  34.7 26.5 %copy-start.10 = (bf16[4,2,128,256]{3,2,1,0:T(8,128)(2,1)}, bf16[4,2,128,256]{3,2,1,0:T(8,128)(2,1)S(1)}, u32[]{:S(2)}) copy-start(bf16[4,2,128,256]{3,2,1,0:T(8,128)(2,1)S(1)} %collective-permute-done.6.refs_5_) | copy-start | bytes 1572868
  105.6 5.5 %copy-start.4 = (bf16[2,128,1024]{2,1,0:T(8,128)(2,1)S(1)}, bf16[2,128,1024]{2,1,0:T(8,128)(2,1)}, u32[]{:S(2)}) copy-start(bf16[2,128,1024]{2,1,0:T(8,128)(2,1)} %get-tuple-element.12) | copy-start | bytes 1572868
  105.6 21.3 %collective-permute-start.12 = (bf16[4,2,128,256]{3,2,1,0:T(8,128)(2,1)}, bf16[4,2,128,256]{3,2,1,0:T(8,128)(2,1)S(1)}, u32[]{:S(2)}, u32[]{:S(2)}) collective-permute-start(bf16[4,2,128,256]{3,2,1,0:T(8,128)(2,1)} %get-tuple-element.17), channel_id=1, source_target_pairs={{0,4},{1,5},{2,6},{3,7},{4,0},{5,1},{6,2},{7,3},{8,12},{9,13},{10,... | collective-permute-start | bytes 1572872 | tf_op jit(solution)/shard_map/ppermute | solution.py:168
  105.7 24.2 %collective-permute-start.13 = (bf16[4,2,128,256]{3,2,1,0:T(8,128)(2,1)}, bf16[4,2,128,256]{3,2,1,0:T(8,128)(2,1)S(1)}, u32[]{:S(2)}, u32[]{:S(2)}) collective-permute-start(bf16[4,2,128,256]{3,2,1,0:T(8,128)(2,1)} %get-tuple-element.18), channel_id=1, source_target_pairs={{0,8},{1,9},{2,10},{3,11},{4,12},{5,13},{6,14},{7,15},{8,0},{9,1},... | collective-permute-start | bytes 1572872 | tf_op jit(solution)/shard_map/ppermute | solution.py:168
  107.0 46.4 %collective-permute-start.14 = (bf16[4,2,128,256]{3,2,1,0:T(8,128)(2,1)}, bf16[4,2,128,256]{3,2,1,0:T(8,128)(2,1)S(1)}, u32[]{:S(2)}, u32[]{:S(2)}) collective-permute-start(bf16[4,2,128,256]{3,2,1,0:T(8,128)(2,1)} %get-tuple-element.19), channel_id=1, source_target_pairs={{0,12},{1,13},{2,14},{3,15},{4,8},{5,9},{6,10},{7,11},{8,4},{9,5},... | collective-permute-start | bytes 1572872 | tf_op jit(solution)/shard_map/ppermute | solution.py:168
  108.3 48.5 %collective-permute-start.9 = (bf16[2,128,1024]{2,1,0:T(8,128)(2,1)}, bf16[2,128,1024]{2,1,0:T(8,128)(2,1)S(1)}, u32[]{:S(2)}, u32[]{:S(2)}) collective-permute-start(bf16[2,128,1024]{2,1,0:T(8,128)(2,1)} %get-tuple-element.13), channel_id=1, source_target_pairs={{0,1},{1,0},{2,3},{3,2},{4,5},{5,4},{6,7},{7,6},{8,9},{9,8},{10,11... | collective-permute-start | bytes 1572872 | tf_op jit(solution)/shard_map/ppermute | solution.py:168
  109.8 47.6 %collective-permute-start.10 = (bf16[2,128,1024]{2,1,0:T(8,128)(2,1)}, bf16[2,128,1024]{2,1,0:T(8,128)(2,1)S(1)}, u32[]{:S(2)}, u32[]{:S(2)}) collective-permute-start(bf16[2,128,1024]{2,1,0:T(8,128)(2,1)} %get-tuple-element.14), channel_id=1, source_target_pairs={{0,2},{1,3},{2,0},{3,1},{4,6},{5,7},{6,4},{7,5},{8,10},{9,11},{10,... | collective-permute-start | bytes 1572872 | tf_op jit(solution)/shard_map/ppermute | solution.py:168
  111.1 15.8 %copy-start.9 = (bf16[2,128,1024]{2,1,0:T(8,128)(2,1)S(1)}, bf16[2,128,1024]{2,1,0:T(8,128)(2,1)}, u32[]{:S(2)}) copy-start(bf16[2,128,1024]{2,1,0:T(8,128)(2,1)} %get-tuple-element.15) | copy-start | bytes 1572868
  111.1 42.3 %copy-start = (f32[4,2,128,256]{3,2,1,0:T(8,128)S(1)}, f32[4,2,128,256]{3,2,1,0:T(8,128)}, u32[]{:S(2)}) copy-start(f32[4,2,128,256]{3,2,1,0:T(8,128)} %get-tuple-element.16) | copy-start | bytes 3145732
  126.9 30.5 %collective-permute-start.11 = (bf16[2,128,1024]{2,1,0:T(8,128)(2,1)S(1)}, bf16[2,128,1024]{2,1,0:T(8,128)(2,1)S(1)}, u32[]{:S(2)}, u32[]{:S(2)}) collective-permute-start(bf16[2,128,1024]{2,1,0:T(8,128)(2,1)S(1)} %copy-done.9), channel_id=1, source_target_pairs={{0,3},{1,2},{2,1},{3,0},{4,7},{5,6},{6,5},{7,4},{8,11},{9,10},{10,... | collective-permute-start | bytes 1572872 | tf_op jit(solution)/shard_map/ppermute | solution.py:168
  153.8 3.8 %collective-permute-start.15 = (bf16[2,128,256]{2,1,0:T(8,128)(2,1)S(1)}, bf16[2,128,256]{2,1,0:T(8,128)(2,1)S(1)}, u32[]{:S(2)}, u32[]{:S(2)}) collective-permute-start(bf16[2,128,256]{2,1,0:T(8,128)(2,1)S(1)} %get-tuple-element.30), channel_id=1, source_target_pairs={{0,1},{1,0},{2,3},{3,2},{4,5},{5,4},{6,7},{7,6},{8,9},{9,8},{10,11... | collective-permute-start | bytes 393224 | tf_op jit(solution)/shard_map/ppermute | solution.py:168
  155.6 5.1 %collective-permute-start.16 = (bf16[2,128,256]{2,1,0:T(8,128)(2,1)S(1)}, bf16[2,128,256]{2,1,0:T(8,128)(2,1)S(1)}, u32[]{:S(2)}, u32[]{:S(2)}) collective-permute-start(bf16[2,128,256]{2,1,0:T(8,128)(2,1)S(1)} %get-tuple-element.29), channel_id=1, source_target_pairs={{0,2},{1,3},{2,0},{3,1},{4,6},{5,7},{6,4},{7,5},{8,10},{9,11},{10,... | collective-permute-start | bytes 393224 | tf_op jit(solution)/shard_map/ppermute | solution.py:168
  156.8 6.8 %collective-permute-start.17 = (bf16[2,128,256]{2,1,0:T(8,128)(2,1)S(1)}, bf16[2,128,256]{2,1,0:T(8,128)(2,1)S(1)}, u32[]{:S(2)}, u32[]{:S(2)}) collective-permute-start(bf16[2,128,256]{2,1,0:T(8,128)(2,1)S(1)} %get-tuple-element.28), channel_id=1, source_target_pairs={{0,3},{1,2},{2,1},{3,0},{4,7},{5,6},{6,5},{7,4},{8,11},{9,10},{10,... | collective-permute-start | bytes 393224 | tf_op jit(solution)/shard_map/ppermute | solution.py:168
  157.5 6.2 %copy-start.1 = (bf16[128,4096]{1,0:T(8,128)(2,1)}, bf16[128,4096]{1,0:T(8,128)(2,1)S(1)}, u32[]{:S(2)}) copy-start(bf16[128,4096]{1,0:T(8,128)(2,1)S(1)} %get-tuple-element.31) | copy-start | bytes 3145732
  157.5 6.2 %copy-start.2 = (bf16[128,4096]{1,0:T(8,128)(2,1)}, bf16[128,4096]{1,0:T(8,128)(2,1)S(1)}, u32[]{:S(2)}) copy-start(bf16[128,4096]{1,0:T(8,128)(2,1)S(1)} %get-tuple-element.32) | copy-start | bytes 3145732
  163.7 0.7 copy-start.6
  163.7 0.8 copy-start.7

commit v2 on v1

v2 whole, which is shorter than its diff:
```python
import functools
import math

import jax
import jax.numpy as jnp
from jax import lax
from jax.experimental import pallas as pl
from jax.experimental.pallas import tpu as pltpu
from jax.sharding import PartitionSpec as P

H = 32
KV = 8
HD = 128
MOST = 1024
GROUP = H // KV
KR = 16
F32 = jnp.float32
BF16 = jnp.bfloat16
SCALE = 1.0 / math.sqrt(HD)
EXP2_SCALE = SCALE * math.log2(math.e)


def query_rows(lanes):
    return max(16, 128 // lanes)


def attend_kernel(head, lanes, depth, start_ref, begin_ref, place_ref, key_place_ref, *refs):
    refs = list(refs)
    take = lambda count: [refs.pop(0) for _ in range(count)]
    query_refs, kv_refs = take(lanes), take(depth)
    out_refs, grad_refs = take(lanes), take(depth)
    key_turned, value_turned, key_sum, value_sum, score_ref, out_sum, query_sum = refs
    rows = query_refs[0].shape[1]
    turn_rows = query_rows(lanes)
    key_tiles, query_tiles = rows // KR, rows // turn_rows
    tile = depth * lanes * KR
    span = lanes * GROUP * turn_rows

    def keys_of(which, step):
        at = pl.ds(pl.multiple_of(step * KR, KR), KR)
        return jnp.concatenate(
            [ref[:, which, at, :].reshape(lanes * KR, HD) for ref in kv_refs], axis=0
        )

    def queries_of(which, step):
        at = pl.ds(pl.multiple_of(step * turn_rows, turn_rows), turn_rows)
        return jnp.concatenate(
            [
                ref[which, at, (head * GROUP + j) * HD : (head * GROUP + j + 1) * HD]
                for j in range(GROUP)
                for ref in query_refs
            ],
            axis=0,
        )

    def put_queries(which, step, value):
        at = pl.ds(pl.multiple_of(step * turn_rows, turn_rows), turn_rows)
        for j in range(GROUP):
            for lane, ref in enumerate(out_refs):
                low = (j * lanes + lane) * turn_rows
                ref[which, at, j * HD : (j + 1) * HD] = value[low : low + turn_rows]

    @pl.loop(0, key_tiles)
    def _(step):
        key_turned[step] = keys_of(0, step).T
        value_turned[step] = keys_of(1, step).T
        key_sum[step] = jnp.zeros((tile, HD), F32)
        value_sum[step] = jnp.zeros((tile, HD), F32)

    @pl.loop(0, query_tiles)
    def _(turn):
        query, grad = queries_of(0, turn), queries_of(1, turn)
        query_t, grad_t = query.T, grad.T
        first = start_ref[turn]
        last = (turn + 1) * (turn_rows // KR)
        begin, place = begin_ref[turn], place_ref[turn]

        def solve(count):
            tops = jnp.full((8, span), -1e30, F32)
            steps = [last - count + i for i in range(count)]
            key_place = jnp.concatenate([key_place_ref[...]] * (span // 128), axis=1)
            for i, step in enumerate(steps):
                base = step * tile
                value = jnp.dot(keys_of(0, step), query_t, preferred_element_type=F32)
                allowed = key_place >= begin - base
                if i >= count - turn_rows // KR:
                    allowed = allowed & (key_place <= place - base)
                value = jnp.where(allowed, value, -1e30)
                score_ref[i] = value
                tops = jnp.maximum(tops, value.reshape(tile // 8, 8, span).max(axis=0))
            top = jnp.max(tops, axis=0, keepdims=True) * EXP2_SCALE
            total = jnp.zeros((8, span), F32)
            out_t = jnp.zeros((HD, span), F32)
            for i, step in enumerate(steps):
                weight = jnp.exp2(score_ref[i] * EXP2_SCALE - top)
                score_ref[i] = weight
                out_t += jnp.dot(
                    value_turned[step], weight.astype(BF16), preferred_element_type=F32
                )
                total += weight.reshape(tile // 8, 8, span).sum(axis=0)
            inverse = 1.0 / jnp.sum(total, axis=0, keepdims=True)
            out_t = (out_t * inverse).astype(BF16).astype(F32)
            delta = jnp.sum(out_t * grad_t.astype(F32), axis=0, keepdims=True)
            put_queries(0, turn, out_t.T.astype(BF16))
            query_total = jnp.zeros((HD, span), F32)
            for i, step in enumerate(steps):
                prob = score_ref[i] * inverse
                value_sum[step] += jnp.dot(prob.astype(BF16), grad, preferred_element_type=F32)
                grad_prob = jnp.dot(keys_of(1, step), grad_t, preferred_element_type=F32)
                grad_score = (prob * (grad_prob - delta)).astype(BF16)
                key_sum[step] += jnp.dot(grad_score, query, preferred_element_type=F32)
                query_total += jnp.dot(
                    key_turned[step], grad_score, preferred_element_type=F32
                )
            put_queries(1, turn, (query_total * SCALE).T.astype(BF16))

        for count in range(1, score_ref.shape[0] + 1):

            @pl.when(last - first == count)
            def _():
                solve(count)

    @pl.loop(0, key_tiles)
    def _(step):
        at = pl.ds(pl.multiple_of(step * KR, KR), KR)
        for which, total, factor in ((0, key_sum, SCALE), (1, value_sum, 1.0)):
            for k, ref in enumerate(grad_refs):
                low = k * lanes * KR
                part = total[step, low : low + lanes * KR, :] * factor
                ref[:, which, at, :] = part.astype(ref.dtype).reshape(lanes, KR, HD)


def attend(head, query_parts, kv_parts, starts, begins, places, key_places):
    lanes, depth = len(query_parts), len(kv_parts)
    rows = query_parts[0].shape[1]
    turn_rows = query_rows(lanes)
    tile, span = depth * lanes * KR, lanes * GROUP * turn_rows
    key_tiles = rows // KR
    reach = turn_rows // KR + -(-(MOST - 1) // tile)
    vmem = pl.BlockSpec(memory_space=pltpu.VMEM)
    pairs = GROUP * rows * lanes * 640
    return pl.pallas_call(
        functools.partial(attend_kernel, head, lanes, depth),
        out_shape=[jax.ShapeDtypeStruct((2, rows, GROUP * HD), BF16)] * lanes
        + [
            jax.ShapeDtypeStruct(part.shape, F32 if k == 0 or (k == 2 and depth == 4) else BF16)
            for k, part in enumerate(kv_parts)
        ],
        in_specs=[pl.BlockSpec(memory_space=pltpu.SMEM)] + [vmem] * (3 + lanes + depth),
        out_specs=[vmem] * (lanes + depth),
        scratch_shapes=[
            pltpu.VMEM((key_tiles, HD, tile), BF16),
            pltpu.VMEM((key_tiles, HD, tile), BF16),
            pltpu.VMEM((key_tiles, tile, HD), F32),
            pltpu.VMEM((key_tiles, tile, HD), F32),
            pltpu.VMEM((min(reach, key_tiles), tile, span), F32),
            pltpu.VMEM((HD, span), F32),
            pltpu.VMEM((HD, span), F32),
        ],
        compiler_params=pltpu.CompilerParams(vmem_limit_bytes=(40 if depth == 4 else 62) << 20),
        cost_estimate=pl.CostEstimate(
            flops=10 * HD * pairs, bytes_accessed=8 << 20, transcendentals=pairs
        ),
    )(starts, begins, places, key_places, *query_parts, *kv_parts)


def moved(tensor, target):
    devices = lax.axis_size("seq")
    return lax.ppermute(tensor, "seq", [(i, target(i)) for i in range(devices)])


def swapped(tensor, mask):
    return moved(tensor, lambda i: i ^ mask)


def middle_swapped(tensor, lanes):
    return moved(tensor, lambda i: i if i // lanes in (0, 3) else i ^ (3 * lanes))


def gathered(own, lanes, depth, inner):
    if depth != 4:
        return [own] + [swapped(own, k * lanes) for k in range(1, depth)]
    two = swapped(own, 2 * lanes)
    one = swapped(own, lanes)
    three = middle_swapped(own, lanes)
    passed = swapped(two, lanes)
    return [own, one, two, jnp.where(inner, three, passed)]


def summed(parts, lanes, depth, inner):
    total = parts[0]
    if depth != 4:
        for k in range(1, depth):
            total = total + swapped(parts[k].astype(BF16), k * lanes).astype(F32)
        return total.astype(BF16)
    passed = swapped(parts[3], lanes)
    one = swapped(parts[1], lanes)
    three = middle_swapped(parts[3], lanes)
    two = (parts[2] + jnp.where(inner, passed.astype(F32), 0.0)).astype(BF16)
    two = swapped(two, 2 * lanes)
    total = total + one.astype(F32) + two.astype(F32)
    return (total + jnp.where(inner, three.astype(F32), 0.0)).astype(BF16)


def on_device(queries, key_vectors, value_vectors, grad_output, document_ids):
    devices = lax.axis_size("seq")
    position = lax.axis_index("seq")
    rows = queries.shape[0]
    lanes = min(KV, devices // 4)
    depth = devices // lanes
    lane = position % lanes
    above = position - lane
    level = position // lanes
    inner = (level > 0) & (level < depth - 1)
    heads = KV // lanes
    wide, narrow = H * HD // lanes, KV * HD // lanes

    def cut(tensor, mask, width):
        return lax.dynamic_slice_in_dim(tensor, (lane ^ mask) * width, width, 1)

    def kv_cut(mask):
        both = jnp.stack([cut(key_vectors, mask, narrow), cut(value_vectors, mask, narrow)])
        return jnp.stack([both[:, :, h * HD : (h + 1) * HD] for h in range(heads)])

    def query_cut(mask):
        return jnp.stack([cut(queries, mask, wide), cut(grad_output, mask, wide)])

    kv_lanes = [kv_cut(0)] + [swapped(kv_cut(mask), mask) for mask in range(1, lanes)]
    query_parts = [query_cut(0)] + [swapped(query_cut(mask), mask) for mask in range(1, lanes)]
    kv_parts = [
        gathered(jnp.stack([part[h] for part in kv_lanes]), lanes, depth, inner)
        for h in range(heads)
    ]

    ids = document_ids.reshape(rows, devices)
    lane_masks = jnp.arange(lanes, dtype=jnp.int32)
    mine = above + (lane ^ lane_masks)
    column = jnp.arange(devices, dtype=jnp.int32)
    own_ids = jnp.sum(
        jnp.where(column[None, None, :] == mine[:, None, None], ids[None], 0), axis=-1
    )
    begin = jnp.sum(
        (document_ids[None, None, :] < own_ids[:, :, None]).astype(jnp.int32), axis=-1
    )
    place = jnp.arange(rows, dtype=jnp.int32)[None, :] * devices + mine[:, None]

    turn_rows = query_rows(lanes)

    def tiled(values):
        parts = values.reshape(lanes, rows // turn_rows, turn_rows).transpose(1, 0, 2)
        parts = parts.reshape(rows // turn_rows, 1, lanes * turn_rows)
        return jnp.tile(parts, (1, 1, GROUP))

    begins, places = tiled(begin), tiled(place)
    starts = jnp.min(begins, axis=(1, 2)) // (KR * devices)
    chunk = (jnp.arange(depth, dtype=jnp.int32) * lanes) ^ above
    key_place = (
        jnp.arange(KR, dtype=jnp.int32)[None, None, :] * devices
        + chunk[:, None, None]
        + (lane ^ lane_masks)[None, :, None]
    ).reshape(depth * lanes * KR, 1)
    key_places = jnp.broadcast_to(key_place, (depth * lanes * KR, 128))

    wholes = [jnp.zeros((rows, H * HD), BF16) for _ in range(2)]
    kv_wholes = [jnp.zeros((rows, KV * HD), BF16) for _ in range(2)]
    for h in range(heads):
        results = attend(h, query_parts, kv_parts[h], starts, begins, places, key_places)
        out_parts, grad_parts = results[:lanes], results[lanes:]
        out_back = [out_parts[0]] + [swapped(out_parts[mask], mask) for mask in range(1, lanes)]
        total = summed(grad_parts, lanes, depth, inner)
        kv_back = [total[0]] + [swapped(total[mask], mask) for mask in range(1, lanes)]
        for which in range(2):
            for mask in range(lanes):
                owner = lane ^ mask
                wholes[which] = lax.dynamic_update_slice_in_dim(
                    wholes[which], out_back[mask][which], owner * wide + h * GROUP * HD, 1
                )
                kv_wholes[which] = lax.dynamic_update_slice_in_dim(
                    kv_wholes[which], kv_back[mask][which], owner * narrow + h * HD, 1
                )
    return (wholes[0], wholes[1], kv_wholes[0], kv_wholes[1])


def solution(mesh):
    placed = P(("group", "seq"), None)
    return jax.shard_map(
        on_device,
        mesh=mesh,
        in_specs=(placed, placed, placed, placed, P("group")),
        out_specs=(placed, placed, placed, placed),
        check_vma=False,
    )
```

time: 163 us -> 145 us (0.89)
  the two profiles are of different devices: /device:TPU:17 before, /device:TPU:0 now
where the time goes in v2:
time: 145 us; the launch traced here: 143 us
  waiting for transfers between devices  69 us (48%)
  starting transfers between devices  39.6 us (27%)
  Pallas kernels  19.1 us (13%)
  other arithmetic  7.36 us (5%)
  local copies, waits for them, and re-layouts  6.5 us (4%)
    ppermute x34, waiting for transfers between devices, moved(): return lax.ppermute(tensor, 'seq', [(i, target(i)) for i in range(devices)])  69 us
    ppermute x34, starting transfers between devices, moved(): return lax.ppermute(tensor, 'seq', [(i, target(i)) for i in range(devices)])  39.6 us
    pallas_call x2, Pallas kernels, attend(): pl.pallas_call(functools.partial(attend_kernel, head, lanes, depth), out_...  19.1 us
  transfers between devices with their start and end apart: 34, of which 11 were waited for; matrix products, arithmetic and copies ran while one was open for 8% of the time, Pallas kernels for 13%

profile of v2, /device:TPU:0, one launch (start us, length us, event | category | flops | bytes accessed | tf_op | source)
XLA Modules:
  0.0 142.9 jit_solution(2168479223235248167)
XLA Ops:
  0.7 1.2 dynamic-slice_bitcast_fusion.14
  3.7 2.5 %collective-permute-start.4 = (bf16[2,2,128,128]{3,2,1,0:T(8,128)(2,1)}, bf16[2,2,128,128]{3,2,1,0:T(8,128)(2,1)}, u32[]{:S(2)}, u32[]{:S(2)}) collective-permute-start(bf16[2,2,128,128]{3,2,1,0:T(8,128)(2,1)} %pad_maximum_fusion.7), channel_id=1, source_target_pairs={{0,2},{1,3},{2,0},{3,1},{4,6},{5,7},{6,4},{7,5},{8,10},{9,11},{10,... | collective-permute-start | bytes 393224 | tf_op jit(solution)/shard_map/ppermute | solution.py:169
  7.0 0.9 dynamic-slice_bitcast_fusion
  8.0 0.9 pad_maximum_fusion.3
  8.8 1.6 %collective-permute-start.2 = (bf16[2,128,1024]{2,1,0:T(8,128)(2,1)}, bf16[2,128,1024]{2,1,0:T(8,128)(2,1)S(1)}, u32[]{:S(2)}, u32[]{:S(2)}) collective-permute-start(bf16[2,128,1024]{2,1,0:T(8,128)(2,1)} %pad_maximum_fusion.3), channel_id=1, source_target_pairs={{0,3},{1,2},{2,1},{3,0},{4,7},{5,6},{6,5},{7,4},{8,11},{9,10},{10,... | collective-permute-start | bytes 1572872 | tf_op jit(solution)/shard_map/ppermute | solution.py:169
  13.4 0.9 fusion.41
  14.3 0.9 fusion.42
  15.3 3.0 %collective-permute-start.14 = (bf16[4,2,128,128]{3,2,1,0:T(8,128)(2,1)S(1)}, bf16[4,2,128,128]{3,2,1,0:T(8,128)(2,1)S(1)}, u32[]{:S(2)}, u32[]{:S(2)}) collective-permute-start(bf16[4,2,128,128]{3,2,1,0:T(8,128)(2,1)S(1)} %pad_maximum_fusion.5.refs_4_), channel_id=1, source_target_pairs={{0,8},{1,9},{2,10},{3,11},{4,12},{5,13},{6,14},{7,15},{8,0},{9,1},... | collective-permute-start | bytes 786440 | tf_op jit(solution)/shard_map/ppermute | solution.py:169
  18.3 1.3 collective-permute-start.15
  19.6 2.2 %collective-permute-start.13 = (bf16[4,2,128,128]{3,2,1,0:T(8,128)(2,1)S(1)}, bf16[4,2,128,128]{3,2,1,0:T(8,128)(2,1)S(1)}, u32[]{:S(2)}, u32[]{:S(2)}) collective-permute-start(bf16[4,2,128,128]{3,2,1,0:T(8,128)(2,1)S(1)} %pad_maximum_fusion.5.refs_4_), channel_id=1, source_target_pairs={{0,4},{1,5},{2,6},{3,7},{4,0},{5,1},{6,2},{7,3},{8,12},{9,13},{10,... | collective-permute-start | bytes 786440 | tf_op jit(solution)/shard_map/ppermute | solution.py:169
  22.8 8.3 %collective-permute-done.14.refs_6_ = bf16[4,2,128,128]{3,2,1,0:T(8,128)(2,1)S(1)} collective-permute-done((bf16[4,2,128,128]{3,2,1,0:T(8,128)(2,1)S(1)}, bf16[4,2,128,128]{3,2,1,0:T(8,128)(2,1)S(1)}, u32[]{:S(2)}, u32[]{:S(2)}) %collective-permute-start.14) | collective-permute-done | bytes 262176 | tf_op jit(solution)/shard_map/ppermute | solution.py:169
  31.1 7.7 %collective-permute-start.7 = (bf16[4,2,128,128]{3,2,1,0:T(8,128)(2,1)S(1)}, bf16[4,2,128,128]{3,2,1,0:T(8,128)(2,1)S(1)}, u32[]{:S(2)}, u32[]{:S(2)}) collective-permute-start(bf16[4,2,128,128]{3,2,1,0:T(8,128)(2,1)S(1)} %pad_maximum_fusion.4.refs_4_), channel_id=1, source_target_pairs={{0,8},{1,9},{2,10},{3,11},{4,12},{5,13},{6,14},{7,15},{8,0},{9,1},... | collective-permute-start | bytes 786440 | tf_op jit(solution)/shard_map/ppermute | solution.py:169
  39.1 11.8 %collective-permute-done.7.refs_6_ = bf16[4,2,128,128]{3,2,1,0:T(8,128)(2,1)S(1)} collective-permute-done((bf16[4,2,128,128]{3,2,1,0:T(8,128)(2,1)S(1)}, bf16[4,2,128,128]{3,2,1,0:T(8,128)(2,1)S(1)}, u32[]{:S(2)}, u32[]{:S(2)}) %collective-permute-start.7) | collective-permute-done | bytes 262176 | tf_op jit(solution)/shard_map/ppermute | solution.py:169
  53.0 1.0 broadcast_select_fusion.refs_7_
  54.0 1.4 collective-permute-start.6
  55.5 9.4 %shard_map.85 = (bf16[2,128,512]{2,1,0:T(8,128)(2,1)S(1)}, bf16[2,128,512]{2,1,0:T(8,128)(2,1)S(1)}, bf16[2,128,512]{2,1,0:T(8,128)(2,1)S(1)}, bf16[2,128,512]{2...) custom-call(s32[4]{0:T(128)S(1)} %and_select_fusion.start_ref, ...), custom_call_target="tpu_custom_call" | custom-call | flops 1677721600 | bytes 8388608 | tf_op jit(solution)/shard_map/pallas_call | solution.py:142
  66.4 9.7 %shard_map.84 = (bf16[2,128,512]{2,1,0:T(8,128)(2,1)S(1)}, bf16[2,128,512]{2,1,0:T(8,128)(2,1)S(1)}, bf16[2,128,512]{2,1,0:T(8,128)(2,1)S(1)}, bf16[2,128,512]{2...) custom-call(s32[4]{0:T(128)S(1)} %and_select_fusion.start_ref, ...), custom_call_target="tpu_custom_call" | custom-call | flops 1677721600 | bytes 8388608 | tf_op jit(solution)/shard_map/pallas_call | solution.py:142
  76.1 2.6 %collective-permute-start.21 = (bf16[4,2,128,128]{3,2,1,0:T(8,128)(2,1)S(1)}, bf16[4,2,128,128]{3,2,1,0:T(8,128)(2,1)S(1)}, u32[]{:S(2)}, u32[]{:S(2)}) collective-permute-start(bf16[4,2,128,128]{3,2,1,0:T(8,128)(2,1)S(1)} %get-tuple-element.31), channel_id=1, source_target_pairs={{0,4},{1,5},{2,6},{3,7},{4,0},{5,1},{6,2},{7,3},{8,12},{9,13},{10,... | collective-permute-start | bytes 786440 | tf_op jit(solution)/shard_map/ppermute | solution.py:169
  78.7 1.5 %collective-permute-start.11 = (bf16[2,128,512]{2,1,0:T(8,128)(2,1)S(1)}, bf16[2,128,512]{2,1,0:T(8,128)(2,1)S(1)}, u32[]{:S(2)}, u32[]{:S(2)}) collective-permute-start(bf16[2,128,512]{2,1,0:T(8,128)(2,1)S(1)} %get-tuple-element.22), channel_id=1, source_target_pairs={{0,2},{1,3},{2,0},{3,1},{4,6},{5,7},{6,4},{7,5},{8,10},{9,11},{10,... | collective-permute-start | bytes 786440 | tf_op jit(solution)/shard_map/ppermute | solution.py:169
  81.2 6.2 %collective-permute-done.11 = bf16[2,128,512]{2,1,0:T(8,128)(2,1)S(1)} collective-permute-done((bf16[2,128,512]{2,1,0:T(8,128)(2,1)S(1)}, bf16[2,128,512]{2,1,0:T(8,128)(2,1)S(1)}, u32[]{:S(2)}, u32[]{:S(2)}) %collective-permute-start.11) | collective-permute-done | bytes 262176 | tf_op jit(solution)/shard_map/ppermute | solution.py:169
  89.3 6.8 %collective-permute-done.12 = bf16[2,128,512]{2,1,0:T(8,128)(2,1)S(1)} collective-permute-done((bf16[2,128,512]{2,1,0:T(8,128)(2,1)S(1)}, bf16[2,128,512]{2,1,0:T(8,128)(2,1)S(1)}, u32[]{:S(2)}, u32[]{:S(2)}) %collective-permute-start.12) | collective-permute-done | bytes 262176 | tf_op jit(solution)/shard_map/ppermute | solution.py:169
  96.0 1.5 %collective-permute-start.18 = (bf16[2,128,512]{2,1,0:T(8,128)(2,1)S(1)}, bf16[2,128,512]{2,1,0:T(8,128)(2,1)S(1)}, u32[]{:S(2)}, u32[]{:S(2)}) collective-permute-start(bf16[2,128,512]{2,1,0:T(8,128)(2,1)S(1)} %get-tuple-element.26), channel_id=1, source_target_pairs={{0,2},{1,3},{2,0},{3,1},{4,6},{5,7},{6,4},{7,5},{8,10},{9,11},{10,... | collective-permute-start | bytes 786440 | tf_op jit(solution)/shard_map/ppermute | solution.py:169
  97.7 7.5 %collective-permute-done.18 = bf16[2,128,512]{2,1,0:T(8,128)(2,1)S(1)} collective-permute-done((bf16[2,128,512]{2,1,0:T(8,128)(2,1)S(1)}, bf16[2,128,512]{2,1,0:T(8,128)(2,1)S(1)}, u32[]{:S(2)}, u32[]{:S(2)}) %collective-permute-start.18) | collective-permute-done | bytes 262176 | tf_op jit(solution)/shard_map/ppermute | solution.py:169
  105.3 3.8 %collective-permute-done.19 = bf16[2,128,512]{2,1,0:T(8,128)(2,1)S(1)} collective-permute-done((bf16[2,128,512]{2,1,0:T(8,128)(2,1)S(1)}, bf16[2,128,512]{2,1,0:T(8,128)(2,1)S(1)}, u32[]{:S(2)}, u32[]{:S(2)}) %collective-permute-start.19) | collective-permute-done | bytes 262176 | tf_op jit(solution)/shard_map/ppermute | solution.py:169
  109.1 1.5 %collective-permute-start.22 = (bf16[4,2,128,128]{3,2,1,0:T(8,128)(2,1)S(1)}, bf16[4,2,128,128]{3,2,1,0:T(8,128)(2,1)S(1)}, u32[]{:S(2)}, u32[]{:S(2)}) collective-permute-start(bf16[4,2,128,128]{3,2,1,0:T(8,128)(2,1)S(1)} %add_convert_fusion.3), channel_id=1, source_target_pairs={{0,8},{1,9},{2,10},{3,11},{4,12},{5,13},{6,14},{7,15},{8,0},{9,1},... | collective-permute-start | bytes 786440 | tf_op jit(solution)/shard_map/ppermute | solution.py:169
  110.7 2.0 %collective-permute-start.27 = (bf16[4,2,128,128]{3,2,1,0:T(8,128)(2,1)S(1)}, bf16[4,2,128,128]{3,2,1,0:T(8,128)(2,1)S(1)}, u32[]{:S(2)}, u32[]{:S(2)}) collective-permute-start(bf16[4,2,128,128]{3,2,1,0:T(8,128)(2,1)S(1)} %get-tuple-element.33), channel_id=1, source_target_pairs={{0,4},{1,5},{2,6},{3,7},{4,0},{5,1},{6,2},{7,3},{8,12},{9,13},{10,... | collective-permute-start | bytes 786440 | tf_op jit(solution)/shard_map/ppermute | solution.py:169
  113.6 11.5 %collective-permute-done.22 = bf16[4,2,128,128]{3,2,1,0:T(8,128)(2,1)S(1)} collective-permute-done((bf16[4,2,128,128]{3,2,1,0:T(8,128)(2,1)S(1)}, bf16[4,2,128,128]{3,2,1,0:T(8,128)(2,1)S(1)}, u32[]{:S(2)}, u32[]{:S(2)}) %collective-permute-start.22) | collective-permute-done | bytes 262176 | tf_op jit(solution)/shard_map/ppermute | solution.py:169
  125.5 1.3 collective-permute-start.25
  127.4 8.7 %collective-permute-done.29 = bf16[4,2,128,128]{3,2,1,0:T(8,128)(2,1)S(1)} collective-permute-done((bf16[4,2,128,128]{3,2,1,0:T(8,128)(2,1)S(1)}, bf16[4,2,128,128]{3,2,1,0:T(8,128)(2,1)S(1)}, u32[]{:S(2)}, u32[]{:S(2)}) %collective-permute-start.29) | collective-permute-done | bytes 262176 | tf_op jit(solution)/shard_map/ppermute | solution.py:169
  136.4 1.3 collective-permute-start.32
  138.4 2.6 %collective-permute-done.32 = bf16[2,128,128]{2,1,0:T(8,128)(2,1)S(1)} collective-permute-done((bf16[2,128,128]{2,1,0:T(8,128)(2,1)S(1)}, bf16[2,128,128]{2,1,0:T(8,128)(2,1)S(1)}, u32[]{:S(2)}, u32[]{:S(2)}) %collective-permute-start.32) | collective-permute-done | bytes 65568 | tf_op jit(solution)/shard_map/ppermute | solution.py:169
  141.0 1.1 collective-permute-done.33
  (131 shorter events, 17.0 us)
Async XLA Ops:
  2.6 10.8 %collective-permute-start.3 = (bf16[2,2,128,128]{3,2,1,0:T(8,128)(2,1)}, bf16[2,2,128,128]{3,2,1,0:T(8,128)(2,1)S(1)}, u32[]{:S(2)}, u32[]{:S(2)}) collective-permute-start(bf16[2,2,128,128]{3,2,1,0:T(8,128)(2,1)} %pad_maximum_fusion.6), channel_id=1, source_target_pairs={{0,1},{1,0},{2,3},{3,2},{4,5},{5,4},{6,7},{7,6},{8,9},{9,8},{10,11... | collective-permute-start | bytes 393224 | tf_op jit(solution)/shard_map/ppermute | solution.py:169
  3.7 9.7 %collective-permute-start.4 = (bf16[2,2,128,128]{3,2,1,0:T(8,128)(2,1)}, bf16[2,2,128,128]{3,2,1,0:T(8,128)(2,1)}, u32[]{:S(2)}, u32[]{:S(2)}) collective-permute-start(bf16[2,2,128,128]{3,2,1,0:T(8,128)(2,1)} %pad_maximum_fusion.7), channel_id=1, source_target_pairs={{0,2},{1,3},{2,0},{3,1},{4,6},{5,7},{6,4},{7,5},{8,10},{9,11},{10,... | collective-permute-start | bytes 393224 | tf_op jit(solution)/shard_map/ppermute | solution.py:169
  6.9 7.4 %collective-permute-start.5 = (bf16[2,2,128,128]{3,2,1,0:T(8,128)(2,1)}, bf16[2,2,128,128]{3,2,1,0:T(8,128)(2,1)}, u32[]{:S(2)}, u32[]{:S(2)}) collective-permute-start(bf16[2,2,128,128]{3,2,1,0:T(8,128)(2,1)} %pad_maximum_fusion.8), channel_id=1, source_target_pairs={{0,3},{1,2},{2,1},{3,0},{4,7},{5,6},{6,5},{7,4},{8,11},{9,10},{10,... | collective-permute-start | bytes 393224 | tf_op jit(solution)/shard_map/ppermute | solution.py:169
  8.8 45.1 %collective-permute-start.2 = (bf16[2,128,1024]{2,1,0:T(8,128)(2,1)}, bf16[2,128,1024]{2,1,0:T(8,128)(2,1)S(1)}, u32[]{:S(2)}, u32[]{:S(2)}) collective-permute-start(bf16[2,128,1024]{2,1,0:T(8,128)(2,1)} %pad_maximum_fusion.3), channel_id=1, source_target_pairs={{0,3},{1,2},{2,1},{3,0},{4,7},{5,6},{6,5},{7,4},{8,11},{9,10},{10,... | collective-permute-start | bytes 1572872 | tf_op jit(solution)/shard_map/ppermute | solution.py:169
  11.3 44.0 %collective-permute-start.1 = (bf16[2,128,1024]{2,1,0:T(8,128)(2,1)}, bf16[2,128,1024]{2,1,0:T(8,128)(2,1)S(1)}, u32[]{:S(2)}, u32[]{:S(2)}) collective-permute-start(bf16[2,128,1024]{2,1,0:T(8,128)(2,1)} %pad_maximum_fusion.2), channel_id=1, source_target_pairs={{0,2},{1,3},{2,0},{3,1},{4,6},{5,7},{6,4},{7,5},{8,10},{9,11},{10,... | collective-permute-start | bytes 1572872 | tf_op jit(solution)/shard_map/ppermute | solution.py:169
  15.3 15.8 %collective-permute-start.14 = (bf16[4,2,128,128]{3,2,1,0:T(8,128)(2,1)S(1)}, bf16[4,2,128,128]{3,2,1,0:T(8,128)(2,1)S(1)}, u32[]{:S(2)}, u32[]{:S(2)}) collective-permute-start(bf16[4,2,128,128]{3,2,1,0:T(8,128)(2,1)S(1)} %pad_maximum_fusion.5.refs_4_), channel_id=1, source_target_pairs={{0,8},{1,9},{2,10},{3,11},{4,12},{5,13},{6,14},{7,15},{8,0},{9,1},... | collective-permute-start | bytes 786440 | tf_op jit(solution)/shard_map/ppermute | solution.py:169
  18.3 12.8 %collective-permute-start.15 = (bf16[4,2,128,128]{3,2,1,0:T(8,128)(2,1)S(1)}, bf16[4,2,128,128]{3,2,1,0:T(8,128)(2,1)}, u32[]{:S(2)}, u32[]{:S(2)}) collective-permute-start(bf16[4,2,128,128]{3,2,1,0:T(8,128)(2,1)S(1)} %pad_maximum_fusion.5.refs_4_), channel_id=1, source_target_pairs={{0,0},{1,1},{2,2},{3,3},{4,8},{5,9},{6,10},{7,11},{8,4},{9,5},{10,... | collective-permute-start | bytes 786440 | tf_op jit(solution)/shard_map/ppermute | solution.py:169
  19.6 19.1 %collective-permute-start.13 = (bf16[4,2,128,128]{3,2,1,0:T(8,128)(2,1)S(1)}, bf16[4,2,128,128]{3,2,1,0:T(8,128)(2,1)S(1)}, u32[]{:S(2)}, u32[]{:S(2)}) collective-permute-start(bf16[4,2,128,128]{3,2,1,0:T(8,128)(2,1)S(1)} %pad_maximum_fusion.5.refs_4_), channel_id=1, source_target_pairs={{0,4},{1,5},{2,6},{3,7},{4,0},{5,1},{6,2},{7,3},{8,12},{9,13},{10,... | collective-permute-start | bytes 786440 | tf_op jit(solution)/shard_map/ppermute | solution.py:169
  31.1 24.3 %collective-permute-start = (bf16[2,128,1024]{2,1,0:T(8,128)(2,1)}, bf16[2,128,1024]{2,1,0:T(8,128)(2,1)S(1)}, u32[]{:S(2)}, u32[]{:S(2)}) collective-permute-start(bf16[2,128,1024]{2,1,0:T(8,128)(2,1)} %pad_maximum_fusion.1), channel_id=1, source_target_pairs={{0,1},{1,0},{2,3},{3,2},{4,5},{5,4},{6,7},{7,6},{8,9},{9,8},{10,11... | collective-permute-start | bytes 1572872 | tf_op jit(solution)/shard_map/ppermute | solution.py:169
  31.1 19.9 %collective-permute-start.7 = (bf16[4,2,128,128]{3,2,1,0:T(8,128)(2,1)S(1)}, bf16[4,2,128,128]{3,2,1,0:T(8,128)(2,1)S(1)}, u32[]{:S(2)}, u32[]{:S(2)}) collective-permute-start(bf16[4,2,128,128]{3,2,1,0:T(8,128)(2,1)S(1)} %pad_maximum_fusion.4.refs_4_), channel_id=1, source_target_pairs={{0,8},{1,9},{2,10},{3,11},{4,12},{5,13},{6,14},{7,15},{8,0},{9,1},... | collective-permute-start | bytes 786440 | tf_op jit(solution)/shard_map/ppermute | solution.py:169
  38.7 13.5 %collective-permute-start.16 = (bf16[4,2,128,128]{3,2,1,0:T(8,128)(2,1)S(1)}, bf16[4,2,128,128]{3,2,1,0:T(8,128)(2,1)}, u32[]{:S(2)}, u32[]{:S(2)}) collective-permute-start(bf16[4,2,128,128]{3,2,1,0:T(8,128)(2,1)S(1)} %collective-permute-done.14.refs_6_), channel_id=1, source_target_pairs={{0,4},{1,5},{2,6},{3,7},{4,0},{5,1},{6,2},{7,3},{8,12},{9,13},{10,... | collective-permute-start | bytes 786440 | tf_op jit(solution)/shard_map/ppermute | solution.py:169
  51.0 15.4 %collective-permute-start.8 = (bf16[4,2,128,128]{3,2,1,0:T(8,128)(2,1)S(1)}, bf16[4,2,128,128]{3,2,1,0:T(8,128)(2,1)S(1)}, u32[]{:S(2)}, u32[]{:S(2)}) collective-permute-start(bf16[4,2,128,128]{3,2,1,0:T(8,128)(2,1)S(1)} %pad_maximum_fusion.4.refs_4_), channel_id=1, source_target_pairs={{0,0},{1,1},{2,2},{3,3},{4,8},{5,9},{6,10},{7,11},{8,4},{9,5},{10,... | collective-permute-start | bytes 786440 | tf_op jit(solution)/shard_map/ppermute | solution.py:169
  52.3 14.1 %collective-permute-start.9 = (bf16[4,2,128,128]{3,2,1,0:T(8,128)(2,1)S(1)}, bf16[4,2,128,128]{3,2,1,0:T(8,128)(2,1)S(1)}, u32[]{:S(2)}, u32[]{:S(2)}) collective-permute-start(bf16[4,2,128,128]{3,2,1,0:T(8,128)(2,1)S(1)} %collective-permute-done.7.refs_6_), channel_id=1, source_target_pairs={{0,4},{1,5},{2,6},{3,7},{4,0},{5,1},{6,2},{7,3},{8,12},{9,13},{10,... | collective-permute-start | bytes 786440 | tf_op jit(solution)/shard_map/ppermute | solution.py:169
  54.0 12.4 %collective-permute-start.6 = (bf16[4,2,128,128]{3,2,1,0:T(8,128)(2,1)S(1)}, bf16[4,2,128,128]{3,2,1,0:T(8,128)(2,1)S(1)}, u32[]{:S(2)}, u32[]{:S(2)}) collective-permute-start(bf16[4,2,128,128]{3,2,1,0:T(8,128)(2,1)S(1)} %pad_maximum_fusion.4.refs_4_), channel_id=1, source_target_pairs={{0,4},{1,5},{2,6},{3,7},{4,0},{5,1},{6,2},{7,3},{8,12},{9,13},{10,... | collective-permute-start | bytes 786440 | tf_op jit(solution)/shard_map/ppermute | solution.py:169
  64.9 45.8 %collective-permute-start.28 = (bf16[4,2,128,128]{3,2,1,0:T(8,128)(2,1)S(1)}, bf16[4,2,128,128]{3,2,1,0:T(8,128)(2,1)S(1)}, u32[]{:S(2)}, u32[]{:S(2)}) collective-permute-start(bf16[4,2,128,128]{3,2,1,0:T(8,128)(2,1)S(1)} %get-tuple-element.35), channel_id=1, source_target_pairs={{0,4},{1,5},{2,6},{3,7},{4,0},{5,1},{6,2},{7,3},{8,12},{9,13},{10,... | collective-permute-start | bytes 786440 | tf_op jit(solution)/shard_map/ppermute | solution.py:169
  65.7 61.8 %collective-permute-start.30 = (bf16[4,2,128,128]{3,2,1,0:T(8,128)(2,1)S(1)}, bf16[4,2,128,128]{3,2,1,0:T(8,128)(2,1)S(1)}, u32[]{:S(2)}, u32[]{:S(2)}) collective-permute-start(bf16[4,2,128,128]{3,2,1,0:T(8,128)(2,1)S(1)} %get-tuple-element.35), channel_id=1, source_target_pairs={{0,0},{1,1},{2,2},{3,3},{4,8},{5,9},{6,10},{7,11},{8,4},{9,5},{10,... | collective-permute-start | bytes 786440 | tf_op jit(solution)/shard_map/ppermute | solution.py:169
  76.1 12.2 %collective-permute-start.21 = (bf16[4,2,128,128]{3,2,1,0:T(8,128)(2,1)S(1)}, bf16[4,2,128,128]{3,2,1,0:T(8,128)(2,1)S(1)}, u32[]{:S(2)}, u32[]{:S(2)}) collective-permute-start(bf16[4,2,128,128]{3,2,1,0:T(8,128)(2,1)S(1)} %get-tuple-element.31), channel_id=1, source_target_pairs={{0,4},{1,5},{2,6},{3,7},{4,0},{5,1},{6,2},{7,3},{8,12},{9,13},{10,... | collective-permute-start | bytes 786440 | tf_op jit(solution)/shard_map/ppermute | solution.py:169
  78.7 8.7 %collective-permute-start.11 = (bf16[2,128,512]{2,1,0:T(8,128)(2,1)S(1)}, bf16[2,128,512]{2,1,0:T(8,128)(2,1)S(1)}, u32[]{:S(2)}, u32[]{:S(2)}) collective-permute-start(bf16[2,128,512]{2,1,0:T(8,128)(2,1)S(1)} %get-tuple-element.22), channel_id=1, source_target_pairs={{0,2},{1,3},{2,0},{3,1},{4,6},{5,7},{6,4},{7,5},{8,10},{9,11},{10,... | collective-permute-start | bytes 786440 | tf_op jit(solution)/shard_map/ppermute | solution.py:169
  80.5 33.1 %collective-permute-start.23 = (bf16[4,2,128,128]{3,2,1,0:T(8,128)(2,1)S(1)}, bf16[4,2,128,128]{3,2,1,0:T(8,128)(2,1)S(1)}, u32[]{:S(2)}, u32[]{:S(2)}) collective-permute-start(bf16[4,2,128,128]{3,2,1,0:T(8,128)(2,1)S(1)} %get-tuple-element.31), channel_id=1, source_target_pairs={{0,0},{1,1},{2,2},{3,3},{4,8},{5,9},{6,10},{7,11},{8,4},{9,5},{10,... | collective-permute-start | bytes 786440 | tf_op jit(solution)/shard_map/ppermute | solution.py:169
  87.5 8.6 %collective-permute-start.12 = (bf16[2,128,512]{2,1,0:T(8,128)(2,1)S(1)}, bf16[2,128,512]{2,1,0:T(8,128)(2,1)S(1)}, u32[]{:S(2)}, u32[]{:S(2)}) collective-permute-start(bf16[2,128,512]{2,1,0:T(8,128)(2,1)S(1)} %get-tuple-element.23), channel_id=1, source_target_pairs={{0,3},{1,2},{2,1},{3,0},{4,7},{5,6},{6,5},{7,4},{8,11},{9,10},{10,... | collective-permute-start | bytes 786440 | tf_op jit(solution)/shard_map/ppermute | solution.py:169
  88.3 9.2 %collective-permute-start.17 = (bf16[2,128,512]{2,1,0:T(8,128)(2,1)S(1)}, bf16[2,128,512]{2,1,0:T(8,128)(2,1)S(1)}, u32[]{:S(2)}, u32[]{:S(2)}) collective-permute-start(bf16[2,128,512]{2,1,0:T(8,128)(2,1)S(1)} %get-tuple-element.25), channel_id=1, source_target_pairs={{0,1},{1,0},{2,3},{3,2},{4,5},{5,4},{6,7},{7,6},{8,9},{9,8},{10,11... | collective-permute-start | bytes 786440 | tf_op jit(solution)/shard_map/ppermute | solution.py:169
  96.0 9.2 %collective-permute-start.18 = (bf16[2,128,512]{2,1,0:T(8,128)(2,1)S(1)}, bf16[2,128,512]{2,1,0:T(8,128)(2,1)S(1)}, u32[]{:S(2)}, u32[]{:S(2)}) collective-permute-start(bf16[2,128,512]{2,1,0:T(8,128)(2,1)S(1)} %get-tuple-element.26), channel_id=1, source_target_pairs={{0,2},{1,3},{2,0},{3,1},{4,6},{5,7},{6,4},{7,5},{8,10},{9,11},{10,... | collective-permute-start | bytes 786440 | tf_op jit(solution)/shard_map/ppermute | solution.py:169
  97.5 11.6 %collective-permute-start.19 = (bf16[2,128,512]{2,1,0:T(8,128)(2,1)S(1)}, bf16[2,128,512]{2,1,0:T(8,128)(2,1)S(1)}, u32[]{:S(2)}, u32[]{:S(2)}) collective-permute-start(bf16[2,128,512]{2,1,0:T(8,128)(2,1)S(1)} %get-tuple-element.27), channel_id=1, source_target_pairs={{0,3},{1,2},{2,1},{3,0},{4,7},{5,6},{6,5},{7,4},{8,11},{9,10},{10,... | collective-permute-start | bytes 786440 | tf_op jit(solution)/shard_map/ppermute | solution.py:169
  105.2 7.6 %collective-permute-start.20 = (bf16[4,2,128,128]{3,2,1,0:T(8,128)(2,1)S(1)}, bf16[4,2,128,128]{3,2,1,0:T(8,128)(2,1)S(1)}, u32[]{:S(2)}, u32[]{:S(2)}) collective-permute-start(bf16[4,2,128,128]{3,2,1,0:T(8,128)(2,1)S(1)} %get-tuple-element.29), channel_id=1, source_target_pairs={{0,4},{1,5},{2,6},{3,7},{4,0},{5,1},{6,2},{7,3},{8,12},{9,13},{10,... | collective-permute-start | bytes 786440 | tf_op jit(solution)/shard_map/ppermute | solution.py:169
  109.1 16.0 %collective-permute-start.22 = (bf16[4,2,128,128]{3,2,1,0:T(8,128)(2,1)S(1)}, bf16[4,2,128,128]{3,2,1,0:T(8,128)(2,1)S(1)}, u32[]{:S(2)}, u32[]{:S(2)}) collective-permute-start(bf16[4,2,128,128]{3,2,1,0:T(8,128)(2,1)S(1)} %add_convert_fusion.3), channel_id=1, source_target_pairs={{0,8},{1,9},{2,10},{3,11},{4,12},{5,13},{6,14},{7,15},{8,0},{9,1},... | collective-permute-start | bytes 786440 | tf_op jit(solution)/shard_map/ppermute | solution.py:169
  110.7 16.1 %collective-permute-start.27 = (bf16[4,2,128,128]{3,2,1,0:T(8,128)(2,1)S(1)}, bf16[4,2,128,128]{3,2,1,0:T(8,128)(2,1)S(1)}, u32[]{:S(2)}, u32[]{:S(2)}) collective-permute-start(bf16[4,2,128,128]{3,2,1,0:T(8,128)(2,1)S(1)} %get-tuple-element.33), channel_id=1, source_target_pairs={{0,4},{1,5},{2,6},{3,7},{4,0},{5,1},{6,2},{7,3},{8,12},{9,13},{10,... | collective-permute-start | bytes 786440 | tf_op jit(solution)/shard_map/ppermute | solution.py:169
  112.8 23.3 %collective-permute-start.29 = (bf16[4,2,128,128]{3,2,1,0:T(8,128)(2,1)S(1)}, bf16[4,2,128,128]{3,2,1,0:T(8,128)(2,1)S(1)}, u32[]{:S(2)}, u32[]{:S(2)}) collective-permute-start(bf16[4,2,128,128]{3,2,1,0:T(8,128)(2,1)S(1)} %add_convert_fusion.1), channel_id=1, source_target_pairs={{0,8},{1,9},{2,10},{3,11},{4,12},{5,13},{6,14},{7,15},{8,0},{9,1},... | collective-permute-start | bytes 786440 | tf_op jit(solution)/shard_map/ppermute | solution.py:169
  125.4 12.4 %collective-permute-start.24 = (bf16[2,128,128]{2,1,0:T(8,128)(2,1)S(1)}, bf16[2,128,128]{2,1,0:T(8,128)(2,1)S(1)}, u32[]{:S(2)}, u32[]{:S(2)}) collective-permute-start(bf16[2,128,128]{2,1,0:T(8,128)(2,1)S(1)} %get-tuple-element.51), channel_id=1, source_target_pairs={{0,1},{1,0},{2,3},{3,2},{4,5},{5,4},{6,7},{7,6},{8,9},{9,8},{10,11... | collective-permute-start | bytes 196616 | tf_op jit(solution)/shard_map/ppermute | solution.py:169
  125.5 12.8 %collective-permute-start.25 = (bf16[2,128,128]{2,1,0:T(8,128)(2,1)S(1)}, bf16[2,128,128]{2,1,0:T(8,128)(2,1)S(1)}, u32[]{:S(2)}, u32[]{:S(2)}) collective-permute-start(bf16[2,128,128]{2,1,0:T(8,128)(2,1)S(1)} %get-tuple-element.50), channel_id=1, source_target_pairs={{0,2},{1,3},{2,0},{3,1},{4,6},{5,7},{6,4},{7,5},{8,10},{9,11},{10,... | collective-permute-start | bytes 196616 | tf_op jit(solution)/shard_map/ppermute | solution.py:169
  126.9 11.4 %collective-permute-start.26 = (bf16[2,128,128]{2,1,0:T(8,128)(2,1)S(1)}, bf16[2,128,128]{2,1,0:T(8,128)(2,1)S(1)}, u32[]{:S(2)}, u32[]{:S(2)}) collective-permute-start(bf16[2,128,128]{2,1,0:T(8,128)(2,1)S(1)} %get-tuple-element.49), channel_id=1, source_target_pairs={{0,3},{1,2},{2,1},{3,0},{4,7},{5,6},{6,5},{7,4},{8,11},{9,10},{10,... | collective-permute-start | bytes 196616 | tf_op jit(solution)/shard_map/ppermute | solution.py:169
  136.4 4.6 %collective-permute-start.32 = (bf16[2,128,128]{2,1,0:T(8,128)(2,1)S(1)}, bf16[2,128,128]{2,1,0:T(8,128)(2,1)S(1)}, u32[]{:S(2)}, u32[]{:S(2)}) collective-permute-start(bf16[2,128,128]{2,1,0:T(8,128)(2,1)S(1)} %get-tuple-element.47), channel_id=1, source_target_pairs={{0,2},{1,3},{2,0},{3,1},{4,6},{5,7},{6,4},{7,5},{8,10},{9,11},{10,... | collective-permute-start | bytes 196616 | tf_op jit(solution)/shard_map/ppermute | solution.py:169
  137.7 4.4 %collective-permute-start.33 = (bf16[2,128,128]{2,1,0:T(8,128)(2,1)S(1)}, bf16[2,128,128]{2,1,0:T(8,128)(2,1)S(1)}, u32[]{:S(2)}, u32[]{:S(2)}) collective-permute-start(bf16[2,128,128]{2,1,0:T(8,128)(2,1)S(1)} %get-tuple-element.46), channel_id=1, source_target_pairs={{0,3},{1,2},{2,1},{3,0},{4,7},{5,6},{6,5},{7,4},{8,11},{9,10},{10,... | collective-permute-start | bytes 196616 | tf_op jit(solution)/shard_map/ppermute | solution.py:169
  (12 other events, 77.2 us)

commit v3 on v2

--- a/solution.py
+++ b/solution.py
@@ -177,29 +177,67 @@
     return moved(tensor, lambda i: i if i // lanes in (0, 3) else i ^ (3 * lanes))
 
 
-def gathered(own, lanes, depth, inner):
-    if depth != 4:
-        return [own] + [swapped(own, k * lanes) for k in range(1, depth)]
-    two = swapped(own, 2 * lanes)
-    one = swapped(own, lanes)
-    three = middle_swapped(own, lanes)
-    passed = swapped(two, lanes)
-    return [own, one, two, jnp.where(inner, three, passed)]
-
-
-def summed(parts, lanes, depth, inner):
-    total = parts[0]
-    if depth != 4:
+def after(tensor, *others):
+    return lax.optimization_barrier((tensor, others))[0]
+
+
+def plain_exchange(query_cuts, kv_owns, lanes, depth, run):
+    heads = len(kv_owns)
+    query_parts = [query_cuts[0]] + [swapped(query_cuts[mask], mask) for mask in range(1, lanes)]
+    outs_back, totals = [], []
+    for h in range(heads):
+        own = kv_owns[h]
+        outs, parts = run(
+            h, query_parts, [own] + [swapped(own, k * lanes) for k in range(1, depth)]
+        )
+        outs_back.append([outs[0]] + [swapped(outs[mask], mask) for mask in range(1, lanes)])
+        total = parts[0]
         for k in range(1, depth):
             total = total + swapped(parts[k].astype(BF16), k * lanes).astype(F32)
-        return total.astype(BF16)
-    passed = swapped(parts[3], lanes)
-    one = swapped(parts[1], lanes)
-    three = middle_swapped(parts[3], lanes)
-    two = (parts[2] + jnp.where(inner, passed.astype(F32), 0.0)).astype(BF16)
-    two = swapped(two, 2 * lanes)
-    total = total + one.astype(F32) + two.astype(F32)
-    return (total + jnp.where(inner, three.astype(F32), 0.0)).astype(BF16)
+        totals.append(total.astype(BF16))
+    return outs_back, totals
+
+
+def ordered_exchange(query_cuts, kv_owns, lanes, inner, run):
+    one, two, three = lanes, 2 * lanes, 3 * lanes
+    query_x, query_d = swapped(query_cuts[2], 2), swapped(query_cuts[3], 3)
+    a_two = swapped(kv_owns[0], two)
+    a_one = swapped(kv_owns[0], one)
+    a_three = middle_swapped(kv_owns[0], lanes)
+    b_two = swapped(after(kv_owns[1], a_one), two)
+    a_passed = swapped(a_two, one)
+    b_three = swapped(after(kv_owns[1], a_three), three)
+    b_one = swapped(after(kv_owns[1], query_x), one)
+    query_c = swapped(after(query_cuts[1], query_d), 1)
+    query_parts = [query_cuts[0], query_c, query_x, query_d]
+    a_parts = [kv_owns[0], a_one, a_two, jnp.where(inner, a_three, a_passed)]
+    outs_a, sum_a = run(0, query_parts, a_parts)
+    a_passed = swapped(sum_a[3], one)
+    a_middle = middle_swapped(sum_a[3], lanes)
+    out_ax = swapped(after(outs_a[2], b_two), 2)
+    out_ad = swapped(after(outs_a[3], b_one), 3)
+    out_ac = swapped(after(outs_a[1], out_ax), 1)
+    outs_b, sum_b = run(1, query_parts, [kv_owns[1], b_one, b_two, b_three])
+
+    def joined_two(parts, passed):
+        return (parts[2] + jnp.where(inner, passed.astype(F32), 0.0)).astype(BF16)
+
+    def total(parts, first, second, middle):
+        value = parts[0] + first.astype(F32) + second.astype(F32)
+        return (value + jnp.where(inner, middle.astype(F32), 0.0)).astype(BF16)
+
+    a_two = swapped(joined_two(sum_a, a_passed), two)
+    b_passed = swapped(sum_b[3], one)
+    a_one = swapped(after(sum_a[1], a_middle), one)
+    b_middle = middle_swapped(after(sum_b[3], out_ax), lanes)
+    b_two = swapped(joined_two(sum_b, b_passed), two)
+    b_one = swapped(after(sum_b[1], a_one), one)
+    out_bx = swapped(after(outs_b[2], out_ad), 2)
+    out_bd = swapped(after(outs_b[3], a_two), 3)
+    out_bc = swapped(after(outs_b[1], out_bx), 1)
+    totals = [total(sum_a, a_one, a_two, a_middle), total(sum_b, b_one, b_two, b_middle)]
+    outs_back = [[outs_a[0], out_ac, out_ax, out_ad], [outs_b[0], out_bc, out_bx, out_bd]]
+    return outs_back, totals
 
 
 def on_device(queries, key_vectors, value_vectors, grad_output, document_ids):
@@ -226,11 +264,9 @@
         return jnp.stack([cut(queries, mask, wide), cut(grad_output, mask, wide)])
 
     kv_lanes = [kv_cut(0)] + [swapped(kv_cut(mask), mask) for mask in range(1, lanes)]
-    query_parts = [query_cut(0)] + [swapped(query_cut(mask), mask) for mask in range(1, lanes)]
-    kv_parts = [
-        gathered(jnp.stack([part[h] for part in kv_lanes]), lanes, depth, inner)
-        for h in range(heads)
-    ]
+    queries, grad_output = (after(tensor, kv_lanes[1]) for tensor in (queries, grad_output))
+    query_cuts = [query_cut(mask) for mask in range(lanes)]
+    kv_owns = [jnp.stack([part[h] for part in kv_lanes]) for h in range(heads)]
 
     ids = document_ids.reshape(rows, devices)
     lane_masks = jnp.arange(lanes, dtype=jnp.int32)
@@ -261,19 +297,24 @@
     ).reshape(depth * lanes * KR, 1)
     key_places = jnp.broadcast_to(key_place, (depth * lanes * KR, 128))
 
+    def run(h, query_parts, kv_parts):
+        results = attend(h, query_parts, kv_parts, starts, begins, places, key_places)
+        return results[:lanes], results[lanes:]
+
+    if depth == 4 and lanes == 4 and heads == 2:
+        outs_back, totals = ordered_exchange(query_cuts, kv_owns, lanes, inner, run)
+    else:
+        outs_back, totals = plain_exchange(query_cuts, kv_owns, lanes, depth, run)
     wholes = [jnp.zeros((rows, H * HD), BF16) for _ in range(2)]
     kv_wholes = [jnp.zeros((rows, KV * HD), BF16) for _ in range(2)]
     for h in range(heads):
-        results = attend(h, query_parts, kv_parts[h], starts, begins, places, key_places)
-        out_parts, grad_parts = results[:lanes], results[lanes:]
-        out_back = [out_parts[0]] + [swapped(out_parts[mask], mask) for mask in range(1, lanes)]
-        total = summed(grad_parts, lanes, depth, inner)
+        total = totals[h]
         kv_back = [total[0]] + [swapped(total[mask], mask) for mask in range(1, lanes)]
         for which in range(2):
             for mask in range(lanes):
                 owner = lane ^ mask
                 wholes[which] = lax.dynamic_update_slice_in_dim(
-                    wholes[which], out_back[mask][which], owner * wide + h * GROUP * HD, 1
+                    wholes[which], outs_back[h][mask][which], owner * wide + h * GROUP * HD, 1
                 )
                 kv_wholes[which] = lax.dynamic_update_slice_in_dim(
                     kv_wholes[which], kv_back[mask][which], owner * narrow + h * HD, 1

time: 145 us -> 115 us (0.79)
  waiting for transfers between devices: 69 us -> 40.3 us
  starting transfers between devices: 39.6 us -> 38 us
    ppermute x34 -> x33, waiting for transfers between devices: 69 us -> 40.3 us  [moved(): return lax.ppermute(tensor, 'seq', [(i, target(i)) for i in range(devices)])]
    ppermute x34 -> x33, starting transfers between devices: 39.6 us -> 38 us  [moved(): return lax.ppermute(tensor, 'seq', [(i, target(i)) for i in range(devices)])]
    another operation x4, other arithmetic: 2.59 us -> 0.99 us  [query_cut(): return jnp.stack([cut(queries, mask, wide), cut(grad_output, mask, wide)])]
  transfers between devices with their start and end apart: 34 -> 33, of which waited for: 11 -> 12; matrix products, arithmetic and copies ran while one was open for 8% -> 9% of each run, Pallas kernels for 13% -> 18%
where the time goes in v3:
time: 115 us; the launch traced here: 113 us
  waiting for transfers between devices  40.3 us (35%)
  starting transfers between devices  38 us (33%)
  Pallas kernels  20 us (17%)
  local copies, waits for them, and re-layouts  7.01 us (6%)
  other arithmetic  6.49 us (6%)
  between operations  1.31 us (1%)
    ppermute x33, waiting for transfers between devices, moved(): return lax.ppermute(tensor, 'seq', [(i, target(i)) for i in range(devices)])  40.3 us
    ppermute x33, starting transfers between devices, moved(): return lax.ppermute(tensor, 'seq', [(i, target(i)) for i in range(devices)])  38 us
    pallas_call x2, Pallas kernels, attend(): pl.pallas_call(functools.partial(attend_kernel, head, lanes, depth), out_...  20 us
  transfers between devices with their start and end apart: 33, of which 12 were waited for; matrix products, arithmetic and copies ran while one was open for 9% of the time, Pallas kernels for 18%

profile of v3, /device:TPU:0, one launch (start us, length us, event | category | flops | bytes accessed | tf_op | source)
XLA Modules:
  0.0 113.1 jit_solution(9918850918125222636)
XLA Ops:
  0.7 1.0 dynamic-slice_bitcast_fusion.13
  1.7 1.0 dynamic-slice_bitcast_fusion.12
  3.4 2.9 %collective-permute-start.4 = (bf16[2,2,128,128]{3,2,1,0:T(8,128)(2,1)}, bf16[2,2,128,128]{3,2,1,0:T(8,128)(2,1)S(1)}, u32[]{:S(2)}, u32[]{:S(2)}) collective-permute-start(bf16[2,2,128,128]{3,2,1,0:T(8,128)(2,1)} %pad_maximum_fusion.7), channel_id=1, source_target_pairs={{0,2},{1,3},{2,0},{3,1},{4,6},{5,7},{6,4},{7,5},{8,10},{9,11},{10,... | collective-permute-start | bytes 393224 | tf_op jit(solution)/shard_map/ppermute | solution.py:169
  9.7 1.7 %collective-permute-start.1 = (bf16[2,128,1024]{2,1,0:T(8,128)(2,1)S(1)}, bf16[2,128,1024]{2,1,0:T(8,128)(2,1)S(1)}, u32[]{:S(2)}, u32[]{:S(2)}) collective-permute-start(bf16[2,128,1024]{2,1,0:T(8,128)(2,1)S(1)} %pad_maximum_fusion.2), channel_id=1, source_target_pairs={{0,3},{1,2},{2,1},{3,0},{4,7},{5,6},{6,5},{7,4},{8,11},{9,10},{10,... | collective-permute-start | bytes 1572872 | tf_op jit(solution)/shard_map/ppermute | solution.py:169
  11.4 0.9 fusion.40
  13.6 2.8 %collective-permute-start.7 = (bf16[4,2,128,128]{3,2,1,0:T(8,128)(2,1)S(1)}, bf16[4,2,128,128]{3,2,1,0:T(8,128)(2,1)S(1)}, u32[]{:S(2)}, u32[]{:S(2)}) collective-permute-start(bf16[4,2,128,128]{3,2,1,0:T(8,128)(2,1)S(1)} %pad_maximum_fusion.4.refs_4_), channel_id=1, source_target_pairs={{0,8},{1,9},{2,10},{3,11},{4,12},{5,13},{6,14},{7,15},{8,0},{9,1},... | collective-permute-start | bytes 786440 | tf_op jit(solution)/shard_map/ppermute | solution.py:169
  16.6 1.4 %collective-permute-start.8 = (bf16[4,2,128,128]{3,2,1,0:T(8,128)(2,1)S(1)}, bf16[4,2,128,128]{3,2,1,0:T(8,128)(2,1)}, u32[]{:S(2)}, u32[]{:S(2)}) collective-permute-start(bf16[4,2,128,128]{3,2,1,0:T(8,128)(2,1)S(1)} %pad_maximum_fusion.4.refs_4_), channel_id=1, source_target_pairs={{0,0},{1,1},{2,2},{3,3},{4,8},{5,9},{6,10},{7,11},{8,4},{9,5},{10,... | collective-permute-start | bytes 786440 | tf_op jit(solution)/shard_map/ppermute | solution.py:169
  17.9 2.2 %collective-permute-start.6 = (bf16[4,2,128,128]{3,2,1,0:T(8,128)(2,1)S(1)}, bf16[4,2,128,128]{3,2,1,0:T(8,128)(2,1)S(1)}, u32[]{:S(2)}, u32[]{:S(2)}) collective-permute-start(bf16[4,2,128,128]{3,2,1,0:T(8,128)(2,1)S(1)} %pad_maximum_fusion.4.refs_4_), channel_id=1, source_target_pairs={{0,4},{1,5},{2,6},{3,7},{4,0},{5,1},{6,2},{7,3},{8,12},{9,13},{10,... | collective-permute-start | bytes 786440 | tf_op jit(solution)/shard_map/ppermute | solution.py:169
  20.1 0.8 pad_maximum_fusion.3
  21.5 7.9 %collective-permute-done.7.refs_6_ = bf16[4,2,128,128]{3,2,1,0:T(8,128)(2,1)S(1)} collective-permute-done((bf16[4,2,128,128]{3,2,1,0:T(8,128)(2,1)S(1)}, bf16[4,2,128,128]{3,2,1,0:T(8,128)(2,1)S(1)}, u32[]{:S(2)}, u32[]{:S(2)}) %collective-permute-start.7) | collective-permute-done | bytes 262176 | tf_op jit(solution)/shard_map/ppermute | solution.py:169
  30.3 0.9 pad_maximum_fusion.5.refs_4_
  31.3 2.9 %collective-permute-start.15 = (bf16[4,2,128,128]{3,2,1,0:T(8,128)(2,1)S(1)}, bf16[4,2,128,128]{3,2,1,0:T(8,128)(2,1)S(1)}, u32[]{:S(2)}, u32[]{:S(2)}) collective-permute-start(bf16[4,2,128,128]{3,2,1,0:T(8,128)(2,1)S(1)} %pad_maximum_fusion.5.refs_4_), channel_id=1, source_target_pairs={{0,12},{1,13},{2,14},{3,15},{4,8},{5,9},{6,10},{7,11},{8,4},{9,5},... | collective-permute-start | bytes 786440 | tf_op jit(solution)/shard_map/ppermute | solution.py:169
  34.2 3.0 %collective-permute-start.10 = (bf16[4,2,128,128]{3,2,1,0:T(8,128)(2,1)S(1)}, bf16[4,2,128,128]{3,2,1,0:T(8,128)(2,1)S(1)}, u32[]{:S(2)}, u32[]{:S(2)}) collective-permute-start(bf16[4,2,128,128]{3,2,1,0:T(8,128)(2,1)S(1)} %pad_maximum_fusion.5.refs_4_), channel_id=1, source_target_pairs={{0,8},{1,9},{2,10},{3,11},{4,12},{5,13},{6,14},{7,15},{8,0},{9,1},... | collective-permute-start | bytes 786440 | tf_op jit(solution)/shard_map/ppermute | solution.py:169
  37.9 1.0 broadcast_select_fusion.refs_7_
  39.0 10.1 %shard_map.84 = (bf16[2,128,512]{2,1,0:T(8,128)(2,1)S(1)}, bf16[2,128,512]{2,1,0:T(8,128)(2,1)S(1)}, bf16[2,128,512]{2,1,0:T(8,128)(2,1)S(1)}, bf16[2,128,512]{2...) custom-call(s32[4]{0:T(128)S(1)} %and_select_fusion.start_ref, ...), custom_call_target="tpu_custom_call" | custom-call | flops 1677721600 | bytes 8388608 | tf_op jit(solution)/shard_map/pallas_call | solution.py:142
  49.8 9.2 %collective-permute-start.18 = (bf16[4,2,128,128]{3,2,1,0:T(8,128)(2,1)S(1)}, bf16[4,2,128,128]{3,2,1,0:T(8,128)(2,1)S(1)}, u32[]{:S(2)}, u32[]{:S(2)}) collective-permute-start(bf16[4,2,128,128]{3,2,1,0:T(8,128)(2,1)S(1)} %get-tuple-element.55), channel_id=1, source_target_pairs={{0,4},{1,5},{2,6},{3,7},{4,0},{5,1},{6,2},{7,3},{8,12},{9,13},{10,... | collective-permute-start | bytes 786440 | tf_op jit(solution)/shard_map/ppermute | solution.py:169
  59.0 2.0 %collective-permute-done.10.refs_6_ = bf16[4,2,128,128]{3,2,1,0:T(8,128)(2,1)S(1)} collective-permute-done((bf16[4,2,128,128]{3,2,1,0:T(8,128)(2,1)S(1)}, bf16[4,2,128,128]{3,2,1,0:T(8,128)(2,1)S(1)}, u32[]{:S(2)}, u32[]{:S(2)}) %collective-permute-start.10) | collective-permute-done | bytes 262176 | tf_op jit(solution)/shard_map/ppermute | solution.py:169
  61.0 10.0 %shard_map.85 = (bf16[2,128,512]{2,1,0:T(8,128)(2,1)S(1)}, bf16[2,128,512]{2,1,0:T(8,128)(2,1)S(1)}, bf16[2,128,512]{2,1,0:T(8,128)(2,1)S(1)}, bf16[2,128,512]{2...) custom-call(s32[4]{0:T(128)S(1)} %and_select_fusion.start_ref, ...), custom_call_target="tpu_custom_call" | custom-call | flops 1677721600 | bytes 8388608 | tf_op jit(solution)/shard_map/pallas_call | solution.py:142
  71.0 1.1 collective-permute-start.11
  72.3 2.0 %collective-permute-start.22 = (bf16[4,2,128,128]{3,2,1,0:T(8,128)(2,1)S(1)}, bf16[4,2,128,128]{3,2,1,0:T(8,128)(2,1)S(1)}, u32[]{:S(2)}, u32[]{:S(2)}) collective-permute-start(bf16[4,2,128,128]{3,2,1,0:T(8,128)(2,1)S(1)} %get-tuple-element.59), channel_id=1, source_target_pairs={{0,4},{1,5},{2,6},{3,7},{4,0},{5,1},{6,2},{7,3},{8,12},{9,13},{10,... | collective-permute-start | bytes 786440 | tf_op jit(solution)/shard_map/ppermute | solution.py:169
  74.7 11.2 %collective-permute-done.27 = bf16[4,2,128,128]{3,2,1,0:T(8,128)(2,1)S(1)} collective-permute-done((bf16[4,2,128,128]{3,2,1,0:T(8,128)(2,1)S(1)}, bf16[4,2,128,128]{3,2,1,0:T(8,128)(2,1)S(1)}, u32[]{:S(2)}, u32[]{:S(2)}) %collective-permute-start.27) | collective-permute-done | bytes 262176 | tf_op jit(solution)/shard_map/ppermute | solution.py:169
  86.8 1.1 collective-permute-start.16
  87.9 2.1 %collective-permute-done.22 = bf16[4,2,128,128]{3,2,1,0:T(8,128)(2,1)S(1)} collective-permute-done((bf16[4,2,128,128]{3,2,1,0:T(8,128)(2,1)S(1)}, bf16[4,2,128,128]{3,2,1,0:T(8,128)(2,1)S(1)}, u32[]{:S(2)}, u32[]{:S(2)}) %collective-permute-start.22) | collective-permute-done | bytes 262176 | tf_op jit(solution)/shard_map/ppermute | solution.py:169
  89.9 6.0 %collective-permute-done.19 = bf16[4,2,128,128]{3,2,1,0:T(8,128)(2,1)S(1)} collective-permute-done((bf16[4,2,128,128]{3,2,1,0:T(8,128)(2,1)S(1)}, bf16[4,2,128,128]{3,2,1,0:T(8,128)(2,1)S(1)}, u32[]{:S(2)}, u32[]{:S(2)}) %collective-permute-start.19) | collective-permute-done | bytes 262176 | tf_op jit(solution)/shard_map/ppermute | solution.py:169
  96.4 1.1 collective-permute-start.24
  97.6 0.8 collective-permute-start.25
  98.4 3.0 %collective-permute-done.24 = bf16[2,128,128]{2,1,0:T(8,128)(2,1)S(1)} collective-permute-done((bf16[2,128,128]{2,1,0:T(8,128)(2,1)S(1)}, bf16[2,128,128]{2,1,0:T(8,128)(2,1)S(1)}, u32[]{:S(2)}, u32[]{:S(2)}) %collective-permute-start.24) | collective-permute-done | bytes 65568 | tf_op jit(solution)/shard_map/ppermute | solution.py:169
  102.6 2.5 %collective-permute-done.26 = bf16[4,2,128,128]{3,2,1,0:T(8,128)(2,1)S(1)} collective-permute-done((bf16[4,2,128,128]{3,2,1,0:T(8,128)(2,1)S(1)}, bf16[4,2,128,128]{3,2,1,0:T(8,128)(2,1)S(1)}, u32[]{:S(2)}, u32[]{:S(2)}) %collective-permute-start.26) | collective-permute-done | bytes 262176 | tf_op jit(solution)/shard_map/ppermute | solution.py:169
  105.4 1.0 collective-permute-start.31
  106.4 0.8 collective-permute-start.32
  107.3 2.6 %collective-permute-done.20 = bf16[2,128,512]{2,1,0:T(8,128)(2,1)S(1)} collective-permute-done((bf16[2,128,512]{2,1,0:T(8,128)(2,1)S(1)}, bf16[2,128,512]{2,1,0:T(8,128)(2,1)S(1)}, u32[]{:S(2)}, u32[]{:S(2)}) %collective-permute-start.20) | collective-permute-done | bytes 262176 | tf_op jit(solution)/shard_map/ppermute | solution.py:169
  110.6 1.8 %collective-permute-done.32 = bf16[2,128,128]{2,1,0:T(8,128)(2,1)S(1)} collective-permute-done((bf16[2,128,128]{2,1,0:T(8,128)(2,1)S(1)}, bf16[2,128,128]{2,1,0:T(8,128)(2,1)S(1)}, u32[]{:S(2)}, u32[]{:S(2)}) %collective-permute-start.32) | collective-permute-done | bytes 65568 | tf_op jit(solution)/shard_map/ppermute | solution.py:169
  (126 shorter events, 13.3 us)
Async XLA Ops:
  3.4 8.9 %collective-permute-start.4 = (bf16[2,2,128,128]{3,2,1,0:T(8,128)(2,1)}, bf16[2,2,128,128]{3,2,1,0:T(8,128)(2,1)S(1)}, u32[]{:S(2)}, u32[]{:S(2)}) collective-permute-start(bf16[2,2,128,128]{3,2,1,0:T(8,128)(2,1)} %pad_maximum_fusion.7), channel_id=1, source_target_pairs={{0,2},{1,3},{2,0},{3,1},{4,6},{5,7},{6,4},{7,5},{8,10},{9,11},{10,... | collective-permute-start | bytes 393224 | tf_op jit(solution)/shard_map/ppermute | solution.py:169
  7.0 6.0 %collective-permute-start.5 = (bf16[2,2,128,128]{3,2,1,0:T(8,128)(2,1)}, bf16[2,2,128,128]{3,2,1,0:T(8,128)(2,1)S(1)}, u32[]{:S(2)}, u32[]{:S(2)}) collective-permute-start(bf16[2,2,128,128]{3,2,1,0:T(8,128)(2,1)} %pad_maximum_fusion.8), channel_id=1, source_target_pairs={{0,3},{1,2},{2,1},{3,0},{4,7},{5,6},{6,5},{7,4},{8,11},{9,10},{10,... | collective-permute-start | bytes 393224 | tf_op jit(solution)/shard_map/ppermute | solution.py:169
  7.0 2.3 %collective-permute-start = (bf16[2,2,128,128]{3,2,1,0:T(8,128)(2,1)S(1)}, bf16[2,2,128,128]{3,2,1,0:T(8,128)(2,1)}, u32[]{:S(2)}, u32[]{:S(2)}) collective-permute-start(bf16[2,2,128,128]{3,2,1,0:T(8,128)(2,1)S(1)} %pad_maximum_fusion.6), channel_id=1, source_target_pairs={{0,1},{1,0},{2,3},{3,2},{4,5},{5,4},{6,7},{7,6},{8,9},{9,8},{10,11... | collective-permute-start | bytes 393224 | tf_op jit(solution)/shard_map/ppermute | solution.py:169
  9.7 20.0 %collective-permute-start.1 = (bf16[2,128,1024]{2,1,0:T(8,128)(2,1)S(1)}, bf16[2,128,1024]{2,1,0:T(8,128)(2,1)S(1)}, u32[]{:S(2)}, u32[]{:S(2)}) collective-permute-start(bf16[2,128,1024]{2,1,0:T(8,128)(2,1)S(1)} %pad_maximum_fusion.2), channel_id=1, source_target_pairs={{0,3},{1,2},{2,1},{3,0},{4,7},{5,6},{6,5},{7,4},{8,11},{9,10},{10,... | collective-permute-start | bytes 1572872 | tf_op jit(solution)/shard_map/ppermute | solution.py:169
  13.6 15.7 %collective-permute-start.7 = (bf16[4,2,128,128]{3,2,1,0:T(8,128)(2,1)S(1)}, bf16[4,2,128,128]{3,2,1,0:T(8,128)(2,1)S(1)}, u32[]{:S(2)}, u32[]{:S(2)}) collective-permute-start(bf16[4,2,128,128]{3,2,1,0:T(8,128)(2,1)S(1)} %pad_maximum_fusion.4.refs_4_), channel_id=1, source_target_pairs={{0,8},{1,9},{2,10},{3,11},{4,12},{5,13},{6,14},{7,15},{8,0},{9,1},... | collective-permute-start | bytes 786440 | tf_op jit(solution)/shard_map/ppermute | solution.py:169
  16.6 14.7 %collective-permute-start.8 = (bf16[4,2,128,128]{3,2,1,0:T(8,128)(2,1)S(1)}, bf16[4,2,128,128]{3,2,1,0:T(8,128)(2,1)}, u32[]{:S(2)}, u32[]{:S(2)}) collective-permute-start(bf16[4,2,128,128]{3,2,1,0:T(8,128)(2,1)S(1)} %pad_maximum_fusion.4.refs_4_), channel_id=1, source_target_pairs={{0,0},{1,1},{2,2},{3,3},{4,8},{5,9},{6,10},{7,11},{8,4},{9,5},{10,... | collective-permute-start | bytes 786440 | tf_op jit(solution)/shard_map/ppermute | solution.py:169
  17.9 16.3 %collective-permute-start.6 = (bf16[4,2,128,128]{3,2,1,0:T(8,128)(2,1)S(1)}, bf16[4,2,128,128]{3,2,1,0:T(8,128)(2,1)S(1)}, u32[]{:S(2)}, u32[]{:S(2)}) collective-permute-start(bf16[4,2,128,128]{3,2,1,0:T(8,128)(2,1)S(1)} %pad_maximum_fusion.4.refs_4_), channel_id=1, source_target_pairs={{0,4},{1,5},{2,6},{3,7},{4,0},{5,1},{6,2},{7,3},{8,12},{9,13},{10,... | collective-permute-start | bytes 786440 | tf_op jit(solution)/shard_map/ppermute | solution.py:169
  21.0 16.3 %collective-permute-start.3 = (bf16[2,128,1024]{2,1,0:T(8,128)(2,1)}, bf16[2,128,1024]{2,1,0:T(8,128)(2,1)S(1)}, u32[]{:S(2)}, u32[]{:S(2)}) collective-permute-start(bf16[2,128,1024]{2,1,0:T(8,128)(2,1)} %pad_maximum_fusion.3), channel_id=1, source_target_pairs={{0,2},{1,3},{2,0},{3,1},{4,6},{5,7},{6,4},{7,5},{8,10},{9,11},{10,... | collective-permute-start | bytes 1572872 | tf_op jit(solution)/shard_map/ppermute | solution.py:169
  29.4 8.5 %collective-permute-start.9 = (bf16[4,2,128,128]{3,2,1,0:T(8,128)(2,1)S(1)}, bf16[4,2,128,128]{3,2,1,0:T(8,128)(2,1)}, u32[]{:S(2)}, u32[]{:S(2)}) collective-permute-start(bf16[4,2,128,128]{3,2,1,0:T(8,128)(2,1)S(1)} %collective-permute-done.7.refs_6_), channel_id=1, source_target_pairs={{0,4},{1,5},{2,6},{3,7},{4,0},{5,1},{6,2},{7,3},{8,12},{9,13},{10,... | collective-permute-start | bytes 786440 | tf_op jit(solution)/shard_map/ppermute | solution.py:169
  29.7 9.2 %collective-permute-start.2 = (bf16[2,128,1024]{2,1,0:T(8,128)(2,1)S(1)}, bf16[2,128,1024]{2,1,0:T(8,128)(2,1)S(1)}, u32[]{:S(2)}, u32[]{:S(2)}) collective-permute-start(bf16[2,128,1024]{2,1,0:T(8,128)(2,1)S(1)} %pad_maximum_fusion.1), channel_id=1, source_target_pairs={{0,1},{1,0},{2,3},{3,2},{4,5},{5,4},{6,7},{7,6},{8,9},{9,8},{10,11... | collective-permute-start | bytes 1572872 | tf_op jit(solution)/shard_map/ppermute | solution.py:169
  31.3 27.7 %collective-permute-start.15 = (bf16[4,2,128,128]{3,2,1,0:T(8,128)(2,1)S(1)}, bf16[4,2,128,128]{3,2,1,0:T(8,128)(2,1)S(1)}, u32[]{:S(2)}, u32[]{:S(2)}) collective-permute-start(bf16[4,2,128,128]{3,2,1,0:T(8,128)(2,1)S(1)} %pad_maximum_fusion.5.refs_4_), channel_id=1, source_target_pairs={{0,12},{1,13},{2,14},{3,15},{4,8},{5,9},{6,10},{7,11},{8,4},{9,5},... | collective-permute-start | bytes 786440 | tf_op jit(solution)/shard_map/ppermute | solution.py:169
  34.2 26.8 %collective-permute-start.10 = (bf16[4,2,128,128]{3,2,1,0:T(8,128)(2,1)S(1)}, bf16[4,2,128,128]{3,2,1,0:T(8,128)(2,1)S(1)}, u32[]{:S(2)}, u32[]{:S(2)}) collective-permute-start(bf16[4,2,128,128]{3,2,1,0:T(8,128)(2,1)S(1)} %pad_maximum_fusion.5.refs_4_), channel_id=1, source_target_pairs={{0,8},{1,9},{2,10},{3,11},{4,12},{5,13},{6,14},{7,15},{8,0},{9,1},... | collective-permute-start | bytes 786440 | tf_op jit(solution)/shard_map/ppermute | solution.py:169
  37.3 23.7 %collective-permute-start.13 = (bf16[4,2,128,128]{3,2,1,0:T(8,128)(2,1)S(1)}, bf16[4,2,128,128]{3,2,1,0:T(8,128)(2,1)S(1)}, u32[]{:S(2)}, u32[]{:S(2)}) collective-permute-start(bf16[4,2,128,128]{3,2,1,0:T(8,128)(2,1)S(1)} %pad_maximum_fusion.5.refs_4_), channel_id=1, source_target_pairs={{0,4},{1,5},{2,6},{3,7},{4,0},{5,1},{6,2},{7,3},{8,12},{9,13},{10,... | collective-permute-start | bytes 786440 | tf_op jit(solution)/shard_map/ppermute | solution.py:169
  49.1 23.1 %collective-permute-start.21 = (bf16[4,2,128,128]{3,2,1,0:T(8,128)(2,1)S(1)}, bf16[4,2,128,128]{3,2,1,0:T(8,128)(2,1)S(1)}, u32[]{:S(2)}, u32[]{:S(2)}) collective-permute-start(bf16[4,2,128,128]{3,2,1,0:T(8,128)(2,1)S(1)} %get-tuple-element.55), channel_id=1, source_target_pairs={{0,0},{1,1},{2,2},{3,3},{4,8},{5,9},{6,10},{7,11},{8,4},{9,5},{10,... | collective-permute-start | bytes 786440 | tf_op jit(solution)/shard_map/ppermute | solution.py:169
  49.8 24.5 %collective-permute-start.18 = (bf16[4,2,128,128]{3,2,1,0:T(8,128)(2,1)S(1)}, bf16[4,2,128,128]{3,2,1,0:T(8,128)(2,1)S(1)}, u32[]{:S(2)}, u32[]{:S(2)}) collective-permute-start(bf16[4,2,128,128]{3,2,1,0:T(8,128)(2,1)S(1)} %get-tuple-element.55), channel_id=1, source_target_pairs={{0,4},{1,5},{2,6},{3,7},{4,0},{5,1},{6,2},{7,3},{8,12},{9,13},{10,... | collective-permute-start | bytes 786440 | tf_op jit(solution)/shard_map/ppermute | solution.py:169
  71.0 14.9 %collective-permute-start.27 = (bf16[4,2,128,128]{3,2,1,0:T(8,128)(2,1)S(1)}, bf16[4,2,128,128]{3,2,1,0:T(8,128)(2,1)S(1)}, u32[]{:S(2)}, u32[]{:S(2)}) collective-permute-start(bf16[4,2,128,128]{3,2,1,0:T(8,128)(2,1)S(1)} %get-tuple-element.65), channel_id=1, source_target_pairs={{0,4},{1,5},{2,6},{3,7},{4,0},{5,1},{6,2},{7,3},{8,12},{9,13},{10,... | collective-permute-start | bytes 786440 | tf_op jit(solution)/shard_map/ppermute | solution.py:169
  71.0 15.0 %collective-permute-start.11 = (bf16[2,128,512]{2,1,0:T(8,128)(2,1)S(1)}, bf16[2,128,512]{2,1,0:T(8,128)(2,1)S(1)}, u32[]{:S(2)}, u32[]{:S(2)}) collective-permute-start(bf16[2,128,512]{2,1,0:T(8,128)(2,1)S(1)} %get-tuple-element.42), channel_id=1, source_target_pairs={{0,2},{1,3},{2,0},{3,1},{4,6},{5,7},{6,4},{7,5},{8,10},{9,11},{10,... | collective-permute-start | bytes 786440 | tf_op jit(solution)/shard_map/ppermute | solution.py:169
  72.1 14.6 %collective-permute-start.14 = (bf16[2,128,512]{2,1,0:T(8,128)(2,1)S(1)}, bf16[2,128,512]{2,1,0:T(8,128)(2,1)S(1)}, u32[]{:S(2)}, u32[]{:S(2)}) collective-permute-start(bf16[2,128,512]{2,1,0:T(8,128)(2,1)S(1)} %get-tuple-element.46), channel_id=1, source_target_pairs={{0,3},{1,2},{2,1},{3,0},{4,7},{5,6},{6,5},{7,4},{8,11},{9,10},{10,... | collective-permute-start | bytes 786440 | tf_op jit(solution)/shard_map/ppermute | solution.py:169
  72.3 17.7 %collective-permute-start.22 = (bf16[4,2,128,128]{3,2,1,0:T(8,128)(2,1)S(1)}, bf16[4,2,128,128]{3,2,1,0:T(8,128)(2,1)S(1)}, u32[]{:S(2)}, u32[]{:S(2)}) collective-permute-start(bf16[4,2,128,128]{3,2,1,0:T(8,128)(2,1)S(1)} %get-tuple-element.59), channel_id=1, source_target_pairs={{0,4},{1,5},{2,6},{3,7},{4,0},{5,1},{6,2},{7,3},{8,12},{9,13},{10,... | collective-permute-start | bytes 786440 | tf_op jit(solution)/shard_map/ppermute | solution.py:169
  74.4 21.5 %collective-permute-start.19 = (bf16[4,2,128,128]{3,2,1,0:T(8,128)(2,1)S(1)}, bf16[4,2,128,128]{3,2,1,0:T(8,128)(2,1)S(1)}, u32[]{:S(2)}, u32[]{:S(2)}) collective-permute-start(bf16[4,2,128,128]{3,2,1,0:T(8,128)(2,1)S(1)} %add_convert_fusion.3), channel_id=1, source_target_pairs={{0,8},{1,9},{2,10},{3,11},{4,12},{5,13},{6,14},{7,15},{8,0},{9,1},... | collective-permute-start | bytes 786440 | tf_op jit(solution)/shard_map/ppermute | solution.py:169
  86.0 16.6 %collective-permute-start.28 = (bf16[4,2,128,128]{3,2,1,0:T(8,128)(2,1)S(1)}, bf16[4,2,128,128]{3,2,1,0:T(8,128)(2,1)S(1)}, u32[]{:S(2)}, u32[]{:S(2)}) collective-permute-start(bf16[4,2,128,128]{3,2,1,0:T(8,128)(2,1)S(1)} %add_convert_fusion.1), channel_id=1, source_target_pairs={{0,8},{1,9},{2,10},{3,11},{4,12},{5,13},{6,14},{7,15},{8,0},{9,1},... | collective-permute-start | bytes 786440 | tf_op jit(solution)/shard_map/ppermute | solution.py:169
  86.1 16.6 %collective-permute-start.29 = (bf16[4,2,128,128]{3,2,1,0:T(8,128)(2,1)S(1)}, bf16[4,2,128,128]{3,2,1,0:T(8,128)(2,1)S(1)}, u32[]{:S(2)}, u32[]{:S(2)}) collective-permute-start(bf16[4,2,128,128]{3,2,1,0:T(8,128)(2,1)S(1)} %get-tuple-element.65), channel_id=1, source_target_pairs={{0,0},{1,1},{2,2},{3,3},{4,8},{5,9},{6,10},{7,11},{8,4},{9,5},{10,... | collective-permute-start | bytes 786440 | tf_op jit(solution)/shard_map/ppermute | solution.py:169
  86.8 9.7 %collective-permute-start.16 = (bf16[2,128,512]{2,1,0:T(8,128)(2,1)S(1)}, bf16[2,128,512]{2,1,0:T(8,128)(2,1)S(1)}, u32[]{:S(2)}, u32[]{:S(2)}) collective-permute-start(bf16[2,128,512]{2,1,0:T(8,128)(2,1)S(1)} %get-tuple-element.51), channel_id=1, source_target_pairs={{0,2},{1,3},{2,0},{3,1},{4,6},{5,7},{6,4},{7,5},{8,10},{9,11},{10,... | collective-permute-start | bytes 786440 | tf_op jit(solution)/shard_map/ppermute | solution.py:169
  89.9 6.1 %collective-permute-start.12 = (bf16[2,128,512]{2,1,0:T(8,128)(2,1)S(1)}, bf16[2,128,512]{2,1,0:T(8,128)(2,1)S(1)}, u32[]{:S(2)}, u32[]{:S(2)}) collective-permute-start(bf16[2,128,512]{2,1,0:T(8,128)(2,1)S(1)} %get-tuple-element.43), channel_id=1, source_target_pairs={{0,1},{1,0},{2,3},{3,2},{4,5},{5,4},{6,7},{7,6},{8,9},{9,8},{10,11... | collective-permute-start | bytes 786440 | tf_op jit(solution)/shard_map/ppermute | solution.py:169
  95.9 9.3 %collective-permute-start.26 = (bf16[4,2,128,128]{3,2,1,0:T(8,128)(2,1)S(1)}, bf16[4,2,128,128]{3,2,1,0:T(8,128)(2,1)S(1)}, u32[]{:S(2)}, u32[]{:S(2)}) collective-permute-start(bf16[4,2,128,128]{3,2,1,0:T(8,128)(2,1)S(1)} %get-tuple-element.62), channel_id=1, source_target_pairs={{0,4},{1,5},{2,6},{3,7},{4,0},{5,1},{6,2},{7,3},{8,12},{9,13},{10,... | collective-permute-start | bytes 786440 | tf_op jit(solution)/shard_map/ppermute | solution.py:169
  96.4 4.9 %collective-permute-start.24 = (bf16[2,128,128]{2,1,0:T(8,128)(2,1)S(1)}, bf16[2,128,128]{2,1,0:T(8,128)(2,1)S(1)}, u32[]{:S(2)}, u32[]{:S(2)}) collective-permute-start(bf16[2,128,128]{2,1,0:T(8,128)(2,1)S(1)} %get-tuple-element.80), channel_id=1, source_target_pairs={{0,2},{1,3},{2,0},{3,1},{4,6},{5,7},{6,4},{7,5},{8,10},{9,11},{10,... | collective-permute-start | bytes 196616 | tf_op jit(solution)/shard_map/ppermute | solution.py:169
  97.6 4.4 %collective-permute-start.25 = (bf16[2,128,128]{2,1,0:T(8,128)(2,1)S(1)}, bf16[2,128,128]{2,1,0:T(8,128)(2,1)S(1)}, u32[]{:S(2)}, u32[]{:S(2)}) collective-permute-start(bf16[2,128,128]{2,1,0:T(8,128)(2,1)S(1)} %get-tuple-element.79), channel_id=1, source_target_pairs={{0,3},{1,2},{2,1},{3,0},{4,7},{5,6},{6,5},{7,4},{8,11},{9,10},{10,... | collective-permute-start | bytes 196616 | tf_op jit(solution)/shard_map/ppermute | solution.py:169
  101.4 8.5 %collective-permute-start.20 = (bf16[2,128,512]{2,1,0:T(8,128)(2,1)S(1)}, bf16[2,128,512]{2,1,0:T(8,128)(2,1)S(1)}, u32[]{:S(2)}, u32[]{:S(2)}) collective-permute-start(bf16[2,128,512]{2,1,0:T(8,128)(2,1)S(1)} %get-tuple-element.56), channel_id=1, source_target_pairs={{0,3},{1,2},{2,1},{3,0},{4,7},{5,6},{6,5},{7,4},{8,11},{9,10},{10,... | collective-permute-start | bytes 786440 | tf_op jit(solution)/shard_map/ppermute | solution.py:169
  102.0 5.3 %collective-permute-start.17 = (bf16[2,128,512]{2,1,0:T(8,128)(2,1)S(1)}, bf16[2,128,512]{2,1,0:T(8,128)(2,1)S(1)}, u32[]{:S(2)}, u32[]{:S(2)}) collective-permute-start(bf16[2,128,512]{2,1,0:T(8,128)(2,1)S(1)} %get-tuple-element.52), channel_id=1, source_target_pairs={{0,1},{1,0},{2,3},{3,2},{4,5},{5,4},{6,7},{7,6},{8,9},{9,8},{10,11... | collective-permute-start | bytes 786440 | tf_op jit(solution)/shard_map/ppermute | solution.py:169
  105.3 4.7 %collective-permute-start.30 = (bf16[2,128,128]{2,1,0:T(8,128)(2,1)S(1)}, bf16[2,128,128]{2,1,0:T(8,128)(2,1)S(1)}, u32[]{:S(2)}, u32[]{:S(2)}) collective-permute-start(bf16[2,128,128]{2,1,0:T(8,128)(2,1)S(1)} %get-tuple-element.78), channel_id=1, source_target_pairs={{0,1},{1,0},{2,3},{3,2},{4,5},{5,4},{6,7},{7,6},{8,9},{9,8},{10,11... | collective-permute-start | bytes 196616 | tf_op jit(solution)/shard_map/ppermute | solution.py:169
  105.4 5.1 %collective-permute-start.31 = (bf16[2,128,128]{2,1,0:T(8,128)(2,1)S(1)}, bf16[2,128,128]{2,1,0:T(8,128)(2,1)S(1)}, u32[]{:S(2)}, u32[]{:S(2)}) collective-permute-start(bf16[2,128,128]{2,1,0:T(8,128)(2,1)S(1)} %get-tuple-element.77), channel_id=1, source_target_pairs={{0,2},{1,3},{2,0},{3,1},{4,6},{5,7},{6,4},{7,5},{8,10},{9,11},{10,... | collective-permute-start | bytes 196616 | tf_op jit(solution)/shard_map/ppermute | solution.py:169
  106.4 5.9 %collective-permute-start.32 = (bf16[2,128,128]{2,1,0:T(8,128)(2,1)S(1)}, bf16[2,128,128]{2,1,0:T(8,128)(2,1)S(1)}, u32[]{:S(2)}, u32[]{:S(2)}) collective-permute-start(bf16[2,128,128]{2,1,0:T(8,128)(2,1)S(1)} %get-tuple-element.76), channel_id=1, source_target_pairs={{0,3},{1,2},{2,1},{3,0},{4,7},{5,6},{6,5},{7,4},{8,11},{9,10},{10,... | collective-permute-start | bytes 196616 | tf_op jit(solution)/shard_map/ppermute | solution.py:169
  (10 other events, 42.4 us)

commit v4 on v3

--- a/solution.py
+++ b/solution.py
@@ -159,7 +159,7 @@
         ],
         compiler_params=pltpu.CompilerParams(vmem_limit_bytes=(40 if depth == 4 else 62) << 20),
         cost_estimate=pl.CostEstimate(
-            flops=10 * HD * pairs, bytes_accessed=8 << 20, transcendentals=pairs
+            flops=80 * HD * pairs, bytes_accessed=8 << 20, transcendentals=pairs
         ),
     )(starts, begins, places, key_places, *query_parts, *kv_parts)
 
@@ -211,31 +211,37 @@
     query_c = swapped(after(query_cuts[1], query_d), 1)
     query_parts = [query_cuts[0], query_c, query_x, query_d]
     a_parts = [kv_owns[0], a_one, a_two, jnp.where(inner, a_three, a_passed)]
+    def joined_two(parts, passed):
+        return (parts[2] + jnp.where(inner, passed.astype(F32), 0.0)).astype(BF16)
+
+    def total(parts, first, second, middle):
+        value = parts[0] + first.astype(F32) + second.astype(F32)
+        return (value + jnp.where(inner, middle.astype(F32), 0.0)).astype(BF16)
+
     outs_a, sum_a = run(0, query_parts, a_parts)
     a_passed = swapped(sum_a[3], one)
     a_middle = middle_swapped(sum_a[3], lanes)
+    a_two = swapped(joined_two(sum_a, a_passed), two)
+    a_one = swapped(after(sum_a[1], b_one), one)
     out_ax = swapped(after(outs_a[2], b_two), 2)
     out_ad = swapped(after(outs_a[3], b_one), 3)
-    out_ac = swapped(after(outs_a[1], out_ax), 1)
-    outs_b, sum_b = run(1, query_parts, [kv_owns[1], b_one, b_two, b_three])
-
-    def joined_two(parts, passed):
-        return (parts[2] + jnp.where(inner, passed.astype(F32), 0.0)).astype(BF16)
-
-    def total(parts, first, second, middle):
-        value = parts[0] + first.astype(F32) + second.astype(F32)
-        return (value + jnp.where(inner, middle.astype(F32), 0.0)).astype(BF16)
-
-    a_two = swapped(joined_two(sum_a, a_passed), two)
+    outs_b, sum_b = run(
+        1, query_parts, after([kv_owns[1], b_one, b_two, b_three], a_passed)
+    )
+    outs_b, sum_b = after((outs_b, sum_b), a_two, a_one, a_middle, out_ax, out_ad)
     b_passed = swapped(sum_b[3], one)
-    a_one = swapped(after(sum_a[1], a_middle), one)
-    b_middle = middle_swapped(after(sum_b[3], out_ax), lanes)
-    b_two = swapped(joined_two(sum_b, b_passed), two)
-    b_one = swapped(after(sum_b[1], a_one), one)
-    out_bx = swapped(after(outs_b[2], out_ad), 2)
-    out_bd = swapped(after(outs_b[3], a_two), 3)
+    out_ac = swapped(after(outs_a[1], a_one), 1)
+    b_middle = middle_swapped(sum_b[3], lanes)
+    out_bx = swapped(outs_b[2], 2)
+    out_bd = swapped(outs_b[3], 3)
+    b_send = joined_two(sum_b, b_passed)
+    b_two = swapped(b_send, two)
+    b_one = swapped(after(sum_b[1], b_send), one)
     out_bc = swapped(after(outs_b[1], out_bx), 1)
-    totals = [total(sum_a, a_one, a_two, a_middle), total(sum_b, b_one, b_two, b_middle)]
+    totals = [
+        after(total(sum_a, a_one, a_two, a_middle), out_bx),
+        total(sum_b, b_one, b_two, b_middle),
+    ]
     outs_back = [[outs_a[0], out_ac, out_ax, out_ad], [outs_b[0], out_bc, out_bx, out_bd]]
     return outs_back, totals
 

time: 115 us -> 112 us (0.974)
  waiting for transfers between devices: 40.3 us -> 32.2 us
  starting transfers between devices: 38 us -> 44.9 us
  other arithmetic: 6.49 us -> 5.19 us
    ppermute x33, waiting for transfers between devices: 40.3 us -> 32.2 us  [moved(): return lax.ppermute(tensor, 'seq', [(i, target(i)) for i in range(devices)])]
    ppermute x33, starting transfers between devices: 38 us -> 44.9 us  [moved(): return lax.ppermute(tensor, 'seq', [(i, target(i)) for i in range(devices)])]
    another operation x6, other arithmetic: 1.45 us -> 0.14 us  [kv_cut(): return jnp.stack([both[:, :, h * HD:(h + 1) * HD] for h in range(heads)])]
  transfers between devices with their start and end apart: 33 -> 33, of which waited for: 12 -> 13; matrix products, arithmetic and copies ran while one was open for 9% -> 8% of each run, Pallas kernels for 18% -> 18%
where the time goes in v4:
time: 112 us; the launch traced here: 110 us
  starting transfers between devices  44.9 us (40%)
  waiting for transfers between devices  32.2 us (29%)
  Pallas kernels  19.8 us (18%)
  local copies, waits for them, and re-layouts  6.11 us (5%)
  other arithmetic  5.19 us (5%)
  between operations  1.34 us (1%)
    ppermute x33, starting transfers between devices, moved(): return lax.ppermute(tensor, 'seq', [(i, target(i)) for i in range(devices)])  44.9 us
    ppermute x33, waiting for transfers between devices, moved(): return lax.ppermute(tensor, 'seq', [(i, target(i)) for i in range(devices)])  32.2 us
    pallas_call x2, Pallas kernels, attend(): pl.pallas_call(functools.partial(attend_kernel, head, lanes, depth), out_...  19.8 us
  transfers between devices with their start and end apart: 33, of which 13 were waited for; matrix products, arithmetic and copies ran while one was open for 8% of the time, Pallas kernels for 18%

profile of v4, /device:TPU:0, one launch (start us, length us, event | category | flops | bytes accessed | tf_op | source)
XLA Modules:
  0.0 109.5 jit_solution(8990200452060755416)
XLA Ops:
  0.7 1.0 dynamic-slice_bitcast_fusion.12
  1.7 1.0 dynamic-slice_bitcast_fusion.13
  2.7 3.0 %collective-permute-start.4 = (bf16[2,2,128,128]{3,2,1,0:T(8,128)(2,1)S(1)}, bf16[2,2,128,128]{3,2,1,0:T(8,128)(2,1)S(1)}, u32[]{:S(2)}, u32[]{:S(2)}) collective-permute-start(bf16[2,2,128,128]{3,2,1,0:T(8,128)(2,1)S(1)} %pad_maximum_fusion.7), channel_id=1, source_target_pairs={{0,2},{1,3},{2,0},{3,1},{4,6},{5,7},{6,4},{7,5},{8,10},{9,11},{10,... | collective-permute-start | bytes 393224 | tf_op jit(solution)/shard_map/ppermute | solution.py:169
  8.5 1.7 %collective-permute-start.1 = (bf16[2,128,1024]{2,1,0:T(8,128)(2,1)S(1)}, bf16[2,128,1024]{2,1,0:T(8,128)(2,1)S(1)}, u32[]{:S(2)}, u32[]{:S(2)}) collective-permute-start(bf16[2,128,1024]{2,1,0:T(8,128)(2,1)S(1)} %pad_maximum_fusion.2), channel_id=1, source_target_pairs={{0,3},{1,2},{2,1},{3,0},{4,7},{5,6},{6,5},{7,4},{8,11},{9,10},{10,... | collective-permute-start | bytes 1572872 | tf_op jit(solution)/shard_map/ppermute | solution.py:169
  12.4 2.6 %collective-permute-start.7 = (bf16[4,2,128,128]{3,2,1,0:T(8,128)(2,1)S(1)}, bf16[4,2,128,128]{3,2,1,0:T(8,128)(2,1)S(1)}, u32[]{:S(2)}, u32[]{:S(2)}) collective-permute-start(bf16[4,2,128,128]{3,2,1,0:T(8,128)(2,1)S(1)} %pad_maximum_fusion.4.refs_4_), channel_id=1, source_target_pairs={{0,8},{1,9},{2,10},{3,11},{4,12},{5,13},{6,14},{7,15},{8,0},{9,1},... | collective-permute-start | bytes 786440 | tf_op jit(solution)/shard_map/ppermute | solution.py:169
  15.1 1.4 %collective-permute-start.8 = (bf16[4,2,128,128]{3,2,1,0:T(8,128)(2,1)S(1)}, bf16[4,2,128,128]{3,2,1,0:T(8,128)(2,1)}, u32[]{:S(2)}, u32[]{:S(2)}) collective-permute-start(bf16[4,2,128,128]{3,2,1,0:T(8,128)(2,1)S(1)} %pad_maximum_fusion.4.refs_4_), channel_id=1, source_target_pairs={{0,0},{1,1},{2,2},{3,3},{4,8},{5,9},{6,10},{7,11},{8,4},{9,5},{10,... | collective-permute-start | bytes 786440 | tf_op jit(solution)/shard_map/ppermute | solution.py:169
  16.5 2.2 %collective-permute-start.6 = (bf16[4,2,128,128]{3,2,1,0:T(8,128)(2,1)S(1)}, bf16[4,2,128,128]{3,2,1,0:T(8,128)(2,1)S(1)}, u32[]{:S(2)}, u32[]{:S(2)}) collective-permute-start(bf16[4,2,128,128]{3,2,1,0:T(8,128)(2,1)S(1)} %pad_maximum_fusion.4.refs_4_), channel_id=1, source_target_pairs={{0,4},{1,5},{2,6},{3,7},{4,0},{5,1},{6,2},{7,3},{8,12},{9,13},{10,... | collective-permute-start | bytes 786440 | tf_op jit(solution)/shard_map/ppermute | solution.py:169
  19.5 1.1 %collective-permute-start.3 = (bf16[2,128,1024]{2,1,0:T(8,128)(2,1)}, bf16[2,128,1024]{2,1,0:T(8,128)(2,1)S(1)}, u32[]{:S(2)}, u32[]{:S(2)}) collective-permute-start(bf16[2,128,1024]{2,1,0:T(8,128)(2,1)} %pad_maximum_fusion.3), channel_id=1, source_target_pairs={{0,2},{1,3},{2,0},{3,1},{4,6},{5,7},{6,4},{7,5},{8,10},{9,11},{10,... | collective-permute-start | bytes 1572872 | tf_op jit(solution)/shard_map/ppermute | solution.py:169
  20.7 7.4 %collective-permute-done.7.refs_6_ = bf16[4,2,128,128]{3,2,1,0:T(8,128)(2,1)S(1)} collective-permute-done((bf16[4,2,128,128]{3,2,1,0:T(8,128)(2,1)S(1)}, bf16[4,2,128,128]{3,2,1,0:T(8,128)(2,1)S(1)}, u32[]{:S(2)}, u32[]{:S(2)}) %collective-permute-start.7) | collective-permute-done | bytes 262176 | tf_op jit(solution)/shard_map/ppermute | solution.py:169
  29.4 0.9 pad_maximum_fusion.5.refs_4_
  30.4 3.0 %collective-permute-start.16 = (bf16[4,2,128,128]{3,2,1,0:T(8,128)(2,1)S(1)}, bf16[4,2,128,128]{3,2,1,0:T(8,128)(2,1)S(1)}, u32[]{:S(2)}, u32[]{:S(2)}) collective-permute-start(bf16[4,2,128,128]{3,2,1,0:T(8,128)(2,1)S(1)} %pad_maximum_fusion.5.refs_4_), channel_id=1, source_target_pairs={{0,12},{1,13},{2,14},{3,15},{4,8},{5,9},{6,10},{7,11},{8,4},{9,5},... | collective-permute-start | bytes 786440 | tf_op jit(solution)/shard_map/ppermute | solution.py:169
  33.4 3.0 %collective-permute-start.13 = (bf16[4,2,128,128]{3,2,1,0:T(8,128)(2,1)S(1)}, bf16[4,2,128,128]{3,2,1,0:T(8,128)(2,1)S(1)}, u32[]{:S(2)}, u32[]{:S(2)}) collective-permute-start(bf16[4,2,128,128]{3,2,1,0:T(8,128)(2,1)S(1)} %pad_maximum_fusion.5.refs_4_), channel_id=1, source_target_pairs={{0,8},{1,9},{2,10},{3,11},{4,12},{5,13},{6,14},{7,15},{8,0},{9,1},... | collective-permute-start | bytes 786440 | tf_op jit(solution)/shard_map/ppermute | solution.py:169
  37.0 1.0 broadcast_select_fusion.refs_7_
  38.2 10.1 %shard_map.84 = (bf16[2,128,512]{2,1,0:T(8,128)(2,1)S(1)}, bf16[2,128,512]{2,1,0:T(8,128)(2,1)S(1)}, bf16[2,128,512]{2,1,0:T(8,128)(2,1)S(1)}, bf16[2,128,512]{2...) custom-call(s32[4]{0:T(128)S(1)} %and_select_fusion.start_ref, ...), custom_call_target="tpu_custom_call" | custom-call | flops 13421772800 | bytes 8388608 | tf_op jit(solution)/shard_map/pallas_call | solution.py:142
  48.3 1.5 %collective-permute-start.17 = (bf16[4,2,128,128]{3,2,1,0:T(8,128)(2,1)S(1)}, bf16[4,2,128,128]{3,2,1,0:T(8,128)(2,1)S(1)}, u32[]{:S(2)}, u32[]{:S(2)}) collective-permute-start(bf16[4,2,128,128]{3,2,1,0:T(8,128)(2,1)S(1)} %get-tuple-element.60), channel_id=1, source_target_pairs={{0,4},{1,5},{2,6},{3,7},{4,0},{5,1},{6,2},{7,3},{8,12},{9,13},{10,... | collective-permute-start | bytes 786440 | tf_op jit(solution)/shard_map/ppermute | solution.py:169
  50.4 1.7 %collective-permute-done.10.refs_5_ = bf16[4,2,128,128]{3,2,1,0:T(8,128)(2,1)S(1)} collective-permute-done((bf16[4,2,128,128]{3,2,1,0:T(8,128)(2,1)S(1)}, bf16[4,2,128,128]{3,2,1,0:T(8,128)(2,1)S(1)}, u32[]{:S(2)}, u32[]{:S(2)}) %collective-permute-start.10) | collective-permute-done | bytes 262176 | tf_op jit(solution)/shard_map/ppermute | solution.py:169
  52.1 8.7 %collective-permute-start.11 = (bf16[4,2,128,128]{3,2,1,0:T(8,128)(2,1)S(1)}, bf16[4,2,128,128]{3,2,1,0:T(8,128)(2,1)S(1)}, u32[]{:S(2)}, u32[]{:S(2)}) collective-permute-start(bf16[4,2,128,128]{3,2,1,0:T(8,128)(2,1)S(1)} %get-tuple-element.52), channel_id=1, source_target_pairs={{0,4},{1,5},{2,6},{3,7},{4,0},{5,1},{6,2},{7,3},{8,12},{9,13},{10,... | collective-permute-start | bytes 786440 | tf_op jit(solution)/shard_map/ppermute | solution.py:169
  61.2 2.0 %collective-permute-done.17 = bf16[4,2,128,128]{3,2,1,0:T(8,128)(2,1)S(1)} collective-permute-done((bf16[4,2,128,128]{3,2,1,0:T(8,128)(2,1)S(1)}, bf16[4,2,128,128]{3,2,1,0:T(8,128)(2,1)S(1)}, u32[]{:S(2)}, u32[]{:S(2)}) %collective-permute-start.17) | collective-permute-done | bytes 262176 | tf_op jit(solution)/shard_map/ppermute | solution.py:169
  63.2 1.2 %collective-permute-start.14 = (bf16[2,128,512]{2,1,0:T(8,128)(2,1)S(1)}, bf16[2,128,512]{2,1,0:T(8,128)(2,1)S(1)}, u32[]{:S(2)}, u32[]{:S(2)}) collective-permute-start(bf16[2,128,512]{2,1,0:T(8,128)(2,1)S(1)} %get-tuple-element.56), channel_id=1, source_target_pairs={{0,2},{1,3},{2,0},{3,1},{4,6},{5,7},{6,4},{7,5},{8,10},{9,11},{10,... | collective-permute-start | bytes 786440 | tf_op jit(solution)/shard_map/ppermute | solution.py:169
  64.4 2.1 %collective-permute-start.18 = (bf16[4,2,128,128]{3,2,1,0:T(8,128)(2,1)S(1)}, bf16[4,2,128,128]{3,2,1,0:T(8,128)(2,1)S(1)}, u32[]{:S(2)}, u32[]{:S(2)}) collective-permute-start(bf16[4,2,128,128]{3,2,1,0:T(8,128)(2,1)S(1)} %add_convert_fusion.3), channel_id=1, source_target_pairs={{0,8},{1,9},{2,10},{3,11},{4,12},{5,13},{6,14},{7,15},{8,0},{9,1},... | collective-permute-start | bytes 786440 | tf_op jit(solution)/shard_map/ppermute | solution.py:169
  67.4 9.7 %shard_map.85 = (bf16[2,128,512]{2,1,0:T(8,128)(2,1)S(1)}, bf16[2,128,512]{2,1,0:T(8,128)(2,1)S(1)}, bf16[2,128,512]{2,1,0:T(8,128)(2,1)S(1)}, bf16[2,128,512]{2...) custom-call(s32[4]{0:T(128)S(1)} %and_select_fusion.start_ref, ...), custom_call_target="tpu_custom_call" | custom-call | flops 13421772800 | bytes 8388608 | tf_op jit(solution)/shard_map/pallas_call | solution.py:142
  77.5 1.3 %collective-permute-start.26 = (bf16[4,2,128,128]{3,2,1,0:T(8,128)(2,1)S(1)}, bf16[4,2,128,128]{3,2,1,0:T(8,128)(2,1)S(1)}, u32[]{:S(2)}, u32[]{:S(2)}) collective-permute-start(bf16[4,2,128,128]{3,2,1,0:T(8,128)(2,1)S(1)} %get-tuple-element.84), channel_id=1, source_target_pairs={{0,4},{1,5},{2,6},{3,7},{4,0},{5,1},{6,2},{7,3},{8,12},{9,13},{10,... | collective-permute-start | bytes 786440 | tf_op jit(solution)/shard_map/ppermute | solution.py:169
  79.5 0.9 collective-permute-start.20
  81.4 4.5 %collective-permute-done.26 = bf16[4,2,128,128]{3,2,1,0:T(8,128)(2,1)S(1)} collective-permute-done((bf16[4,2,128,128]{3,2,1,0:T(8,128)(2,1)S(1)}, bf16[4,2,128,128]{3,2,1,0:T(8,128)(2,1)S(1)}, u32[]{:S(2)}, u32[]{:S(2)}) %collective-permute-start.26) | collective-permute-done | bytes 262176 | tf_op jit(solution)/shard_map/ppermute | solution.py:169
  86.0 3.9 %collective-permute-start.28 = (bf16[4,2,128,128]{3,2,1,0:T(8,128)(2,1)S(1)}, bf16[4,2,128,128]{3,2,1,0:T(8,128)(2,1)S(1)}, u32[]{:S(2)}, u32[]{:S(2)}) collective-permute-start(bf16[4,2,128,128]{3,2,1,0:T(8,128)(2,1)S(1)} %add_convert_fusion.1), channel_id=1, source_target_pairs={{0,8},{1,9},{2,10},{3,11},{4,12},{5,13},{6,14},{7,15},{8,0},{9,1},... | collective-permute-start | bytes 786440 | tf_op jit(solution)/shard_map/ppermute | solution.py:169
  89.9 1.7 %collective-permute-start.27 = (bf16[4,2,128,128]{3,2,1,0:T(8,128)(2,1)S(1)}, bf16[4,2,128,128]{3,2,1,0:T(8,128)(2,1)S(1)}, u32[]{:S(2)}, u32[]{:S(2)}) collective-permute-start(bf16[4,2,128,128]{3,2,1,0:T(8,128)(2,1)S(1)} %get-tuple-element.85), channel_id=1, source_target_pairs={{0,4},{1,5},{2,6},{3,7},{4,0},{5,1},{6,2},{7,3},{8,12},{9,13},{10,... | collective-permute-start | bytes 786440 | tf_op jit(solution)/shard_map/ppermute | solution.py:169
  91.9 1.2 %collective-permute-done.23 = bf16[2,128,128]{2,1,0:T(8,128)(2,1)S(1)} collective-permute-done((bf16[2,128,128]{2,1,0:T(8,128)(2,1)S(1)}, bf16[2,128,128]{2,1,0:T(8,128)(2,1)S(1)}, u32[]{:S(2)}, u32[]{:S(2)}) %collective-permute-start.23) | collective-permute-done | bytes 65568 | tf_op jit(solution)/shard_map/ppermute | solution.py:169
  93.1 4.2 %collective-permute-done.24 = bf16[2,128,128]{2,1,0:T(8,128)(2,1)S(1)} collective-permute-done((bf16[2,128,128]{2,1,0:T(8,128)(2,1)S(1)}, bf16[2,128,128]{2,1,0:T(8,128)(2,1)S(1)}, u32[]{:S(2)}, u32[]{:S(2)}) %collective-permute-start.24) | collective-permute-done | bytes 65568 | tf_op jit(solution)/shard_map/ppermute | solution.py:169
  97.3 3.9 %collective-permute-done.25 = bf16[2,128,128]{2,1,0:T(8,128)(2,1)S(1)} collective-permute-done((bf16[2,128,128]{2,1,0:T(8,128)(2,1)S(1)}, bf16[2,128,128]{2,1,0:T(8,128)(2,1)S(1)}, u32[]{:S(2)}, u32[]{:S(2)}) %collective-permute-start.25) | collective-permute-done | bytes 65568 | tf_op jit(solution)/shard_map/ppermute | solution.py:169
  101.2 1.8 %collective-permute-done.27 = bf16[4,2,128,128]{3,2,1,0:T(8,128)(2,1)S(1)} collective-permute-done((bf16[4,2,128,128]{3,2,1,0:T(8,128)(2,1)S(1)}, bf16[4,2,128,128]{3,2,1,0:T(8,128)(2,1)S(1)}, u32[]{:S(2)}, u32[]{:S(2)}) %collective-permute-start.27) | collective-permute-done | bytes 262176 | tf_op jit(solution)/shard_map/ppermute | solution.py:169
  103.3 1.8 %collective-permute-start.32 = (bf16[2,128,128]{2,1,0:T(8,128)(2,1)S(1)}, bf16[2,128,128]{2,1,0:T(8,128)(2,1)S(1)}, u32[]{:S(2)}, u32[]{:S(2)}) collective-permute-start(bf16[2,128,128]{2,1,0:T(8,128)(2,1)S(1)} %get-tuple-element.96), channel_id=1, source_target_pairs={{0,3},{1,2},{2,1},{3,0},{4,7},{5,6},{6,5},{7,4},{8,11},{9,10},{10,... | collective-permute-start | bytes 196616 | tf_op jit(solution)/shard_map/ppermute | solution.py:169
  105.3 2.9 %collective-permute-done.31 = bf16[2,128,128]{2,1,0:T(8,128)(2,1)S(1)} collective-permute-done((bf16[2,128,128]{2,1,0:T(8,128)(2,1)S(1)}, bf16[2,128,128]{2,1,0:T(8,128)(2,1)S(1)}, u32[]{:S(2)}, u32[]{:S(2)}) %collective-permute-start.31) | collective-permute-done | bytes 65568 | tf_op jit(solution)/shard_map/ppermute | solution.py:169
  (126 shorter events, 13.9 us)
Async XLA Ops:
  2.7 7.5 %collective-permute-start.4 = (bf16[2,2,128,128]{3,2,1,0:T(8,128)(2,1)S(1)}, bf16[2,2,128,128]{3,2,1,0:T(8,128)(2,1)S(1)}, u32[]{:S(2)}, u32[]{:S(2)}) collective-permute-start(bf16[2,2,128,128]{3,2,1,0:T(8,128)(2,1)S(1)} %pad_maximum_fusion.7), channel_id=1, source_target_pairs={{0,2},{1,3},{2,0},{3,1},{4,6},{5,7},{6,4},{7,5},{8,10},{9,11},{10,... | collective-permute-start | bytes 393224 | tf_op jit(solution)/shard_map/ppermute | solution.py:169
  5.8 5.9 %collective-permute-start.5 = (bf16[2,2,128,128]{3,2,1,0:T(8,128)(2,1)S(1)}, bf16[2,2,128,128]{3,2,1,0:T(8,128)(2,1)S(1)}, u32[]{:S(2)}, u32[]{:S(2)}) collective-permute-start(bf16[2,2,128,128]{3,2,1,0:T(8,128)(2,1)S(1)} %pad_maximum_fusion.8), channel_id=1, source_target_pairs={{0,3},{1,2},{2,1},{3,0},{4,7},{5,6},{6,5},{7,4},{8,11},{9,10},{10,... | collective-permute-start | bytes 393224 | tf_op jit(solution)/shard_map/ppermute | solution.py:169
  5.9 2.3 %collective-permute-start = (bf16[2,2,128,128]{3,2,1,0:T(8,128)(2,1)S(1)}, bf16[2,2,128,128]{3,2,1,0:T(8,128)(2,1)S(1)}, u32[]{:S(2)}, u32[]{:S(2)}) collective-permute-start(bf16[2,2,128,128]{3,2,1,0:T(8,128)(2,1)S(1)} %pad_maximum_fusion.6), channel_id=1, source_target_pairs={{0,1},{1,0},{2,3},{3,2},{4,5},{5,4},{6,7},{7,6},{8,9},{9,8},{10,11... | collective-permute-start | bytes 393224 | tf_op jit(solution)/shard_map/ppermute | solution.py:169
  8.5 20.2 %collective-permute-start.1 = (bf16[2,128,1024]{2,1,0:T(8,128)(2,1)S(1)}, bf16[2,128,1024]{2,1,0:T(8,128)(2,1)S(1)}, u32[]{:S(2)}, u32[]{:S(2)}) collective-permute-start(bf16[2,128,1024]{2,1,0:T(8,128)(2,1)S(1)} %pad_maximum_fusion.2), channel_id=1, source_target_pairs={{0,3},{1,2},{2,1},{3,0},{4,7},{5,6},{6,5},{7,4},{8,11},{9,10},{10,... | collective-permute-start | bytes 1572872 | tf_op jit(solution)/shard_map/ppermute | solution.py:169
  12.4 15.8 %collective-permute-start.7 = (bf16[4,2,128,128]{3,2,1,0:T(8,128)(2,1)S(1)}, bf16[4,2,128,128]{3,2,1,0:T(8,128)(2,1)S(1)}, u32[]{:S(2)}, u32[]{:S(2)}) collective-permute-start(bf16[4,2,128,128]{3,2,1,0:T(8,128)(2,1)S(1)} %pad_maximum_fusion.4.refs_4_), channel_id=1, source_target_pairs={{0,8},{1,9},{2,10},{3,11},{4,12},{5,13},{6,14},{7,15},{8,0},{9,1},... | collective-permute-start | bytes 786440 | tf_op jit(solution)/shard_map/ppermute | solution.py:169
  15.1 15.3 %collective-permute-start.8 = (bf16[4,2,128,128]{3,2,1,0:T(8,128)(2,1)S(1)}, bf16[4,2,128,128]{3,2,1,0:T(8,128)(2,1)}, u32[]{:S(2)}, u32[]{:S(2)}) collective-permute-start(bf16[4,2,128,128]{3,2,1,0:T(8,128)(2,1)S(1)} %pad_maximum_fusion.4.refs_4_), channel_id=1, source_target_pairs={{0,0},{1,1},{2,2},{3,3},{4,8},{5,9},{6,10},{7,11},{8,4},{9,5},{10,... | collective-permute-start | bytes 786440 | tf_op jit(solution)/shard_map/ppermute | solution.py:169
  16.5 16.9 %collective-permute-start.6 = (bf16[4,2,128,128]{3,2,1,0:T(8,128)(2,1)S(1)}, bf16[4,2,128,128]{3,2,1,0:T(8,128)(2,1)S(1)}, u32[]{:S(2)}, u32[]{:S(2)}) collective-permute-start(bf16[4,2,128,128]{3,2,1,0:T(8,128)(2,1)S(1)} %pad_maximum_fusion.4.refs_4_), channel_id=1, source_target_pairs={{0,4},{1,5},{2,6},{3,7},{4,0},{5,1},{6,2},{7,3},{8,12},{9,13},{10,... | collective-permute-start | bytes 786440 | tf_op jit(solution)/shard_map/ppermute | solution.py:169
  19.5 16.9 %collective-permute-start.3 = (bf16[2,128,1024]{2,1,0:T(8,128)(2,1)}, bf16[2,128,1024]{2,1,0:T(8,128)(2,1)S(1)}, u32[]{:S(2)}, u32[]{:S(2)}) collective-permute-start(bf16[2,128,1024]{2,1,0:T(8,128)(2,1)} %pad_maximum_fusion.3), channel_id=1, source_target_pairs={{0,2},{1,3},{2,0},{3,1},{4,6},{5,7},{6,4},{7,5},{8,10},{9,11},{10,... | collective-permute-start | bytes 1572872 | tf_op jit(solution)/shard_map/ppermute | solution.py:169
  28.2 8.9 %collective-permute-start.9 = (bf16[4,2,128,128]{3,2,1,0:T(8,128)(2,1)S(1)}, bf16[4,2,128,128]{3,2,1,0:T(8,128)(2,1)}, u32[]{:S(2)}, u32[]{:S(2)}) collective-permute-start(bf16[4,2,128,128]{3,2,1,0:T(8,128)(2,1)S(1)} %collective-permute-done.7.refs_6_), channel_id=1, source_target_pairs={{0,4},{1,5},{2,6},{3,7},{4,0},{5,1},{6,2},{7,3},{8,12},{9,13},{10,... | collective-permute-start | bytes 786440 | tf_op jit(solution)/shard_map/ppermute | solution.py:169
  28.7 9.3 %collective-permute-start.2 = (bf16[2,128,1024]{2,1,0:T(8,128)(2,1)S(1)}, bf16[2,128,1024]{2,1,0:T(8,128)(2,1)S(1)}, u32[]{:S(2)}, u32[]{:S(2)}) collective-permute-start(bf16[2,128,1024]{2,1,0:T(8,128)(2,1)S(1)} %pad_maximum_fusion.1), channel_id=1, source_target_pairs={{0,1},{1,0},{2,3},{3,2},{4,5},{5,4},{6,7},{7,6},{8,9},{9,8},{10,11... | collective-permute-start | bytes 1572872 | tf_op jit(solution)/shard_map/ppermute | solution.py:169
  30.4 34.0 %collective-permute-start.16 = (bf16[4,2,128,128]{3,2,1,0:T(8,128)(2,1)S(1)}, bf16[4,2,128,128]{3,2,1,0:T(8,128)(2,1)S(1)}, u32[]{:S(2)}, u32[]{:S(2)}) collective-permute-start(bf16[4,2,128,128]{3,2,1,0:T(8,128)(2,1)S(1)} %pad_maximum_fusion.5.refs_4_), channel_id=1, source_target_pairs={{0,12},{1,13},{2,14},{3,15},{4,8},{5,9},{6,10},{7,11},{8,4},{9,5},... | collective-permute-start | bytes 786440 | tf_op jit(solution)/shard_map/ppermute | solution.py:169
  33.4 27.7 %collective-permute-start.13 = (bf16[4,2,128,128]{3,2,1,0:T(8,128)(2,1)S(1)}, bf16[4,2,128,128]{3,2,1,0:T(8,128)(2,1)S(1)}, u32[]{:S(2)}, u32[]{:S(2)}) collective-permute-start(bf16[4,2,128,128]{3,2,1,0:T(8,128)(2,1)S(1)} %pad_maximum_fusion.5.refs_4_), channel_id=1, source_target_pairs={{0,8},{1,9},{2,10},{3,11},{4,12},{5,13},{6,14},{7,15},{8,0},{9,1},... | collective-permute-start | bytes 786440 | tf_op jit(solution)/shard_map/ppermute | solution.py:169
  36.4 15.7 %collective-permute-start.10 = (bf16[4,2,128,128]{3,2,1,0:T(8,128)(2,1)S(1)}, bf16[4,2,128,128]{3,2,1,0:T(8,128)(2,1)S(1)}, u32[]{:S(2)}, u32[]{:S(2)}) collective-permute-start(bf16[4,2,128,128]{3,2,1,0:T(8,128)(2,1)S(1)} %pad_maximum_fusion.5.refs_4_), channel_id=1, source_target_pairs={{0,4},{1,5},{2,6},{3,7},{4,0},{5,1},{6,2},{7,3},{8,12},{9,13},{10,... | collective-permute-start | bytes 786440 | tf_op jit(solution)/shard_map/ppermute | solution.py:169
  48.3 14.9 %collective-permute-start.17 = (bf16[4,2,128,128]{3,2,1,0:T(8,128)(2,1)S(1)}, bf16[4,2,128,128]{3,2,1,0:T(8,128)(2,1)S(1)}, u32[]{:S(2)}, u32[]{:S(2)}) collective-permute-start(bf16[4,2,128,128]{3,2,1,0:T(8,128)(2,1)S(1)} %get-tuple-element.60), channel_id=1, source_target_pairs={{0,4},{1,5},{2,6},{3,7},{4,0},{5,1},{6,2},{7,3},{8,12},{9,13},{10,... | collective-permute-start | bytes 786440 | tf_op jit(solution)/shard_map/ppermute | solution.py:169
  49.7 27.4 %collective-permute-start.19 = (bf16[4,2,128,128]{3,2,1,0:T(8,128)(2,1)S(1)}, bf16[4,2,128,128]{3,2,1,0:T(8,128)(2,1)S(1)}, u32[]{:S(2)}, u32[]{:S(2)}) collective-permute-start(bf16[4,2,128,128]{3,2,1,0:T(8,128)(2,1)S(1)} %get-tuple-element.60), channel_id=1, source_target_pairs={{0,0},{1,1},{2,2},{3,3},{4,8},{5,9},{6,10},{7,11},{8,4},{9,5},{10,... | collective-permute-start | bytes 786440 | tf_op jit(solution)/shard_map/ppermute | solution.py:169
  52.1 15.3 %collective-permute-start.11 = (bf16[4,2,128,128]{3,2,1,0:T(8,128)(2,1)S(1)}, bf16[4,2,128,128]{3,2,1,0:T(8,128)(2,1)S(1)}, u32[]{:S(2)}, u32[]{:S(2)}) collective-permute-start(bf16[4,2,128,128]{3,2,1,0:T(8,128)(2,1)S(1)} %get-tuple-element.52), channel_id=1, source_target_pairs={{0,4},{1,5},{2,6},{3,7},{4,0},{5,1},{6,2},{7,3},{8,12},{9,13},{10,... | collective-permute-start | bytes 786440 | tf_op jit(solution)/shard_map/ppermute | solution.py:169
  61.1 16.0 %collective-permute-start.15 = (bf16[2,128,512]{2,1,0:T(8,128)(2,1)S(1)}, bf16[2,128,512]{2,1,0:T(8,128)(2,1)S(1)}, u32[]{:S(2)}, u32[]{:S(2)}) collective-permute-start(bf16[2,128,512]{2,1,0:T(8,128)(2,1)S(1)} %get-tuple-element.58), channel_id=1, source_target_pairs={{0,3},{1,2},{2,1},{3,0},{4,7},{5,6},{6,5},{7,4},{8,11},{9,10},{10,... | collective-permute-start | bytes 786440 | tf_op jit(solution)/shard_map/ppermute | solution.py:169
  63.2 13.9 %collective-permute-start.14 = (bf16[2,128,512]{2,1,0:T(8,128)(2,1)S(1)}, bf16[2,128,512]{2,1,0:T(8,128)(2,1)S(1)}, u32[]{:S(2)}, u32[]{:S(2)}) collective-permute-start(bf16[2,128,512]{2,1,0:T(8,128)(2,1)S(1)} %get-tuple-element.56), channel_id=1, source_target_pairs={{0,2},{1,3},{2,0},{3,1},{4,6},{5,7},{6,4},{7,5},{8,10},{9,11},{10,... | collective-permute-start | bytes 786440 | tf_op jit(solution)/shard_map/ppermute | solution.py:169
  64.4 13.1 %collective-permute-start.18 = (bf16[4,2,128,128]{3,2,1,0:T(8,128)(2,1)S(1)}, bf16[4,2,128,128]{3,2,1,0:T(8,128)(2,1)S(1)}, u32[]{:S(2)}, u32[]{:S(2)}) collective-permute-start(bf16[4,2,128,128]{3,2,1,0:T(8,128)(2,1)S(1)} %add_convert_fusion.3), channel_id=1, source_target_pairs={{0,8},{1,9},{2,10},{3,11},{4,12},{5,13},{6,14},{7,15},{8,0},{9,1},... | collective-permute-start | bytes 786440 | tf_op jit(solution)/shard_map/ppermute | solution.py:169
  67.4 13.9 %collective-permute-start.12 = (bf16[2,128,512]{2,1,0:T(8,128)(2,1)S(1)}, bf16[2,128,512]{2,1,0:T(8,128)(2,1)S(1)}, u32[]{:S(2)}, u32[]{:S(2)}) collective-permute-start(bf16[2,128,512]{2,1,0:T(8,128)(2,1)S(1)} %get-tuple-element.53), channel_id=1, source_target_pairs={{0,1},{1,0},{2,3},{3,2},{4,5},{5,4},{6,7},{7,6},{8,9},{9,8},{10,11... | collective-permute-start | bytes 786440 | tf_op jit(solution)/shard_map/ppermute | solution.py:169
  77.5 8.4 %collective-permute-start.26 = (bf16[4,2,128,128]{3,2,1,0:T(8,128)(2,1)S(1)}, bf16[4,2,128,128]{3,2,1,0:T(8,128)(2,1)S(1)}, u32[]{:S(2)}, u32[]{:S(2)}) collective-permute-start(bf16[4,2,128,128]{3,2,1,0:T(8,128)(2,1)S(1)} %get-tuple-element.84), channel_id=1, source_target_pairs={{0,4},{1,5},{2,6},{3,7},{4,0},{5,1},{6,2},{7,3},{8,12},{9,13},{10,... | collective-permute-start | bytes 786440 | tf_op jit(solution)/shard_map/ppermute | solution.py:169
  78.8 22.4 %collective-permute-start.29 = (bf16[4,2,128,128]{3,2,1,0:T(8,128)(2,1)S(1)}, bf16[4,2,128,128]{3,2,1,0:T(8,128)(2,1)S(1)}, u32[]{:S(2)}, u32[]{:S(2)}) collective-permute-start(bf16[4,2,128,128]{3,2,1,0:T(8,128)(2,1)S(1)} %get-tuple-element.84), channel_id=1, source_target_pairs={{0,0},{1,1},{2,2},{3,3},{4,8},{5,9},{6,10},{7,11},{8,4},{9,5},{10,... | collective-permute-start | bytes 786440 | tf_op jit(solution)/shard_map/ppermute | solution.py:169
  79.5 12.2 %collective-permute-start.20 = (bf16[2,128,512]{2,1,0:T(8,128)(2,1)S(1)}, bf16[2,128,512]{2,1,0:T(8,128)(2,1)S(1)}, u32[]{:S(2)}, u32[]{:S(2)}) collective-permute-start(bf16[2,128,512]{2,1,0:T(8,128)(2,1)S(1)} %get-tuple-element.76), channel_id=1, source_target_pairs={{0,2},{1,3},{2,0},{3,1},{4,6},{5,7},{6,4},{7,5},{8,10},{9,11},{10,... | collective-permute-start | bytes 786440 | tf_op jit(solution)/shard_map/ppermute | solution.py:169
  80.4 24.8 %collective-permute-start.22 = (bf16[2,128,512]{2,1,0:T(8,128)(2,1)S(1)}, bf16[2,128,512]{2,1,0:T(8,128)(2,1)S(1)}, u32[]{:S(2)}, u32[]{:S(2)}) collective-permute-start(bf16[2,128,512]{2,1,0:T(8,128)(2,1)S(1)} %get-tuple-element.78), channel_id=1, source_target_pairs={{0,3},{1,2},{2,1},{3,0},{4,7},{5,6},{6,5},{7,4},{8,11},{9,10},{10,... | collective-permute-start | bytes 786440 | tf_op jit(solution)/shard_map/ppermute | solution.py:169
  86.0 17.0 %collective-permute-start.28 = (bf16[4,2,128,128]{3,2,1,0:T(8,128)(2,1)S(1)}, bf16[4,2,128,128]{3,2,1,0:T(8,128)(2,1)S(1)}, u32[]{:S(2)}, u32[]{:S(2)}) collective-permute-start(bf16[4,2,128,128]{3,2,1,0:T(8,128)(2,1)S(1)} %add_convert_fusion.1), channel_id=1, source_target_pairs={{0,8},{1,9},{2,10},{3,11},{4,12},{5,13},{6,14},{7,15},{8,0},{9,1},... | collective-permute-start | bytes 786440 | tf_op jit(solution)/shard_map/ppermute | solution.py:169
  89.9 13.1 %collective-permute-start.27 = (bf16[4,2,128,128]{3,2,1,0:T(8,128)(2,1)S(1)}, bf16[4,2,128,128]{3,2,1,0:T(8,128)(2,1)S(1)}, u32[]{:S(2)}, u32[]{:S(2)}) collective-permute-start(bf16[4,2,128,128]{3,2,1,0:T(8,128)(2,1)S(1)} %get-tuple-element.85), channel_id=1, source_target_pairs={{0,4},{1,5},{2,6},{3,7},{4,0},{5,1},{6,2},{7,3},{8,12},{9,13},{10,... | collective-permute-start | bytes 786440 | tf_op jit(solution)/shard_map/ppermute | solution.py:169
  93.0 4.3 %collective-permute-start.24 = (bf16[2,128,128]{2,1,0:T(8,128)(2,1)S(1)}, bf16[2,128,128]{2,1,0:T(8,128)(2,1)S(1)}, u32[]{:S(2)}, u32[]{:S(2)}) collective-permute-start(bf16[2,128,128]{2,1,0:T(8,128)(2,1)S(1)} %get-tuple-element.100), channel_id=1, source_target_pairs={{0,2},{1,3},{2,0},{3,1},{4,6},{5,7},{6,4},{7,5},{8,10},{9,11},{10,... | collective-permute-start | bytes 196616 | tf_op jit(solution)/shard_map/ppermute | solution.py:169
  97.3 3.9 %collective-permute-start.25 = (bf16[2,128,128]{2,1,0:T(8,128)(2,1)S(1)}, bf16[2,128,128]{2,1,0:T(8,128)(2,1)S(1)}, u32[]{:S(2)}, u32[]{:S(2)}) collective-permute-start(bf16[2,128,128]{2,1,0:T(8,128)(2,1)S(1)} %get-tuple-element.99), channel_id=1, source_target_pairs={{0,3},{1,2},{2,1},{3,0},{4,7},{5,6},{6,5},{7,4},{8,11},{9,10},{10,... | collective-permute-start | bytes 196616 | tf_op jit(solution)/shard_map/ppermute | solution.py:169
  101.2 3.9 %collective-permute-start.21 = (bf16[2,128,512]{2,1,0:T(8,128)(2,1)S(1)}, bf16[2,128,512]{2,1,0:T(8,128)(2,1)S(1)}, u32[]{:S(2)}, u32[]{:S(2)}) collective-permute-start(bf16[2,128,512]{2,1,0:T(8,128)(2,1)S(1)} %get-tuple-element.77), channel_id=1, source_target_pairs={{0,1},{1,0},{2,3},{3,2},{4,5},{5,4},{6,7},{7,6},{8,9},{9,8},{10,11... | collective-permute-start | bytes 786440 | tf_op jit(solution)/shard_map/ppermute | solution.py:169
  103.2 2.1 %collective-permute-start.30 = (bf16[2,128,128]{2,1,0:T(8,128)(2,1)S(1)}, bf16[2,128,128]{2,1,0:T(8,128)(2,1)S(1)}, u32[]{:S(2)}, u32[]{:S(2)}) collective-permute-start(bf16[2,128,128]{2,1,0:T(8,128)(2,1)S(1)} %get-tuple-element.98), channel_id=1, source_target_pairs={{0,1},{1,0},{2,3},{3,2},{4,5},{5,4},{6,7},{7,6},{8,9},{9,8},{10,11... | collective-permute-start | bytes 196616 | tf_op jit(solution)/shard_map/ppermute | solution.py:169
  103.3 5.0 %collective-permute-start.31 = (bf16[2,128,128]{2,1,0:T(8,128)(2,1)S(1)}, bf16[2,128,128]{2,1,0:T(8,128)(2,1)S(1)}, u32[]{:S(2)}, u32[]{:S(2)}) collective-permute-start(bf16[2,128,128]{2,1,0:T(8,128)(2,1)S(1)} %get-tuple-element.97), channel_id=1, source_target_pairs={{0,2},{1,3},{2,0},{3,1},{4,6},{5,7},{6,4},{7,5},{8,10},{9,11},{10,... | collective-permute-start | bytes 196616 | tf_op jit(solution)/shard_map/ppermute | solution.py:169
  103.3 5.4 %collective-permute-start.32 = (bf16[2,128,128]{2,1,0:T(8,128)(2,1)S(1)}, bf16[2,128,128]{2,1,0:T(8,128)(2,1)S(1)}, u32[]{:S(2)}, u32[]{:S(2)}) collective-permute-start(bf16[2,128,128]{2,1,0:T(8,128)(2,1)S(1)} %get-tuple-element.96), channel_id=1, source_target_pairs={{0,3},{1,2},{2,1},{3,0},{4,7},{5,6},{6,5},{7,4},{8,11},{9,10},{10,... | collective-permute-start | bytes 196616 | tf_op jit(solution)/shard_map/ppermute | solution.py:169
  (10 other events, 41.2 us)

commit v5 on v4

--- a/solution.py
+++ b/solution.py
@@ -219,16 +219,13 @@
         return (value + jnp.where(inner, middle.astype(F32), 0.0)).astype(BF16)
 
     outs_a, sum_a = run(0, query_parts, a_parts)
-    a_passed = swapped(sum_a[3], one)
-    a_middle = middle_swapped(sum_a[3], lanes)
-    a_two = swapped(joined_two(sum_a, a_passed), two)
-    a_one = swapped(after(sum_a[1], b_one), one)
-    out_ax = swapped(after(outs_a[2], b_two), 2)
+    a_one = swapped(sum_a[1], one)
+    out_ax = swapped(outs_a[2], 2)
+    a_two = swapped(after(sum_a[2].astype(BF16), b_two), two)
+    a_three = swapped(after(sum_a[3], b_three), three)
     out_ad = swapped(after(outs_a[3], b_one), 3)
-    outs_b, sum_b = run(
-        1, query_parts, after([kv_owns[1], b_one, b_two, b_three], a_passed)
-    )
-    outs_b, sum_b = after((outs_b, sum_b), a_two, a_one, a_middle, out_ax, out_ad)
+    outs_b, sum_b = run(1, query_parts, [kv_owns[1], b_one, b_two, b_three])
+    outs_b, sum_b = after((outs_b, sum_b), a_two, a_one, a_three, out_ax, out_ad)
     b_passed = swapped(sum_b[3], one)
     out_ac = swapped(after(outs_a[1], a_one), 1)
     b_middle = middle_swapped(sum_b[3], lanes)
@@ -239,7 +236,12 @@
     b_one = swapped(after(sum_b[1], b_send), one)
     out_bc = swapped(after(outs_b[1], out_bx), 1)
     totals = [
-        after(total(sum_a, a_one, a_two, a_middle), out_bx),
+        after(
+            (
+                sum_a[0] + a_one.astype(F32) + a_two.astype(F32) + a_three.astype(F32)
+            ).astype(BF16),
+            out_bx,
+        ),
         total(sum_b, b_one, b_two, b_middle),
     ]
     outs_back = [[outs_a[0], out_ac, out_ax, out_ad], [outs_b[0], out_bc, out_bx, out_bd]]

time: 112 us -> 115 us (1.027)
  waiting for transfers between devices: 32.2 us -> 36.2 us
  starting transfers between devices: 44.9 us -> 42.9 us
  Pallas kernels: 19.8 us -> 21 us
    ppermute x33 -> x32, waiting for transfers between devices: 32.2 us -> 36.2 us  [moved(): return lax.ppermute(tensor, 'seq', [(i, target(i)) for i in range(devices)])]
    ppermute x33 -> x32, starting transfers between devices: 44.9 us -> 42.9 us  [moved(): return lax.ppermute(tensor, 'seq', [(i, target(i)) for i in range(devices)])]
    pallas_call x2, Pallas kernels: 19.8 us -> 21 us  [attend(): pl.pallas_call(functools.partial(attend_kernel, head, lanes, depth), out_...]
  transfers between devices with their start and end apart: 33 -> 32, of which waited for: 13 -> 11; matrix products, arithmetic and copies ran while one was open for 8% -> 8% of each run, Pallas kernels for 18% -> 19%
where the time goes in v5:
time: 115 us; the launch traced here: 113 us
  starting transfers between devices  42.9 us (37%)
  waiting for transfers between devices  36.2 us (31%)
  Pallas kernels  21 us (18%)
  local copies, waits for them, and re-layouts  6.2 us (5%)
  other arithmetic  5.13 us (4%)
  between operations  1.32 us (1%)
    ppermute x32, starting transfers between devices, moved(): return lax.ppermute(tensor, 'seq', [(i, target(i)) for i in range(devices)])  42.9 us
    ppermute x32, waiting for transfers between devices, moved(): return lax.ppermute(tensor, 'seq', [(i, target(i)) for i in range(devices)])  36.2 us
    pallas_call x2, Pallas kernels, attend(): pl.pallas_call(functools.partial(attend_kernel, head, lanes, depth), out_...  21 us
  transfers between devices with their start and end apart: 32, of which 11 were waited for; matrix products, arithmetic and copies ran while one was open for 8% of the time, Pallas kernels for 19%

profile of v5, /device:TPU:0, one launch (start us, length us, event | category | flops | bytes accessed | tf_op | source)
XLA Modules:
  0.0 112.9 jit_solution(11444103921912945572)
XLA Ops:
  0.7 1.0 dynamic-slice_bitcast_fusion.12
  1.7 1.0 dynamic-slice_bitcast_fusion.13
  2.7 3.0 %collective-permute-start.4 = (bf16[2,2,128,128]{3,2,1,0:T(8,128)(2,1)S(1)}, bf16[2,2,128,128]{3,2,1,0:T(8,128)(2,1)S(1)}, u32[]{:S(2)}, u32[]{:S(2)}) collective-permute-start(bf16[2,2,128,128]{3,2,1,0:T(8,128)(2,1)S(1)} %pad_maximum_fusion.7), channel_id=1, source_target_pairs={{0,2},{1,3},{2,0},{3,1},{4,6},{5,7},{6,4},{7,5},{8,10},{9,11},{10,... | collective-permute-start | bytes 393224 | tf_op jit(solution)/shard_map/ppermute | solution.py:169
  8.5 1.7 %collective-permute-start.1 = (bf16[2,128,1024]{2,1,0:T(8,128)(2,1)S(1)}, bf16[2,128,1024]{2,1,0:T(8,128)(2,1)S(1)}, u32[]{:S(2)}, u32[]{:S(2)}) collective-permute-start(bf16[2,128,1024]{2,1,0:T(8,128)(2,1)S(1)} %pad_maximum_fusion.2), channel_id=1, source_target_pairs={{0,3},{1,2},{2,1},{3,0},{4,7},{5,6},{6,5},{7,4},{8,11},{9,10},{10,... | collective-permute-start | bytes 1572872 | tf_op jit(solution)/shard_map/ppermute | solution.py:169
  12.4 2.6 %collective-permute-start.7 = (bf16[4,2,128,128]{3,2,1,0:T(8,128)(2,1)S(1)}, bf16[4,2,128,128]{3,2,1,0:T(8,128)(2,1)S(1)}, u32[]{:S(2)}, u32[]{:S(2)}) collective-permute-start(bf16[4,2,128,128]{3,2,1,0:T(8,128)(2,1)S(1)} %pad_maximum_fusion.4.refs_4_), channel_id=1, source_target_pairs={{0,8},{1,9},{2,10},{3,11},{4,12},{5,13},{6,14},{7,15},{8,0},{9,1},... | collective-permute-start | bytes 786440 | tf_op jit(solution)/shard_map/ppermute | solution.py:169
  15.1 1.4 %collective-permute-start.8 = (bf16[4,2,128,128]{3,2,1,0:T(8,128)(2,1)S(1)}, bf16[4,2,128,128]{3,2,1,0:T(8,128)(2,1)}, u32[]{:S(2)}, u32[]{:S(2)}) collective-permute-start(bf16[4,2,128,128]{3,2,1,0:T(8,128)(2,1)S(1)} %pad_maximum_fusion.4.refs_4_), channel_id=1, source_target_pairs={{0,0},{1,1},{2,2},{3,3},{4,8},{5,9},{6,10},{7,11},{8,4},{9,5},{10,... | collective-permute-start | bytes 786440 | tf_op jit(solution)/shard_map/ppermute | solution.py:169
  16.5 2.2 %collective-permute-start.6 = (bf16[4,2,128,128]{3,2,1,0:T(8,128)(2,1)S(1)}, bf16[4,2,128,128]{3,2,1,0:T(8,128)(2,1)S(1)}, u32[]{:S(2)}, u32[]{:S(2)}) collective-permute-start(bf16[4,2,128,128]{3,2,1,0:T(8,128)(2,1)S(1)} %pad_maximum_fusion.4.refs_4_), channel_id=1, source_target_pairs={{0,4},{1,5},{2,6},{3,7},{4,0},{5,1},{6,2},{7,3},{8,12},{9,13},{10,... | collective-permute-start | bytes 786440 | tf_op jit(solution)/shard_map/ppermute | solution.py:169
  18.7 0.8 pad_maximum_fusion.3
  19.5 1.1 %collective-permute-start.3 = (bf16[2,128,1024]{2,1,0:T(8,128)(2,1)}, bf16[2,128,1024]{2,1,0:T(8,128)(2,1)S(1)}, u32[]{:S(2)}, u32[]{:S(2)}) collective-permute-start(bf16[2,128,1024]{2,1,0:T(8,128)(2,1)} %pad_maximum_fusion.3), channel_id=1, source_target_pairs={{0,2},{1,3},{2,0},{3,1},{4,6},{5,7},{6,4},{7,5},{8,10},{9,11},{10,... | collective-permute-start | bytes 1572872 | tf_op jit(solution)/shard_map/ppermute | solution.py:169
  20.7 7.4 %collective-permute-done.7.refs_6_ = bf16[4,2,128,128]{3,2,1,0:T(8,128)(2,1)S(1)} collective-permute-done((bf16[4,2,128,128]{3,2,1,0:T(8,128)(2,1)S(1)}, bf16[4,2,128,128]{3,2,1,0:T(8,128)(2,1)S(1)}, u32[]{:S(2)}, u32[]{:S(2)}) %collective-permute-start.7) | collective-permute-done | bytes 262176 | tf_op jit(solution)/shard_map/ppermute | solution.py:169
  29.4 0.9 pad_maximum_fusion.5.refs_4_
  30.4 3.0 %collective-permute-start.16 = (bf16[4,2,128,128]{3,2,1,0:T(8,128)(2,1)S(1)}, bf16[4,2,128,128]{3,2,1,0:T(8,128)(2,1)S(1)}, u32[]{:S(2)}, u32[]{:S(2)}) collective-permute-start(bf16[4,2,128,128]{3,2,1,0:T(8,128)(2,1)S(1)} %pad_maximum_fusion.5.refs_4_), channel_id=1, source_target_pairs={{0,12},{1,13},{2,14},{3,15},{4,8},{5,9},{6,10},{7,11},{8,4},{9,5},... | collective-permute-start | bytes 786440 | tf_op jit(solution)/shard_map/ppermute | solution.py:169
  33.4 3.0 %collective-permute-start.15 = (bf16[4,2,128,128]{3,2,1,0:T(8,128)(2,1)S(1)}, bf16[4,2,128,128]{3,2,1,0:T(8,128)(2,1)S(1)}, u32[]{:S(2)}, u32[]{:S(2)}) collective-permute-start(bf16[4,2,128,128]{3,2,1,0:T(8,128)(2,1)S(1)} %pad_maximum_fusion.5.refs_4_), channel_id=1, source_target_pairs={{0,8},{1,9},{2,10},{3,11},{4,12},{5,13},{6,14},{7,15},{8,0},{9,1},... | collective-permute-start | bytes 786440 | tf_op jit(solution)/shard_map/ppermute | solution.py:169
  37.0 1.0 broadcast_select_fusion.refs_7_
  38.1 10.7 %shard_map.84 = (bf16[2,128,512]{2,1,0:T(8,128)(2,1)S(1)}, bf16[2,128,512]{2,1,0:T(8,128)(2,1)S(1)}, bf16[2,128,512]{2,1,0:T(8,128)(2,1)S(1)}, bf16[2,128,512]{2...) custom-call(s32[4]{0:T(128)S(1)} %and_select_fusion.start_ref, ...), custom_call_target="tpu_custom_call" | custom-call | flops 13421772800 | bytes 8388608 | tf_op jit(solution)/shard_map/pallas_call | solution.py:142
  48.9 9.4 %collective-permute-start.18 = (bf16[4,2,128,128]{3,2,1,0:T(8,128)(2,1)S(1)}, bf16[4,2,128,128]{3,2,1,0:T(8,128)(2,1)S(1)}, u32[]{:S(2)}, u32[]{:S(2)}) collective-permute-start(bf16[4,2,128,128]{3,2,1,0:T(8,128)(2,1)S(1)} %get-tuple-element.65), channel_id=1, source_target_pairs={{0,12},{1,13},{2,14},{3,15},{4,8},{5,9},{6,10},{7,11},{8,4},{9,5},... | collective-permute-start | bytes 786440 | tf_op jit(solution)/shard_map/ppermute | solution.py:169
  58.4 7.4 %collective-permute-done.15.refs_6_ = bf16[4,2,128,128]{3,2,1,0:T(8,128)(2,1)S(1)} collective-permute-done((bf16[4,2,128,128]{3,2,1,0:T(8,128)(2,1)S(1)}, bf16[4,2,128,128]{3,2,1,0:T(8,128)(2,1)S(1)}, u32[]{:S(2)}, u32[]{:S(2)}) %collective-permute-start.15) | collective-permute-done | bytes 262176 | tf_op jit(solution)/shard_map/ppermute | solution.py:169
  66.0 2.0 %collective-permute-start.10 = (bf16[4,2,128,128]{3,2,1,0:T(8,128)(2,1)S(1)}, bf16[4,2,128,128]{3,2,1,0:T(8,128)(2,1)S(1)}, u32[]{:S(2)}, u32[]{:S(2)}) collective-permute-start(bf16[4,2,128,128]{3,2,1,0:T(8,128)(2,1)S(1)} %get-tuple-element.46), channel_id=1, source_target_pairs={{0,4},{1,5},{2,6},{3,7},{4,0},{5,1},{6,2},{7,3},{8,12},{9,13},{10,... | collective-permute-start | bytes 786440 | tf_op jit(solution)/shard_map/ppermute | solution.py:169
  68.1 0.8 collective-permute-start.12
  68.9 10.3 %shard_map.85 = (bf16[2,128,512]{2,1,0:T(8,128)(2,1)S(1)}, bf16[2,128,512]{2,1,0:T(8,128)(2,1)S(1)}, bf16[2,128,512]{2,1,0:T(8,128)(2,1)S(1)}, bf16[2,128,512]{2...) custom-call(s32[4]{0:T(128)S(1)} %and_select_fusion.start_ref, ...), custom_call_target="tpu_custom_call" | custom-call | flops 13421772800 | bytes 8388608 | tf_op jit(solution)/shard_map/pallas_call | solution.py:142
  79.5 2.8 %collective-permute-done.17 = bf16[4,2,128,128]{3,2,1,0:T(8,128)(2,1)S(1)} collective-permute-done((bf16[4,2,128,128]{3,2,1,0:T(8,128)(2,1)S(1)}, bf16[4,2,128,128]{3,2,1,0:T(8,128)(2,1)S(1)}, u32[]{:S(2)}, u32[]{:S(2)}) %collective-permute-start.17) | collective-permute-done | bytes 262176 | tf_op jit(solution)/shard_map/ppermute | solution.py:169
  83.0 1.3 %collective-permute-start.19 = (bf16[2,128,512]{2,1,0:T(8,128)(2,1)S(1)}, bf16[2,128,512]{2,1,0:T(8,128)(2,1)S(1)}, u32[]{:S(2)}, u32[]{:S(2)}) collective-permute-start(bf16[2,128,512]{2,1,0:T(8,128)(2,1)S(1)} %get-tuple-element.68), channel_id=1, source_target_pairs={{0,2},{1,3},{2,0},{3,1},{4,6},{5,7},{6,4},{7,5},{8,10},{9,11},{10,... | collective-permute-start | bytes 786440 | tf_op jit(solution)/shard_map/ppermute | solution.py:169
  84.3 0.9 collective-permute-start.21
  85.4 5.0 %collective-permute-done.25 = bf16[4,2,128,128]{3,2,1,0:T(8,128)(2,1)S(1)} collective-permute-done((bf16[4,2,128,128]{3,2,1,0:T(8,128)(2,1)S(1)}, bf16[4,2,128,128]{3,2,1,0:T(8,128)(2,1)S(1)}, u32[]{:S(2)}, u32[]{:S(2)}) %collective-permute-start.25) | collective-permute-done | bytes 262176 | tf_op jit(solution)/shard_map/ppermute | solution.py:169
  91.1 1.2 %collective-permute-done.19 = bf16[2,128,512]{2,1,0:T(8,128)(2,1)S(1)} collective-permute-done((bf16[2,128,512]{2,1,0:T(8,128)(2,1)S(1)}, bf16[2,128,512]{2,1,0:T(8,128)(2,1)S(1)}, u32[]{:S(2)}, u32[]{:S(2)}) %collective-permute-start.19) | collective-permute-done | bytes 262176 | tf_op jit(solution)/shard_map/ppermute | solution.py:169
  92.3 3.9 %collective-permute-start.26 = (bf16[4,2,128,128]{3,2,1,0:T(8,128)(2,1)S(1)}, bf16[4,2,128,128]{3,2,1,0:T(8,128)(2,1)S(1)}, u32[]{:S(2)}, u32[]{:S(2)}) collective-permute-start(bf16[4,2,128,128]{3,2,1,0:T(8,128)(2,1)S(1)} %get-tuple-element.77), channel_id=1, source_target_pairs={{0,4},{1,5},{2,6},{3,7},{4,0},{5,1},{6,2},{7,3},{8,12},{9,13},{10,... | collective-permute-start | bytes 786440 | tf_op jit(solution)/shard_map/ppermute | solution.py:169
  96.5 1.0 collective-permute-done.22
  97.6 1.2 %collective-permute-start.23 = (bf16[2,128,128]{2,1,0:T(8,128)(2,1)S(1)}, bf16[2,128,128]{2,1,0:T(8,128)(2,1)S(1)}, u32[]{:S(2)}, u32[]{:S(2)}) collective-permute-start(bf16[2,128,128]{2,1,0:T(8,128)(2,1)S(1)} %get-tuple-element.92), channel_id=1, source_target_pairs={{0,2},{1,3},{2,0},{3,1},{4,6},{5,7},{6,4},{7,5},{8,10},{9,11},{10,... | collective-permute-start | bytes 196616 | tf_op jit(solution)/shard_map/ppermute | solution.py:169
  98.9 3.0 %collective-permute-done.23 = bf16[2,128,128]{2,1,0:T(8,128)(2,1)S(1)} collective-permute-done((bf16[2,128,128]{2,1,0:T(8,128)(2,1)S(1)}, bf16[2,128,128]{2,1,0:T(8,128)(2,1)S(1)}, u32[]{:S(2)}, u32[]{:S(2)}) %collective-permute-start.23) | collective-permute-done | bytes 65568 | tf_op jit(solution)/shard_map/ppermute | solution.py:169
  102.0 4.0 %collective-permute-done.24 = bf16[2,128,128]{2,1,0:T(8,128)(2,1)S(1)} collective-permute-done((bf16[2,128,128]{2,1,0:T(8,128)(2,1)S(1)}, bf16[2,128,128]{2,1,0:T(8,128)(2,1)S(1)}, u32[]{:S(2)}, u32[]{:S(2)}) %collective-permute-start.24) | collective-permute-done | bytes 65568 | tf_op jit(solution)/shard_map/ppermute | solution.py:169
  106.8 0.9 collective-permute-start.30
  108.5 3.1 %collective-permute-done.30 = bf16[2,128,128]{2,1,0:T(8,128)(2,1)S(1)} collective-permute-done((bf16[2,128,128]{2,1,0:T(8,128)(2,1)S(1)}, bf16[2,128,128]{2,1,0:T(8,128)(2,1)S(1)}, u32[]{:S(2)}, u32[]{:S(2)}) %collective-permute-start.30) | collective-permute-done | bytes 65568 | tf_op jit(solution)/shard_map/ppermute | solution.py:169
  (124 shorter events, 12.4 us)
Async XLA Ops:
  2.7 7.5 %collective-permute-start.4 = (bf16[2,2,128,128]{3,2,1,0:T(8,128)(2,1)S(1)}, bf16[2,2,128,128]{3,2,1,0:T(8,128)(2,1)S(1)}, u32[]{:S(2)}, u32[]{:S(2)}) collective-permute-start(bf16[2,2,128,128]{3,2,1,0:T(8,128)(2,1)S(1)} %pad_maximum_fusion.7), channel_id=1, source_target_pairs={{0,2},{1,3},{2,0},{3,1},{4,6},{5,7},{6,4},{7,5},{8,10},{9,11},{10,... | collective-permute-start | bytes 393224 | tf_op jit(solution)/shard_map/ppermute | solution.py:169
  5.8 5.9 %collective-permute-start.5 = (bf16[2,2,128,128]{3,2,1,0:T(8,128)(2,1)S(1)}, bf16[2,2,128,128]{3,2,1,0:T(8,128)(2,1)S(1)}, u32[]{:S(2)}, u32[]{:S(2)}) collective-permute-start(bf16[2,2,128,128]{3,2,1,0:T(8,128)(2,1)S(1)} %pad_maximum_fusion.8), channel_id=1, source_target_pairs={{0,3},{1,2},{2,1},{3,0},{4,7},{5,6},{6,5},{7,4},{8,11},{9,10},{10,... | collective-permute-start | bytes 393224 | tf_op jit(solution)/shard_map/ppermute | solution.py:169
  5.9 2.3 %collective-permute-start = (bf16[2,2,128,128]{3,2,1,0:T(8,128)(2,1)S(1)}, bf16[2,2,128,128]{3,2,1,0:T(8,128)(2,1)S(1)}, u32[]{:S(2)}, u32[]{:S(2)}) collective-permute-start(bf16[2,2,128,128]{3,2,1,0:T(8,128)(2,1)S(1)} %pad_maximum_fusion.6), channel_id=1, source_target_pairs={{0,1},{1,0},{2,3},{3,2},{4,5},{5,4},{6,7},{7,6},{8,9},{9,8},{10,11... | collective-permute-start | bytes 393224 | tf_op jit(solution)/shard_map/ppermute | solution.py:169
  8.5 20.2 %collective-permute-start.1 = (bf16[2,128,1024]{2,1,0:T(8,128)(2,1)S(1)}, bf16[2,128,1024]{2,1,0:T(8,128)(2,1)S(1)}, u32[]{:S(2)}, u32[]{:S(2)}) collective-permute-start(bf16[2,128,1024]{2,1,0:T(8,128)(2,1)S(1)} %pad_maximum_fusion.2), channel_id=1, source_target_pairs={{0,3},{1,2},{2,1},{3,0},{4,7},{5,6},{6,5},{7,4},{8,11},{9,10},{10,... | collective-permute-start | bytes 1572872 | tf_op jit(solution)/shard_map/ppermute | solution.py:169
  12.4 15.8 %collective-permute-start.7 = (bf16[4,2,128,128]{3,2,1,0:T(8,128)(2,1)S(1)}, bf16[4,2,128,128]{3,2,1,0:T(8,128)(2,1)S(1)}, u32[]{:S(2)}, u32[]{:S(2)}) collective-permute-start(bf16[4,2,128,128]{3,2,1,0:T(8,128)(2,1)S(1)} %pad_maximum_fusion.4.refs_4_), channel_id=1, source_target_pairs={{0,8},{1,9},{2,10},{3,11},{4,12},{5,13},{6,14},{7,15},{8,0},{9,1},... | collective-permute-start | bytes 786440 | tf_op jit(solution)/shard_map/ppermute | solution.py:169
  15.1 15.3 %collective-permute-start.8 = (bf16[4,2,128,128]{3,2,1,0:T(8,128)(2,1)S(1)}, bf16[4,2,128,128]{3,2,1,0:T(8,128)(2,1)}, u32[]{:S(2)}, u32[]{:S(2)}) collective-permute-start(bf16[4,2,128,128]{3,2,1,0:T(8,128)(2,1)S(1)} %pad_maximum_fusion.4.refs_4_), channel_id=1, source_target_pairs={{0,0},{1,1},{2,2},{3,3},{4,8},{5,9},{6,10},{7,11},{8,4},{9,5},{10,... | collective-permute-start | bytes 786440 | tf_op jit(solution)/shard_map/ppermute | solution.py:169
  16.5 16.9 %collective-permute-start.6 = (bf16[4,2,128,128]{3,2,1,0:T(8,128)(2,1)S(1)}, bf16[4,2,128,128]{3,2,1,0:T(8,128)(2,1)S(1)}, u32[]{:S(2)}, u32[]{:S(2)}) collective-permute-start(bf16[4,2,128,128]{3,2,1,0:T(8,128)(2,1)S(1)} %pad_maximum_fusion.4.refs_4_), channel_id=1, source_target_pairs={{0,4},{1,5},{2,6},{3,7},{4,0},{5,1},{6,2},{7,3},{8,12},{9,13},{10,... | collective-permute-start | bytes 786440 | tf_op jit(solution)/shard_map/ppermute | solution.py:169
  19.5 16.8 %collective-permute-start.3 = (bf16[2,128,1024]{2,1,0:T(8,128)(2,1)}, bf16[2,128,1024]{2,1,0:T(8,128)(2,1)S(1)}, u32[]{:S(2)}, u32[]{:S(2)}) collective-permute-start(bf16[2,128,1024]{2,1,0:T(8,128)(2,1)} %pad_maximum_fusion.3), channel_id=1, source_target_pairs={{0,2},{1,3},{2,0},{3,1},{4,6},{5,7},{6,4},{7,5},{8,10},{9,11},{10,... | collective-permute-start | bytes 1572872 | tf_op jit(solution)/shard_map/ppermute | solution.py:169
  28.2 8.8 %collective-permute-start.9 = (bf16[4,2,128,128]{3,2,1,0:T(8,128)(2,1)S(1)}, bf16[4,2,128,128]{3,2,1,0:T(8,128)(2,1)}, u32[]{:S(2)}, u32[]{:S(2)}) collective-permute-start(bf16[4,2,128,128]{3,2,1,0:T(8,128)(2,1)S(1)} %collective-permute-done.7.refs_6_), channel_id=1, source_target_pairs={{0,4},{1,5},{2,6},{3,7},{4,0},{5,1},{6,2},{7,3},{8,12},{9,13},{10,... | collective-permute-start | bytes 786440 | tf_op jit(solution)/shard_map/ppermute | solution.py:169
  28.7 9.3 %collective-permute-start.2 = (bf16[2,128,1024]{2,1,0:T(8,128)(2,1)S(1)}, bf16[2,128,1024]{2,1,0:T(8,128)(2,1)S(1)}, u32[]{:S(2)}, u32[]{:S(2)}) collective-permute-start(bf16[2,128,1024]{2,1,0:T(8,128)(2,1)S(1)} %pad_maximum_fusion.1), channel_id=1, source_target_pairs={{0,1},{1,0},{2,3},{3,2},{4,5},{5,4},{6,7},{7,6},{8,9},{9,8},{10,11... | collective-permute-start | bytes 1572872 | tf_op jit(solution)/shard_map/ppermute | solution.py:169
  30.4 18.5 %collective-permute-start.16 = (bf16[4,2,128,128]{3,2,1,0:T(8,128)(2,1)S(1)}, bf16[4,2,128,128]{3,2,1,0:T(8,128)(2,1)S(1)}, u32[]{:S(2)}, u32[]{:S(2)}) collective-permute-start(bf16[4,2,128,128]{3,2,1,0:T(8,128)(2,1)S(1)} %pad_maximum_fusion.5.refs_4_), channel_id=1, source_target_pairs={{0,12},{1,13},{2,14},{3,15},{4,8},{5,9},{6,10},{7,11},{8,4},{9,5},... | collective-permute-start | bytes 786440 | tf_op jit(solution)/shard_map/ppermute | solution.py:169
  33.4 32.4 %collective-permute-start.15 = (bf16[4,2,128,128]{3,2,1,0:T(8,128)(2,1)S(1)}, bf16[4,2,128,128]{3,2,1,0:T(8,128)(2,1)S(1)}, u32[]{:S(2)}, u32[]{:S(2)}) collective-permute-start(bf16[4,2,128,128]{3,2,1,0:T(8,128)(2,1)S(1)} %pad_maximum_fusion.5.refs_4_), channel_id=1, source_target_pairs={{0,8},{1,9},{2,10},{3,11},{4,12},{5,13},{6,14},{7,15},{8,0},{9,1},... | collective-permute-start | bytes 786440 | tf_op jit(solution)/shard_map/ppermute | solution.py:169
  36.4 29.4 %collective-permute-start.13 = (bf16[4,2,128,128]{3,2,1,0:T(8,128)(2,1)S(1)}, bf16[4,2,128,128]{3,2,1,0:T(8,128)(2,1)S(1)}, u32[]{:S(2)}, u32[]{:S(2)}) collective-permute-start(bf16[4,2,128,128]{3,2,1,0:T(8,128)(2,1)S(1)} %pad_maximum_fusion.5.refs_4_), channel_id=1, source_target_pairs={{0,4},{1,5},{2,6},{3,7},{4,0},{5,1},{6,2},{7,3},{8,12},{9,13},{10,... | collective-permute-start | bytes 786440 | tf_op jit(solution)/shard_map/ppermute | solution.py:169
  48.9 30.6 %collective-permute-start.18 = (bf16[4,2,128,128]{3,2,1,0:T(8,128)(2,1)S(1)}, bf16[4,2,128,128]{3,2,1,0:T(8,128)(2,1)S(1)}, u32[]{:S(2)}, u32[]{:S(2)}) collective-permute-start(bf16[4,2,128,128]{3,2,1,0:T(8,128)(2,1)S(1)} %get-tuple-element.65), channel_id=1, source_target_pairs={{0,12},{1,13},{2,14},{3,15},{4,8},{5,9},{6,10},{7,11},{8,4},{9,5},... | collective-permute-start | bytes 786440 | tf_op jit(solution)/shard_map/ppermute | solution.py:169
  65.7 16.5 %collective-permute-start.17 = (bf16[4,2,128,128]{3,2,1,0:T(8,128)(2,1)S(1)}, bf16[4,2,128,128]{3,2,1,0:T(8,128)(2,1)S(1)}, u32[]{:S(2)}, u32[]{:S(2)}) collective-permute-start(bf16[4,2,128,128]{3,2,1,0:T(8,128)(2,1)S(1)} %convert_element_type.37), channel_id=1, source_target_pairs={{0,8},{1,9},{2,10},{3,11},{4,12},{5,13},{6,14},{7,15},{8,0},{9,1},... | collective-permute-start | bytes 786440 | tf_op jit(solution)/shard_map/ppermute | solution.py:169
  65.7 16.5 %collective-permute-start.14 = (bf16[2,128,512]{2,1,0:T(8,128)(2,1)S(1)}, bf16[2,128,512]{2,1,0:T(8,128)(2,1)S(1)}, u32[]{:S(2)}, u32[]{:S(2)}) collective-permute-start(bf16[2,128,512]{2,1,0:T(8,128)(2,1)S(1)} %get-tuple-element.51), channel_id=1, source_target_pairs={{0,3},{1,2},{2,1},{3,0},{4,7},{5,6},{6,5},{7,4},{8,11},{9,10},{10,... | collective-permute-start | bytes 786440 | tf_op jit(solution)/shard_map/ppermute | solution.py:169
  66.0 16.2 %collective-permute-start.10 = (bf16[4,2,128,128]{3,2,1,0:T(8,128)(2,1)S(1)}, bf16[4,2,128,128]{3,2,1,0:T(8,128)(2,1)S(1)}, u32[]{:S(2)}, u32[]{:S(2)}) collective-permute-start(bf16[4,2,128,128]{3,2,1,0:T(8,128)(2,1)S(1)} %get-tuple-element.46), channel_id=1, source_target_pairs={{0,4},{1,5},{2,6},{3,7},{4,0},{5,1},{6,2},{7,3},{8,12},{9,13},{10,... | collective-permute-start | bytes 786440 | tf_op jit(solution)/shard_map/ppermute | solution.py:169
  68.1 14.2 %collective-permute-start.12 = (bf16[2,128,512]{2,1,0:T(8,128)(2,1)S(1)}, bf16[2,128,512]{2,1,0:T(8,128)(2,1)S(1)}, u32[]{:S(2)}, u32[]{:S(2)}) collective-permute-start(bf16[2,128,512]{2,1,0:T(8,128)(2,1)S(1)} %get-tuple-element.48), channel_id=1, source_target_pairs={{0,2},{1,3},{2,0},{3,1},{4,6},{5,7},{6,4},{7,5},{8,10},{9,11},{10,... | collective-permute-start | bytes 786440 | tf_op jit(solution)/shard_map/ppermute | solution.py:169
  82.3 8.1 %collective-permute-start.25 = (bf16[4,2,128,128]{3,2,1,0:T(8,128)(2,1)S(1)}, bf16[4,2,128,128]{3,2,1,0:T(8,128)(2,1)S(1)}, u32[]{:S(2)}, u32[]{:S(2)}) collective-permute-start(bf16[4,2,128,128]{3,2,1,0:T(8,128)(2,1)S(1)} %get-tuple-element.76), channel_id=1, source_target_pairs={{0,4},{1,5},{2,6},{3,7},{4,0},{5,1},{6,2},{7,3},{8,12},{9,13},{10,... | collective-permute-start | bytes 786440 | tf_op jit(solution)/shard_map/ppermute | solution.py:169
  82.3 23.7 %collective-permute-start.28 = (bf16[4,2,128,128]{3,2,1,0:T(8,128)(2,1)S(1)}, bf16[4,2,128,128]{3,2,1,0:T(8,128)(2,1)S(1)}, u32[]{:S(2)}, u32[]{:S(2)}) collective-permute-start(bf16[4,2,128,128]{3,2,1,0:T(8,128)(2,1)S(1)} %get-tuple-element.76), channel_id=1, source_target_pairs={{0,0},{1,1},{2,2},{3,3},{4,8},{5,9},{6,10},{7,11},{8,4},{9,5},{10,... | collective-permute-start | bytes 786440 | tf_op jit(solution)/shard_map/ppermute | solution.py:169
  83.0 9.3 %collective-permute-start.19 = (bf16[2,128,512]{2,1,0:T(8,128)(2,1)S(1)}, bf16[2,128,512]{2,1,0:T(8,128)(2,1)S(1)}, u32[]{:S(2)}, u32[]{:S(2)}) collective-permute-start(bf16[2,128,512]{2,1,0:T(8,128)(2,1)S(1)} %get-tuple-element.68), channel_id=1, source_target_pairs={{0,2},{1,3},{2,0},{3,1},{4,6},{5,7},{6,4},{7,5},{8,10},{9,11},{10,... | collective-permute-start | bytes 786440 | tf_op jit(solution)/shard_map/ppermute | solution.py:169
  84.3 12.0 %collective-permute-start.11 = (bf16[2,128,512]{2,1,0:T(8,128)(2,1)S(1)}, bf16[2,128,512]{2,1,0:T(8,128)(2,1)S(1)}, u32[]{:S(2)}, u32[]{:S(2)}) collective-permute-start(bf16[2,128,512]{2,1,0:T(8,128)(2,1)S(1)} %get-tuple-element.47), channel_id=1, source_target_pairs={{0,1},{1,0},{2,3},{3,2},{4,5},{5,4},{6,7},{7,6},{8,9},{9,8},{10,11... | collective-permute-start | bytes 786440 | tf_op jit(solution)/shard_map/ppermute | solution.py:169
  84.3 24.0 %collective-permute-start.21 = (bf16[2,128,512]{2,1,0:T(8,128)(2,1)S(1)}, bf16[2,128,512]{2,1,0:T(8,128)(2,1)S(1)}, u32[]{:S(2)}, u32[]{:S(2)}) collective-permute-start(bf16[2,128,512]{2,1,0:T(8,128)(2,1)S(1)} %get-tuple-element.70), channel_id=1, source_target_pairs={{0,3},{1,2},{2,1},{3,0},{4,7},{5,6},{6,5},{7,4},{8,11},{9,10},{10,... | collective-permute-start | bytes 786440 | tf_op jit(solution)/shard_map/ppermute | solution.py:169
  90.4 15.7 %collective-permute-start.27 = (bf16[4,2,128,128]{3,2,1,0:T(8,128)(2,1)S(1)}, bf16[4,2,128,128]{3,2,1,0:T(8,128)(2,1)S(1)}, u32[]{:S(2)}, u32[]{:S(2)}) collective-permute-start(bf16[4,2,128,128]{3,2,1,0:T(8,128)(2,1)S(1)} %add_convert_fusion.1), channel_id=1, source_target_pairs={{0,8},{1,9},{2,10},{3,11},{4,12},{5,13},{6,14},{7,15},{8,0},{9,1},... | collective-permute-start | bytes 786440 | tf_op jit(solution)/shard_map/ppermute | solution.py:169
  92.3 13.8 %collective-permute-start.26 = (bf16[4,2,128,128]{3,2,1,0:T(8,128)(2,1)S(1)}, bf16[4,2,128,128]{3,2,1,0:T(8,128)(2,1)S(1)}, u32[]{:S(2)}, u32[]{:S(2)}) collective-permute-start(bf16[4,2,128,128]{3,2,1,0:T(8,128)(2,1)S(1)} %get-tuple-element.77), channel_id=1, source_target_pairs={{0,4},{1,5},{2,6},{3,7},{4,0},{5,1},{6,2},{7,3},{8,12},{9,13},{10,... | collective-permute-start | bytes 786440 | tf_op jit(solution)/shard_map/ppermute | solution.py:169
  96.3 1.3 %collective-permute-start.22 = (bf16[2,128,128]{2,1,0:T(8,128)(2,1)S(1)}, bf16[2,128,128]{2,1,0:T(8,128)(2,1)S(1)}, u32[]{:S(2)}, u32[]{:S(2)}) collective-permute-start(bf16[2,128,128]{2,1,0:T(8,128)(2,1)S(1)} %get-tuple-element.93), channel_id=1, source_target_pairs={{0,1},{1,0},{2,3},{3,2},{4,5},{5,4},{6,7},{7,6},{8,9},{9,8},{10,11... | collective-permute-start | bytes 196616 | tf_op jit(solution)/shard_map/ppermute | solution.py:169
  97.6 4.3 %collective-permute-start.23 = (bf16[2,128,128]{2,1,0:T(8,128)(2,1)S(1)}, bf16[2,128,128]{2,1,0:T(8,128)(2,1)S(1)}, u32[]{:S(2)}, u32[]{:S(2)}) collective-permute-start(bf16[2,128,128]{2,1,0:T(8,128)(2,1)S(1)} %get-tuple-element.92), channel_id=1, source_target_pairs={{0,2},{1,3},{2,0},{3,1},{4,6},{5,7},{6,4},{7,5},{8,10},{9,11},{10,... | collective-permute-start | bytes 196616 | tf_op jit(solution)/shard_map/ppermute | solution.py:169
  101.9 4.2 %collective-permute-start.24 = (bf16[2,128,128]{2,1,0:T(8,128)(2,1)S(1)}, bf16[2,128,128]{2,1,0:T(8,128)(2,1)S(1)}, u32[]{:S(2)}, u32[]{:S(2)}) collective-permute-start(bf16[2,128,128]{2,1,0:T(8,128)(2,1)S(1)} %get-tuple-element.91), channel_id=1, source_target_pairs={{0,3},{1,2},{2,1},{3,0},{4,7},{5,6},{6,5},{7,4},{8,11},{9,10},{10,... | collective-permute-start | bytes 196616 | tf_op jit(solution)/shard_map/ppermute | solution.py:169
  106.0 2.2 %collective-permute-start.20 = (bf16[2,128,512]{2,1,0:T(8,128)(2,1)S(1)}, bf16[2,128,512]{2,1,0:T(8,128)(2,1)S(1)}, u32[]{:S(2)}, u32[]{:S(2)}) collective-permute-start(bf16[2,128,512]{2,1,0:T(8,128)(2,1)S(1)} %get-tuple-element.69), channel_id=1, source_target_pairs={{0,1},{1,0},{2,3},{3,2},{4,5},{5,4},{6,7},{7,6},{8,9},{9,8},{10,11... | collective-permute-start | bytes 786440 | tf_op jit(solution)/shard_map/ppermute | solution.py:169
  106.3 2.2 %collective-permute-start.29 = (bf16[2,128,128]{2,1,0:T(8,128)(2,1)S(1)}, bf16[2,128,128]{2,1,0:T(8,128)(2,1)S(1)}, u32[]{:S(2)}, u32[]{:S(2)}) collective-permute-start(bf16[2,128,128]{2,1,0:T(8,128)(2,1)S(1)} %get-tuple-element.90), channel_id=1, source_target_pairs={{0,1},{1,0},{2,3},{3,2},{4,5},{5,4},{6,7},{7,6},{8,9},{9,8},{10,11... | collective-permute-start | bytes 196616 | tf_op jit(solution)/shard_map/ppermute | solution.py:169
  106.8 4.7 %collective-permute-start.30 = (bf16[2,128,128]{2,1,0:T(8,128)(2,1)S(1)}, bf16[2,128,128]{2,1,0:T(8,128)(2,1)S(1)}, u32[]{:S(2)}, u32[]{:S(2)}) collective-permute-start(bf16[2,128,128]{2,1,0:T(8,128)(2,1)S(1)} %get-tuple-element.89), channel_id=1, source_target_pairs={{0,2},{1,3},{2,0},{3,1},{4,6},{5,7},{6,4},{7,5},{8,10},{9,11},{10,... | collective-permute-start | bytes 196616 | tf_op jit(solution)/shard_map/ppermute | solution.py:169
  107.8 4.3 %collective-permute-start.31 = (bf16[2,128,128]{2,1,0:T(8,128)(2,1)S(1)}, bf16[2,128,128]{2,1,0:T(8,128)(2,1)S(1)}, u32[]{:S(2)}, u32[]{:S(2)}) collective-permute-start(bf16[2,128,128]{2,1,0:T(8,128)(2,1)S(1)} %get-tuple-element.88), channel_id=1, source_target_pairs={{0,3},{1,2},{2,1},{3,0},{4,7},{5,6},{6,5},{7,4},{8,11},{9,10},{10,... | collective-permute-start | bytes 196616 | tf_op jit(solution)/shard_map/ppermute | solution.py:169
  (9 other events, 40.2 us)

commit v6 on v4

--- a/solution.py
+++ b/solution.py
@@ -200,17 +200,25 @@
 
 def ordered_exchange(query_cuts, kv_owns, lanes, inner, run):
     one, two, three = lanes, 2 * lanes, 3 * lanes
-    query_x, query_d = swapped(query_cuts[2], 2), swapped(query_cuts[3], 3)
-    a_two = swapped(kv_owns[0], two)
+    query_d = swapped(query_cuts[3], 3)
+    query_x = swapped(query_cuts[2], 2)
     a_one = swapped(kv_owns[0], one)
-    a_three = middle_swapped(kv_owns[0], lanes)
-    b_two = swapped(after(kv_owns[1], a_one), two)
-    a_passed = swapped(a_two, one)
-    b_three = swapped(after(kv_owns[1], a_three), three)
-    b_one = swapped(after(kv_owns[1], query_x), one)
-    query_c = swapped(after(query_cuts[1], query_d), 1)
+    a_near = middle_swapped(kv_owns[0], lanes)
+    a_far = middle_swapped(after(a_one, query_d), lanes)
+    a_two = swapped(a_near, one)
+    a_three = swapped(a_far, one)
+    b_two = swapped(after(kv_owns[1], a_far), two)
+    b_three = swapped(after(kv_owns[1], a_two), three)
+    b_one = swapped(after(kv_owns[1], a_three), one)
+    query_c = swapped(after(query_cuts[1], a_two), 1)
     query_parts = [query_cuts[0], query_c, query_x, query_d]
-    a_parts = [kv_owns[0], a_one, a_two, jnp.where(inner, a_three, a_passed)]
+    a_parts = [
+        kv_owns[0],
+        a_one,
+        jnp.where(inner, a_far, a_two),
+        jnp.where(inner, a_near, a_three),
+    ]
+
     def joined_two(parts, passed):
         return (parts[2] + jnp.where(inner, passed.astype(F32), 0.0)).astype(BF16)
 
@@ -218,22 +226,20 @@
         value = parts[0] + first.astype(F32) + second.astype(F32)
         return (value + jnp.where(inner, middle.astype(F32), 0.0)).astype(BF16)
 
-    outs_a, sum_a = run(0, query_parts, a_parts)
+    outs_a, sum_a = after(run(0, query_parts, a_parts), b_two, b_three, b_one)
     a_passed = swapped(sum_a[3], one)
     a_middle = middle_swapped(sum_a[3], lanes)
     a_two = swapped(joined_two(sum_a, a_passed), two)
-    a_one = swapped(after(sum_a[1], b_one), one)
-    out_ax = swapped(after(outs_a[2], b_two), 2)
-    out_ad = swapped(after(outs_a[3], b_one), 3)
+    a_one = swapped(sum_a[1], one)
     outs_b, sum_b = run(
         1, query_parts, after([kv_owns[1], b_one, b_two, b_three], a_passed)
     )
+    out_ax, out_ad = swapped(outs_a[2], 2), swapped(outs_a[3], 3)
     outs_b, sum_b = after((outs_b, sum_b), a_two, a_one, a_middle, out_ax, out_ad)
     b_passed = swapped(sum_b[3], one)
-    out_ac = swapped(after(outs_a[1], a_one), 1)
+    out_ac = swapped(after(outs_a[1], b_passed), 1)
     b_middle = middle_swapped(sum_b[3], lanes)
-    out_bx = swapped(outs_b[2], 2)
-    out_bd = swapped(outs_b[3], 3)
+    out_bx, out_bd = swapped(outs_b[2], 2), swapped(outs_b[3], 3)
     b_send = joined_two(sum_b, b_passed)
     b_two = swapped(b_send, two)
     b_one = swapped(after(sum_b[1], b_send), one)

time: 112 us -> 114 us (1.018)
  starting transfers between devices: 44.9 us -> 34.2 us
  waiting for transfers between devices: 32.2 us -> 39.2 us
  local copies, waits for them, and re-layouts: 6.11 us -> 12.2 us
  Pallas kernels: 19.8 us -> 21.1 us
    ppermute x33 -> x34, starting transfers between devices: 44.9 us -> 34.2 us  [moved(): return lax.ppermute(tensor, 'seq', [(i, target(i)) for i in range(devices)])]
    ppermute x33 -> x34, waiting for transfers between devices: 32.2 us -> 39.2 us  [moved(): return lax.ppermute(tensor, 'seq', [(i, target(i)) for i in range(devices)])]
    slice x3, local copies, waits for them, and re-layouts: 1.29 us -> 3.9 us  [on_device(): kv_owns = [jnp.stack([part[h] for part in kv_lanes]) for h in range(heads)]]
    add x4, local copies, waits for them, and re-layouts: 0.25 us -> 2.69 us  [on_device(): place = jnp.arange(rows, dtype=jnp.int32)[None, :] * devices + mine[:, None]]
    another operation x6, other arithmetic: 0.14 us -> 1.45 us  [kv_cut(): return jnp.stack([both[:, :, h * HD:(h + 1) * HD] for h in range(heads)])]
    pallas_call x2, Pallas kernels: 19.8 us -> 21.1 us  [attend(): pl.pallas_call(functools.partial(attend_kernel, head, lanes, depth), out_...]
  transfers between devices with their start and end apart: 33 -> 34, of which waited for: 13 -> 13; matrix products, arithmetic and copies ran while one was open for 8% -> 12% of each run, Pallas kernels for 18% -> 19%
where the time goes in v6:
time: 114 us; the launch traced here: 113 us
  waiting for transfers between devices  39.2 us (34%)
  starting transfers between devices  34.2 us (30%)
  Pallas kernels  21.1 us (19%)
  local copies, waits for them, and re-layouts  12.2 us (11%)
  other arithmetic  4.59 us (4%)
  between operations  1.3 us (1%)
    ppermute x34, waiting for transfers between devices, moved(): return lax.ppermute(tensor, 'seq', [(i, target(i)) for i in range(devices)])  39.2 us
    ppermute x34, starting transfers between devices, moved(): return lax.ppermute(tensor, 'seq', [(i, target(i)) for i in range(devices)])  34.2 us
    pallas_call x2, Pallas kernels, attend(): pl.pallas_call(functools.partial(attend_kernel, head, lanes, depth), out_...  21.1 us
    slice x3, local copies, waits for them, and re-layouts, on_device(): kv_owns = [jnp.stack([part[h] for part in kv_lanes]) for h in range(heads)]  3.9 us
    add x4, local copies, waits for them, and re-layouts, on_device(): place = jnp.arange(rows, dtype=jnp.int32)[None, :] * devices + mine[:, None]  2.69 us
  transfers between devices with their start and end apart: 34, of which 13 were waited for; matrix products, arithmetic and copies ran while one was open for 12% of the time, Pallas kernels for 19%

profile of v6, /device:TPU:0, one launch (start us, length us, event | category | flops | bytes accessed | tf_op | source)
XLA Modules:
  0.0 112.5 jit_solution(4943883850497182527)
XLA Ops:
  0.7 1.0 dynamic-slice_bitcast_fusion.12
  1.7 1.0 dynamic-slice_bitcast_fusion.13
  3.4 2.9 %collective-permute-start.1 = (bf16[2,2,128,128]{3,2,1,0:T(8,128)(2,1)}, bf16[2,2,128,128]{3,2,1,0:T(8,128)(2,1)}, u32[]{:S(2)}, u32[]{:S(2)}) collective-permute-start(bf16[2,2,128,128]{3,2,1,0:T(8,128)(2,1)} %pad_maximum_fusion.7), channel_id=1, source_target_pairs={{0,2},{1,3},{2,0},{3,1},{4,6},{5,7},{6,4},{7,5},{8,10},{9,11},{10,... | collective-permute-start | bytes 393224 | tf_op jit(solution)/shard_map/ppermute | solution.py:169
  9.1 0.9 dynamic-slice_bitcast_fusion
  10.0 1.7 %collective-permute-start.7 = (bf16[2,128,1024]{2,1,0:T(8,128)(2,1)S(1)}, bf16[2,128,1024]{2,1,0:T(8,128)(2,1)S(1)}, u32[]{:S(2)}, u32[]{:S(2)}) collective-permute-start(bf16[2,128,1024]{2,1,0:T(8,128)(2,1)S(1)} %pad_maximum_fusion.3), channel_id=1, source_target_pairs={{0,3},{1,2},{2,1},{3,0},{4,7},{5,6},{6,5},{7,4},{8,11},{9,10},{10,... | collective-permute-start | bytes 1572872 | tf_op jit(solution)/shard_map/ppermute | solution.py:169
  11.7 0.9 fusion.38
  12.6 1.5 %fusion.39 = (bf16[1,2,128,128]{3,2,1,0:T(8,128)(2,1)}, bf16[1,2,128,128]{3,2,1,0:T(8,128)(2,1)S(1)}) fusion(bf16[2,2,128,128]{3,2,1,0:T(8,128)(2,1)} %collective-permute-done.1), kind=kLoop, calls=%fused_computation.136 | loop fusion | bytes 262144 | tf_op jit(solution)/shard_map/slice | solution.py:281
  14.1 1.5 %fusion.40 = (bf16[1,2,128,128]{3,2,1,0:T(8,128)(2,1)}, bf16[1,2,128,128]{3,2,1,0:T(8,128)(2,1)S(1)}) fusion(bf16[2,2,128,128]{3,2,1,0:T(8,128)(2,1)} %collective-permute-done.2), kind=kLoop, calls=%fused_computation.137 | loop fusion | bytes 262144 | tf_op jit(solution)/shard_map/slice | solution.py:281
  15.7 1.6 %collective-permute-start.8 = (bf16[4,2,128,128]{3,2,1,0:T(8,128)(2,1)S(1)}, bf16[4,2,128,128]{3,2,1,0:T(8,128)(2,1)S(1)}, u32[]{:S(2)}, u32[]{:S(2)}) collective-permute-start(bf16[4,2,128,128]{3,2,1,0:T(8,128)(2,1)S(1)} %pad_maximum_fusion.4.refs_4_), channel_id=1, source_target_pairs={{0,4},{1,5},{2,6},{3,7},{4,0},{5,1},{6,2},{7,3},{8,12},{9,13},{10,... | collective-permute-start | bytes 786440 | tf_op jit(solution)/shard_map/ppermute | solution.py:169
  19.2 0.7 add.238
  20.6 0.7 add.236
  21.9 0.7 broadcast_add_fusion.2
  22.6 6.4 %collective-permute-start.4 = (bf16[4,2,128,128]{3,2,1,0:T(8,128)(2,1)S(1)}, bf16[4,2,128,128]{3,2,1,0:T(8,128)(2,1)S(1)}, u32[]{:S(2)}, u32[]{:S(2)}) collective-permute-start(bf16[4,2,128,128]{3,2,1,0:T(8,128)(2,1)S(1)} %collective-permute-done.3), channel_id=1, source_target_pairs={{0,4},{1,5},{2,6},{3,7},{4,0},{5,1},{6,2},{7,3},{8,12},{9,13},{10,... | collective-permute-start | bytes 786440 | tf_op jit(solution)/shard_map/ppermute | solution.py:169
  30.5 4.7 %collective-permute-done.4 = bf16[4,2,128,128]{3,2,1,0:T(8,128)(2,1)S(1)} collective-permute-done((bf16[4,2,128,128]{3,2,1,0:T(8,128)(2,1)S(1)}, bf16[4,2,128,128]{3,2,1,0:T(8,128)(2,1)S(1)}, u32[]{:S(2)}, u32[]{:S(2)}) %collective-permute-start.4) | collective-permute-done | bytes 262176 | tf_op jit(solution)/shard_map/ppermute | solution.py:169
  35.2 3.6 %collective-permute-start.10 = (bf16[4,2,128,128]{3,2,1,0:T(8,128)(2,1)S(1)}, bf16[4,2,128,128]{3,2,1,0:T(8,128)(2,1)S(1)}, u32[]{:S(2)}, u32[]{:S(2)}) collective-permute-start(bf16[4,2,128,128]{3,2,1,0:T(8,128)(2,1)S(1)} %collective-permute-done.9), channel_id=1, source_target_pairs={{0,4},{1,5},{2,6},{3,7},{4,0},{5,1},{6,2},{7,3},{8,12},{9,13},{10,... | collective-permute-start | bytes 786440 | tf_op jit(solution)/shard_map/ppermute | solution.py:169
  38.9 2.4 %collective-permute-start.12 = (bf16[4,2,128,128]{3,2,1,0:T(8,128)(2,1)S(1)}, bf16[4,2,128,128]{3,2,1,0:T(8,128)(2,1)S(1)}, u32[]{:S(2)}, u32[]{:S(2)}) collective-permute-start(bf16[4,2,128,128]{3,2,1,0:T(8,128)(2,1)S(1)} %pad_maximum_fusion.5.refs_4_), channel_id=1, source_target_pairs={{0,12},{1,13},{2,14},{3,15},{4,8},{5,9},{6,10},{7,11},{8,4},{9,5},... | collective-permute-start | bytes 786440 | tf_op jit(solution)/shard_map/ppermute | solution.py:169
  41.3 6.6 %collective-permute-done.10 = bf16[4,2,128,128]{3,2,1,0:T(8,128)(2,1)S(1)} collective-permute-done((bf16[4,2,128,128]{3,2,1,0:T(8,128)(2,1)S(1)}, bf16[4,2,128,128]{3,2,1,0:T(8,128)(2,1)S(1)}, u32[]{:S(2)}, u32[]{:S(2)}) %collective-permute-start.10) | collective-permute-done | bytes 262176 | tf_op jit(solution)/shard_map/ppermute | solution.py:169
  48.3 10.7 %shard_map.84 = (bf16[2,128,512]{2,1,0:T(8,128)(2,1)S(1)}, bf16[2,128,512]{2,1,0:T(8,128)(2,1)S(1)}, bf16[2,128,512]{2,1,0:T(8,128)(2,1)S(1)}, bf16[2,128,512]{2...) custom-call(s32[4]{0:T(128)S(1)} %and_select_fusion.start_ref, ...), custom_call_target="tpu_custom_call" | custom-call | flops 13421772800 | bytes 8388608 | tf_op jit(solution)/shard_map/pallas_call | solution.py:142
  59.1 3.3 %collective-permute-done.11.refs_6_ = bf16[4,2,128,128]{3,2,1,0:T(8,128)(2,1)S(1)} collective-permute-done((bf16[4,2,128,128]{3,2,1,0:T(8,128)(2,1)S(1)}, bf16[4,2,128,128]{3,2,1,0:T(8,128)(2,1)S(1)}, u32[]{:S(2)}, u32[]{:S(2)}) %collective-permute-start.11) | collective-permute-done | bytes 262176 | tf_op jit(solution)/shard_map/ppermute | solution.py:169
  63.5 4.1 %collective-permute-start.16 = (bf16[4,2,128,128]{3,2,1,0:T(8,128)(2,1)S(1)}, bf16[4,2,128,128]{3,2,1,0:T(8,128)(2,1)S(1)}, u32[]{:S(2)}, u32[]{:S(2)}) collective-permute-start(bf16[4,2,128,128]{3,2,1,0:T(8,128)(2,1)S(1)} %get-tuple-element.82), channel_id=1, source_target_pairs={{0,4},{1,5},{2,6},{3,7},{4,0},{5,1},{6,2},{7,3},{8,12},{9,13},{10,... | collective-permute-start | bytes 786440 | tf_op jit(solution)/shard_map/ppermute | solution.py:169
  68.3 2.9 %collective-permute-done.14 = bf16[4,2,128,128]{3,2,1,0:T(8,128)(2,1)S(1)} collective-permute-done((bf16[4,2,128,128]{3,2,1,0:T(8,128)(2,1)S(1)}, bf16[4,2,128,128]{3,2,1,0:T(8,128)(2,1)S(1)}, u32[]{:S(2)}, u32[]{:S(2)}) %collective-permute-start.14) | collective-permute-done | bytes 262176 | tf_op jit(solution)/shard_map/ppermute | solution.py:169
  71.3 0.8 collective-permute-start.15
  72.1 10.3 %shard_map.85 = (bf16[2,128,512]{2,1,0:T(8,128)(2,1)S(1)}, bf16[2,128,512]{2,1,0:T(8,128)(2,1)S(1)}, bf16[2,128,512]{2,1,0:T(8,128)(2,1)S(1)}, bf16[2,128,512]{2...) custom-call(s32[4]{0:T(128)S(1)} %and_select_fusion.start_ref, ...), custom_call_target="tpu_custom_call" | custom-call | flops 13421772800 | bytes 8388608 | tf_op jit(solution)/shard_map/pallas_call | solution.py:142
  82.5 2.1 %collective-permute-done.15 = bf16[4,2,128,128]{3,2,1,0:T(8,128)(2,1)S(1)} collective-permute-done((bf16[4,2,128,128]{3,2,1,0:T(8,128)(2,1)S(1)}, bf16[4,2,128,128]{3,2,1,0:T(8,128)(2,1)S(1)}, u32[]{:S(2)}, u32[]{:S(2)}) %collective-permute-start.15) | collective-permute-done | bytes 262176 | tf_op jit(solution)/shard_map/ppermute | solution.py:169
  86.0 5.7 %collective-permute-done.20 = bf16[4,2,128,128]{3,2,1,0:T(8,128)(2,1)S(1)} collective-permute-done((bf16[4,2,128,128]{3,2,1,0:T(8,128)(2,1)S(1)}, bf16[4,2,128,128]{3,2,1,0:T(8,128)(2,1)S(1)}, u32[]{:S(2)}, u32[]{:S(2)}) %collective-permute-start.20) | collective-permute-done | bytes 262176 | tf_op jit(solution)/shard_map/ppermute | solution.py:169
  92.3 1.7 %collective-permute-start.28 = (bf16[4,2,128,128]{3,2,1,0:T(8,128)(2,1)S(1)}, bf16[4,2,128,128]{3,2,1,0:T(8,128)(2,1)S(1)}, u32[]{:S(2)}, u32[]{:S(2)}) collective-permute-start(bf16[4,2,128,128]{3,2,1,0:T(8,128)(2,1)S(1)} %get-tuple-element.97), channel_id=1, source_target_pairs={{0,4},{1,5},{2,6},{3,7},{4,0},{5,1},{6,2},{7,3},{8,12},{9,13},{10,... | collective-permute-start | bytes 786440 | tf_op jit(solution)/shard_map/ppermute | solution.py:169
  94.8 1.2 %collective-permute-done.25 = bf16[2,128,128]{2,1,0:T(8,128)(2,1)S(1)} collective-permute-done((bf16[2,128,128]{2,1,0:T(8,128)(2,1)S(1)}, bf16[2,128,128]{2,1,0:T(8,128)(2,1)S(1)}, u32[]{:S(2)}, u32[]{:S(2)}) %collective-permute-start.25) | collective-permute-done | bytes 65568 | tf_op jit(solution)/shard_map/ppermute | solution.py:169
  96.5 3.7 %collective-permute-done.26 = bf16[2,128,128]{2,1,0:T(8,128)(2,1)S(1)} collective-permute-done((bf16[2,128,128]{2,1,0:T(8,128)(2,1)S(1)}, bf16[2,128,128]{2,1,0:T(8,128)(2,1)S(1)}, u32[]{:S(2)}, u32[]{:S(2)}) %collective-permute-start.26) | collective-permute-done | bytes 65568 | tf_op jit(solution)/shard_map/ppermute | solution.py:169
  100.3 3.9 %collective-permute-done.27 = bf16[2,128,128]{2,1,0:T(8,128)(2,1)S(1)} collective-permute-done((bf16[2,128,128]{2,1,0:T(8,128)(2,1)S(1)}, bf16[2,128,128]{2,1,0:T(8,128)(2,1)S(1)}, u32[]{:S(2)}, u32[]{:S(2)}) %collective-permute-start.27) | collective-permute-done | bytes 65568 | tf_op jit(solution)/shard_map/ppermute | solution.py:169
  104.7 1.3 %collective-permute-done.29 = bf16[4,2,128,128]{3,2,1,0:T(8,128)(2,1)S(1)} collective-permute-done((bf16[4,2,128,128]{3,2,1,0:T(8,128)(2,1)S(1)}, bf16[4,2,128,128]{3,2,1,0:T(8,128)(2,1)S(1)}, u32[]{:S(2)}, u32[]{:S(2)}) %collective-permute-start.29) | collective-permute-done | bytes 262176 | tf_op jit(solution)/shard_map/ppermute | solution.py:169
  106.9 1.3 %collective-permute-start.33 = (bf16[2,128,128]{2,1,0:T(8,128)(2,1)S(1)}, bf16[2,128,128]{2,1,0:T(8,128)(2,1)S(1)}, u32[]{:S(2)}, u32[]{:S(2)}) collective-permute-start(bf16[2,128,128]{2,1,0:T(8,128)(2,1)S(1)} %get-tuple-element.108), channel_id=1, source_target_pairs={{0,3},{1,2},{2,1},{3,0},{4,7},{5,6},{6,5},{7,4},{8,11},{9,10},{10,... | collective-permute-start | bytes 196616 | tf_op jit(solution)/shard_map/ppermute | solution.py:169
  108.5 2.7 %collective-permute-done.32 = bf16[2,128,128]{2,1,0:T(8,128)(2,1)S(1)} collective-permute-done((bf16[2,128,128]{2,1,0:T(8,128)(2,1)S(1)}, bf16[2,128,128]{2,1,0:T(8,128)(2,1)S(1)}, u32[]{:S(2)}, u32[]{:S(2)}) %collective-permute-start.32) | collective-permute-done | bytes 65568 | tf_op jit(solution)/shard_map/ppermute | solution.py:169
  (135 shorter events, 16.7 us)
Async XLA Ops:
  3.4 9.2 %collective-permute-start.1 = (bf16[2,2,128,128]{3,2,1,0:T(8,128)(2,1)}, bf16[2,2,128,128]{3,2,1,0:T(8,128)(2,1)}, u32[]{:S(2)}, u32[]{:S(2)}) collective-permute-start(bf16[2,2,128,128]{3,2,1,0:T(8,128)(2,1)} %pad_maximum_fusion.7), channel_id=1, source_target_pairs={{0,2},{1,3},{2,0},{3,1},{4,6},{5,7},{6,4},{7,5},{8,10},{9,11},{10,... | collective-permute-start | bytes 393224 | tf_op jit(solution)/shard_map/ppermute | solution.py:169
  7.0 7.2 %collective-permute-start.2 = (bf16[2,2,128,128]{3,2,1,0:T(8,128)(2,1)}, bf16[2,2,128,128]{3,2,1,0:T(8,128)(2,1)}, u32[]{:S(2)}, u32[]{:S(2)}) collective-permute-start(bf16[2,2,128,128]{3,2,1,0:T(8,128)(2,1)} %pad_maximum_fusion.8), channel_id=1, source_target_pairs={{0,3},{1,2},{2,1},{3,0},{4,7},{5,6},{6,5},{7,4},{8,11},{9,10},{10,... | collective-permute-start | bytes 393224 | tf_op jit(solution)/shard_map/ppermute | solution.py:169
  10.0 19.0 %collective-permute-start.7 = (bf16[2,128,1024]{2,1,0:T(8,128)(2,1)S(1)}, bf16[2,128,1024]{2,1,0:T(8,128)(2,1)S(1)}, u32[]{:S(2)}, u32[]{:S(2)}) collective-permute-start(bf16[2,128,1024]{2,1,0:T(8,128)(2,1)S(1)} %pad_maximum_fusion.3), channel_id=1, source_target_pairs={{0,3},{1,2},{2,1},{3,0},{4,7},{5,6},{6,5},{7,4},{8,11},{9,10},{10,... | collective-permute-start | bytes 1572872 | tf_op jit(solution)/shard_map/ppermute | solution.py:169
  15.7 13.4 %collective-permute-start.8 = (bf16[4,2,128,128]{3,2,1,0:T(8,128)(2,1)S(1)}, bf16[4,2,128,128]{3,2,1,0:T(8,128)(2,1)S(1)}, u32[]{:S(2)}, u32[]{:S(2)}) collective-permute-start(bf16[4,2,128,128]{3,2,1,0:T(8,128)(2,1)S(1)} %pad_maximum_fusion.4.refs_4_), channel_id=1, source_target_pairs={{0,4},{1,5},{2,6},{3,7},{4,0},{5,1},{6,2},{7,3},{8,12},{9,13},{10,... | collective-permute-start | bytes 786440 | tf_op jit(solution)/shard_map/ppermute | solution.py:169
  17.3 5.3 %collective-permute-start.3 = (bf16[4,2,128,128]{3,2,1,0:T(8,128)(2,1)S(1)}, bf16[4,2,128,128]{3,2,1,0:T(8,128)(2,1)S(1)}, u32[]{:S(2)}, u32[]{:S(2)}) collective-permute-start(bf16[4,2,128,128]{3,2,1,0:T(8,128)(2,1)S(1)} %pad_maximum_fusion.4.refs_4_), channel_id=1, source_target_pairs={{0,0},{1,1},{2,2},{3,3},{4,8},{5,9},{6,10},{7,11},{8,4},{9,5},{10,... | collective-permute-start | bytes 786440 | tf_op jit(solution)/shard_map/ppermute | solution.py:169
  22.6 12.6 %collective-permute-start.4 = (bf16[4,2,128,128]{3,2,1,0:T(8,128)(2,1)S(1)}, bf16[4,2,128,128]{3,2,1,0:T(8,128)(2,1)S(1)}, u32[]{:S(2)}, u32[]{:S(2)}) collective-permute-start(bf16[4,2,128,128]{3,2,1,0:T(8,128)(2,1)S(1)} %collective-permute-done.3), channel_id=1, source_target_pairs={{0,4},{1,5},{2,6},{3,7},{4,0},{5,1},{6,2},{7,3},{8,12},{9,13},{10,... | collective-permute-start | bytes 786440 | tf_op jit(solution)/shard_map/ppermute | solution.py:169
  29.1 6.2 %collective-permute-start.9 = (bf16[4,2,128,128]{3,2,1,0:T(8,128)(2,1)S(1)}, bf16[4,2,128,128]{3,2,1,0:T(8,128)(2,1)S(1)}, u32[]{:S(2)}, u32[]{:S(2)}) collective-permute-start(bf16[4,2,128,128]{3,2,1,0:T(8,128)(2,1)S(1)} %collective-permute-done.8.refs_5_), channel_id=1, source_target_pairs={{0,0},{1,1},{2,2},{3,3},{4,8},{5,9},{6,10},{7,11},{8,4},{9,5},{10,... | collective-permute-start | bytes 786440 | tf_op jit(solution)/shard_map/ppermute | solution.py:169
  29.8 18.3 %collective-permute-start.6 = (bf16[2,128,1024]{2,1,0:T(8,128)(2,1)S(1)}, bf16[2,128,1024]{2,1,0:T(8,128)(2,1)S(1)}, u32[]{:S(2)}, u32[]{:S(2)}) collective-permute-start(bf16[2,128,1024]{2,1,0:T(8,128)(2,1)S(1)} %pad_maximum_fusion.2), channel_id=1, source_target_pairs={{0,2},{1,3},{2,0},{3,1},{4,6},{5,7},{6,4},{7,5},{8,10},{9,11},{10,... | collective-permute-start | bytes 1572872 | tf_op jit(solution)/shard_map/ppermute | solution.py:169
  35.2 12.9 %collective-permute-start.5 = (bf16[2,128,1024]{2,1,0:T(8,128)(2,1)S(1)}, bf16[2,128,1024]{2,1,0:T(8,128)(2,1)S(1)}, u32[]{:S(2)}, u32[]{:S(2)}) collective-permute-start(bf16[2,128,1024]{2,1,0:T(8,128)(2,1)S(1)} %pad_maximum_fusion.1), channel_id=1, source_target_pairs={{0,1},{1,0},{2,3},{3,2},{4,5},{5,4},{6,7},{7,6},{8,9},{9,8},{10,11... | collective-permute-start | bytes 1572872 | tf_op jit(solution)/shard_map/ppermute | solution.py:169
  35.2 12.7 %collective-permute-start.10 = (bf16[4,2,128,128]{3,2,1,0:T(8,128)(2,1)S(1)}, bf16[4,2,128,128]{3,2,1,0:T(8,128)(2,1)S(1)}, u32[]{:S(2)}, u32[]{:S(2)}) collective-permute-start(bf16[4,2,128,128]{3,2,1,0:T(8,128)(2,1)S(1)} %collective-permute-done.9), channel_id=1, source_target_pairs={{0,4},{1,5},{2,6},{3,7},{4,0},{5,1},{6,2},{7,3},{8,12},{9,13},{10,... | collective-permute-start | bytes 786440 | tf_op jit(solution)/shard_map/ppermute | solution.py:169
  38.9 20.1 %collective-permute-start.12 = (bf16[4,2,128,128]{3,2,1,0:T(8,128)(2,1)S(1)}, bf16[4,2,128,128]{3,2,1,0:T(8,128)(2,1)S(1)}, u32[]{:S(2)}, u32[]{:S(2)}) collective-permute-start(bf16[4,2,128,128]{3,2,1,0:T(8,128)(2,1)S(1)} %pad_maximum_fusion.5.refs_4_), channel_id=1, source_target_pairs={{0,12},{1,13},{2,14},{3,15},{4,8},{5,9},{6,10},{7,11},{8,4},{9,5},... | collective-permute-start | bytes 786440 | tf_op jit(solution)/shard_map/ppermute | solution.py:169
  41.3 21.0 %collective-permute-start.11 = (bf16[4,2,128,128]{3,2,1,0:T(8,128)(2,1)S(1)}, bf16[4,2,128,128]{3,2,1,0:T(8,128)(2,1)S(1)}, u32[]{:S(2)}, u32[]{:S(2)}) collective-permute-start(bf16[4,2,128,128]{3,2,1,0:T(8,128)(2,1)S(1)} %pad_maximum_fusion.5.refs_4_), channel_id=1, source_target_pairs={{0,8},{1,9},{2,10},{3,11},{4,12},{5,13},{6,14},{7,15},{8,0},{9,1},... | collective-permute-start | bytes 786440 | tf_op jit(solution)/shard_map/ppermute | solution.py:169
  48.0 14.4 %collective-permute-start.13 = (bf16[4,2,128,128]{3,2,1,0:T(8,128)(2,1)S(1)}, bf16[4,2,128,128]{3,2,1,0:T(8,128)(2,1)S(1)}, u32[]{:S(2)}, u32[]{:S(2)}) collective-permute-start(bf16[4,2,128,128]{3,2,1,0:T(8,128)(2,1)S(1)} %pad_maximum_fusion.5.refs_4_), channel_id=1, source_target_pairs={{0,4},{1,5},{2,6},{3,7},{4,0},{5,1},{6,2},{7,3},{8,12},{9,13},{10,... | collective-permute-start | bytes 786440 | tf_op jit(solution)/shard_map/ppermute | solution.py:169
  62.3 8.9 %collective-permute-start.14 = (bf16[4,2,128,128]{3,2,1,0:T(8,128)(2,1)S(1)}, bf16[4,2,128,128]{3,2,1,0:T(8,128)(2,1)S(1)}, u32[]{:S(2)}, u32[]{:S(2)}) collective-permute-start(bf16[4,2,128,128]{3,2,1,0:T(8,128)(2,1)S(1)} %get-tuple-element.68), channel_id=1, source_target_pairs={{0,4},{1,5},{2,6},{3,7},{4,0},{5,1},{6,2},{7,3},{8,12},{9,13},{10,... | collective-permute-start | bytes 786440 | tf_op jit(solution)/shard_map/ppermute | solution.py:169
  62.8 19.6 %collective-permute-start.17 = (bf16[4,2,128,128]{3,2,1,0:T(8,128)(2,1)S(1)}, bf16[4,2,128,128]{3,2,1,0:T(8,128)(2,1)S(1)}, u32[]{:S(2)}, u32[]{:S(2)}) collective-permute-start(bf16[4,2,128,128]{3,2,1,0:T(8,128)(2,1)S(1)} %get-tuple-element.68), channel_id=1, source_target_pairs={{0,0},{1,1},{2,2},{3,3},{4,8},{5,9},{6,10},{7,11},{8,4},{9,5},{10,... | collective-permute-start | bytes 786440 | tf_op jit(solution)/shard_map/ppermute | solution.py:169
  63.5 19.0 %collective-permute-start.16 = (bf16[4,2,128,128]{3,2,1,0:T(8,128)(2,1)S(1)}, bf16[4,2,128,128]{3,2,1,0:T(8,128)(2,1)S(1)}, u32[]{:S(2)}, u32[]{:S(2)}) collective-permute-start(bf16[4,2,128,128]{3,2,1,0:T(8,128)(2,1)S(1)} %get-tuple-element.82), channel_id=1, source_target_pairs={{0,4},{1,5},{2,6},{3,7},{4,0},{5,1},{6,2},{7,3},{8,12},{9,13},{10,... | collective-permute-start | bytes 786440 | tf_op jit(solution)/shard_map/ppermute | solution.py:169
  67.5 14.9 %collective-permute-start.18 = (bf16[2,128,512]{2,1,0:T(8,128)(2,1)S(1)}, bf16[2,128,512]{2,1,0:T(8,128)(2,1)S(1)}, u32[]{:S(2)}, u32[]{:S(2)}) collective-permute-start(bf16[2,128,512]{2,1,0:T(8,128)(2,1)S(1)} %get-tuple-element.83), channel_id=1, source_target_pairs={{0,2},{1,3},{2,0},{3,1},{4,6},{5,7},{6,4},{7,5},{8,10},{9,11},{10,... | collective-permute-start | bytes 786440 | tf_op jit(solution)/shard_map/ppermute | solution.py:169
  68.1 14.4 %collective-permute-start.19 = (bf16[2,128,512]{2,1,0:T(8,128)(2,1)S(1)}, bf16[2,128,512]{2,1,0:T(8,128)(2,1)S(1)}, u32[]{:S(2)}, u32[]{:S(2)}) collective-permute-start(bf16[2,128,512]{2,1,0:T(8,128)(2,1)S(1)} %get-tuple-element.84), channel_id=1, source_target_pairs={{0,3},{1,2},{2,1},{3,0},{4,7},{5,6},{6,5},{7,4},{8,11},{9,10},{10,... | collective-permute-start | bytes 786440 | tf_op jit(solution)/shard_map/ppermute | solution.py:169
  71.3 13.3 %collective-permute-start.15 = (bf16[4,2,128,128]{3,2,1,0:T(8,128)(2,1)S(1)}, bf16[4,2,128,128]{3,2,1,0:T(8,128)(2,1)S(1)}, u32[]{:S(2)}, u32[]{:S(2)}) collective-permute-start(bf16[4,2,128,128]{3,2,1,0:T(8,128)(2,1)S(1)} %add_convert_fusion.3), channel_id=1, source_target_pairs={{0,8},{1,9},{2,10},{3,11},{4,12},{5,13},{6,14},{7,15},{8,0},{9,1},... | collective-permute-start | bytes 786440 | tf_op jit(solution)/shard_map/ppermute | solution.py:169
  84.6 7.1 %collective-permute-start.20 = (bf16[4,2,128,128]{3,2,1,0:T(8,128)(2,1)S(1)}, bf16[4,2,128,128]{3,2,1,0:T(8,128)(2,1)S(1)}, u32[]{:S(2)}, u32[]{:S(2)}) collective-permute-start(bf16[4,2,128,128]{3,2,1,0:T(8,128)(2,1)S(1)} %get-tuple-element.85), channel_id=1, source_target_pairs={{0,4},{1,5},{2,6},{3,7},{4,0},{5,1},{6,2},{7,3},{8,12},{9,13},{10,... | collective-permute-start | bytes 786440 | tf_op jit(solution)/shard_map/ppermute | solution.py:169
  84.6 19.5 %collective-permute-start.30 = (bf16[4,2,128,128]{3,2,1,0:T(8,128)(2,1)S(1)}, bf16[4,2,128,128]{3,2,1,0:T(8,128)(2,1)S(1)}, u32[]{:S(2)}, u32[]{:S(2)}) collective-permute-start(bf16[4,2,128,128]{3,2,1,0:T(8,128)(2,1)S(1)} %get-tuple-element.85), channel_id=1, source_target_pairs={{0,0},{1,1},{2,2},{3,3},{4,8},{5,9},{6,10},{7,11},{8,4},{9,5},{10,... | collective-permute-start | bytes 786440 | tf_op jit(solution)/shard_map/ppermute | solution.py:169
  85.3 9.3 %collective-permute-start.22 = (bf16[2,128,512]{2,1,0:T(8,128)(2,1)S(1)}, bf16[2,128,512]{2,1,0:T(8,128)(2,1)S(1)}, u32[]{:S(2)}, u32[]{:S(2)}) collective-permute-start(bf16[2,128,512]{2,1,0:T(8,128)(2,1)S(1)} %get-tuple-element.89), channel_id=1, source_target_pairs={{0,2},{1,3},{2,0},{3,1},{4,6},{5,7},{6,4},{7,5},{8,10},{9,11},{10,... | collective-permute-start | bytes 786440 | tf_op jit(solution)/shard_map/ppermute | solution.py:169
  85.9 22.5 %collective-permute-start.24 = (bf16[2,128,512]{2,1,0:T(8,128)(2,1)S(1)}, bf16[2,128,512]{2,1,0:T(8,128)(2,1)S(1)}, u32[]{:S(2)}, u32[]{:S(2)}) collective-permute-start(bf16[2,128,512]{2,1,0:T(8,128)(2,1)S(1)} %get-tuple-element.91), channel_id=1, source_target_pairs={{0,3},{1,2},{2,1},{3,0},{4,7},{5,6},{6,5},{7,4},{8,11},{9,10},{10,... | collective-permute-start | bytes 786440 | tf_op jit(solution)/shard_map/ppermute | solution.py:169
  91.8 14.2 %collective-permute-start.29 = (bf16[4,2,128,128]{3,2,1,0:T(8,128)(2,1)S(1)}, bf16[4,2,128,128]{3,2,1,0:T(8,128)(2,1)S(1)}, u32[]{:S(2)}, u32[]{:S(2)}) collective-permute-start(bf16[4,2,128,128]{3,2,1,0:T(8,128)(2,1)S(1)} %add_convert_fusion.1), channel_id=1, source_target_pairs={{0,8},{1,9},{2,10},{3,11},{4,12},{5,13},{6,14},{7,15},{8,0},{9,1},... | collective-permute-start | bytes 786440 | tf_op jit(solution)/shard_map/ppermute | solution.py:169
  92.3 12.4 %collective-permute-start.28 = (bf16[4,2,128,128]{3,2,1,0:T(8,128)(2,1)S(1)}, bf16[4,2,128,128]{3,2,1,0:T(8,128)(2,1)S(1)}, u32[]{:S(2)}, u32[]{:S(2)}) collective-permute-start(bf16[4,2,128,128]{3,2,1,0:T(8,128)(2,1)S(1)} %get-tuple-element.97), channel_id=1, source_target_pairs={{0,4},{1,5},{2,6},{3,7},{4,0},{5,1},{6,2},{7,3},{8,12},{9,13},{10,... | collective-permute-start | bytes 786440 | tf_op jit(solution)/shard_map/ppermute | solution.py:169
  96.0 4.3 %collective-permute-start.26 = (bf16[2,128,128]{2,1,0:T(8,128)(2,1)S(1)}, bf16[2,128,128]{2,1,0:T(8,128)(2,1)S(1)}, u32[]{:S(2)}, u32[]{:S(2)}) collective-permute-start(bf16[2,128,128]{2,1,0:T(8,128)(2,1)S(1)} %get-tuple-element.112), channel_id=1, source_target_pairs={{0,2},{1,3},{2,0},{3,1},{4,6},{5,7},{6,4},{7,5},{8,10},{9,11},{10,... | collective-permute-start | bytes 196616 | tf_op jit(solution)/shard_map/ppermute | solution.py:169
  100.2 3.9 %collective-permute-start.27 = (bf16[2,128,128]{2,1,0:T(8,128)(2,1)S(1)}, bf16[2,128,128]{2,1,0:T(8,128)(2,1)S(1)}, u32[]{:S(2)}, u32[]{:S(2)}) collective-permute-start(bf16[2,128,128]{2,1,0:T(8,128)(2,1)S(1)} %get-tuple-element.111), channel_id=1, source_target_pairs={{0,3},{1,2},{2,1},{3,0},{4,7},{5,6},{6,5},{7,4},{8,11},{9,10},{10,... | collective-permute-start | bytes 196616 | tf_op jit(solution)/shard_map/ppermute | solution.py:169
  104.1 4.2 %collective-permute-start.23 = (bf16[2,128,512]{2,1,0:T(8,128)(2,1)S(1)}, bf16[2,128,512]{2,1,0:T(8,128)(2,1)S(1)}, u32[]{:S(2)}, u32[]{:S(2)}) collective-permute-start(bf16[2,128,512]{2,1,0:T(8,128)(2,1)S(1)} %get-tuple-element.90), channel_id=1, source_target_pairs={{0,1},{1,0},{2,3},{3,2},{4,5},{5,4},{6,7},{7,6},{8,9},{9,8},{10,11... | collective-permute-start | bytes 786440 | tf_op jit(solution)/shard_map/ppermute | solution.py:169
  104.2 2.7 %collective-permute-start.21 = (bf16[2,128,512]{2,1,0:T(8,128)(2,1)S(1)}, bf16[2,128,512]{2,1,0:T(8,128)(2,1)S(1)}, u32[]{:S(2)}, u32[]{:S(2)}) collective-permute-start(bf16[2,128,512]{2,1,0:T(8,128)(2,1)S(1)} %get-tuple-element.86), channel_id=1, source_target_pairs={{0,1},{1,0},{2,3},{3,2},{4,5},{5,4},{6,7},{7,6},{8,9},{9,8},{10,11... | collective-permute-start | bytes 786440 | tf_op jit(solution)/shard_map/ppermute | solution.py:169
  106.2 2.3 %collective-permute-start.31 = (bf16[2,128,128]{2,1,0:T(8,128)(2,1)S(1)}, bf16[2,128,128]{2,1,0:T(8,128)(2,1)S(1)}, u32[]{:S(2)}, u32[]{:S(2)}) collective-permute-start(bf16[2,128,128]{2,1,0:T(8,128)(2,1)S(1)} %get-tuple-element.110), channel_id=1, source_target_pairs={{0,1},{1,0},{2,3},{3,2},{4,5},{5,4},{6,7},{7,6},{8,9},{9,8},{10,11... | collective-permute-start | bytes 196616 | tf_op jit(solution)/shard_map/ppermute | solution.py:169
  106.3 5.0 %collective-permute-start.32 = (bf16[2,128,128]{2,1,0:T(8,128)(2,1)S(1)}, bf16[2,128,128]{2,1,0:T(8,128)(2,1)S(1)}, u32[]{:S(2)}, u32[]{:S(2)}) collective-permute-start(bf16[2,128,128]{2,1,0:T(8,128)(2,1)S(1)} %get-tuple-element.109), channel_id=1, source_target_pairs={{0,2},{1,3},{2,0},{3,1},{4,6},{5,7},{6,4},{7,5},{8,10},{9,11},{10,... | collective-permute-start | bytes 196616 | tf_op jit(solution)/shard_map/ppermute | solution.py:169
  106.9 4.9 %collective-permute-start.33 = (bf16[2,128,128]{2,1,0:T(8,128)(2,1)S(1)}, bf16[2,128,128]{2,1,0:T(8,128)(2,1)S(1)}, u32[]{:S(2)}, u32[]{:S(2)}) collective-permute-start(bf16[2,128,128]{2,1,0:T(8,128)(2,1)S(1)} %get-tuple-element.108), channel_id=1, source_target_pairs={{0,3},{1,2},{2,1},{3,0},{4,7},{5,6},{6,5},{7,4},{8,11},{9,10},{10,... | collective-permute-start | bytes 196616 | tf_op jit(solution)/shard_map/ppermute | solution.py:169
  (14 other events, 76.6 us)

commit v7 on v6

--- a/solution.py
+++ b/solution.py
@@ -24,17 +24,32 @@
     return max(16, 128 // lanes)
 
 
-def attend_kernel(head, lanes, depth, start_ref, begin_ref, place_ref, key_place_ref, *refs):
+def attend_kernel(lanes, depth, start_ref, begin_ref, *refs):
     refs = list(refs)
     take = lambda count: [refs.pop(0) for _ in range(count)]
     query_refs, kv_refs = take(lanes), take(depth)
     out_refs, grad_refs = take(lanes), take(depth)
-    key_turned, value_turned, key_sum, value_sum, score_ref, out_sum, query_sum = refs
+    key_turned, value_turned, key_sum, value_sum, score_ref, key_place_ref = refs
     rows = query_refs[0].shape[1]
     turn_rows = query_rows(lanes)
     key_tiles, query_tiles = rows // KR, rows // turn_rows
     tile = depth * lanes * KR
     span = lanes * GROUP * turn_rows
+    devices = lanes * depth
+    position = lax.axis_index("seq")
+    lane = lax.rem(position, lanes)
+    above = position - lane
+    at = lax.broadcasted_iota(jnp.int32, (tile, 128), 0)
+    key_place_ref[...] = (
+        lax.rem(at, KR) * devices
+        + ((at // (KR * lanes) * lanes) ^ above)
+        + (lax.rem(at // KR, lanes) ^ lane)
+    )
+    at = lax.broadcasted_iota(jnp.int32, (1, lanes * turn_rows), 1)
+    row_place = lax.rem(at, turn_rows) * devices + above + ((at // turn_rows) ^ lane)
+
+    def widened(row):
+        return jnp.concatenate([row] * GROUP, axis=1)
 
     def keys_of(which, step):
         at = pl.ds(pl.multiple_of(step * KR, KR), KR)
@@ -46,7 +61,7 @@
         at = pl.ds(pl.multiple_of(step * turn_rows, turn_rows), turn_rows)
         return jnp.concatenate(
             [
-                ref[which, at, (head * GROUP + j) * HD : (head * GROUP + j + 1) * HD]
+                ref[which, at, j * HD : (j + 1) * HD]
                 for j in range(GROUP)
                 for ref in query_refs
             ],
@@ -73,7 +88,8 @@
         query_t, grad_t = query.T, grad.T
         first = start_ref[turn]
         last = (turn + 1) * (turn_rows // KR)
-        begin, place = begin_ref[turn], place_ref[turn]
+        begin = widened(begin_ref[turn])
+        place = widened(row_place + turn * (turn_rows * devices))
 
         def solve(count):
             tops = jnp.full((8, span), -1e30, F32)
@@ -130,7 +146,7 @@
                 ref[:, which, at, :] = part.astype(ref.dtype).reshape(lanes, KR, HD)
 
 
-def attend(head, query_parts, kv_parts, starts, begins, places, key_places):
+def attend(query_parts, kv_parts, starts, begins):
     lanes, depth = len(query_parts), len(kv_parts)
     rows = query_parts[0].shape[1]
     turn_rows = query_rows(lanes)
@@ -140,13 +156,13 @@
     vmem = pl.BlockSpec(memory_space=pltpu.VMEM)
     pairs = GROUP * rows * lanes * 640
     return pl.pallas_call(
-        functools.partial(attend_kernel, head, lanes, depth),
+        functools.partial(attend_kernel, lanes, depth),
         out_shape=[jax.ShapeDtypeStruct((2, rows, GROUP * HD), BF16)] * lanes
         + [
             jax.ShapeDtypeStruct(part.shape, F32 if k == 0 or (k == 2 and depth == 4) else BF16)
             for k, part in enumerate(kv_parts)
         ],
-        in_specs=[pl.BlockSpec(memory_space=pltpu.SMEM)] + [vmem] * (3 + lanes + depth),
+        in_specs=[pl.BlockSpec(memory_space=pltpu.SMEM)] + [vmem] * (1 + lanes + depth),
         out_specs=[vmem] * (lanes + depth),
         scratch_shapes=[
             pltpu.VMEM((key_tiles, HD, tile), BF16),
@@ -154,14 +170,54 @@
             pltpu.VMEM((key_tiles, tile, HD), F32),
             pltpu.VMEM((key_tiles, tile, HD), F32),
             pltpu.VMEM((min(reach, key_tiles), tile, span), F32),
-            pltpu.VMEM((HD, span), F32),
-            pltpu.VMEM((HD, span), F32),
+            pltpu.VMEM((tile, 128), jnp.int32),
         ],
         compiler_params=pltpu.CompilerParams(vmem_limit_bytes=(40 if depth == 4 else 62) << 20),
         cost_estimate=pl.CostEstimate(
             flops=80 * HD * pairs, bytes_accessed=8 << 20, transcendentals=pairs
         ),
-    )(starts, begins, places, key_places, *query_parts, *kv_parts)
+    )(starts, begins, *query_parts, *kv_parts)
+
+
+def packed_by_lane(pair, lanes, pieces):
+    rows, columns = pair[0].shape
+    width = columns // lanes
+    shape = (2, rows, width // pieces)
+
+    def pack(*refs):
+        lane = lax.rem(lax.axis_index("seq"), lanes)
+        for which in range(2):
+            for mask in range(lanes):
+                for piece in range(pieces):
+                    at = (lane ^ mask) * width + piece * (width // pieces)
+                    columns = pl.ds(pl.multiple_of(at, 128), width // pieces)
+                    refs[2 + piece * lanes + mask][which] = refs[which][:, columns]
+
+    vmem = pl.BlockSpec(memory_space=pltpu.VMEM)
+    return pl.pallas_call(
+        pack,
+        out_shape=[jax.ShapeDtypeStruct(shape, BF16)] * (lanes * pieces),
+        in_specs=[vmem] * 2,
+        out_specs=[vmem] * (lanes * pieces),
+    )(*pair)
+
+
+def stacked_by_piece(parts):
+    _, rows, width = parts[0].shape
+    pieces, lanes, width = width // HD, len(parts), HD
+
+    def stack(*refs):
+        for piece in range(pieces):
+            for lane in range(lanes):
+                refs[lanes + piece][lane] = refs[lane][:, :, piece * HD : (piece + 1) * HD]
+
+    vmem = pl.BlockSpec(memory_space=pltpu.VMEM)
+    return pl.pallas_call(
+        stack,
+        out_shape=[jax.ShapeDtypeStruct((lanes, 2, rows, width), BF16)] * pieces,
+        in_specs=[vmem] * lanes,
+        out_specs=[vmem] * pieces,
+    )(*parts)
 
 
 def moved(tensor, target):
@@ -183,12 +239,12 @@
 
 def plain_exchange(query_cuts, kv_owns, lanes, depth, run):
     heads = len(kv_owns)
-    query_parts = [query_cuts[0]] + [swapped(query_cuts[mask], mask) for mask in range(1, lanes)]
     outs_back, totals = [], []
     for h in range(heads):
-        own = kv_owns[h]
+        own, cuts = kv_owns[h], query_cuts[h]
         outs, parts = run(
-            h, query_parts, [own] + [swapped(own, k * lanes) for k in range(1, depth)]
+            [cuts[0]] + [swapped(cuts[mask], mask) for mask in range(1, lanes)],
+            [own] + [swapped(own, k * lanes) for k in range(1, depth)],
         )
         outs_back.append([outs[0]] + [swapped(outs[mask], mask) for mask in range(1, lanes)])
         total = parts[0]
@@ -200,18 +256,19 @@
 
 def ordered_exchange(query_cuts, kv_owns, lanes, inner, run):
     one, two, three = lanes, 2 * lanes, 3 * lanes
-    query_d = swapped(query_cuts[3], 3)
-    query_x = swapped(query_cuts[2], 2)
+    cuts_a, cuts_b = query_cuts
+    qa_x, qa_d, qa_c = (swapped(cuts_a[mask], mask) for mask in (2, 3, 1))
     a_one = swapped(kv_owns[0], one)
     a_near = middle_swapped(kv_owns[0], lanes)
-    a_far = middle_swapped(after(a_one, query_d), lanes)
+    a_far = middle_swapped(a_one, lanes)
     a_two = swapped(a_near, one)
-    a_three = swapped(a_far, one)
+    a_three = swapped(after(a_far, qa_x, qa_d), one)
     b_two = swapped(after(kv_owns[1], a_far), two)
     b_three = swapped(after(kv_owns[1], a_two), three)
     b_one = swapped(after(kv_owns[1], a_three), one)
-    query_c = swapped(after(query_cuts[1], a_two), 1)
-    query_parts = [query_cuts[0], query_c, query_x, query_d]
+    qb_x = swapped(after(cuts_b[2], a_three), 2)
+    qb_d = swapped(after(cuts_b[3], a_three), 3)
+    qb_c = swapped(after(cuts_b[1], b_two), 1)
     a_parts = [
         kv_owns[0],
         a_one,
@@ -226,16 +283,16 @@
         value = parts[0] + first.astype(F32) + second.astype(F32)
         return (value + jnp.where(inner, middle.astype(F32), 0.0)).astype(BF16)
 
-    outs_a, sum_a = after(run(0, query_parts, a_parts), b_two, b_three, b_one)
+    outs_a, sum_a = after(
+        run([cuts_a[0], qa_c, qa_x, qa_d], a_parts), b_two, b_three, b_one, qb_x, qb_d
+    )
     a_passed = swapped(sum_a[3], one)
     a_middle = middle_swapped(sum_a[3], lanes)
     a_two = swapped(joined_two(sum_a, a_passed), two)
     a_one = swapped(sum_a[1], one)
-    outs_b, sum_b = run(
-        1, query_parts, after([kv_owns[1], b_one, b_two, b_three], a_passed)
-    )
+    outs_b, sum_b = run([cuts_b[0], qb_c, qb_x, qb_d], [kv_owns[1], b_one, b_two, b_three])
     out_ax, out_ad = swapped(outs_a[2], 2), swapped(outs_a[3], 3)
-    outs_b, sum_b = after((outs_b, sum_b), a_two, a_one, a_middle, out_ax, out_ad)
+    outs_b, sum_b = after((outs_b, sum_b), a_passed, a_one, a_middle, out_ax, out_ad)
     b_passed = swapped(sum_b[3], one)
     out_ac = swapped(after(outs_a[1], b_passed), 1)
     b_middle = middle_swapped(sum_b[3], lanes)
@@ -265,20 +322,12 @@
     heads = KV // lanes
     wide, narrow = H * HD // lanes, KV * HD // lanes
 
-    def cut(tensor, mask, width):
-        return lax.dynamic_slice_in_dim(tensor, (lane ^ mask) * width, width, 1)
-
-    def kv_cut(mask):
-        both = jnp.stack([cut(key_vectors, mask, narrow), cut(value_vectors, mask, narrow)])
-        return jnp.stack([both[:, :, h * HD : (h + 1) * HD] for h in range(heads)])
-
-    def query_cut(mask):
-        return jnp.stack([cut(queries, mask, wide), cut(grad_output, mask, wide)])
-
-    kv_lanes = [kv_cut(0)] + [swapped(kv_cut(mask), mask) for mask in range(1, lanes)]
-    queries, grad_output = (after(tensor, kv_lanes[1]) for tensor in (queries, grad_output))
-    query_cuts = [query_cut(mask) for mask in range(lanes)]
-    kv_owns = [jnp.stack([part[h] for part in kv_lanes]) for h in range(heads)]
+    kv_cuts = packed_by_lane((key_vectors, value_vectors), lanes, 1)
+    kv_lanes = [kv_cuts[0]] + [swapped(kv_cuts[mask], mask) for mask in range(1, lanes)]
+    kv_owns = stacked_by_piece(kv_lanes)
+    queries, grad_output = (after(tensor, kv_owns[0]) for tensor in (queries, grad_output))
+    packs = packed_by_lane((queries, grad_output), lanes, heads)
+    query_cuts = [packs[h * lanes : (h + 1) * lanes] for h in range(heads)]
 
     ids = document_ids.reshape(rows, devices)
     lane_masks = jnp.arange(lanes, dtype=jnp.int32)
@@ -290,27 +339,15 @@
     begin = jnp.sum(
         (document_ids[None, None, :] < own_ids[:, :, None]).astype(jnp.int32), axis=-1
     )
-    place = jnp.arange(rows, dtype=jnp.int32)[None, :] * devices + mine[:, None]
 
     turn_rows = query_rows(lanes)
 
-    def tiled(values):
-        parts = values.reshape(lanes, rows // turn_rows, turn_rows).transpose(1, 0, 2)
-        parts = parts.reshape(rows // turn_rows, 1, lanes * turn_rows)
-        return jnp.tile(parts, (1, 1, GROUP))
-
-    begins, places = tiled(begin), tiled(place)
-    starts = jnp.min(begins, axis=(1, 2)) // (KR * devices)
-    chunk = (jnp.arange(depth, dtype=jnp.int32) * lanes) ^ above
-    key_place = (
-        jnp.arange(KR, dtype=jnp.int32)[None, None, :] * devices
-        + chunk[:, None, None]
-        + (lane ^ lane_masks)[None, :, None]
-    ).reshape(depth * lanes * KR, 1)
-    key_places = jnp.broadcast_to(key_place, (depth * lanes * KR, 128))
-
-    def run(h, query_parts, kv_parts):
-        results = attend(h, query_parts, kv_parts, starts, begins, places, key_places)
+    begins = begin.reshape(lanes, rows // turn_rows, turn_rows).transpose(1, 0, 2)
+    starts = lax.div(jnp.min(begins, axis=(1, 2)), jnp.int32(KR * devices))
+    begins = begins.reshape(rows // turn_rows, 1, lanes * turn_rows)
+
+    def run(query_parts, kv_parts):
+        results = attend(query_parts, kv_parts, starts, begins)
         return results[:lanes], results[lanes:]
 
     if depth == 4 and lanes == 4 and heads == 2:

time: 114 us -> 127 us (1.11)
  waiting for transfers between devices: 39.2 us -> 56.7 us
  local copies, waits for them, and re-layouts: 12.2 us -> 2.5 us
  Pallas kernels: 21.1 us -> 27.8 us
  other arithmetic: 4.59 us -> 1.42 us
  starting transfers between devices: 34.2 us -> 37.1 us
    ppermute x34 -> x37, waiting for transfers between devices: 39.2 us -> 56.7 us  [moved(): return lax.ppermute(tensor, 'seq', [(i, target(i)) for i in range(devices)])]
    pallas_call x2 -> x5, Pallas kernels: 21.1 us -> 27.8 us  [the longest x2 20.9 us: attend(): pl.pallas_call(functools.partial(attend_kernel, lanes, depth), out_shape=...]
    slice x3 -> x0, local copies, waits for them, and re-layouts: 3.9 us -> none  [on_device(): kv_owns = [jnp.stack([part[h] for part in kv_lanes]) for h in range(heads)]]
    add x5 -> x0, local copies, waits for them, and re-layouts: 3.34 us -> none  [the longest x4 2.69 us: on_device(): place = jnp.arange(rows, dtype=jnp.int32)[None, :] * devices + mine[:, None]]
    ppermute x34 -> x37, starting transfers between devices: 34.2 us -> 37.1 us  [moved(): return lax.ppermute(tensor, 'seq', [(i, target(i)) for i in range(devices)])]
    another operation x10 -> x4, local copies, waits for them, and re-layouts: 3.16 us -> 0.23 us  [the longest x2 1.94 us: kv_cut(): jnp.stack([cut(key_vectors, mask, narrow), cut(value_vectors, mask, narro...]
    another operation x12 -> x0, other arithmetic: 1.72 us -> none  [the longest x6 1.45 us: kv_cut(): return jnp.stack([both[:, :, h * HD:(h + 1) * HD] for h in range(heads)])]
  transfers between devices with their start and end apart: 34 -> 37, of which waited for: 13 -> 16; matrix products, arithmetic and copies ran while one was open for 12% -> 2% of each run, Pallas kernels for 19% -> 19%
where the time goes in v7:
time: 127 us
  waiting for transfers between devices  56.7 us (45%)
  starting transfers between devices  37.1 us (29%)
  Pallas kernels  27.8 us (22%)
  local copies, waits for them, and re-layouts  2.5 us (2%)
  other arithmetic  1.42 us (1%)
    ppermute x37, waiting for transfers between devices, moved(): return lax.ppermute(tensor, 'seq', [(i, target(i)) for i in range(devices)])  56.7 us
    ppermute x37, starting transfers between devices, moved(): return lax.ppermute(tensor, 'seq', [(i, target(i)) for i in range(devices)])  37.1 us
    pallas_call x2, Pallas kernels, attend(): pl.pallas_call(functools.partial(attend_kernel, lanes, depth), out_shape=...  20.9 us
    pallas_call x2, Pallas kernels, packed_by_lane(): pl.pallas_call(pack, out_shape=[jax.ShapeDtypeStruct(shape, BF16)] * (lan...  4.92 us
  transfers between devices with their start and end apart: 37, of which 16 were waited for; matrix products, arithmetic and copies ran while one was open for 2% of the time, Pallas kernels for 19%

profile of v7, /device:TPU:0, one launch (start us, length us, event | category | flops | bytes accessed | tf_op | source)
XLA Modules:
  0.0 126.8 jit_solution(7479694788252371770)
XLA Ops:
  0.6 1.9 %shard_map.84 = (bf16[2,128,256]{2,1,0:T(8,128)(2,1)}, bf16[2,128,256]{2,1,0:T(8,128)(2,1)}, bf16[2,128,256]{2,1,0:T(8,128)(2,1)}, bf16[2,128,256]{2,1,0:T(8,128)(2,1)}) custom-call(bf16[128,1024]{1,0:T(8,128)(2,1)} %refs_0_.1, bf16[128,1024]{1,0:T(8,128)(2,1)} %refs_1_.1), custom_call_target="tpu_custom_call" | custom-call | tf_op jit(solution)/shard_map/pallas_call | solution.py:197
  3.0 2.5 %collective-permute-start.1 = (bf16[2,128,256]{2,1,0:T(8,128)(2,1)}, bf16[2,128,256]{2,1,0:T(8,128)(2,1)S(1)}, u32[]{:S(2)}, u32[]{:S(2)}) collective-permute-start(bf16[2,128,256]{2,1,0:T(8,128)(2,1)} %get-tuple-element.65), channel_id=1, source_target_pairs={{0,2},{1,3},{2,0},{3,1},{4,6},{5,7},{6,4},{7,5},{8,10},{9,11},{10,... | collective-permute-start | bytes 393224 | tf_op jit(solution)/shard_map/ppermute | solution.py:225
  5.6 4.4 %collective-permute-done.1.refs_2_ = bf16[2,128,256]{2,1,0:T(8,128)(2,1)S(1)} collective-permute-done((bf16[2,128,256]{2,1,0:T(8,128)(2,1)}, bf16[2,128,256]{2,1,0:T(8,128)(2,1)S(1)}, u32[]{:S(2)}, u32[]{:S(2)}) %collective-permute-start.1) | collective-permute-done | bytes 131104 | tf_op jit(solution)/shard_map/ppermute | solution.py:225
  10.0 2.4 %collective-permute-done.2.refs_3_ = bf16[2,128,256]{2,1,0:T(8,128)(2,1)S(1)} collective-permute-done((bf16[2,128,256]{2,1,0:T(8,128)(2,1)}, bf16[2,128,256]{2,1,0:T(8,128)(2,1)S(1)}, u32[]{:S(2)}, u32[]{:S(2)}) %collective-permute-start.2) | collective-permute-done | bytes 131104 | tf_op jit(solution)/shard_map/ppermute | solution.py:225
  13.1 2.0 %shard_map.85 = (bf16[4,2,128,128]{3,2,1,0:T(8,128)(2,1)}, bf16[4,2,128,128]{3,2,1,0:T(8,128)(2,1)}) custom-call(bf16[2,128,256]{2,1,0:T(8,128)(2,1)} %get-tuple-element.63.refs_0_, bf16[2,128,256]{2,1,0:T(8,128)(2,1)} %copy-done.8, bf16[2,128,256]{2,1,0:T(8,128)(2,1)} %copy-done.9, bf16[2,128,256]{2,1,0:T(8,128)(2,1)} %copy-done.10), custom_call_target="tpu_custom_call" | custom-call | tf_op jit(solution)/shard_map/pallas_call | solution.py:215
  15.1 1.6 %collective-permute-start.6 = (bf16[4,2,128,128]{3,2,1,0:T(8,128)(2,1)}, bf16[4,2,128,128]{3,2,1,0:T(8,128)(2,1)S(1)}, u32[]{:S(2)}, u32[]{:S(2)}) collective-permute-start(bf16[4,2,128,128]{3,2,1,0:T(8,128)(2,1)} %get-tuple-element.67.refs_4_), channel_id=1, source_target_pairs={{0,4},{1,5},{2,6},{3,7},{4,0},{5,1},{6,2},{7,3},{8,12},{9,13},{10,... | collective-permute-start | bytes 786440 | tf_op jit(solution)/shard_map/ppermute | solution.py:225
  16.9 1.6 %collective-permute-start.8 = (bf16[4,2,128,128]{3,2,1,0:T(8,128)(2,1)}, bf16[4,2,128,128]{3,2,1,0:T(8,128)(2,1)S(1)}, u32[]{:S(2)}, u32[]{:S(2)}) collective-permute-start(bf16[4,2,128,128]{3,2,1,0:T(8,128)(2,1)} %get-tuple-element.67.refs_4_), channel_id=1, source_target_pairs={{0,0},{1,1},{2,2},{3,3},{4,8},{5,9},{6,10},{7,11},{8,4},{9,5},{10,... | collective-permute-start | bytes 786440 | tf_op jit(solution)/shard_map/ppermute | solution.py:225
  18.6 3.0 %shard_map.86 = (bf16[2,128,512]{2,1,0:T(8,128)(2,1)}, bf16[2,128,512]{2,1,0:T(8,128)(2,1)}, bf16[2,128,512]{2,1,0:T(8,128)(2,1)}, bf16[2,128,512]{2,1,0:T(8,128...) custom-call(bf16[128,4096]{1,0:T(8,128)(2,1)} %refs_0_.2, ...), custom_call_target="tpu_custom_call" | custom-call | tf_op jit(solution)/shard_map/pallas_call | solution.py:197
  21.6 1.6 %collective-permute-start.4 = (bf16[2,128,512]{2,1,0:T(8,128)(2,1)}, bf16[2,128,512]{2,1,0:T(8,128)(2,1)S(1)}, u32[]{:S(2)}, u32[]{:S(2)}) collective-permute-start(bf16[2,128,512]{2,1,0:T(8,128)(2,1)} %get-tuple-element.72), channel_id=1, source_target_pairs={{0,2},{1,3},{2,0},{3,1},{4,6},{5,7},{6,4},{7,5},{8,10},{9,11},{10,... | collective-permute-start | bytes 786440 | tf_op jit(solution)/shard_map/ppermute | solution.py:225
  24.4 4.6 %collective-permute-start.9 = (bf16[4,2,128,128]{3,2,1,0:T(8,128)(2,1)S(1)}, bf16[4,2,128,128]{3,2,1,0:T(8,128)(2,1)S(1)}, u32[]{:S(2)}, u32[]{:S(2)}) collective-permute-start(bf16[4,2,128,128]{3,2,1,0:T(8,128)(2,1)S(1)} %collective-permute-done.8), channel_id=1, source_target_pairs={{0,4},{1,5},{2,6},{3,7},{4,0},{5,1},{6,2},{7,3},{8,12},{9,13},{10,... | collective-permute-start | bytes 786440 | tf_op jit(solution)/shard_map/ppermute | solution.py:225
  29.9 1.2 collective-permute-done.4.refs_2_
  31.1 3.7 %collective-permute-done.5.refs_3_ = bf16[2,128,512]{2,1,0:T(8,128)(2,1)S(1)} collective-permute-done((bf16[2,128,512]{2,1,0:T(8,128)(2,1)}, bf16[2,128,512]{2,1,0:T(8,128)(2,1)S(1)}, u32[]{:S(2)}, u32[]{:S(2)}) %collective-permute-start.5) | collective-permute-done | bytes 262176 | tf_op jit(solution)/shard_map/ppermute | solution.py:225
  34.8 3.2 %collective-permute-start.10 = (bf16[4,2,128,128]{3,2,1,0:T(8,128)(2,1)S(1)}, bf16[4,2,128,128]{3,2,1,0:T(8,128)(2,1)S(1)}, u32[]{:S(2)}, u32[]{:S(2)}) collective-permute-start(bf16[4,2,128,128]{3,2,1,0:T(8,128)(2,1)S(1)} %collective-permute-done.7), channel_id=1, source_target_pairs={{0,4},{1,5},{2,6},{3,7},{4,0},{5,1},{6,2},{7,3},{8,12},{9,13},{10,... | collective-permute-start | bytes 786440 | tf_op jit(solution)/shard_map/ppermute | solution.py:225
  38.8 2.3 %collective-permute-start.12 = (bf16[4,2,128,128]{3,2,1,0:T(8,128)(2,1)S(1)}, bf16[4,2,128,128]{3,2,1,0:T(8,128)(2,1)S(1)}, u32[]{:S(2)}, u32[]{:S(2)}) collective-permute-start(bf16[4,2,128,128]{3,2,1,0:T(8,128)(2,1)S(1)} %copy-done), channel_id=1, source_target_pairs={{0,12},{1,13},{2,14},{3,15},{4,8},{5,9},{6,10},{7,11},{8,4},{9,5},... | collective-permute-start | bytes 786440 | tf_op jit(solution)/shard_map/ppermute | solution.py:225
  41.1 8.4 %collective-permute-done.10 = bf16[4,2,128,128]{3,2,1,0:T(8,128)(2,1)S(1)} collective-permute-done((bf16[4,2,128,128]{3,2,1,0:T(8,128)(2,1)S(1)}, bf16[4,2,128,128]{3,2,1,0:T(8,128)(2,1)S(1)}, u32[]{:S(2)}, u32[]{:S(2)}) %collective-permute-start.10) | collective-permute-done | bytes 262176 | tf_op jit(solution)/shard_map/ppermute | solution.py:225
  50.2 1.2 collective-permute-start.14
  51.3 7.9 %collective-permute-done.11.refs_6_ = bf16[4,2,128,128]{3,2,1,0:T(8,128)(2,1)S(1)} collective-permute-done((bf16[4,2,128,128]{3,2,1,0:T(8,128)(2,1)S(1)}, bf16[4,2,128,128]{3,2,1,0:T(8,128)(2,1)S(1)}, u32[]{:S(2)}, u32[]{:S(2)}) %collective-permute-start.11) | collective-permute-done | bytes 262176 | tf_op jit(solution)/shard_map/ppermute | solution.py:225
  59.4 10.4 %shard_map.87 = (bf16[2,128,512]{2,1,0:T(8,128)(2,1)S(1)}, bf16[2,128,512]{2,1,0:T(8,128)(2,1)S(1)}, bf16[2,128,512]{2,1,0:T(8,128)(2,1)S(1)}, bf16[2,128,512]{2...) custom-call(s32[4]{0:T(128)S(1)} %compare_select_fusion.start_ref, ...), custom_call_target="tpu_custom_call" | custom-call | flops 13421772800 | bytes 8388608 | tf_op jit(solution)/shard_map/pallas_call | solution.py:158
  69.9 2.1 %collective-permute-start.17 = (bf16[4,2,128,128]{3,2,1,0:T(8,128)(2,1)S(1)}, bf16[4,2,128,128]{3,2,1,0:T(8,128)(2,1)S(1)}, u32[]{:S(2)}, u32[]{:S(2)}) collective-permute-start(bf16[4,2,128,128]{3,2,1,0:T(8,128)(2,1)S(1)} %get-tuple-element.104), channel_id=1, source_target_pairs={{0,4},{1,5},{2,6},{3,7},{4,0},{5,1},{6,2},{7,3},{8,12},{9,13},{10,... | collective-permute-start | bytes 786440 | tf_op jit(solution)/shard_map/ppermute | solution.py:225
  72.8 1.7 %collective-permute-start.18 = (bf16[4,2,128,128]{3,2,1,0:T(8,128)(2,1)S(1)}, bf16[4,2,128,128]{3,2,1,0:T(8,128)(2,1)S(1)}, u32[]{:S(2)}, u32[]{:S(2)}) collective-permute-start(bf16[4,2,128,128]{3,2,1,0:T(8,128)(2,1)S(1)} %get-tuple-element.105), channel_id=1, source_target_pairs={{0,4},{1,5},{2,6},{3,7},{4,0},{5,1},{6,2},{7,3},{8,12},{9,13},{10,... | collective-permute-start | bytes 786440 | tf_op jit(solution)/shard_map/ppermute | solution.py:225
  74.5 1.3 %collective-permute-start.20 = (bf16[2,128,512]{2,1,0:T(8,128)(2,1)S(1)}, bf16[2,128,512]{2,1,0:T(8,128)(2,1)S(1)}, u32[]{:S(2)}, u32[]{:S(2)}) collective-permute-start(bf16[2,128,512]{2,1,0:T(8,128)(2,1)S(1)} %get-tuple-element.106), channel_id=1, source_target_pairs={{0,2},{1,3},{2,0},{3,1},{4,6},{5,7},{6,4},{7,5},{8,10},{9,11},{10,... | collective-permute-start | bytes 786440 | tf_op jit(solution)/shard_map/ppermute | solution.py:225
  75.9 10.5 %shard_map.88 = (bf16[2,128,512]{2,1,0:T(8,128)(2,1)S(1)}, bf16[2,128,512]{2,1,0:T(8,128)(2,1)S(1)}, bf16[2,128,512]{2,1,0:T(8,128)(2,1)S(1)}, bf16[2,128,512]{2...) custom-call(s32[4]{0:T(128)S(1)} %compare_select_fusion.start_ref, ...), custom_call_target="tpu_custom_call" | custom-call | flops 13421772800 | bytes 8388608 | tf_op jit(solution)/shard_map/pallas_call | solution.py:158
  87.7 2.8 %collective-permute-start.27 = (bf16[4,2,128,128]{3,2,1,0:T(8,128)(2,1)S(1)}, bf16[4,2,128,128]{3,2,1,0:T(8,128)(2,1)S(1)}, u32[]{:S(2)}, u32[]{:S(2)}) collective-permute-start(bf16[4,2,128,128]{3,2,1,0:T(8,128)(2,1)S(1)} %add_convert_fusion.3), channel_id=1, source_target_pairs={{0,8},{1,9},{2,10},{3,11},{4,12},{5,13},{6,14},{7,15},{8,0},{9,1},... | collective-permute-start | bytes 786440 | tf_op jit(solution)/shard_map/ppermute | solution.py:225
  93.0 8.6 %collective-permute-done.22 = bf16[4,2,128,128]{3,2,1,0:T(8,128)(2,1)S(1)} collective-permute-done((bf16[4,2,128,128]{3,2,1,0:T(8,128)(2,1)S(1)}, bf16[4,2,128,128]{3,2,1,0:T(8,128)(2,1)S(1)}, u32[]{:S(2)}, u32[]{:S(2)}) %collective-permute-start.22) | collective-permute-done | bytes 262176 | tf_op jit(solution)/shard_map/ppermute | solution.py:225
  101.8 1.7 %collective-permute-done.27 = bf16[4,2,128,128]{3,2,1,0:T(8,128)(2,1)S(1)} collective-permute-done((bf16[4,2,128,128]{3,2,1,0:T(8,128)(2,1)S(1)}, bf16[4,2,128,128]{3,2,1,0:T(8,128)(2,1)S(1)}, u32[]{:S(2)}, u32[]{:S(2)}) %collective-permute-start.27) | collective-permute-done | bytes 262176 | tf_op jit(solution)/shard_map/ppermute | solution.py:225
  104.1 1.1 collective-permute-done.28
  105.3 1.3 %collective-permute-start.29 = (bf16[2,128,128]{2,1,0:T(8,128)(2,1)S(1)}, bf16[2,128,128]{2,1,0:T(8,128)(2,1)S(1)}, u32[]{:S(2)}, u32[]{:S(2)}) collective-permute-start(bf16[2,128,128]{2,1,0:T(8,128)(2,1)S(1)} %get-tuple-element.128), channel_id=1, source_target_pairs={{0,2},{1,3},{2,0},{3,1},{4,6},{5,7},{6,4},{7,5},{8,10},{9,11},{10,... | collective-permute-start | bytes 196616 | tf_op jit(solution)/shard_map/ppermute | solution.py:225
  106.6 3.0 %collective-permute-done.29 = bf16[2,128,128]{2,1,0:T(8,128)(2,1)S(1)} collective-permute-done((bf16[2,128,128]{2,1,0:T(8,128)(2,1)S(1)}, bf16[2,128,128]{2,1,0:T(8,128)(2,1)S(1)}, u32[]{:S(2)}, u32[]{:S(2)}) %collective-permute-start.29) | collective-permute-done | bytes 65568 | tf_op jit(solution)/shard_map/ppermute | solution.py:225
  109.7 4.0 %collective-permute-done.30 = bf16[2,128,128]{2,1,0:T(8,128)(2,1)S(1)} collective-permute-done((bf16[2,128,128]{2,1,0:T(8,128)(2,1)S(1)}, bf16[2,128,128]{2,1,0:T(8,128)(2,1)S(1)}, u32[]{:S(2)}, u32[]{:S(2)}) %collective-permute-start.30) | collective-permute-done | bytes 65568 | tf_op jit(solution)/shard_map/ppermute | solution.py:225
  114.4 5.7 %collective-permute-done.32 = bf16[4,2,128,128]{3,2,1,0:T(8,128)(2,1)S(1)} collective-permute-done((bf16[4,2,128,128]{3,2,1,0:T(8,128)(2,1)S(1)}, bf16[4,2,128,128]{3,2,1,0:T(8,128)(2,1)S(1)}, u32[]{:S(2)}, u32[]{:S(2)}) %collective-permute-start.32) | collective-permute-done | bytes 262176 | tf_op jit(solution)/shard_map/ppermute | solution.py:225
  120.3 1.3 %collective-permute-start.35 = (bf16[2,128,128]{2,1,0:T(8,128)(2,1)S(1)}, bf16[2,128,128]{2,1,0:T(8,128)(2,1)S(1)}, u32[]{:S(2)}, u32[]{:S(2)}) collective-permute-start(bf16[2,128,128]{2,1,0:T(8,128)(2,1)S(1)} %get-tuple-element.125), channel_id=1, source_target_pairs={{0,2},{1,3},{2,0},{3,1},{4,6},{5,7},{6,4},{7,5},{8,10},{9,11},{10,... | collective-permute-start | bytes 196616 | tf_op jit(solution)/shard_map/ppermute | solution.py:225
  122.5 2.6 %collective-permute-done.35 = bf16[2,128,128]{2,1,0:T(8,128)(2,1)S(1)} collective-permute-done((bf16[2,128,128]{2,1,0:T(8,128)(2,1)S(1)}, bf16[2,128,128]{2,1,0:T(8,128)(2,1)S(1)}, u32[]{:S(2)}, u32[]{:S(2)}) %collective-permute-start.35) | collective-permute-done | bytes 65568 | tf_op jit(solution)/shard_map/ppermute | solution.py:225
  (116 shorter events, 14.0 us)
Async XLA Ops:
  3.0 7.0 %collective-permute-start.1 = (bf16[2,128,256]{2,1,0:T(8,128)(2,1)}, bf16[2,128,256]{2,1,0:T(8,128)(2,1)S(1)}, u32[]{:S(2)}, u32[]{:S(2)}) collective-permute-start(bf16[2,128,256]{2,1,0:T(8,128)(2,1)} %get-tuple-element.65), channel_id=1, source_target_pairs={{0,2},{1,3},{2,0},{3,1},{4,6},{5,7},{6,4},{7,5},{8,10},{9,11},{10,... | collective-permute-start | bytes 393224 | tf_op jit(solution)/shard_map/ppermute | solution.py:225
  5.5 7.0 %collective-permute-start.2 = (bf16[2,128,256]{2,1,0:T(8,128)(2,1)}, bf16[2,128,256]{2,1,0:T(8,128)(2,1)S(1)}, u32[]{:S(2)}, u32[]{:S(2)}) collective-permute-start(bf16[2,128,256]{2,1,0:T(8,128)(2,1)} %get-tuple-element.66), channel_id=1, source_target_pairs={{0,3},{1,2},{2,1},{3,0},{4,7},{5,6},{6,5},{7,4},{8,11},{9,10},{10,... | collective-permute-start | bytes 393224 | tf_op jit(solution)/shard_map/ppermute | solution.py:225
  15.1 8.5 %collective-permute-start.6 = (bf16[4,2,128,128]{3,2,1,0:T(8,128)(2,1)}, bf16[4,2,128,128]{3,2,1,0:T(8,128)(2,1)S(1)}, u32[]{:S(2)}, u32[]{:S(2)}) collective-permute-start(bf16[4,2,128,128]{3,2,1,0:T(8,128)(2,1)} %get-tuple-element.67.refs_4_), channel_id=1, source_target_pairs={{0,4},{1,5},{2,6},{3,7},{4,0},{5,1},{6,2},{7,3},{8,12},{9,13},{10,... | collective-permute-start | bytes 786440 | tf_op jit(solution)/shard_map/ppermute | solution.py:225
  16.9 7.5 %collective-permute-start.8 = (bf16[4,2,128,128]{3,2,1,0:T(8,128)(2,1)}, bf16[4,2,128,128]{3,2,1,0:T(8,128)(2,1)S(1)}, u32[]{:S(2)}, u32[]{:S(2)}) collective-permute-start(bf16[4,2,128,128]{3,2,1,0:T(8,128)(2,1)} %get-tuple-element.67.refs_4_), channel_id=1, source_target_pairs={{0,0},{1,1},{2,2},{3,3},{4,8},{5,9},{6,10},{7,11},{8,4},{9,5},{10,... | collective-permute-start | bytes 786440 | tf_op jit(solution)/shard_map/ppermute | solution.py:225
  21.6 9.5 %collective-permute-start.4 = (bf16[2,128,512]{2,1,0:T(8,128)(2,1)}, bf16[2,128,512]{2,1,0:T(8,128)(2,1)S(1)}, u32[]{:S(2)}, u32[]{:S(2)}) collective-permute-start(bf16[2,128,512]{2,1,0:T(8,128)(2,1)} %get-tuple-element.72), channel_id=1, source_target_pairs={{0,2},{1,3},{2,0},{3,1},{4,6},{5,7},{6,4},{7,5},{8,10},{9,11},{10,... | collective-permute-start | bytes 786440 | tf_op jit(solution)/shard_map/ppermute | solution.py:225
  23.2 11.6 %collective-permute-start.5 = (bf16[2,128,512]{2,1,0:T(8,128)(2,1)}, bf16[2,128,512]{2,1,0:T(8,128)(2,1)S(1)}, u32[]{:S(2)}, u32[]{:S(2)}) collective-permute-start(bf16[2,128,512]{2,1,0:T(8,128)(2,1)} %get-tuple-element.73), channel_id=1, source_target_pairs={{0,3},{1,2},{2,1},{3,0},{4,7},{5,6},{6,5},{7,4},{8,11},{9,10},{10,... | collective-permute-start | bytes 786440 | tf_op jit(solution)/shard_map/ppermute | solution.py:225
  23.6 11.1 %collective-permute-start.7 = (bf16[4,2,128,128]{3,2,1,0:T(8,128)(2,1)S(1)}, bf16[4,2,128,128]{3,2,1,0:T(8,128)(2,1)S(1)}, u32[]{:S(2)}, u32[]{:S(2)}) collective-permute-start(bf16[4,2,128,128]{3,2,1,0:T(8,128)(2,1)S(1)} %collective-permute-done.6.refs_5_), channel_id=1, source_target_pairs={{0,0},{1,1},{2,2},{3,3},{4,8},{5,9},{6,10},{7,11},{8,4},{9,5},{10,... | collective-permute-start | bytes 786440 | tf_op jit(solution)/shard_map/ppermute | solution.py:225
  24.4 14.4 %collective-permute-start.9 = (bf16[4,2,128,128]{3,2,1,0:T(8,128)(2,1)S(1)}, bf16[4,2,128,128]{3,2,1,0:T(8,128)(2,1)S(1)}, u32[]{:S(2)}, u32[]{:S(2)}) collective-permute-start(bf16[4,2,128,128]{3,2,1,0:T(8,128)(2,1)S(1)} %collective-permute-done.8), channel_id=1, source_target_pairs={{0,4},{1,5},{2,6},{3,7},{4,0},{5,1},{6,2},{7,3},{8,12},{9,13},{10,... | collective-permute-start | bytes 786440 | tf_op jit(solution)/shard_map/ppermute | solution.py:225
  34.8 14.8 %collective-permute-start.10 = (bf16[4,2,128,128]{3,2,1,0:T(8,128)(2,1)S(1)}, bf16[4,2,128,128]{3,2,1,0:T(8,128)(2,1)S(1)}, u32[]{:S(2)}, u32[]{:S(2)}) collective-permute-start(bf16[4,2,128,128]{3,2,1,0:T(8,128)(2,1)S(1)} %collective-permute-done.7), channel_id=1, source_target_pairs={{0,4},{1,5},{2,6},{3,7},{4,0},{5,1},{6,2},{7,3},{8,12},{9,13},{10,... | collective-permute-start | bytes 786440 | tf_op jit(solution)/shard_map/ppermute | solution.py:225
  38.0 21.3 %collective-permute-start.11 = (bf16[4,2,128,128]{3,2,1,0:T(8,128)(2,1)S(1)}, bf16[4,2,128,128]{3,2,1,0:T(8,128)(2,1)S(1)}, u32[]{:S(2)}, u32[]{:S(2)}) collective-permute-start(bf16[4,2,128,128]{3,2,1,0:T(8,128)(2,1)S(1)} %copy-done), channel_id=1, source_target_pairs={{0,8},{1,9},{2,10},{3,11},{4,12},{5,13},{6,14},{7,15},{8,0},{9,1},... | collective-permute-start | bytes 786440 | tf_op jit(solution)/shard_map/ppermute | solution.py:225
  38.2 21.1 %collective-permute-start.3 = (bf16[2,128,512]{2,1,0:T(8,128)(2,1)}, bf16[2,128,512]{2,1,0:T(8,128)(2,1)S(1)}, u32[]{:S(2)}, u32[]{:S(2)}) collective-permute-start(bf16[2,128,512]{2,1,0:T(8,128)(2,1)} %get-tuple-element.71), channel_id=1, source_target_pairs={{0,1},{1,0},{2,3},{3,2},{4,5},{5,4},{6,7},{7,6},{8,9},{9,8},{10,11... | collective-permute-start | bytes 786440 | tf_op jit(solution)/shard_map/ppermute | solution.py:225
  38.8 31.1 %collective-permute-start.12 = (bf16[4,2,128,128]{3,2,1,0:T(8,128)(2,1)S(1)}, bf16[4,2,128,128]{3,2,1,0:T(8,128)(2,1)S(1)}, u32[]{:S(2)}, u32[]{:S(2)}) collective-permute-start(bf16[4,2,128,128]{3,2,1,0:T(8,128)(2,1)S(1)} %copy-done), channel_id=1, source_target_pairs={{0,12},{1,13},{2,14},{3,15},{4,8},{5,9},{6,10},{7,11},{8,4},{9,5},... | collective-permute-start | bytes 786440 | tf_op jit(solution)/shard_map/ppermute | solution.py:225
  49.6 20.3 %collective-permute-start.15 = (bf16[2,128,512]{2,1,0:T(8,128)(2,1)}, bf16[2,128,512]{2,1,0:T(8,128)(2,1)S(1)}, u32[]{:S(2)}, u32[]{:S(2)}) collective-permute-start(bf16[2,128,512]{2,1,0:T(8,128)(2,1)} %get-tuple-element.90), channel_id=1, source_target_pairs={{0,3},{1,2},{2,1},{3,0},{4,7},{5,6},{6,5},{7,4},{8,11},{9,10},{10,... | collective-permute-start | bytes 786440 | tf_op jit(solution)/shard_map/ppermute | solution.py:225
  50.2 19.7 %collective-permute-start.14 = (bf16[2,128,512]{2,1,0:T(8,128)(2,1)}, bf16[2,128,512]{2,1,0:T(8,128)(2,1)S(1)}, u32[]{:S(2)}, u32[]{:S(2)}) collective-permute-start(bf16[2,128,512]{2,1,0:T(8,128)(2,1)} %get-tuple-element.88), channel_id=1, source_target_pairs={{0,2},{1,3},{2,0},{3,1},{4,6},{5,7},{6,4},{7,5},{8,10},{9,11},{10,... | collective-permute-start | bytes 786440 | tf_op jit(solution)/shard_map/ppermute | solution.py:225
  59.2 10.6 %collective-permute-start.13 = (bf16[4,2,128,128]{3,2,1,0:T(8,128)(2,1)S(1)}, bf16[4,2,128,128]{3,2,1,0:T(8,128)(2,1)S(1)}, u32[]{:S(2)}, u32[]{:S(2)}) collective-permute-start(bf16[4,2,128,128]{3,2,1,0:T(8,128)(2,1)S(1)} %copy-done), channel_id=1, source_target_pairs={{0,4},{1,5},{2,6},{3,7},{4,0},{5,1},{6,2},{7,3},{8,12},{9,13},{10,... | collective-permute-start | bytes 786440 | tf_op jit(solution)/shard_map/ppermute | solution.py:225
  59.3 16.5 %collective-permute-start.16 = (bf16[2,128,512]{2,1,0:T(8,128)(2,1)S(1)}, bf16[2,128,512]{2,1,0:T(8,128)(2,1)S(1)}, u32[]{:S(2)}, u32[]{:S(2)}) collective-permute-start(bf16[2,128,512]{2,1,0:T(8,128)(2,1)S(1)} %copy-done.12), channel_id=1, source_target_pairs={{0,1},{1,0},{2,3},{3,2},{4,5},{5,4},{6,7},{7,6},{8,9},{9,8},{10,11... | collective-permute-start | bytes 786440 | tf_op jit(solution)/shard_map/ppermute | solution.py:225
  69.9 16.6 %collective-permute-start.17 = (bf16[4,2,128,128]{3,2,1,0:T(8,128)(2,1)S(1)}, bf16[4,2,128,128]{3,2,1,0:T(8,128)(2,1)S(1)}, u32[]{:S(2)}, u32[]{:S(2)}) collective-permute-start(bf16[4,2,128,128]{3,2,1,0:T(8,128)(2,1)S(1)} %get-tuple-element.104), channel_id=1, source_target_pairs={{0,4},{1,5},{2,6},{3,7},{4,0},{5,1},{6,2},{7,3},{8,12},{9,13},{10,... | collective-permute-start | bytes 786440 | tf_op jit(solution)/shard_map/ppermute | solution.py:225
  71.9 14.6 %collective-permute-start.19 = (bf16[4,2,128,128]{3,2,1,0:T(8,128)(2,1)S(1)}, bf16[4,2,128,128]{3,2,1,0:T(8,128)(2,1)S(1)}, u32[]{:S(2)}, u32[]{:S(2)}) collective-permute-start(bf16[4,2,128,128]{3,2,1,0:T(8,128)(2,1)S(1)} %get-tuple-element.104), channel_id=1, source_target_pairs={{0,0},{1,1},{2,2},{3,3},{4,8},{5,9},{6,10},{7,11},{8,4},{9,5},{10,... | collective-permute-start | bytes 786440 | tf_op jit(solution)/shard_map/ppermute | solution.py:225
  72.8 13.7 %collective-permute-start.18 = (bf16[4,2,128,128]{3,2,1,0:T(8,128)(2,1)S(1)}, bf16[4,2,128,128]{3,2,1,0:T(8,128)(2,1)S(1)}, u32[]{:S(2)}, u32[]{:S(2)}) collective-permute-start(bf16[4,2,128,128]{3,2,1,0:T(8,128)(2,1)S(1)} %get-tuple-element.105), channel_id=1, source_target_pairs={{0,4},{1,5},{2,6},{3,7},{4,0},{5,1},{6,2},{7,3},{8,12},{9,13},{10,... | collective-permute-start | bytes 786440 | tf_op jit(solution)/shard_map/ppermute | solution.py:225
  74.5 12.0 %collective-permute-start.20 = (bf16[2,128,512]{2,1,0:T(8,128)(2,1)S(1)}, bf16[2,128,512]{2,1,0:T(8,128)(2,1)S(1)}, u32[]{:S(2)}, u32[]{:S(2)}) collective-permute-start(bf16[2,128,512]{2,1,0:T(8,128)(2,1)S(1)} %get-tuple-element.106), channel_id=1, source_target_pairs={{0,2},{1,3},{2,0},{3,1},{4,6},{5,7},{6,4},{7,5},{8,10},{9,11},{10,... | collective-permute-start | bytes 786440 | tf_op jit(solution)/shard_map/ppermute | solution.py:225
  75.8 11.3 %collective-permute-start.21 = (bf16[2,128,512]{2,1,0:T(8,128)(2,1)S(1)}, bf16[2,128,512]{2,1,0:T(8,128)(2,1)S(1)}, u32[]{:S(2)}, u32[]{:S(2)}) collective-permute-start(bf16[2,128,512]{2,1,0:T(8,128)(2,1)S(1)} %get-tuple-element.107), channel_id=1, source_target_pairs={{0,3},{1,2},{2,1},{3,0},{4,7},{5,6},{6,5},{7,4},{8,11},{9,10},{10,... | collective-permute-start | bytes 786440 | tf_op jit(solution)/shard_map/ppermute | solution.py:225
  87.2 14.4 %collective-permute-start.22 = (bf16[4,2,128,128]{3,2,1,0:T(8,128)(2,1)S(1)}, bf16[4,2,128,128]{3,2,1,0:T(8,128)(2,1)S(1)}, u32[]{:S(2)}, u32[]{:S(2)}) collective-permute-start(bf16[4,2,128,128]{3,2,1,0:T(8,128)(2,1)S(1)} %get-tuple-element.108), channel_id=1, source_target_pairs={{0,4},{1,5},{2,6},{3,7},{4,0},{5,1},{6,2},{7,3},{8,12},{9,13},{10,... | collective-permute-start | bytes 786440 | tf_op jit(solution)/shard_map/ppermute | solution.py:225
  87.7 15.8 %collective-permute-start.27 = (bf16[4,2,128,128]{3,2,1,0:T(8,128)(2,1)S(1)}, bf16[4,2,128,128]{3,2,1,0:T(8,128)(2,1)S(1)}, u32[]{:S(2)}, u32[]{:S(2)}) collective-permute-start(bf16[4,2,128,128]{3,2,1,0:T(8,128)(2,1)S(1)} %add_convert_fusion.3), channel_id=1, source_target_pairs={{0,8},{1,9},{2,10},{3,11},{4,12},{5,13},{6,14},{7,15},{8,0},{9,1},... | collective-permute-start | bytes 786440 | tf_op jit(solution)/shard_map/ppermute | solution.py:225
  90.6 23.2 %collective-permute-start.33 = (bf16[4,2,128,128]{3,2,1,0:T(8,128)(2,1)S(1)}, bf16[4,2,128,128]{3,2,1,0:T(8,128)(2,1)S(1)}, u32[]{:S(2)}, u32[]{:S(2)}) collective-permute-start(bf16[4,2,128,128]{3,2,1,0:T(8,128)(2,1)S(1)} %get-tuple-element.108), channel_id=1, source_target_pairs={{0,0},{1,1},{2,2},{3,3},{4,8},{5,9},{6,10},{7,11},{8,4},{9,5},{10,... | collective-permute-start | bytes 786440 | tf_op jit(solution)/shard_map/ppermute | solution.py:225
  91.3 12.7 %collective-permute-start.24 = (bf16[2,128,512]{2,1,0:T(8,128)(2,1)S(1)}, bf16[2,128,512]{2,1,0:T(8,128)(2,1)S(1)}, u32[]{:S(2)}, u32[]{:S(2)}) collective-permute-start(bf16[2,128,512]{2,1,0:T(8,128)(2,1)S(1)} %get-tuple-element.112), channel_id=1, source_target_pairs={{0,2},{1,3},{2,0},{3,1},{4,6},{5,7},{6,4},{7,5},{8,10},{9,11},{10,... | collective-permute-start | bytes 786440 | tf_op jit(solution)/shard_map/ppermute | solution.py:225
  92.4 30.0 %collective-permute-start.26 = (bf16[2,128,512]{2,1,0:T(8,128)(2,1)S(1)}, bf16[2,128,512]{2,1,0:T(8,128)(2,1)S(1)}, u32[]{:S(2)}, u32[]{:S(2)}) collective-permute-start(bf16[2,128,512]{2,1,0:T(8,128)(2,1)S(1)} %get-tuple-element.114), channel_id=1, source_target_pairs={{0,3},{1,2},{2,1},{3,0},{4,7},{5,6},{6,5},{7,4},{8,11},{9,10},{10,... | collective-permute-start | bytes 786440 | tf_op jit(solution)/shard_map/ppermute | solution.py:225
  101.7 18.4 %collective-permute-start.32 = (bf16[4,2,128,128]{3,2,1,0:T(8,128)(2,1)S(1)}, bf16[4,2,128,128]{3,2,1,0:T(8,128)(2,1)S(1)}, u32[]{:S(2)}, u32[]{:S(2)}) collective-permute-start(bf16[4,2,128,128]{3,2,1,0:T(8,128)(2,1)S(1)} %add_convert_fusion.1), channel_id=1, source_target_pairs={{0,8},{1,9},{2,10},{3,11},{4,12},{5,13},{6,14},{7,15},{8,0},{9,1},... | collective-permute-start | bytes 786440 | tf_op jit(solution)/shard_map/ppermute | solution.py:225
  103.5 10.9 %collective-permute-start.31 = (bf16[4,2,128,128]{3,2,1,0:T(8,128)(2,1)S(1)}, bf16[4,2,128,128]{3,2,1,0:T(8,128)(2,1)S(1)}, u32[]{:S(2)}, u32[]{:S(2)}) collective-permute-start(bf16[4,2,128,128]{3,2,1,0:T(8,128)(2,1)S(1)} %get-tuple-element.121), channel_id=1, source_target_pairs={{0,4},{1,5},{2,6},{3,7},{4,0},{5,1},{6,2},{7,3},{8,12},{9,13},{10,... | collective-permute-start | bytes 786440 | tf_op jit(solution)/shard_map/ppermute | solution.py:225
  113.8 8.5 %collective-permute-start.25 = (bf16[2,128,512]{2,1,0:T(8,128)(2,1)S(1)}, bf16[2,128,512]{2,1,0:T(8,128)(2,1)S(1)}, u32[]{:S(2)}, u32[]{:S(2)}) collective-permute-start(bf16[2,128,512]{2,1,0:T(8,128)(2,1)S(1)} %get-tuple-element.113), channel_id=1, source_target_pairs={{0,1},{1,0},{2,3},{3,2},{4,5},{5,4},{6,7},{7,6},{8,9},{9,8},{10,11... | collective-permute-start | bytes 786440 | tf_op jit(solution)/shard_map/ppermute | solution.py:225
  113.8 7.8 %collective-permute-start.23 = (bf16[2,128,512]{2,1,0:T(8,128)(2,1)S(1)}, bf16[2,128,512]{2,1,0:T(8,128)(2,1)S(1)}, u32[]{:S(2)}, u32[]{:S(2)}) collective-permute-start(bf16[2,128,512]{2,1,0:T(8,128)(2,1)S(1)} %get-tuple-element.109), channel_id=1, source_target_pairs={{0,1},{1,0},{2,3},{3,2},{4,5},{5,4},{6,7},{7,6},{8,9},{9,8},{10,11... | collective-permute-start | bytes 786440 | tf_op jit(solution)/shard_map/ppermute | solution.py:225
  120.3 4.8 %collective-permute-start.35 = (bf16[2,128,128]{2,1,0:T(8,128)(2,1)S(1)}, bf16[2,128,128]{2,1,0:T(8,128)(2,1)S(1)}, u32[]{:S(2)}, u32[]{:S(2)}) collective-permute-start(bf16[2,128,128]{2,1,0:T(8,128)(2,1)S(1)} %get-tuple-element.125), channel_id=1, source_target_pairs={{0,2},{1,3},{2,0},{3,1},{4,6},{5,7},{6,4},{7,5},{8,10},{9,11},{10,... | collective-permute-start | bytes 196616 | tf_op jit(solution)/shard_map/ppermute | solution.py:225
  121.6 4.3 %collective-permute-start.36 = (bf16[2,128,128]{2,1,0:T(8,128)(2,1)S(1)}, bf16[2,128,128]{2,1,0:T(8,128)(2,1)S(1)}, u32[]{:S(2)}, u32[]{:S(2)}) collective-permute-start(bf16[2,128,128]{2,1,0:T(8,128)(2,1)S(1)} %get-tuple-element.124), channel_id=1, source_target_pairs={{0,3},{1,2},{2,1},{3,0},{4,7},{5,6},{6,5},{7,4},{8,11},{9,10},{10,... | collective-permute-start | bytes 196616 | tf_op jit(solution)/shard_map/ppermute | solution.py:225
  (18 other events, 198.9 us)

commit v8 on v4

--- a/solution.py
+++ b/solution.py
@@ -204,9 +204,9 @@
     a_two = swapped(kv_owns[0], two)
     a_one = swapped(kv_owns[0], one)
     a_three = middle_swapped(kv_owns[0], lanes)
-    b_two = swapped(after(kv_owns[1], a_one), two)
     a_passed = swapped(a_two, one)
-    b_three = swapped(after(kv_owns[1], a_three), three)
+    b_three = middle_swapped(after(kv_owns[1], a_three, a_one), lanes)
+    b_two = swapped(after(kv_owns[1], a_passed), two)
     b_one = swapped(after(kv_owns[1], query_x), one)
     query_c = swapped(after(query_cuts[1], query_d), 1)
     query_parts = [query_cuts[0], query_c, query_x, query_d]
@@ -219,11 +219,13 @@
         return (value + jnp.where(inner, middle.astype(F32), 0.0)).astype(BF16)
 
     outs_a, sum_a = run(0, query_parts, a_parts)
+    b_passed = swapped(after(b_two, sum_a[0]), one)
+    b_three = jnp.where(inner, b_three, b_passed)
     a_passed = swapped(sum_a[3], one)
     a_middle = middle_swapped(sum_a[3], lanes)
     a_two = swapped(joined_two(sum_a, a_passed), two)
-    a_one = swapped(after(sum_a[1], b_one), one)
-    out_ax = swapped(after(outs_a[2], b_two), 2)
+    a_one = swapped(after(sum_a[1], b_passed), one)
+    out_ax = swapped(after(outs_a[2], b_one), 2)
     out_ad = swapped(after(outs_a[3], b_one), 3)
     outs_b, sum_b = run(
         1, query_parts, after([kv_owns[1], b_one, b_two, b_three], a_passed)

time: 112 us -> 113 us (level); the launches traced: 110 us -> 113 us
  waiting for transfers between devices: 32.2 us -> 47.8 us
  starting transfers between devices: 44.9 us -> 33.6 us
    ppermute x33 -> x34, waiting for transfers between devices: 32.2 us -> 47.8 us  [moved(): return lax.ppermute(tensor, 'seq', [(i, target(i)) for i in range(devices)])]
    ppermute x33 -> x34, starting transfers between devices: 44.9 us -> 33.6 us  [moved(): return lax.ppermute(tensor, 'seq', [(i, target(i)) for i in range(devices)])]
  transfers between devices with their start and end apart: 33 -> 34, of which waited for: 13 -> 14; matrix products, arithmetic and copies ran while one was open for 8% -> 8% of each run, Pallas kernels for 18% -> 17%
where the time goes in v8:
time: 113 us
  waiting for transfers between devices  47.8 us (42%)
  starting transfers between devices  33.6 us (30%)
  Pallas kernels  18.8 us (17%)
  local copies, waits for them, and re-layouts  6.18 us (5%)
  other arithmetic  5.23 us (5%)
  between operations  1.35 us (1%)
    ppermute x34, waiting for transfers between devices, moved(): return lax.ppermute(tensor, 'seq', [(i, target(i)) for i in range(devices)])  47.8 us
    ppermute x34, starting transfers between devices, moved(): return lax.ppermute(tensor, 'seq', [(i, target(i)) for i in range(devices)])  33.6 us
    pallas_call x2, Pallas kernels, attend(): pl.pallas_call(functools.partial(attend_kernel, head, lanes, depth), out_...  18.8 us
  transfers between devices with their start and end apart: 34, of which 14 were waited for; matrix products, arithmetic and copies ran while one was open for 8% of the time, Pallas kernels for 17%

profile of v8, /device:TPU:0, one launch (start us, length us, event | category | flops | bytes accessed | tf_op | source)
XLA Modules:
  0.0 113.0 jit_solution(9626880079975448596)
XLA Ops:
  0.7 1.0 dynamic-slice_bitcast_fusion.12
  1.7 1.0 dynamic-slice_bitcast_fusion.13
  2.7 3.0 %collective-permute-start.4 = (bf16[2,2,128,128]{3,2,1,0:T(8,128)(2,1)S(1)}, bf16[2,2,128,128]{3,2,1,0:T(8,128)(2,1)S(1)}, u32[]{:S(2)}, u32[]{:S(2)}) collective-permute-start(bf16[2,2,128,128]{3,2,1,0:T(8,128)(2,1)S(1)} %pad_maximum_fusion.7), channel_id=1, source_target_pairs={{0,2},{1,3},{2,0},{3,1},{4,6},{5,7},{6,4},{7,5},{8,10},{9,11},{10,... | collective-permute-start | bytes 393224 | tf_op jit(solution)/shard_map/ppermute | solution.py:169
  8.5 1.7 %collective-permute-start.1 = (bf16[2,128,1024]{2,1,0:T(8,128)(2,1)S(1)}, bf16[2,128,1024]{2,1,0:T(8,128)(2,1)S(1)}, u32[]{:S(2)}, u32[]{:S(2)}) collective-permute-start(bf16[2,128,1024]{2,1,0:T(8,128)(2,1)S(1)} %pad_maximum_fusion.2), channel_id=1, source_target_pairs={{0,3},{1,2},{2,1},{3,0},{4,7},{5,6},{6,5},{7,4},{8,11},{9,10},{10,... | collective-permute-start | bytes 1572872 | tf_op jit(solution)/shard_map/ppermute | solution.py:169
  12.4 2.6 %collective-permute-start.7 = (bf16[4,2,128,128]{3,2,1,0:T(8,128)(2,1)S(1)}, bf16[4,2,128,128]{3,2,1,0:T(8,128)(2,1)S(1)}, u32[]{:S(2)}, u32[]{:S(2)}) collective-permute-start(bf16[4,2,128,128]{3,2,1,0:T(8,128)(2,1)S(1)} %pad_maximum_fusion.4.refs_4_), channel_id=1, source_target_pairs={{0,8},{1,9},{2,10},{3,11},{4,12},{5,13},{6,14},{7,15},{8,0},{9,1},... | collective-permute-start | bytes 786440 | tf_op jit(solution)/shard_map/ppermute | solution.py:169
  15.1 1.6 %collective-permute-start.6 = (bf16[4,2,128,128]{3,2,1,0:T(8,128)(2,1)S(1)}, bf16[4,2,128,128]{3,2,1,0:T(8,128)(2,1)S(1)}, u32[]{:S(2)}, u32[]{:S(2)}) collective-permute-start(bf16[4,2,128,128]{3,2,1,0:T(8,128)(2,1)S(1)} %pad_maximum_fusion.4.refs_4_), channel_id=1, source_target_pairs={{0,4},{1,5},{2,6},{3,7},{4,0},{5,1},{6,2},{7,3},{8,12},{9,13},{10,... | collective-permute-start | bytes 786440 | tf_op jit(solution)/shard_map/ppermute | solution.py:169
  16.8 1.4 %collective-permute-start.8 = (bf16[4,2,128,128]{3,2,1,0:T(8,128)(2,1)S(1)}, bf16[4,2,128,128]{3,2,1,0:T(8,128)(2,1)}, u32[]{:S(2)}, u32[]{:S(2)}) collective-permute-start(bf16[4,2,128,128]{3,2,1,0:T(8,128)(2,1)S(1)} %pad_maximum_fusion.4.refs_4_), channel_id=1, source_target_pairs={{0,0},{1,1},{2,2},{3,3},{4,8},{5,9},{6,10},{7,11},{8,4},{9,5},{10,... | collective-permute-start | bytes 786440 | tf_op jit(solution)/shard_map/ppermute | solution.py:169
  19.0 1.1 %collective-permute-start.3 = (bf16[2,128,1024]{2,1,0:T(8,128)(2,1)}, bf16[2,128,1024]{2,1,0:T(8,128)(2,1)S(1)}, u32[]{:S(2)}, u32[]{:S(2)}) collective-permute-start(bf16[2,128,1024]{2,1,0:T(8,128)(2,1)} %pad_maximum_fusion.3), channel_id=1, source_target_pairs={{0,2},{1,3},{2,0},{3,1},{4,6},{5,7},{6,4},{7,5},{8,10},{9,11},{10,... | collective-permute-start | bytes 1572872 | tf_op jit(solution)/shard_map/ppermute | solution.py:169
  20.2 8.0 %collective-permute-done.7.refs_6_ = bf16[4,2,128,128]{3,2,1,0:T(8,128)(2,1)S(1)} collective-permute-done((bf16[4,2,128,128]{3,2,1,0:T(8,128)(2,1)S(1)}, bf16[4,2,128,128]{3,2,1,0:T(8,128)(2,1)S(1)}, u32[]{:S(2)}, u32[]{:S(2)}) %collective-permute-start.7) | collective-permute-done | bytes 262176 | tf_op jit(solution)/shard_map/ppermute | solution.py:169
  29.4 0.9 pad_maximum_fusion.5.refs_4_
  31.1 5.2 %collective-permute-done.9 = bf16[4,2,128,128]{3,2,1,0:T(8,128)(2,1)} collective-permute-done((bf16[4,2,128,128]{3,2,1,0:T(8,128)(2,1)S(1)}, bf16[4,2,128,128]{3,2,1,0:T(8,128)(2,1)}, u32[]{:S(2)}, u32[]{:S(2)}) %collective-permute-start.9) | collective-permute-done | bytes 262176 | tf_op jit(solution)/shard_map/ppermute | solution.py:169
  36.3 2.4 %collective-permute-start.10 = (bf16[4,2,128,128]{3,2,1,0:T(8,128)(2,1)S(1)}, bf16[4,2,128,128]{3,2,1,0:T(8,128)(2,1)S(1)}, u32[]{:S(2)}, u32[]{:S(2)}) collective-permute-start(bf16[4,2,128,128]{3,2,1,0:T(8,128)(2,1)S(1)} %pad_maximum_fusion.5.refs_4_), channel_id=1, source_target_pairs={{0,8},{1,9},{2,10},{3,11},{4,12},{5,13},{6,14},{7,15},{8,0},{9,1},... | collective-permute-start | bytes 786440 | tf_op jit(solution)/shard_map/ppermute | solution.py:169
  38.8 1.7 %collective-permute-start.14 = (bf16[4,2,128,128]{3,2,1,0:T(8,128)(2,1)S(1)}, bf16[4,2,128,128]{3,2,1,0:T(8,128)(2,1)S(1)}, u32[]{:S(2)}, u32[]{:S(2)}) collective-permute-start(bf16[4,2,128,128]{3,2,1,0:T(8,128)(2,1)S(1)} %pad_maximum_fusion.5.refs_4_), channel_id=1, source_target_pairs={{0,4},{1,5},{2,6},{3,7},{4,0},{5,1},{6,2},{7,3},{8,12},{9,13},{10,... | collective-permute-start | bytes 786440 | tf_op jit(solution)/shard_map/ppermute | solution.py:169
  40.5 1.0 broadcast_select_fusion.1.refs_7_
  41.6 9.6 %shard_map.84 = (bf16[2,128,512]{2,1,0:T(8,128)(2,1)S(1)}, bf16[2,128,512]{2,1,0:T(8,128)(2,1)S(1)}, bf16[2,128,512]{2,1,0:T(8,128)(2,1)S(1)}, bf16[2,128,512]{2...) custom-call(s32[4]{0:T(128)S(1)} %and_select_fusion.start_ref, ...), custom_call_target="tpu_custom_call" | custom-call | flops 13421772800 | bytes 8388608 | tf_op jit(solution)/shard_map/pallas_call | solution.py:142
  52.3 4.1 %collective-permute-done.10.refs_6_ = bf16[4,2,128,128]{3,2,1,0:T(8,128)(2,1)S(1)} collective-permute-done((bf16[4,2,128,128]{3,2,1,0:T(8,128)(2,1)S(1)}, bf16[4,2,128,128]{3,2,1,0:T(8,128)(2,1)S(1)}, u32[]{:S(2)}, u32[]{:S(2)}) %collective-permute-start.10) | collective-permute-done | bytes 262176 | tf_op jit(solution)/shard_map/ppermute | solution.py:169
  57.0 1.2 %collective-permute-start.15 = (bf16[2,128,512]{2,1,0:T(8,128)(2,1)S(1)}, bf16[2,128,512]{2,1,0:T(8,128)(2,1)S(1)}, u32[]{:S(2)}, u32[]{:S(2)}) collective-permute-start(bf16[2,128,512]{2,1,0:T(8,128)(2,1)S(1)} %get-tuple-element.59), channel_id=1, source_target_pairs={{0,2},{1,3},{2,0},{3,1},{4,6},{5,7},{6,4},{7,5},{8,10},{9,11},{10,... | collective-permute-start | bytes 786440 | tf_op jit(solution)/shard_map/ppermute | solution.py:169
  58.2 9.1 %collective-permute-done.11 = bf16[4,2,128,128]{3,2,1,0:T(8,128)(2,1)S(1)} collective-permute-done((bf16[4,2,128,128]{3,2,1,0:T(8,128)(2,1)S(1)}, bf16[4,2,128,128]{3,2,1,0:T(8,128)(2,1)S(1)}, u32[]{:S(2)}, u32[]{:S(2)}) %collective-permute-start.11) | collective-permute-done | bytes 262176 | tf_op jit(solution)/shard_map/ppermute | solution.py:169
  68.2 2.5 %collective-permute-start.12 = (bf16[4,2,128,128]{3,2,1,0:T(8,128)(2,1)S(1)}, bf16[4,2,128,128]{3,2,1,0:T(8,128)(2,1)S(1)}, u32[]{:S(2)}, u32[]{:S(2)}) collective-permute-start(bf16[4,2,128,128]{3,2,1,0:T(8,128)(2,1)S(1)} %get-tuple-element.55), channel_id=1, source_target_pairs={{0,4},{1,5},{2,6},{3,7},{4,0},{5,1},{6,2},{7,3},{8,12},{9,13},{10,... | collective-permute-start | bytes 786440 | tf_op jit(solution)/shard_map/ppermute | solution.py:169
  70.7 9.2 %shard_map.85 = (bf16[2,128,512]{2,1,0:T(8,128)(2,1)S(1)}, bf16[2,128,512]{2,1,0:T(8,128)(2,1)S(1)}, bf16[2,128,512]{2,1,0:T(8,128)(2,1)S(1)}, bf16[2,128,512]{2...) custom-call(s32[4]{0:T(128)S(1)} %and_select_fusion.start_ref, ...), custom_call_target="tpu_custom_call" | custom-call | flops 13421772800 | bytes 8388608 | tf_op jit(solution)/shard_map/pallas_call | solution.py:142
  79.9 2.4 %collective-permute-done.19 = bf16[4,2,128,128]{3,2,1,0:T(8,128)(2,1)S(1)} collective-permute-done((bf16[4,2,128,128]{3,2,1,0:T(8,128)(2,1)S(1)}, bf16[4,2,128,128]{3,2,1,0:T(8,128)(2,1)S(1)}, u32[]{:S(2)}, u32[]{:S(2)}) %collective-permute-start.19) | collective-permute-done | bytes 262176 | tf_op jit(solution)/shard_map/ppermute | solution.py:169
  83.2 1.2 %collective-permute-start.21 = (bf16[2,128,512]{2,1,0:T(8,128)(2,1)S(1)}, bf16[2,128,512]{2,1,0:T(8,128)(2,1)S(1)}, u32[]{:S(2)}, u32[]{:S(2)}) collective-permute-start(bf16[2,128,512]{2,1,0:T(8,128)(2,1)S(1)} %get-tuple-element.79), channel_id=1, source_target_pairs={{0,2},{1,3},{2,0},{3,1},{4,6},{5,7},{6,4},{7,5},{8,10},{9,11},{10,... | collective-permute-start | bytes 786440 | tf_op jit(solution)/shard_map/ppermute | solution.py:169
  84.4 1.0 collective-permute-start.23
  85.5 5.0 %collective-permute-done.27 = bf16[4,2,128,128]{3,2,1,0:T(8,128)(2,1)S(1)} collective-permute-done((bf16[4,2,128,128]{3,2,1,0:T(8,128)(2,1)S(1)}, bf16[4,2,128,128]{3,2,1,0:T(8,128)(2,1)S(1)}, u32[]{:S(2)}, u32[]{:S(2)}) %collective-permute-start.27) | collective-permute-done | bytes 262176 | tf_op jit(solution)/shard_map/ppermute | solution.py:169
  91.1 1.3 %collective-permute-done.21 = bf16[2,128,512]{2,1,0:T(8,128)(2,1)S(1)} collective-permute-done((bf16[2,128,512]{2,1,0:T(8,128)(2,1)S(1)}, bf16[2,128,512]{2,1,0:T(8,128)(2,1)S(1)}, u32[]{:S(2)}, u32[]{:S(2)}) %collective-permute-start.21) | collective-permute-done | bytes 262176 | tf_op jit(solution)/shard_map/ppermute | solution.py:169
  92.4 4.0 %collective-permute-start.28 = (bf16[4,2,128,128]{3,2,1,0:T(8,128)(2,1)S(1)}, bf16[4,2,128,128]{3,2,1,0:T(8,128)(2,1)S(1)}, u32[]{:S(2)}, u32[]{:S(2)}) collective-permute-start(bf16[4,2,128,128]{3,2,1,0:T(8,128)(2,1)S(1)} %get-tuple-element.87), channel_id=1, source_target_pairs={{0,4},{1,5},{2,6},{3,7},{4,0},{5,1},{6,2},{7,3},{8,12},{9,13},{10,... | collective-permute-start | bytes 786440 | tf_op jit(solution)/shard_map/ppermute | solution.py:169
  96.7 1.0 collective-permute-done.24
  97.8 1.2 %collective-permute-start.25 = (bf16[2,128,128]{2,1,0:T(8,128)(2,1)S(1)}, bf16[2,128,128]{2,1,0:T(8,128)(2,1)S(1)}, u32[]{:S(2)}, u32[]{:S(2)}) collective-permute-start(bf16[2,128,128]{2,1,0:T(8,128)(2,1)S(1)} %get-tuple-element.102), channel_id=1, source_target_pairs={{0,2},{1,3},{2,0},{3,1},{4,6},{5,7},{6,4},{7,5},{8,10},{9,11},{10,... | collective-permute-start | bytes 196616 | tf_op jit(solution)/shard_map/ppermute | solution.py:169
  99.0 3.1 %collective-permute-done.25 = bf16[2,128,128]{2,1,0:T(8,128)(2,1)S(1)} collective-permute-done((bf16[2,128,128]{2,1,0:T(8,128)(2,1)S(1)}, bf16[2,128,128]{2,1,0:T(8,128)(2,1)S(1)}, u32[]{:S(2)}, u32[]{:S(2)}) %collective-permute-start.25) | collective-permute-done | bytes 65568 | tf_op jit(solution)/shard_map/ppermute | solution.py:169
  102.2 4.0 %collective-permute-done.26 = bf16[2,128,128]{2,1,0:T(8,128)(2,1)S(1)} collective-permute-done((bf16[2,128,128]{2,1,0:T(8,128)(2,1)S(1)}, bf16[2,128,128]{2,1,0:T(8,128)(2,1)S(1)}, u32[]{:S(2)}, u32[]{:S(2)}) %collective-permute-start.26) | collective-permute-done | bytes 65568 | tf_op jit(solution)/shard_map/ppermute | solution.py:169
  107.0 0.9 collective-permute-start.32
  108.6 3.1 %collective-permute-done.32 = bf16[2,128,128]{2,1,0:T(8,128)(2,1)S(1)} collective-permute-done((bf16[2,128,128]{2,1,0:T(8,128)(2,1)S(1)}, bf16[2,128,128]{2,1,0:T(8,128)(2,1)S(1)}, u32[]{:S(2)}, u32[]{:S(2)}) %collective-permute-start.32) | collective-permute-done | bytes 65568 | tf_op jit(solution)/shard_map/ppermute | solution.py:169
  (129 shorter events, 15.1 us)
Async XLA Ops:
  2.7 7.5 %collective-permute-start.4 = (bf16[2,2,128,128]{3,2,1,0:T(8,128)(2,1)S(1)}, bf16[2,2,128,128]{3,2,1,0:T(8,128)(2,1)S(1)}, u32[]{:S(2)}, u32[]{:S(2)}) collective-permute-start(bf16[2,2,128,128]{3,2,1,0:T(8,128)(2,1)S(1)} %pad_maximum_fusion.7), channel_id=1, source_target_pairs={{0,2},{1,3},{2,0},{3,1},{4,6},{5,7},{6,4},{7,5},{8,10},{9,11},{10,... | collective-permute-start | bytes 393224 | tf_op jit(solution)/shard_map/ppermute | solution.py:169
  5.8 5.9 %collective-permute-start.5 = (bf16[2,2,128,128]{3,2,1,0:T(8,128)(2,1)S(1)}, bf16[2,2,128,128]{3,2,1,0:T(8,128)(2,1)S(1)}, u32[]{:S(2)}, u32[]{:S(2)}) collective-permute-start(bf16[2,2,128,128]{3,2,1,0:T(8,128)(2,1)S(1)} %pad_maximum_fusion.8), channel_id=1, source_target_pairs={{0,3},{1,2},{2,1},{3,0},{4,7},{5,6},{6,5},{7,4},{8,11},{9,10},{10,... | collective-permute-start | bytes 393224 | tf_op jit(solution)/shard_map/ppermute | solution.py:169
  5.9 2.3 %collective-permute-start = (bf16[2,2,128,128]{3,2,1,0:T(8,128)(2,1)S(1)}, bf16[2,2,128,128]{3,2,1,0:T(8,128)(2,1)S(1)}, u32[]{:S(2)}, u32[]{:S(2)}) collective-permute-start(bf16[2,2,128,128]{3,2,1,0:T(8,128)(2,1)S(1)} %pad_maximum_fusion.6), channel_id=1, source_target_pairs={{0,1},{1,0},{2,3},{3,2},{4,5},{5,4},{6,7},{7,6},{8,9},{9,8},{10,11... | collective-permute-start | bytes 393224 | tf_op jit(solution)/shard_map/ppermute | solution.py:169
  8.5 20.2 %collective-permute-start.1 = (bf16[2,128,1024]{2,1,0:T(8,128)(2,1)S(1)}, bf16[2,128,1024]{2,1,0:T(8,128)(2,1)S(1)}, u32[]{:S(2)}, u32[]{:S(2)}) collective-permute-start(bf16[2,128,1024]{2,1,0:T(8,128)(2,1)S(1)} %pad_maximum_fusion.2), channel_id=1, source_target_pairs={{0,3},{1,2},{2,1},{3,0},{4,7},{5,6},{6,5},{7,4},{8,11},{9,10},{10,... | collective-permute-start | bytes 1572872 | tf_op jit(solution)/shard_map/ppermute | solution.py:169
  12.4 15.8 %collective-permute-start.7 = (bf16[4,2,128,128]{3,2,1,0:T(8,128)(2,1)S(1)}, bf16[4,2,128,128]{3,2,1,0:T(8,128)(2,1)S(1)}, u32[]{:S(2)}, u32[]{:S(2)}) collective-permute-start(bf16[4,2,128,128]{3,2,1,0:T(8,128)(2,1)S(1)} %pad_maximum_fusion.4.refs_4_), channel_id=1, source_target_pairs={{0,8},{1,9},{2,10},{3,11},{4,12},{5,13},{6,14},{7,15},{8,0},{9,1},... | collective-permute-start | bytes 786440 | tf_op jit(solution)/shard_map/ppermute | solution.py:169
  15.1 15.3 %collective-permute-start.6 = (bf16[4,2,128,128]{3,2,1,0:T(8,128)(2,1)S(1)}, bf16[4,2,128,128]{3,2,1,0:T(8,128)(2,1)S(1)}, u32[]{:S(2)}, u32[]{:S(2)}) collective-permute-start(bf16[4,2,128,128]{3,2,1,0:T(8,128)(2,1)S(1)} %pad_maximum_fusion.4.refs_4_), channel_id=1, source_target_pairs={{0,4},{1,5},{2,6},{3,7},{4,0},{5,1},{6,2},{7,3},{8,12},{9,13},{10,... | collective-permute-start | bytes 786440 | tf_op jit(solution)/shard_map/ppermute | solution.py:169
  16.8 13.6 %collective-permute-start.8 = (bf16[4,2,128,128]{3,2,1,0:T(8,128)(2,1)S(1)}, bf16[4,2,128,128]{3,2,1,0:T(8,128)(2,1)}, u32[]{:S(2)}, u32[]{:S(2)}) collective-permute-start(bf16[4,2,128,128]{3,2,1,0:T(8,128)(2,1)S(1)} %pad_maximum_fusion.4.refs_4_), channel_id=1, source_target_pairs={{0,0},{1,1},{2,2},{3,3},{4,8},{5,9},{6,10},{7,11},{8,4},{9,5},{10,... | collective-permute-start | bytes 786440 | tf_op jit(solution)/shard_map/ppermute | solution.py:169
  19.0 19.8 %collective-permute-start.3 = (bf16[2,128,1024]{2,1,0:T(8,128)(2,1)}, bf16[2,128,1024]{2,1,0:T(8,128)(2,1)S(1)}, u32[]{:S(2)}, u32[]{:S(2)}) collective-permute-start(bf16[2,128,1024]{2,1,0:T(8,128)(2,1)} %pad_maximum_fusion.3), channel_id=1, source_target_pairs={{0,2},{1,3},{2,0},{3,1},{4,6},{5,7},{6,4},{7,5},{8,10},{9,11},{10,... | collective-permute-start | bytes 1572872 | tf_op jit(solution)/shard_map/ppermute | solution.py:169
  28.2 8.2 %collective-permute-start.9 = (bf16[4,2,128,128]{3,2,1,0:T(8,128)(2,1)S(1)}, bf16[4,2,128,128]{3,2,1,0:T(8,128)(2,1)}, u32[]{:S(2)}, u32[]{:S(2)}) collective-permute-start(bf16[4,2,128,128]{3,2,1,0:T(8,128)(2,1)S(1)} %collective-permute-done.7.refs_6_), channel_id=1, source_target_pairs={{0,4},{1,5},{2,6},{3,7},{4,0},{5,1},{6,2},{7,3},{8,12},{9,13},{10,... | collective-permute-start | bytes 786440 | tf_op jit(solution)/shard_map/ppermute | solution.py:169
  28.7 12.8 %collective-permute-start.2 = (bf16[2,128,1024]{2,1,0:T(8,128)(2,1)S(1)}, bf16[2,128,1024]{2,1,0:T(8,128)(2,1)S(1)}, u32[]{:S(2)}, u32[]{:S(2)}) collective-permute-start(bf16[2,128,1024]{2,1,0:T(8,128)(2,1)S(1)} %pad_maximum_fusion.1), channel_id=1, source_target_pairs={{0,1},{1,0},{2,3},{3,2},{4,5},{5,4},{6,7},{7,6},{8,9},{9,8},{10,11... | collective-permute-start | bytes 1572872 | tf_op jit(solution)/shard_map/ppermute | solution.py:169
  30.4 26.6 %collective-permute-start.17 = (bf16[4,2,128,128]{3,2,1,0:T(8,128)(2,1)S(1)}, bf16[4,2,128,128]{3,2,1,0:T(8,128)(2,1)S(1)}, u32[]{:S(2)}, u32[]{:S(2)}) collective-permute-start(bf16[4,2,128,128]{3,2,1,0:T(8,128)(2,1)S(1)} %pad_maximum_fusion.5.refs_4_), channel_id=1, source_target_pairs={{0,0},{1,1},{2,2},{3,3},{4,8},{5,9},{6,10},{7,11},{8,4},{9,5},{10,... | collective-permute-start | bytes 786440 | tf_op jit(solution)/shard_map/ppermute | solution.py:169
  36.3 20.1 %collective-permute-start.10 = (bf16[4,2,128,128]{3,2,1,0:T(8,128)(2,1)S(1)}, bf16[4,2,128,128]{3,2,1,0:T(8,128)(2,1)S(1)}, u32[]{:S(2)}, u32[]{:S(2)}) collective-permute-start(bf16[4,2,128,128]{3,2,1,0:T(8,128)(2,1)S(1)} %pad_maximum_fusion.5.refs_4_), channel_id=1, source_target_pairs={{0,8},{1,9},{2,10},{3,11},{4,12},{5,13},{6,14},{7,15},{8,0},{9,1},... | collective-permute-start | bytes 786440 | tf_op jit(solution)/shard_map/ppermute | solution.py:169
  38.8 18.0 %collective-permute-start.14 = (bf16[4,2,128,128]{3,2,1,0:T(8,128)(2,1)S(1)}, bf16[4,2,128,128]{3,2,1,0:T(8,128)(2,1)S(1)}, u32[]{:S(2)}, u32[]{:S(2)}) collective-permute-start(bf16[4,2,128,128]{3,2,1,0:T(8,128)(2,1)S(1)} %pad_maximum_fusion.5.refs_4_), channel_id=1, source_target_pairs={{0,4},{1,5},{2,6},{3,7},{4,0},{5,1},{6,2},{7,3},{8,12},{9,13},{10,... | collective-permute-start | bytes 786440 | tf_op jit(solution)/shard_map/ppermute | solution.py:169
  51.3 16.0 %collective-permute-start.18 = (bf16[4,2,128,128]{3,2,1,0:T(8,128)(2,1)S(1)}, bf16[4,2,128,128]{3,2,1,0:T(8,128)(2,1)S(1)}, u32[]{:S(2)}, u32[]{:S(2)}) collective-permute-start(bf16[4,2,128,128]{3,2,1,0:T(8,128)(2,1)S(1)} %get-tuple-element.63), channel_id=1, source_target_pairs={{0,4},{1,5},{2,6},{3,7},{4,0},{5,1},{6,2},{7,3},{8,12},{9,13},{10,... | collective-permute-start | bytes 786440 | tf_op jit(solution)/shard_map/ppermute | solution.py:169
  51.6 28.3 %collective-permute-start.20 = (bf16[4,2,128,128]{3,2,1,0:T(8,128)(2,1)S(1)}, bf16[4,2,128,128]{3,2,1,0:T(8,128)(2,1)S(1)}, u32[]{:S(2)}, u32[]{:S(2)}) collective-permute-start(bf16[4,2,128,128]{3,2,1,0:T(8,128)(2,1)S(1)} %get-tuple-element.63), channel_id=1, source_target_pairs={{0,0},{1,1},{2,2},{3,3},{4,8},{5,9},{6,10},{7,11},{8,4},{9,5},{10,... | collective-permute-start | bytes 786440 | tf_op jit(solution)/shard_map/ppermute | solution.py:169
  56.4 10.9 %collective-permute-start.11 = (bf16[4,2,128,128]{3,2,1,0:T(8,128)(2,1)S(1)}, bf16[4,2,128,128]{3,2,1,0:T(8,128)(2,1)S(1)}, u32[]{:S(2)}, u32[]{:S(2)}) collective-permute-start(bf16[4,2,128,128]{3,2,1,0:T(8,128)(2,1)S(1)} %collective-permute-done.10.refs_6_), channel_id=1, source_target_pairs={{0,4},{1,5},{2,6},{3,7},{4,0},{5,1},{6,2},{7,3},{8,12},{9,13},{10,... | collective-permute-start | bytes 786440 | tf_op jit(solution)/shard_map/ppermute | solution.py:169
  56.7 23.2 %collective-permute-start.16 = (bf16[2,128,512]{2,1,0:T(8,128)(2,1)S(1)}, bf16[2,128,512]{2,1,0:T(8,128)(2,1)S(1)}, u32[]{:S(2)}, u32[]{:S(2)}) collective-permute-start(bf16[2,128,512]{2,1,0:T(8,128)(2,1)S(1)} %get-tuple-element.61), channel_id=1, source_target_pairs={{0,3},{1,2},{2,1},{3,0},{4,7},{5,6},{6,5},{7,4},{8,11},{9,10},{10,... | collective-permute-start | bytes 786440 | tf_op jit(solution)/shard_map/ppermute | solution.py:169
  57.0 22.9 %collective-permute-start.15 = (bf16[2,128,512]{2,1,0:T(8,128)(2,1)S(1)}, bf16[2,128,512]{2,1,0:T(8,128)(2,1)S(1)}, u32[]{:S(2)}, u32[]{:S(2)}) collective-permute-start(bf16[2,128,512]{2,1,0:T(8,128)(2,1)S(1)} %get-tuple-element.59), channel_id=1, source_target_pairs={{0,2},{1,3},{2,0},{3,1},{4,6},{5,7},{6,4},{7,5},{8,10},{9,11},{10,... | collective-permute-start | bytes 786440 | tf_op jit(solution)/shard_map/ppermute | solution.py:169
  67.4 14.9 %collective-permute-start.19 = (bf16[4,2,128,128]{3,2,1,0:T(8,128)(2,1)S(1)}, bf16[4,2,128,128]{3,2,1,0:T(8,128)(2,1)S(1)}, u32[]{:S(2)}, u32[]{:S(2)}) collective-permute-start(bf16[4,2,128,128]{3,2,1,0:T(8,128)(2,1)S(1)} %add_convert_fusion.3), channel_id=1, source_target_pairs={{0,8},{1,9},{2,10},{3,11},{4,12},{5,13},{6,14},{7,15},{8,0},{9,1},... | collective-permute-start | bytes 786440 | tf_op jit(solution)/shard_map/ppermute | solution.py:169
  68.2 14.3 %collective-permute-start.12 = (bf16[4,2,128,128]{3,2,1,0:T(8,128)(2,1)S(1)}, bf16[4,2,128,128]{3,2,1,0:T(8,128)(2,1)S(1)}, u32[]{:S(2)}, u32[]{:S(2)}) collective-permute-start(bf16[4,2,128,128]{3,2,1,0:T(8,128)(2,1)S(1)} %get-tuple-element.55), channel_id=1, source_target_pairs={{0,4},{1,5},{2,6},{3,7},{4,0},{5,1},{6,2},{7,3},{8,12},{9,13},{10,... | collective-permute-start | bytes 786440 | tf_op jit(solution)/shard_map/ppermute | solution.py:169
  82.5 8.0 %collective-permute-start.27 = (bf16[4,2,128,128]{3,2,1,0:T(8,128)(2,1)S(1)}, bf16[4,2,128,128]{3,2,1,0:T(8,128)(2,1)S(1)}, u32[]{:S(2)}, u32[]{:S(2)}) collective-permute-start(bf16[4,2,128,128]{3,2,1,0:T(8,128)(2,1)S(1)} %get-tuple-element.86), channel_id=1, source_target_pairs={{0,4},{1,5},{2,6},{3,7},{4,0},{5,1},{6,2},{7,3},{8,12},{9,13},{10,... | collective-permute-start | bytes 786440 | tf_op jit(solution)/shard_map/ppermute | solution.py:169
  82.5 23.7 %collective-permute-start.30 = (bf16[4,2,128,128]{3,2,1,0:T(8,128)(2,1)S(1)}, bf16[4,2,128,128]{3,2,1,0:T(8,128)(2,1)S(1)}, u32[]{:S(2)}, u32[]{:S(2)}) collective-permute-start(bf16[4,2,128,128]{3,2,1,0:T(8,128)(2,1)S(1)} %get-tuple-element.86), channel_id=1, source_target_pairs={{0,0},{1,1},{2,2},{3,3},{4,8},{5,9},{6,10},{7,11},{8,4},{9,5},{10,... | collective-permute-start | bytes 786440 | tf_op jit(solution)/shard_map/ppermute | solution.py:169
  83.2 9.3 %collective-permute-start.21 = (bf16[2,128,512]{2,1,0:T(8,128)(2,1)S(1)}, bf16[2,128,512]{2,1,0:T(8,128)(2,1)S(1)}, u32[]{:S(2)}, u32[]{:S(2)}) collective-permute-start(bf16[2,128,512]{2,1,0:T(8,128)(2,1)S(1)} %get-tuple-element.79), channel_id=1, source_target_pairs={{0,2},{1,3},{2,0},{3,1},{4,6},{5,7},{6,4},{7,5},{8,10},{9,11},{10,... | collective-permute-start | bytes 786440 | tf_op jit(solution)/shard_map/ppermute | solution.py:169
  84.4 12.1 %collective-permute-start.13 = (bf16[2,128,512]{2,1,0:T(8,128)(2,1)S(1)}, bf16[2,128,512]{2,1,0:T(8,128)(2,1)S(1)}, u32[]{:S(2)}, u32[]{:S(2)}) collective-permute-start(bf16[2,128,512]{2,1,0:T(8,128)(2,1)S(1)} %get-tuple-element.56), channel_id=1, source_target_pairs={{0,1},{1,0},{2,3},{3,2},{4,5},{5,4},{6,7},{7,6},{8,9},{9,8},{10,11... | collective-permute-start | bytes 786440 | tf_op jit(solution)/shard_map/ppermute | solution.py:169
  84.4 24.1 %collective-permute-start.23 = (bf16[2,128,512]{2,1,0:T(8,128)(2,1)S(1)}, bf16[2,128,512]{2,1,0:T(8,128)(2,1)S(1)}, u32[]{:S(2)}, u32[]{:S(2)}) collective-permute-start(bf16[2,128,512]{2,1,0:T(8,128)(2,1)S(1)} %get-tuple-element.81), channel_id=1, source_target_pairs={{0,3},{1,2},{2,1},{3,0},{4,7},{5,6},{6,5},{7,4},{8,11},{9,10},{10,... | collective-permute-start | bytes 786440 | tf_op jit(solution)/shard_map/ppermute | solution.py:169
  90.6 15.6 %collective-permute-start.29 = (bf16[4,2,128,128]{3,2,1,0:T(8,128)(2,1)S(1)}, bf16[4,2,128,128]{3,2,1,0:T(8,128)(2,1)S(1)}, u32[]{:S(2)}, u32[]{:S(2)}) collective-permute-start(bf16[4,2,128,128]{3,2,1,0:T(8,128)(2,1)S(1)} %add_convert_fusion.1), channel_id=1, source_target_pairs={{0,8},{1,9},{2,10},{3,11},{4,12},{5,13},{6,14},{7,15},{8,0},{9,1},... | collective-permute-start | bytes 786440 | tf_op jit(solution)/shard_map/ppermute | solution.py:169
  92.4 13.8 %collective-permute-start.28 = (bf16[4,2,128,128]{3,2,1,0:T(8,128)(2,1)S(1)}, bf16[4,2,128,128]{3,2,1,0:T(8,128)(2,1)S(1)}, u32[]{:S(2)}, u32[]{:S(2)}) collective-permute-start(bf16[4,2,128,128]{3,2,1,0:T(8,128)(2,1)S(1)} %get-tuple-element.87), channel_id=1, source_target_pairs={{0,4},{1,5},{2,6},{3,7},{4,0},{5,1},{6,2},{7,3},{8,12},{9,13},{10,... | collective-permute-start | bytes 786440 | tf_op jit(solution)/shard_map/ppermute | solution.py:169
  97.8 4.3 %collective-permute-start.25 = (bf16[2,128,128]{2,1,0:T(8,128)(2,1)S(1)}, bf16[2,128,128]{2,1,0:T(8,128)(2,1)S(1)}, u32[]{:S(2)}, u32[]{:S(2)}) collective-permute-start(bf16[2,128,128]{2,1,0:T(8,128)(2,1)S(1)} %get-tuple-element.102), channel_id=1, source_target_pairs={{0,2},{1,3},{2,0},{3,1},{4,6},{5,7},{6,4},{7,5},{8,10},{9,11},{10,... | collective-permute-start | bytes 196616 | tf_op jit(solution)/shard_map/ppermute | solution.py:169
  102.1 4.1 %collective-permute-start.26 = (bf16[2,128,128]{2,1,0:T(8,128)(2,1)S(1)}, bf16[2,128,128]{2,1,0:T(8,128)(2,1)S(1)}, u32[]{:S(2)}, u32[]{:S(2)}) collective-permute-start(bf16[2,128,128]{2,1,0:T(8,128)(2,1)S(1)} %get-tuple-element.101), channel_id=1, source_target_pairs={{0,3},{1,2},{2,1},{3,0},{4,7},{5,6},{6,5},{7,4},{8,11},{9,10},{10,... | collective-permute-start | bytes 196616 | tf_op jit(solution)/shard_map/ppermute | solution.py:169
  106.2 2.2 %collective-permute-start.22 = (bf16[2,128,512]{2,1,0:T(8,128)(2,1)S(1)}, bf16[2,128,512]{2,1,0:T(8,128)(2,1)S(1)}, u32[]{:S(2)}, u32[]{:S(2)}) collective-permute-start(bf16[2,128,512]{2,1,0:T(8,128)(2,1)S(1)} %get-tuple-element.80), channel_id=1, source_target_pairs={{0,1},{1,0},{2,3},{3,2},{4,5},{5,4},{6,7},{7,6},{8,9},{9,8},{10,11... | collective-permute-start | bytes 786440 | tf_op jit(solution)/shard_map/ppermute | solution.py:169
  107.0 4.7 %collective-permute-start.32 = (bf16[2,128,128]{2,1,0:T(8,128)(2,1)S(1)}, bf16[2,128,128]{2,1,0:T(8,128)(2,1)S(1)}, u32[]{:S(2)}, u32[]{:S(2)}) collective-permute-start(bf16[2,128,128]{2,1,0:T(8,128)(2,1)S(1)} %get-tuple-element.99), channel_id=1, source_target_pairs={{0,2},{1,3},{2,0},{3,1},{4,6},{5,7},{6,4},{7,5},{8,10},{9,11},{10,... | collective-permute-start | bytes 196616 | tf_op jit(solution)/shard_map/ppermute | solution.py:169
  107.9 4.3 %collective-permute-start.33 = (bf16[2,128,128]{2,1,0:T(8,128)(2,1)S(1)}, bf16[2,128,128]{2,1,0:T(8,128)(2,1)S(1)}, u32[]{:S(2)}, u32[]{:S(2)}) collective-permute-start(bf16[2,128,128]{2,1,0:T(8,128)(2,1)S(1)} %get-tuple-element.98), channel_id=1, source_target_pairs={{0,3},{1,2},{2,1},{3,0},{4,7},{5,6},{6,5},{7,4},{8,11},{9,10},{10,... | collective-permute-start | bytes 196616 | tf_op jit(solution)/shard_map/ppermute | solution.py:169
  (11 other events, 50.7 us)

commit v9 on v8

--- a/solution.py
+++ b/solution.py
@@ -177,6 +177,10 @@
     return moved(tensor, lambda i: i if i // lanes in (0, 3) else i ^ (3 * lanes))
 
 
+def outer_swapped(tensor, lanes):
+    return moved(tensor, lambda i: i ^ (3 * lanes) if i // lanes in (0, 3) else i)
+
+
 def after(tensor, *others):
     return lax.optimization_barrier((tensor, others))[0]
 
@@ -205,8 +209,9 @@
     a_one = swapped(kv_owns[0], one)
     a_three = middle_swapped(kv_owns[0], lanes)
     a_passed = swapped(a_two, one)
-    b_three = middle_swapped(after(kv_owns[1], a_three, a_one), lanes)
-    b_two = swapped(after(kv_owns[1], a_passed), two)
+    b_three = middle_swapped(after(kv_owns[1], a_three, a_one, query_d), lanes)
+    b_two = swapped(after(kv_owns[1], a_passed, b_three), two)
+    b_far = outer_swapped(after(kv_owns[1], a_passed, b_three), lanes)
     b_one = swapped(after(kv_owns[1], query_x), one)
     query_c = swapped(after(query_cuts[1], query_d), 1)
     query_parts = [query_cuts[0], query_c, query_x, query_d]
@@ -219,12 +224,11 @@
         return (value + jnp.where(inner, middle.astype(F32), 0.0)).astype(BF16)
 
     outs_a, sum_a = run(0, query_parts, a_parts)
-    b_passed = swapped(after(b_two, sum_a[0]), one)
-    b_three = jnp.where(inner, b_three, b_passed)
+    b_three = jnp.where(inner, b_three, after(b_far, sum_a[0]))
     a_passed = swapped(sum_a[3], one)
     a_middle = middle_swapped(sum_a[3], lanes)
     a_two = swapped(joined_two(sum_a, a_passed), two)
-    a_one = swapped(after(sum_a[1], b_passed), one)
+    a_one = swapped(after(sum_a[1], b_far), one)
     out_ax = swapped(after(outs_a[2], b_one), 2)
     out_ad = swapped(after(outs_a[3], b_one), 3)
     outs_b, sum_b = run(

time: 113 us -> 113 us (level)
  waiting for transfers between devices: 47.8 us -> 40.8 us
  starting transfers between devices: 33.6 us -> 36.1 us
  Pallas kernels: 18.8 us -> 21.1 us
  other arithmetic: 5.23 us -> 6.52 us
    ppermute x34, waiting for transfers between devices: 47.8 us -> 40.8 us  [moved(): return lax.ppermute(tensor, 'seq', [(i, target(i)) for i in range(devices)])]
    ppermute x34, starting transfers between devices: 33.6 us -> 36.1 us  [moved(): return lax.ppermute(tensor, 'seq', [(i, target(i)) for i in range(devices)])]
    pallas_call x2, Pallas kernels: 18.8 us -> 21.1 us  [attend(): pl.pallas_call(functools.partial(attend_kernel, head, lanes, depth), out_...]
    another operation x6, other arithmetic: 0.14 us -> 1.45 us  [kv_cut(): return jnp.stack([both[:, :, h * HD:(h + 1) * HD] for h in range(heads)])]
  transfers between devices with their start and end apart: 34 -> 34, of which waited for: 14 -> 13; matrix products, arithmetic and copies ran while one was open for 8% -> 8% of each run, Pallas kernels for 17% -> 19%
where the time goes in v9:
time: 113 us; the launch traced here: 112 us
  waiting for transfers between devices  40.8 us (36%)
  starting transfers between devices  36.1 us (32%)
  Pallas kernels  21.1 us (19%)
  local copies, waits for them, and re-layouts  6.64 us (6%)
  other arithmetic  6.52 us (6%)
  between operations  1.36 us (1%)
    ppermute x34, waiting for transfers between devices, moved(): return lax.ppermute(tensor, 'seq', [(i, target(i)) for i in range(devices)])  40.8 us
    ppermute x34, starting transfers between devices, moved(): return lax.ppermute(tensor, 'seq', [(i, target(i)) for i in range(devices)])  36.1 us
    pallas_call x2, Pallas kernels, attend(): pl.pallas_call(functools.partial(attend_kernel, head, lanes, depth), out_...  21.1 us
  transfers between devices with their start and end apart: 34, of which 13 were waited for; matrix products, arithmetic and copies ran while one was open for 8% of the time, Pallas kernels for 19%

profile of v9, /device:TPU:0, one launch (start us, length us, event | category | flops | bytes accessed | tf_op | source)
XLA Modules:
  0.0 112.5 jit_solution(1696123725209093867)
XLA Ops:
  0.7 1.0 dynamic-slice_bitcast_fusion.12
  1.7 1.0 dynamic-slice_bitcast_fusion.13
  3.4 2.9 %collective-permute-start.4 = (bf16[2,2,128,128]{3,2,1,0:T(8,128)(2,1)}, bf16[2,2,128,128]{3,2,1,0:T(8,128)(2,1)S(1)}, u32[]{:S(2)}, u32[]{:S(2)}) collective-permute-start(bf16[2,2,128,128]{3,2,1,0:T(8,128)(2,1)} %pad_maximum_fusion.7), channel_id=1, source_target_pairs={{0,2},{1,3},{2,0},{3,1},{4,6},{5,7},{6,4},{7,5},{8,10},{9,11},{10,... | collective-permute-start | bytes 393224 | tf_op jit(solution)/shard_map/ppermute | solution.py:169
  10.1 1.7 %collective-permute-start.1 = (bf16[2,128,1024]{2,1,0:T(8,128)(2,1)S(1)}, bf16[2,128,1024]{2,1,0:T(8,128)(2,1)S(1)}, u32[]{:S(2)}, u32[]{:S(2)}) collective-permute-start(bf16[2,128,1024]{2,1,0:T(8,128)(2,1)S(1)} %pad_maximum_fusion.2), channel_id=1, source_target_pairs={{0,3},{1,2},{2,1},{3,0},{4,7},{5,6},{6,5},{7,4},{8,11},{9,10},{10,... | collective-permute-start | bytes 1572872 | tf_op jit(solution)/shard_map/ppermute | solution.py:169
  13.5 2.9 %collective-permute-start.7 = (bf16[4,2,128,128]{3,2,1,0:T(8,128)(2,1)S(1)}, bf16[4,2,128,128]{3,2,1,0:T(8,128)(2,1)S(1)}, u32[]{:S(2)}, u32[]{:S(2)}) collective-permute-start(bf16[4,2,128,128]{3,2,1,0:T(8,128)(2,1)S(1)} %pad_maximum_fusion.4.refs_4_), channel_id=1, source_target_pairs={{0,8},{1,9},{2,10},{3,11},{4,12},{5,13},{6,14},{7,15},{8,0},{9,1},... | collective-permute-start | bytes 786440 | tf_op jit(solution)/shard_map/ppermute | solution.py:169
  16.6 1.6 %collective-permute-start.6 = (bf16[4,2,128,128]{3,2,1,0:T(8,128)(2,1)S(1)}, bf16[4,2,128,128]{3,2,1,0:T(8,128)(2,1)S(1)}, u32[]{:S(2)}, u32[]{:S(2)}) collective-permute-start(bf16[4,2,128,128]{3,2,1,0:T(8,128)(2,1)S(1)} %pad_maximum_fusion.4.refs_4_), channel_id=1, source_target_pairs={{0,4},{1,5},{2,6},{3,7},{4,0},{5,1},{6,2},{7,3},{8,12},{9,13},{10,... | collective-permute-start | bytes 786440 | tf_op jit(solution)/shard_map/ppermute | solution.py:169
  18.2 1.4 %collective-permute-start.8 = (bf16[4,2,128,128]{3,2,1,0:T(8,128)(2,1)S(1)}, bf16[4,2,128,128]{3,2,1,0:T(8,128)(2,1)}, u32[]{:S(2)}, u32[]{:S(2)}) collective-permute-start(bf16[4,2,128,128]{3,2,1,0:T(8,128)(2,1)S(1)} %pad_maximum_fusion.4.refs_4_), channel_id=1, source_target_pairs={{0,0},{1,1},{2,2},{3,3},{4,8},{5,9},{6,10},{7,11},{8,4},{9,5},{10,... | collective-permute-start | bytes 786440 | tf_op jit(solution)/shard_map/ppermute | solution.py:169
  21.0 8.2 %collective-permute-done.7.refs_6_ = bf16[4,2,128,128]{3,2,1,0:T(8,128)(2,1)S(1)} collective-permute-done((bf16[4,2,128,128]{3,2,1,0:T(8,128)(2,1)S(1)}, bf16[4,2,128,128]{3,2,1,0:T(8,128)(2,1)S(1)}, u32[]{:S(2)}, u32[]{:S(2)}) %collective-permute-start.7) | collective-permute-done | bytes 262176 | tf_op jit(solution)/shard_map/ppermute | solution.py:169
  31.8 3.9 %collective-permute-done.3.refs_2_ = bf16[2,128,1024]{2,1,0:T(8,128)(2,1)S(1)} collective-permute-done((bf16[2,128,1024]{2,1,0:T(8,128)(2,1)}, bf16[2,128,1024]{2,1,0:T(8,128)(2,1)S(1)}, u32[]{:S(2)}, u32[]{:S(2)}) %collective-permute-start.3) | collective-permute-done | bytes 524320 | tf_op jit(solution)/shard_map/ppermute | solution.py:169
  35.7 3.9 %collective-permute-start.14 = (bf16[4,2,128,128]{3,2,1,0:T(8,128)(2,1)S(1)}, bf16[4,2,128,128]{3,2,1,0:T(8,128)(2,1)S(1)}, u32[]{:S(2)}, u32[]{:S(2)}) collective-permute-start(bf16[4,2,128,128]{3,2,1,0:T(8,128)(2,1)S(1)} %pad_maximum_fusion.5.refs_4_), channel_id=1, source_target_pairs={{0,4},{1,5},{2,6},{3,7},{4,0},{5,1},{6,2},{7,3},{8,12},{9,13},{10,... | collective-permute-start | bytes 786440 | tf_op jit(solution)/shard_map/ppermute | solution.py:169
  39.6 1.0 broadcast_select_fusion.1.refs_7_
  40.6 2.8 %collective-permute-start.11 = (bf16[4,2,128,128]{3,2,1,0:T(8,128)(2,1)S(1)}, bf16[4,2,128,128]{3,2,1,0:T(8,128)(2,1)S(1)}, u32[]{:S(2)}, u32[]{:S(2)}) collective-permute-start(bf16[4,2,128,128]{3,2,1,0:T(8,128)(2,1)S(1)} %pad_maximum_fusion.5.refs_4_), channel_id=1, source_target_pairs={{0,12},{1,13},{2,14},{3,15},{4,4},{5,5},{6,6},{7,7},{8,8},{9,9},{1... | collective-permute-start | bytes 786440 | tf_op jit(solution)/shard_map/ppermute | solution.py:169
  43.4 4.4 %collective-permute-start.17 = (bf16[4,2,128,128]{3,2,1,0:T(8,128)(2,1)S(1)}, bf16[4,2,128,128]{3,2,1,0:T(8,128)(2,1)S(1)}, u32[]{:S(2)}, u32[]{:S(2)}) collective-permute-start(bf16[4,2,128,128]{3,2,1,0:T(8,128)(2,1)S(1)} %pad_maximum_fusion.5.refs_4_), channel_id=1, source_target_pairs={{0,8},{1,9},{2,10},{3,11},{4,12},{5,13},{6,14},{7,15},{8,0},{9,1},... | collective-permute-start | bytes 786440 | tf_op jit(solution)/shard_map/ppermute | solution.py:169
  48.0 10.7 %shard_map.84 = (bf16[2,128,512]{2,1,0:T(8,128)(2,1)S(1)}, bf16[2,128,512]{2,1,0:T(8,128)(2,1)S(1)}, bf16[2,128,512]{2,1,0:T(8,128)(2,1)S(1)}, bf16[2,128,512]{2...) custom-call(s32[4]{0:T(128)S(1)} %and_select_fusion.start_ref, ...), custom_call_target="tpu_custom_call" | custom-call | flops 13421772800 | bytes 8388608 | tf_op jit(solution)/shard_map/pallas_call | solution.py:142
  59.8 1.4 %collective-permute-start.15 = (bf16[2,128,512]{2,1,0:T(8,128)(2,1)S(1)}, bf16[2,128,512]{2,1,0:T(8,128)(2,1)S(1)}, u32[]{:S(2)}, u32[]{:S(2)}) collective-permute-start(bf16[2,128,512]{2,1,0:T(8,128)(2,1)S(1)} %get-tuple-element.58), channel_id=1, source_target_pairs={{0,2},{1,3},{2,0},{3,1},{4,6},{5,7},{6,4},{7,5},{8,10},{9,11},{10,... | collective-permute-start | bytes 786440 | tf_op jit(solution)/shard_map/ppermute | solution.py:169
  61.2 2.5 %collective-permute-done.17.refs_6_ = bf16[4,2,128,128]{3,2,1,0:T(8,128)(2,1)S(1)} collective-permute-done((bf16[4,2,128,128]{3,2,1,0:T(8,128)(2,1)S(1)}, bf16[4,2,128,128]{3,2,1,0:T(8,128)(2,1)S(1)}, u32[]{:S(2)}, u32[]{:S(2)}) %collective-permute-start.17) | collective-permute-done | bytes 262176 | tf_op jit(solution)/shard_map/ppermute | solution.py:169
  63.7 1.1 collective-permute-start.12
  64.8 4.4 %collective-permute-done.18 = bf16[4,2,128,128]{3,2,1,0:T(8,128)(2,1)S(1)} collective-permute-done((bf16[4,2,128,128]{3,2,1,0:T(8,128)(2,1)S(1)}, bf16[4,2,128,128]{3,2,1,0:T(8,128)(2,1)S(1)}, u32[]{:S(2)}, u32[]{:S(2)}) %collective-permute-start.18) | collective-permute-done | bytes 262176 | tf_op jit(solution)/shard_map/ppermute | solution.py:169
  69.5 10.3 %shard_map.85 = (bf16[2,128,512]{2,1,0:T(8,128)(2,1)S(1)}, bf16[2,128,512]{2,1,0:T(8,128)(2,1)S(1)}, bf16[2,128,512]{2,1,0:T(8,128)(2,1)S(1)}, bf16[2,128,512]{2...) custom-call(s32[4]{0:T(128)S(1)} %and_select_fusion.start_ref, ...), custom_call_target="tpu_custom_call" | custom-call | flops 13421772800 | bytes 8388608 | tf_op jit(solution)/shard_map/pallas_call | solution.py:142
  80.0 4.1 %collective-permute-done.19 = bf16[4,2,128,128]{3,2,1,0:T(8,128)(2,1)S(1)} collective-permute-done((bf16[4,2,128,128]{3,2,1,0:T(8,128)(2,1)S(1)}, bf16[4,2,128,128]{3,2,1,0:T(8,128)(2,1)S(1)}, u32[]{:S(2)}, u32[]{:S(2)}) %collective-permute-start.19) | collective-permute-done | bytes 262176 | tf_op jit(solution)/shard_map/ppermute | solution.py:169
  84.8 1.3 %collective-permute-start.21 = (bf16[2,128,512]{2,1,0:T(8,128)(2,1)S(1)}, bf16[2,128,512]{2,1,0:T(8,128)(2,1)S(1)}, u32[]{:S(2)}, u32[]{:S(2)}) collective-permute-start(bf16[2,128,512]{2,1,0:T(8,128)(2,1)S(1)} %get-tuple-element.79), channel_id=1, source_target_pairs={{0,2},{1,3},{2,0},{3,1},{4,6},{5,7},{6,4},{7,5},{8,10},{9,11},{10,... | collective-permute-start | bytes 786440 | tf_op jit(solution)/shard_map/ppermute | solution.py:169
  86.4 5.0 %collective-permute-done.27 = bf16[4,2,128,128]{3,2,1,0:T(8,128)(2,1)S(1)} collective-permute-done((bf16[4,2,128,128]{3,2,1,0:T(8,128)(2,1)S(1)}, bf16[4,2,128,128]{3,2,1,0:T(8,128)(2,1)S(1)}, u32[]{:S(2)}, u32[]{:S(2)}) %collective-permute-start.27) | collective-permute-done | bytes 262176 | tf_op jit(solution)/shard_map/ppermute | solution.py:169
  91.5 1.3 %collective-permute-start.29 = (bf16[4,2,128,128]{3,2,1,0:T(8,128)(2,1)S(1)}, bf16[4,2,128,128]{3,2,1,0:T(8,128)(2,1)S(1)}, u32[]{:S(2)}, u32[]{:S(2)}) collective-permute-start(bf16[4,2,128,128]{3,2,1,0:T(8,128)(2,1)S(1)} %add_convert_fusion.1), channel_id=1, source_target_pairs={{0,8},{1,9},{2,10},{3,11},{4,12},{5,13},{6,14},{7,15},{8,0},{9,1},... | collective-permute-start | bytes 786440 | tf_op jit(solution)/shard_map/ppermute | solution.py:169
  92.7 1.7 %collective-permute-start.28 = (bf16[4,2,128,128]{3,2,1,0:T(8,128)(2,1)S(1)}, bf16[4,2,128,128]{3,2,1,0:T(8,128)(2,1)S(1)}, u32[]{:S(2)}, u32[]{:S(2)}) collective-permute-start(bf16[4,2,128,128]{3,2,1,0:T(8,128)(2,1)S(1)} %get-tuple-element.87), channel_id=1, source_target_pairs={{0,4},{1,5},{2,6},{3,7},{4,0},{5,1},{6,2},{7,3},{8,12},{9,13},{10,... | collective-permute-start | bytes 786440 | tf_op jit(solution)/shard_map/ppermute | solution.py:169
  94.7 1.2 %collective-permute-done.24 = bf16[2,128,128]{2,1,0:T(8,128)(2,1)S(1)} collective-permute-done((bf16[2,128,128]{2,1,0:T(8,128)(2,1)S(1)}, bf16[2,128,128]{2,1,0:T(8,128)(2,1)S(1)}, u32[]{:S(2)}, u32[]{:S(2)}) %collective-permute-start.24) | collective-permute-done | bytes 65568 | tf_op jit(solution)/shard_map/ppermute | solution.py:169
  95.9 1.6 %collective-permute-start.25 = (bf16[2,128,128]{2,1,0:T(8,128)(2,1)S(1)}, bf16[2,128,128]{2,1,0:T(8,128)(2,1)S(1)}, u32[]{:S(2)}, u32[]{:S(2)}) collective-permute-start(bf16[2,128,128]{2,1,0:T(8,128)(2,1)S(1)} %get-tuple-element.102), channel_id=1, source_target_pairs={{0,2},{1,3},{2,0},{3,1},{4,6},{5,7},{6,4},{7,5},{8,10},{9,11},{10,... | collective-permute-start | bytes 196616 | tf_op jit(solution)/shard_map/ppermute | solution.py:169
  97.5 2.7 %collective-permute-done.25 = bf16[2,128,128]{2,1,0:T(8,128)(2,1)S(1)} collective-permute-done((bf16[2,128,128]{2,1,0:T(8,128)(2,1)S(1)}, bf16[2,128,128]{2,1,0:T(8,128)(2,1)S(1)}, u32[]{:S(2)}, u32[]{:S(2)}) %collective-permute-start.25) | collective-permute-done | bytes 65568 | tf_op jit(solution)/shard_map/ppermute | solution.py:169
  100.6 3.8 %collective-permute-done.26 = bf16[2,128,128]{2,1,0:T(8,128)(2,1)S(1)} collective-permute-done((bf16[2,128,128]{2,1,0:T(8,128)(2,1)S(1)}, bf16[2,128,128]{2,1,0:T(8,128)(2,1)S(1)}, u32[]{:S(2)}, u32[]{:S(2)}) %collective-permute-start.26) | collective-permute-done | bytes 65568 | tf_op jit(solution)/shard_map/ppermute | solution.py:169
  104.7 1.0 collective-permute-done.29
  106.0 1.4 %collective-permute-start.32 = (bf16[2,128,128]{2,1,0:T(8,128)(2,1)S(1)}, bf16[2,128,128]{2,1,0:T(8,128)(2,1)S(1)}, u32[]{:S(2)}, u32[]{:S(2)}) collective-permute-start(bf16[2,128,128]{2,1,0:T(8,128)(2,1)S(1)} %get-tuple-element.99), channel_id=1, source_target_pairs={{0,2},{1,3},{2,0},{3,1},{4,6},{5,7},{6,4},{7,5},{8,10},{9,11},{10,... | collective-permute-start | bytes 196616 | tf_op jit(solution)/shard_map/ppermute | solution.py:169
  108.0 2.6 %collective-permute-done.32 = bf16[2,128,128]{2,1,0:T(8,128)(2,1)S(1)} collective-permute-done((bf16[2,128,128]{2,1,0:T(8,128)(2,1)S(1)}, bf16[2,128,128]{2,1,0:T(8,128)(2,1)S(1)}, u32[]{:S(2)}, u32[]{:S(2)}) %collective-permute-start.32) | collective-permute-done | bytes 65568 | tf_op jit(solution)/shard_map/ppermute | solution.py:169
  110.7 1.0 collective-permute-done.33
  (133 shorter events, 15.3 us)
Async XLA Ops:
  3.4 8.5 %collective-permute-start.4 = (bf16[2,2,128,128]{3,2,1,0:T(8,128)(2,1)}, bf16[2,2,128,128]{3,2,1,0:T(8,128)(2,1)S(1)}, u32[]{:S(2)}, u32[]{:S(2)}) collective-permute-start(bf16[2,2,128,128]{3,2,1,0:T(8,128)(2,1)} %pad_maximum_fusion.7), channel_id=1, source_target_pairs={{0,2},{1,3},{2,0},{3,1},{4,6},{5,7},{6,4},{7,5},{8,10},{9,11},{10,... | collective-permute-start | bytes 393224 | tf_op jit(solution)/shard_map/ppermute | solution.py:169
  7.0 5.8 %collective-permute-start.5 = (bf16[2,2,128,128]{3,2,1,0:T(8,128)(2,1)}, bf16[2,2,128,128]{3,2,1,0:T(8,128)(2,1)S(1)}, u32[]{:S(2)}, u32[]{:S(2)}) collective-permute-start(bf16[2,2,128,128]{3,2,1,0:T(8,128)(2,1)} %pad_maximum_fusion.8), channel_id=1, source_target_pairs={{0,3},{1,2},{2,1},{3,0},{4,7},{5,6},{6,5},{7,4},{8,11},{9,10},{10,... | collective-permute-start | bytes 393224 | tf_op jit(solution)/shard_map/ppermute | solution.py:169
  7.0 2.3 %collective-permute-start = (bf16[2,2,128,128]{3,2,1,0:T(8,128)(2,1)S(1)}, bf16[2,2,128,128]{3,2,1,0:T(8,128)(2,1)S(1)}, u32[]{:S(2)}, u32[]{:S(2)}) collective-permute-start(bf16[2,2,128,128]{3,2,1,0:T(8,128)(2,1)S(1)} %pad_maximum_fusion.6), channel_id=1, source_target_pairs={{0,1},{1,0},{2,3},{3,2},{4,5},{5,4},{6,7},{7,6},{8,9},{9,8},{10,11... | collective-permute-start | bytes 393224 | tf_op jit(solution)/shard_map/ppermute | solution.py:169
  10.1 19.3 %collective-permute-start.1 = (bf16[2,128,1024]{2,1,0:T(8,128)(2,1)S(1)}, bf16[2,128,1024]{2,1,0:T(8,128)(2,1)S(1)}, u32[]{:S(2)}, u32[]{:S(2)}) collective-permute-start(bf16[2,128,1024]{2,1,0:T(8,128)(2,1)S(1)} %pad_maximum_fusion.2), channel_id=1, source_target_pairs={{0,3},{1,2},{2,1},{3,0},{4,7},{5,6},{6,5},{7,4},{8,11},{9,10},{10,... | collective-permute-start | bytes 1572872 | tf_op jit(solution)/shard_map/ppermute | solution.py:169
  13.5 15.8 %collective-permute-start.7 = (bf16[4,2,128,128]{3,2,1,0:T(8,128)(2,1)S(1)}, bf16[4,2,128,128]{3,2,1,0:T(8,128)(2,1)S(1)}, u32[]{:S(2)}, u32[]{:S(2)}) collective-permute-start(bf16[4,2,128,128]{3,2,1,0:T(8,128)(2,1)S(1)} %pad_maximum_fusion.4.refs_4_), channel_id=1, source_target_pairs={{0,8},{1,9},{2,10},{3,11},{4,12},{5,13},{6,14},{7,15},{8,0},{9,1},... | collective-permute-start | bytes 786440 | tf_op jit(solution)/shard_map/ppermute | solution.py:169
  16.6 14.5 %collective-permute-start.6 = (bf16[4,2,128,128]{3,2,1,0:T(8,128)(2,1)S(1)}, bf16[4,2,128,128]{3,2,1,0:T(8,128)(2,1)S(1)}, u32[]{:S(2)}, u32[]{:S(2)}) collective-permute-start(bf16[4,2,128,128]{3,2,1,0:T(8,128)(2,1)S(1)} %pad_maximum_fusion.4.refs_4_), channel_id=1, source_target_pairs={{0,4},{1,5},{2,6},{3,7},{4,0},{5,1},{6,2},{7,3},{8,12},{9,13},{10,... | collective-permute-start | bytes 786440 | tf_op jit(solution)/shard_map/ppermute | solution.py:169
  18.2 12.8 %collective-permute-start.8 = (bf16[4,2,128,128]{3,2,1,0:T(8,128)(2,1)S(1)}, bf16[4,2,128,128]{3,2,1,0:T(8,128)(2,1)}, u32[]{:S(2)}, u32[]{:S(2)}) collective-permute-start(bf16[4,2,128,128]{3,2,1,0:T(8,128)(2,1)S(1)} %pad_maximum_fusion.4.refs_4_), channel_id=1, source_target_pairs={{0,0},{1,1},{2,2},{3,3},{4,8},{5,9},{6,10},{7,11},{8,4},{9,5},{10,... | collective-permute-start | bytes 786440 | tf_op jit(solution)/shard_map/ppermute | solution.py:169
  20.4 15.3 %collective-permute-start.3 = (bf16[2,128,1024]{2,1,0:T(8,128)(2,1)}, bf16[2,128,1024]{2,1,0:T(8,128)(2,1)S(1)}, u32[]{:S(2)}, u32[]{:S(2)}) collective-permute-start(bf16[2,128,1024]{2,1,0:T(8,128)(2,1)} %pad_maximum_fusion.3), channel_id=1, source_target_pairs={{0,2},{1,3},{2,0},{3,1},{4,6},{5,7},{6,4},{7,5},{8,10},{9,11},{10,... | collective-permute-start | bytes 1572872 | tf_op jit(solution)/shard_map/ppermute | solution.py:169
  29.3 10.3 %collective-permute-start.9 = (bf16[4,2,128,128]{3,2,1,0:T(8,128)(2,1)S(1)}, bf16[4,2,128,128]{3,2,1,0:T(8,128)(2,1)}, u32[]{:S(2)}, u32[]{:S(2)}) collective-permute-start(bf16[4,2,128,128]{3,2,1,0:T(8,128)(2,1)S(1)} %collective-permute-done.7.refs_6_), channel_id=1, source_target_pairs={{0,4},{1,5},{2,6},{3,7},{4,0},{5,1},{6,2},{7,3},{8,12},{9,13},{10,... | collective-permute-start | bytes 786440 | tf_op jit(solution)/shard_map/ppermute | solution.py:169
  29.4 18.4 %collective-permute-start.2 = (bf16[2,128,1024]{2,1,0:T(8,128)(2,1)S(1)}, bf16[2,128,1024]{2,1,0:T(8,128)(2,1)S(1)}, u32[]{:S(2)}, u32[]{:S(2)}) collective-permute-start(bf16[2,128,1024]{2,1,0:T(8,128)(2,1)S(1)} %pad_maximum_fusion.1), channel_id=1, source_target_pairs={{0,1},{1,0},{2,3},{3,2},{4,5},{5,4},{6,7},{7,6},{8,9},{9,8},{10,11... | collective-permute-start | bytes 1572872 | tf_op jit(solution)/shard_map/ppermute | solution.py:169
  31.0 9.5 %collective-permute-start.10 = (bf16[4,2,128,128]{3,2,1,0:T(8,128)(2,1)S(1)}, bf16[4,2,128,128]{3,2,1,0:T(8,128)(2,1)S(1)}, u32[]{:S(2)}, u32[]{:S(2)}) collective-permute-start(bf16[4,2,128,128]{3,2,1,0:T(8,128)(2,1)S(1)} %pad_maximum_fusion.5.refs_4_), channel_id=1, source_target_pairs={{0,0},{1,1},{2,2},{3,3},{4,8},{5,9},{6,10},{7,11},{8,4},{9,5},{10,... | collective-permute-start | bytes 786440 | tf_op jit(solution)/shard_map/ppermute | solution.py:169
  35.7 23.8 %collective-permute-start.14 = (bf16[4,2,128,128]{3,2,1,0:T(8,128)(2,1)S(1)}, bf16[4,2,128,128]{3,2,1,0:T(8,128)(2,1)S(1)}, u32[]{:S(2)}, u32[]{:S(2)}) collective-permute-start(bf16[4,2,128,128]{3,2,1,0:T(8,128)(2,1)S(1)} %pad_maximum_fusion.5.refs_4_), channel_id=1, source_target_pairs={{0,4},{1,5},{2,6},{3,7},{4,0},{5,1},{6,2},{7,3},{8,12},{9,13},{10,... | collective-permute-start | bytes 786440 | tf_op jit(solution)/shard_map/ppermute | solution.py:169
  40.6 19.3 %collective-permute-start.11 = (bf16[4,2,128,128]{3,2,1,0:T(8,128)(2,1)S(1)}, bf16[4,2,128,128]{3,2,1,0:T(8,128)(2,1)S(1)}, u32[]{:S(2)}, u32[]{:S(2)}) collective-permute-start(bf16[4,2,128,128]{3,2,1,0:T(8,128)(2,1)S(1)} %pad_maximum_fusion.5.refs_4_), channel_id=1, source_target_pairs={{0,12},{1,13},{2,14},{3,15},{4,4},{5,5},{6,6},{7,7},{8,8},{9,9},{1... | collective-permute-start | bytes 786440 | tf_op jit(solution)/shard_map/ppermute | solution.py:169
  43.4 20.3 %collective-permute-start.17 = (bf16[4,2,128,128]{3,2,1,0:T(8,128)(2,1)S(1)}, bf16[4,2,128,128]{3,2,1,0:T(8,128)(2,1)S(1)}, u32[]{:S(2)}, u32[]{:S(2)}) collective-permute-start(bf16[4,2,128,128]{3,2,1,0:T(8,128)(2,1)S(1)} %pad_maximum_fusion.5.refs_4_), channel_id=1, source_target_pairs={{0,8},{1,9},{2,10},{3,11},{4,12},{5,13},{6,14},{7,15},{8,0},{9,1},... | collective-permute-start | bytes 786440 | tf_op jit(solution)/shard_map/ppermute | solution.py:169
  58.7 10.6 %collective-permute-start.18 = (bf16[4,2,128,128]{3,2,1,0:T(8,128)(2,1)S(1)}, bf16[4,2,128,128]{3,2,1,0:T(8,128)(2,1)S(1)}, u32[]{:S(2)}, u32[]{:S(2)}) collective-permute-start(bf16[4,2,128,128]{3,2,1,0:T(8,128)(2,1)S(1)} %get-tuple-element.63), channel_id=1, source_target_pairs={{0,4},{1,5},{2,6},{3,7},{4,0},{5,1},{6,2},{7,3},{8,12},{9,13},{10,... | collective-permute-start | bytes 786440 | tf_op jit(solution)/shard_map/ppermute | solution.py:169
  58.8 21.2 %collective-permute-start.20 = (bf16[4,2,128,128]{3,2,1,0:T(8,128)(2,1)S(1)}, bf16[4,2,128,128]{3,2,1,0:T(8,128)(2,1)S(1)}, u32[]{:S(2)}, u32[]{:S(2)}) collective-permute-start(bf16[4,2,128,128]{3,2,1,0:T(8,128)(2,1)S(1)} %get-tuple-element.63), channel_id=1, source_target_pairs={{0,0},{1,1},{2,2},{3,3},{4,8},{5,9},{6,10},{7,11},{8,4},{9,5},{10,... | collective-permute-start | bytes 786440 | tf_op jit(solution)/shard_map/ppermute | solution.py:169
  59.5 20.5 %collective-permute-start.16 = (bf16[2,128,512]{2,1,0:T(8,128)(2,1)S(1)}, bf16[2,128,512]{2,1,0:T(8,128)(2,1)S(1)}, u32[]{:S(2)}, u32[]{:S(2)}) collective-permute-start(bf16[2,128,512]{2,1,0:T(8,128)(2,1)S(1)} %get-tuple-element.60), channel_id=1, source_target_pairs={{0,3},{1,2},{2,1},{3,0},{4,7},{5,6},{6,5},{7,4},{8,11},{9,10},{10,... | collective-permute-start | bytes 786440 | tf_op jit(solution)/shard_map/ppermute | solution.py:169
  59.8 20.1 %collective-permute-start.15 = (bf16[2,128,512]{2,1,0:T(8,128)(2,1)S(1)}, bf16[2,128,512]{2,1,0:T(8,128)(2,1)S(1)}, u32[]{:S(2)}, u32[]{:S(2)}) collective-permute-start(bf16[2,128,512]{2,1,0:T(8,128)(2,1)S(1)} %get-tuple-element.58), channel_id=1, source_target_pairs={{0,2},{1,3},{2,0},{3,1},{4,6},{5,7},{6,4},{7,5},{8,10},{9,11},{10,... | collective-permute-start | bytes 786440 | tf_op jit(solution)/shard_map/ppermute | solution.py:169
  63.7 16.2 %collective-permute-start.12 = (bf16[4,2,128,128]{3,2,1,0:T(8,128)(2,1)S(1)}, bf16[4,2,128,128]{3,2,1,0:T(8,128)(2,1)S(1)}, u32[]{:S(2)}, u32[]{:S(2)}) collective-permute-start(bf16[4,2,128,128]{3,2,1,0:T(8,128)(2,1)S(1)} %get-tuple-element.54), channel_id=1, source_target_pairs={{0,4},{1,5},{2,6},{3,7},{4,0},{5,1},{6,2},{7,3},{8,12},{9,13},{10,... | collective-permute-start | bytes 786440 | tf_op jit(solution)/shard_map/ppermute | solution.py:169
  69.3 14.8 %collective-permute-start.19 = (bf16[4,2,128,128]{3,2,1,0:T(8,128)(2,1)S(1)}, bf16[4,2,128,128]{3,2,1,0:T(8,128)(2,1)S(1)}, u32[]{:S(2)}, u32[]{:S(2)}) collective-permute-start(bf16[4,2,128,128]{3,2,1,0:T(8,128)(2,1)S(1)} %add_convert_fusion.3), channel_id=1, source_target_pairs={{0,8},{1,9},{2,10},{3,11},{4,12},{5,13},{6,14},{7,15},{8,0},{9,1},... | collective-permute-start | bytes 786440 | tf_op jit(solution)/shard_map/ppermute | solution.py:169
  79.9 6.4 %collective-permute-start.13 = (bf16[2,128,512]{2,1,0:T(8,128)(2,1)S(1)}, bf16[2,128,512]{2,1,0:T(8,128)(2,1)S(1)}, u32[]{:S(2)}, u32[]{:S(2)}) collective-permute-start(bf16[2,128,512]{2,1,0:T(8,128)(2,1)S(1)} %get-tuple-element.55), channel_id=1, source_target_pairs={{0,1},{1,0},{2,3},{3,2},{4,5},{5,4},{6,7},{7,6},{8,9},{9,8},{10,11... | collective-permute-start | bytes 786440 | tf_op jit(solution)/shard_map/ppermute | solution.py:169
  84.1 7.3 %collective-permute-start.27 = (bf16[4,2,128,128]{3,2,1,0:T(8,128)(2,1)S(1)}, bf16[4,2,128,128]{3,2,1,0:T(8,128)(2,1)S(1)}, u32[]{:S(2)}, u32[]{:S(2)}) collective-permute-start(bf16[4,2,128,128]{3,2,1,0:T(8,128)(2,1)S(1)} %get-tuple-element.86), channel_id=1, source_target_pairs={{0,4},{1,5},{2,6},{3,7},{4,0},{5,1},{6,2},{7,3},{8,12},{9,13},{10,... | collective-permute-start | bytes 786440 | tf_op jit(solution)/shard_map/ppermute | solution.py:169
  84.1 20.6 %collective-permute-start.30 = (bf16[4,2,128,128]{3,2,1,0:T(8,128)(2,1)S(1)}, bf16[4,2,128,128]{3,2,1,0:T(8,128)(2,1)S(1)}, u32[]{:S(2)}, u32[]{:S(2)}) collective-permute-start(bf16[4,2,128,128]{3,2,1,0:T(8,128)(2,1)S(1)} %get-tuple-element.86), channel_id=1, source_target_pairs={{0,0},{1,1},{2,2},{3,3},{4,8},{5,9},{6,10},{7,11},{8,4},{9,5},{10,... | collective-permute-start | bytes 786440 | tf_op jit(solution)/shard_map/ppermute | solution.py:169
  84.8 9.7 %collective-permute-start.21 = (bf16[2,128,512]{2,1,0:T(8,128)(2,1)S(1)}, bf16[2,128,512]{2,1,0:T(8,128)(2,1)S(1)}, u32[]{:S(2)}, u32[]{:S(2)}) collective-permute-start(bf16[2,128,512]{2,1,0:T(8,128)(2,1)S(1)} %get-tuple-element.79), channel_id=1, source_target_pairs={{0,2},{1,3},{2,0},{3,1},{4,6},{5,7},{6,4},{7,5},{8,10},{9,11},{10,... | collective-permute-start | bytes 786440 | tf_op jit(solution)/shard_map/ppermute | solution.py:169
  86.1 21.8 %collective-permute-start.23 = (bf16[2,128,512]{2,1,0:T(8,128)(2,1)S(1)}, bf16[2,128,512]{2,1,0:T(8,128)(2,1)S(1)}, u32[]{:S(2)}, u32[]{:S(2)}) collective-permute-start(bf16[2,128,512]{2,1,0:T(8,128)(2,1)S(1)} %get-tuple-element.81), channel_id=1, source_target_pairs={{0,3},{1,2},{2,1},{3,0},{4,7},{5,6},{6,5},{7,4},{8,11},{9,10},{10,... | collective-permute-start | bytes 786440 | tf_op jit(solution)/shard_map/ppermute | solution.py:169
  91.5 14.2 %collective-permute-start.29 = (bf16[4,2,128,128]{3,2,1,0:T(8,128)(2,1)S(1)}, bf16[4,2,128,128]{3,2,1,0:T(8,128)(2,1)S(1)}, u32[]{:S(2)}, u32[]{:S(2)}) collective-permute-start(bf16[4,2,128,128]{3,2,1,0:T(8,128)(2,1)S(1)} %add_convert_fusion.1), channel_id=1, source_target_pairs={{0,8},{1,9},{2,10},{3,11},{4,12},{5,13},{6,14},{7,15},{8,0},{9,1},... | collective-permute-start | bytes 786440 | tf_op jit(solution)/shard_map/ppermute | solution.py:169
  92.7 11.9 %collective-permute-start.28 = (bf16[4,2,128,128]{3,2,1,0:T(8,128)(2,1)S(1)}, bf16[4,2,128,128]{3,2,1,0:T(8,128)(2,1)S(1)}, u32[]{:S(2)}, u32[]{:S(2)}) collective-permute-start(bf16[4,2,128,128]{3,2,1,0:T(8,128)(2,1)S(1)} %get-tuple-element.87), channel_id=1, source_target_pairs={{0,4},{1,5},{2,6},{3,7},{4,0},{5,1},{6,2},{7,3},{8,12},{9,13},{10,... | collective-permute-start | bytes 786440 | tf_op jit(solution)/shard_map/ppermute | solution.py:169
  95.9 4.3 %collective-permute-start.25 = (bf16[2,128,128]{2,1,0:T(8,128)(2,1)S(1)}, bf16[2,128,128]{2,1,0:T(8,128)(2,1)S(1)}, u32[]{:S(2)}, u32[]{:S(2)}) collective-permute-start(bf16[2,128,128]{2,1,0:T(8,128)(2,1)S(1)} %get-tuple-element.102), channel_id=1, source_target_pairs={{0,2},{1,3},{2,0},{3,1},{4,6},{5,7},{6,4},{7,5},{8,10},{9,11},{10,... | collective-permute-start | bytes 196616 | tf_op jit(solution)/shard_map/ppermute | solution.py:169
  100.1 4.3 %collective-permute-start.26 = (bf16[2,128,128]{2,1,0:T(8,128)(2,1)S(1)}, bf16[2,128,128]{2,1,0:T(8,128)(2,1)S(1)}, u32[]{:S(2)}, u32[]{:S(2)}) collective-permute-start(bf16[2,128,128]{2,1,0:T(8,128)(2,1)S(1)} %get-tuple-element.101), channel_id=1, source_target_pairs={{0,3},{1,2},{2,1},{3,0},{4,7},{5,6},{6,5},{7,4},{8,11},{9,10},{10,... | collective-permute-start | bytes 196616 | tf_op jit(solution)/shard_map/ppermute | solution.py:169
  104.4 3.4 %collective-permute-start.22 = (bf16[2,128,512]{2,1,0:T(8,128)(2,1)S(1)}, bf16[2,128,512]{2,1,0:T(8,128)(2,1)S(1)}, u32[]{:S(2)}, u32[]{:S(2)}) collective-permute-start(bf16[2,128,512]{2,1,0:T(8,128)(2,1)S(1)} %get-tuple-element.80), channel_id=1, source_target_pairs={{0,1},{1,0},{2,3},{3,2},{4,5},{5,4},{6,7},{7,6},{8,9},{9,8},{10,11... | collective-permute-start | bytes 786440 | tf_op jit(solution)/shard_map/ppermute | solution.py:169
  106.0 4.7 %collective-permute-start.32 = (bf16[2,128,128]{2,1,0:T(8,128)(2,1)S(1)}, bf16[2,128,128]{2,1,0:T(8,128)(2,1)S(1)}, u32[]{:S(2)}, u32[]{:S(2)}) collective-permute-start(bf16[2,128,128]{2,1,0:T(8,128)(2,1)S(1)} %get-tuple-element.99), channel_id=1, source_target_pairs={{0,2},{1,3},{2,0},{3,1},{4,6},{5,7},{6,4},{7,5},{8,10},{9,11},{10,... | collective-permute-start | bytes 196616 | tf_op jit(solution)/shard_map/ppermute | solution.py:169
  107.3 4.3 %collective-permute-start.33 = (bf16[2,128,128]{2,1,0:T(8,128)(2,1)S(1)}, bf16[2,128,128]{2,1,0:T(8,128)(2,1)S(1)}, u32[]{:S(2)}, u32[]{:S(2)}) collective-permute-start(bf16[2,128,128]{2,1,0:T(8,128)(2,1)S(1)} %get-tuple-element.98), channel_id=1, source_target_pairs={{0,3},{1,2},{2,1},{3,0},{4,7},{5,6},{6,5},{7,4},{8,11},{9,10},{10,... | collective-permute-start | bytes 196616 | tf_op jit(solution)/shard_map/ppermute | solution.py:169
  (13 other events, 67.8 us)

commit v10 on v9

--- a/solution.py
+++ b/solution.py
@@ -210,8 +210,8 @@
     a_three = middle_swapped(kv_owns[0], lanes)
     a_passed = swapped(a_two, one)
     b_three = middle_swapped(after(kv_owns[1], a_three, a_one, query_d), lanes)
-    b_two = swapped(after(kv_owns[1], a_passed, b_three), two)
-    b_far = outer_swapped(after(kv_owns[1], a_passed, b_three), lanes)
+    b_two = swapped(after(kv_owns[1], a_passed), two)
+    b_far = outer_swapped(after(kv_owns[1], a_passed), lanes)
     b_one = swapped(after(kv_owns[1], query_x), one)
     query_c = swapped(after(query_cuts[1], query_d), 1)
     query_parts = [query_cuts[0], query_c, query_x, query_d]

time: 113 us -> 117 us (1.035)
  starting transfers between devices: 36.1 us -> 40 us
  other arithmetic: 6.52 us -> 5.22 us
    ppermute x34, starting transfers between devices: 36.1 us -> 40 us  [moved(): return lax.ppermute(tensor, 'seq', [(i, target(i)) for i in range(devices)])]
    another operation x6, other arithmetic: 1.45 us -> 0.14 us  [kv_cut(): return jnp.stack([both[:, :, h * HD:(h + 1) * HD] for h in range(heads)])]
  transfers between devices with their start and end apart: 34 -> 34, of which waited for: 13 -> 11; matrix products, arithmetic and copies ran while one was open for 8% -> 7% of each run, Pallas kernels for 19% -> 19%
where the time goes in v10:
time: 117 us
  waiting for transfers between devices  41.8 us (36%)
  starting transfers between devices  40 us (34%)
  Pallas kernels  22 us (19%)
  local copies, waits for them, and re-layouts  6.18 us (5%)
  other arithmetic  5.22 us (4%)
  between operations  1.39 us (1%)
    ppermute x34, waiting for transfers between devices, moved(): return lax.ppermute(tensor, 'seq', [(i, target(i)) for i in range(devices)])  41.8 us
    ppermute x34, starting transfers between devices, moved(): return lax.ppermute(tensor, 'seq', [(i, target(i)) for i in range(devices)])  40 us
    pallas_call x2, Pallas kernels, attend(): pl.pallas_call(functools.partial(attend_kernel, head, lanes, depth), out_...  22 us
  transfers between devices with their start and end apart: 34, of which 11 were waited for; matrix products, arithmetic and copies ran while one was open for 7% of the time, Pallas kernels for 19%

profile of v10, /device:TPU:0, one launch (start us, length us, event | category | flops | bytes accessed | tf_op | source)
XLA Modules:
  0.0 116.5 jit_solution(11410742359992248990)
XLA Ops:
  0.7 1.0 dynamic-slice_bitcast_fusion.12
  1.7 1.0 dynamic-slice_bitcast_fusion.13
  2.7 3.0 %collective-permute-start.4 = (bf16[2,2,128,128]{3,2,1,0:T(8,128)(2,1)S(1)}, bf16[2,2,128,128]{3,2,1,0:T(8,128)(2,1)S(1)}, u32[]{:S(2)}, u32[]{:S(2)}) collective-permute-start(bf16[2,2,128,128]{3,2,1,0:T(8,128)(2,1)S(1)} %pad_maximum_fusion.7), channel_id=1, source_target_pairs={{0,2},{1,3},{2,0},{3,1},{4,6},{5,7},{6,4},{7,5},{8,10},{9,11},{10,... | collective-permute-start | bytes 393224 | tf_op jit(solution)/shard_map/ppermute | solution.py:169
  8.5 1.7 %collective-permute-start.1 = (bf16[2,128,1024]{2,1,0:T(8,128)(2,1)S(1)}, bf16[2,128,1024]{2,1,0:T(8,128)(2,1)S(1)}, u32[]{:S(2)}, u32[]{:S(2)}) collective-permute-start(bf16[2,128,1024]{2,1,0:T(8,128)(2,1)S(1)} %pad_maximum_fusion.2), channel_id=1, source_target_pairs={{0,3},{1,2},{2,1},{3,0},{4,7},{5,6},{6,5},{7,4},{8,11},{9,10},{10,... | collective-permute-start | bytes 1572872 | tf_op jit(solution)/shard_map/ppermute | solution.py:169
  12.4 2.6 %collective-permute-start.7 = (bf16[4,2,128,128]{3,2,1,0:T(8,128)(2,1)S(1)}, bf16[4,2,128,128]{3,2,1,0:T(8,128)(2,1)S(1)}, u32[]{:S(2)}, u32[]{:S(2)}) collective-permute-start(bf16[4,2,128,128]{3,2,1,0:T(8,128)(2,1)S(1)} %pad_maximum_fusion.4.refs_4_), channel_id=1, source_target_pairs={{0,8},{1,9},{2,10},{3,11},{4,12},{5,13},{6,14},{7,15},{8,0},{9,1},... | collective-permute-start | bytes 786440 | tf_op jit(solution)/shard_map/ppermute | solution.py:169
  15.1 1.4 %collective-permute-start.8 = (bf16[4,2,128,128]{3,2,1,0:T(8,128)(2,1)S(1)}, bf16[4,2,128,128]{3,2,1,0:T(8,128)(2,1)}, u32[]{:S(2)}, u32[]{:S(2)}) collective-permute-start(bf16[4,2,128,128]{3,2,1,0:T(8,128)(2,1)S(1)} %pad_maximum_fusion.4.refs_4_), channel_id=1, source_target_pairs={{0,0},{1,1},{2,2},{3,3},{4,8},{5,9},{6,10},{7,11},{8,4},{9,5},{10,... | collective-permute-start | bytes 786440 | tf_op jit(solution)/shard_map/ppermute | solution.py:169
  16.5 2.2 %collective-permute-start.6 = (bf16[4,2,128,128]{3,2,1,0:T(8,128)(2,1)S(1)}, bf16[4,2,128,128]{3,2,1,0:T(8,128)(2,1)S(1)}, u32[]{:S(2)}, u32[]{:S(2)}) collective-permute-start(bf16[4,2,128,128]{3,2,1,0:T(8,128)(2,1)S(1)} %pad_maximum_fusion.4.refs_4_), channel_id=1, source_target_pairs={{0,4},{1,5},{2,6},{3,7},{4,0},{5,1},{6,2},{7,3},{8,12},{9,13},{10,... | collective-permute-start | bytes 786440 | tf_op jit(solution)/shard_map/ppermute | solution.py:169
  19.5 1.1 collective-permute-start.3
  20.7 7.4 %collective-permute-done.7.refs_6_ = bf16[4,2,128,128]{3,2,1,0:T(8,128)(2,1)S(1)} collective-permute-done((bf16[4,2,128,128]{3,2,1,0:T(8,128)(2,1)S(1)}, bf16[4,2,128,128]{3,2,1,0:T(8,128)(2,1)S(1)}, u32[]{:S(2)}, u32[]{:S(2)}) %collective-permute-start.7) | collective-permute-done | bytes 262176 | tf_op jit(solution)/shard_map/ppermute | solution.py:169
  29.4 0.9 pad_maximum_fusion.5.refs_4_
  30.4 5.9 %collective-permute-done.9 = bf16[4,2,128,128]{3,2,1,0:T(8,128)(2,1)} collective-permute-done((bf16[4,2,128,128]{3,2,1,0:T(8,128)(2,1)S(1)}, bf16[4,2,128,128]{3,2,1,0:T(8,128)(2,1)}, u32[]{:S(2)}, u32[]{:S(2)}) %collective-permute-start.9) | collective-permute-done | bytes 262176 | tf_op jit(solution)/shard_map/ppermute | solution.py:169
  36.3 5.6 %collective-permute-start.10 = (bf16[4,2,128,128]{3,2,1,0:T(8,128)(2,1)S(1)}, bf16[4,2,128,128]{3,2,1,0:T(8,128)(2,1)S(1)}, u32[]{:S(2)}, u32[]{:S(2)}) collective-permute-start(bf16[4,2,128,128]{3,2,1,0:T(8,128)(2,1)S(1)} %pad_maximum_fusion.5.refs_4_), channel_id=1, source_target_pairs={{0,12},{1,13},{2,14},{3,15},{4,4},{5,5},{6,6},{7,7},{8,8},{9,9},{1... | collective-permute-start | bytes 786440 | tf_op jit(solution)/shard_map/ppermute | solution.py:169
  42.7 4.8 %collective-permute-start.13 = (bf16[4,2,128,128]{3,2,1,0:T(8,128)(2,1)S(1)}, bf16[4,2,128,128]{3,2,1,0:T(8,128)(2,1)S(1)}, u32[]{:S(2)}, u32[]{:S(2)}) collective-permute-start(bf16[4,2,128,128]{3,2,1,0:T(8,128)(2,1)S(1)} %pad_maximum_fusion.5.refs_4_), channel_id=1, source_target_pairs={{0,4},{1,5},{2,6},{3,7},{4,0},{5,1},{6,2},{7,3},{8,12},{9,13},{10,... | collective-permute-start | bytes 786440 | tf_op jit(solution)/shard_map/ppermute | solution.py:169
  47.4 1.0 broadcast_select_fusion.1.refs_7_
  48.6 11.2 %shard_map.84 = (bf16[2,128,512]{2,1,0:T(8,128)(2,1)S(1)}, bf16[2,128,512]{2,1,0:T(8,128)(2,1)S(1)}, bf16[2,128,512]{2,1,0:T(8,128)(2,1)S(1)}, bf16[2,128,512]{2...) custom-call(s32[4]{0:T(128)S(1)} %and_select_fusion.start_ref, ...), custom_call_target="tpu_custom_call" | custom-call | flops 13421772800 | bytes 8388608 | tf_op jit(solution)/shard_map/pallas_call | solution.py:142
  60.7 4.6 %collective-permute-start.11 = (bf16[4,2,128,128]{3,2,1,0:T(8,128)(2,1)S(1)}, bf16[4,2,128,128]{3,2,1,0:T(8,128)(2,1)S(1)}, u32[]{:S(2)}, u32[]{:S(2)}) collective-permute-start(bf16[4,2,128,128]{3,2,1,0:T(8,128)(2,1)S(1)} %get-tuple-element.53), channel_id=1, source_target_pairs={{0,4},{1,5},{2,6},{3,7},{4,0},{5,1},{6,2},{7,3},{8,12},{9,13},{10,... | collective-permute-start | bytes 786440 | tf_op jit(solution)/shard_map/ppermute | solution.py:169
  65.6 1.5 %collective-permute-start.14 = (bf16[2,128,512]{2,1,0:T(8,128)(2,1)S(1)}, bf16[2,128,512]{2,1,0:T(8,128)(2,1)S(1)}, u32[]{:S(2)}, u32[]{:S(2)}) collective-permute-start(bf16[2,128,512]{2,1,0:T(8,128)(2,1)S(1)} %get-tuple-element.57), channel_id=1, source_target_pairs={{0,2},{1,3},{2,0},{3,1},{4,6},{5,7},{6,4},{7,5},{8,10},{9,11},{10,... | collective-permute-start | bytes 786440 | tf_op jit(solution)/shard_map/ppermute | solution.py:169
  67.2 1.5 %collective-permute-start.19 = (bf16[4,2,128,128]{3,2,1,0:T(8,128)(2,1)S(1)}, bf16[4,2,128,128]{3,2,1,0:T(8,128)(2,1)S(1)}, u32[]{:S(2)}, u32[]{:S(2)}) collective-permute-start(bf16[4,2,128,128]{3,2,1,0:T(8,128)(2,1)S(1)} %add_convert_fusion.3), channel_id=1, source_target_pairs={{0,8},{1,9},{2,10},{3,11},{4,12},{5,13},{6,14},{7,15},{8,0},{9,1},... | collective-permute-start | bytes 786440 | tf_op jit(solution)/shard_map/ppermute | solution.py:169
  68.7 7.2 %collective-permute-done.11 = bf16[4,2,128,128]{3,2,1,0:T(8,128)(2,1)S(1)} collective-permute-done((bf16[4,2,128,128]{3,2,1,0:T(8,128)(2,1)S(1)}, bf16[4,2,128,128]{3,2,1,0:T(8,128)(2,1)S(1)}, u32[]{:S(2)}, u32[]{:S(2)}) %collective-permute-start.11) | collective-permute-done | bytes 262176 | tf_op jit(solution)/shard_map/ppermute | solution.py:169
  75.9 10.8 %shard_map.85 = (bf16[2,128,512]{2,1,0:T(8,128)(2,1)S(1)}, bf16[2,128,512]{2,1,0:T(8,128)(2,1)S(1)}, bf16[2,128,512]{2,1,0:T(8,128)(2,1)S(1)}, bf16[2,128,512]{2...) custom-call(s32[4]{0:T(128)S(1)} %and_select_fusion.start_ref, ...), custom_call_target="tpu_custom_call" | custom-call | flops 13421772800 | bytes 8388608 | tf_op jit(solution)/shard_map/pallas_call | solution.py:142
  87.5 1.0 collective-permute-start.21
  88.4 1.0 collective-permute-start.23
  89.7 5.8 %collective-permute-done.27 = bf16[4,2,128,128]{3,2,1,0:T(8,128)(2,1)S(1)} collective-permute-done((bf16[4,2,128,128]{3,2,1,0:T(8,128)(2,1)S(1)}, bf16[4,2,128,128]{3,2,1,0:T(8,128)(2,1)S(1)}, u32[]{:S(2)}, u32[]{:S(2)}) %collective-permute-start.27) | collective-permute-done | bytes 262176 | tf_op jit(solution)/shard_map/ppermute | solution.py:169
  96.2 1.0 collective-permute-start.28
  97.5 1.2 %collective-permute-done.24 = bf16[2,128,128]{2,1,0:T(8,128)(2,1)S(1)} collective-permute-done((bf16[2,128,128]{2,1,0:T(8,128)(2,1)S(1)}, bf16[2,128,128]{2,1,0:T(8,128)(2,1)S(1)}, u32[]{:S(2)}, u32[]{:S(2)}) %collective-permute-start.24) | collective-permute-done | bytes 65568 | tf_op jit(solution)/shard_map/ppermute | solution.py:169
  98.7 1.1 collective-permute-start.25
  99.8 3.5 %collective-permute-done.25 = bf16[2,128,128]{2,1,0:T(8,128)(2,1)S(1)} collective-permute-done((bf16[2,128,128]{2,1,0:T(8,128)(2,1)S(1)}, bf16[2,128,128]{2,1,0:T(8,128)(2,1)S(1)}, u32[]{:S(2)}, u32[]{:S(2)}) %collective-permute-start.25) | collective-permute-done | bytes 65568 | tf_op jit(solution)/shard_map/ppermute | solution.py:169
  103.4 4.2 %collective-permute-done.26 = bf16[2,128,128]{2,1,0:T(8,128)(2,1)S(1)} collective-permute-done((bf16[2,128,128]{2,1,0:T(8,128)(2,1)S(1)}, bf16[2,128,128]{2,1,0:T(8,128)(2,1)S(1)}, u32[]{:S(2)}, u32[]{:S(2)}) %collective-permute-start.26) | collective-permute-done | bytes 65568 | tf_op jit(solution)/shard_map/ppermute | solution.py:169
  107.6 2.4 %collective-permute-done.29 = bf16[4,2,128,128]{3,2,1,0:T(8,128)(2,1)S(1)} collective-permute-done((bf16[4,2,128,128]{3,2,1,0:T(8,128)(2,1)S(1)}, bf16[4,2,128,128]{3,2,1,0:T(8,128)(2,1)S(1)}, u32[]{:S(2)}, u32[]{:S(2)}) %collective-permute-start.29) | collective-permute-done | bytes 262176 | tf_op jit(solution)/shard_map/ppermute | solution.py:169
  110.3 1.0 collective-permute-start.32
  111.2 0.9 collective-permute-start.33
  112.3 2.9 %collective-permute-done.32 = bf16[2,128,128]{2,1,0:T(8,128)(2,1)S(1)} collective-permute-done((bf16[2,128,128]{2,1,0:T(8,128)(2,1)S(1)}, bf16[2,128,128]{2,1,0:T(8,128)(2,1)S(1)}, u32[]{:S(2)}, u32[]{:S(2)}) %collective-permute-start.32) | collective-permute-done | bytes 65568 | tf_op jit(solution)/shard_map/ppermute | solution.py:169
  (129 shorter events, 12.9 us)
Async XLA Ops:
  2.7 7.5 %collective-permute-start.4 = (bf16[2,2,128,128]{3,2,1,0:T(8,128)(2,1)S(1)}, bf16[2,2,128,128]{3,2,1,0:T(8,128)(2,1)S(1)}, u32[]{:S(2)}, u32[]{:S(2)}) collective-permute-start(bf16[2,2,128,128]{3,2,1,0:T(8,128)(2,1)S(1)} %pad_maximum_fusion.7), channel_id=1, source_target_pairs={{0,2},{1,3},{2,0},{3,1},{4,6},{5,7},{6,4},{7,5},{8,10},{9,11},{10,... | collective-permute-start | bytes 393224 | tf_op jit(solution)/shard_map/ppermute | solution.py:169
  5.8 5.9 %collective-permute-start.5 = (bf16[2,2,128,128]{3,2,1,0:T(8,128)(2,1)S(1)}, bf16[2,2,128,128]{3,2,1,0:T(8,128)(2,1)S(1)}, u32[]{:S(2)}, u32[]{:S(2)}) collective-permute-start(bf16[2,2,128,128]{3,2,1,0:T(8,128)(2,1)S(1)} %pad_maximum_fusion.8), channel_id=1, source_target_pairs={{0,3},{1,2},{2,1},{3,0},{4,7},{5,6},{6,5},{7,4},{8,11},{9,10},{10,... | collective-permute-start | bytes 393224 | tf_op jit(solution)/shard_map/ppermute | solution.py:169
  5.9 2.3 %collective-permute-start = (bf16[2,2,128,128]{3,2,1,0:T(8,128)(2,1)S(1)}, bf16[2,2,128,128]{3,2,1,0:T(8,128)(2,1)S(1)}, u32[]{:S(2)}, u32[]{:S(2)}) collective-permute-start(bf16[2,2,128,128]{3,2,1,0:T(8,128)(2,1)S(1)} %pad_maximum_fusion.6), channel_id=1, source_target_pairs={{0,1},{1,0},{2,3},{3,2},{4,5},{5,4},{6,7},{7,6},{8,9},{9,8},{10,11... | collective-permute-start | bytes 393224 | tf_op jit(solution)/shard_map/ppermute | solution.py:169
  8.5 20.2 %collective-permute-start.1 = (bf16[2,128,1024]{2,1,0:T(8,128)(2,1)S(1)}, bf16[2,128,1024]{2,1,0:T(8,128)(2,1)S(1)}, u32[]{:S(2)}, u32[]{:S(2)}) collective-permute-start(bf16[2,128,1024]{2,1,0:T(8,128)(2,1)S(1)} %pad_maximum_fusion.2), channel_id=1, source_target_pairs={{0,3},{1,2},{2,1},{3,0},{4,7},{5,6},{6,5},{7,4},{8,11},{9,10},{10,... | collective-permute-start | bytes 1572872 | tf_op jit(solution)/shard_map/ppermute | solution.py:169
  12.4 15.8 %collective-permute-start.7 = (bf16[4,2,128,128]{3,2,1,0:T(8,128)(2,1)S(1)}, bf16[4,2,128,128]{3,2,1,0:T(8,128)(2,1)S(1)}, u32[]{:S(2)}, u32[]{:S(2)}) collective-permute-start(bf16[4,2,128,128]{3,2,1,0:T(8,128)(2,1)S(1)} %pad_maximum_fusion.4.refs_4_), channel_id=1, source_target_pairs={{0,8},{1,9},{2,10},{3,11},{4,12},{5,13},{6,14},{7,15},{8,0},{9,1},... | collective-permute-start | bytes 786440 | tf_op jit(solution)/shard_map/ppermute | solution.py:169
  15.1 26.8 %collective-permute-start.8 = (bf16[4,2,128,128]{3,2,1,0:T(8,128)(2,1)S(1)}, bf16[4,2,128,128]{3,2,1,0:T(8,128)(2,1)}, u32[]{:S(2)}, u32[]{:S(2)}) collective-permute-start(bf16[4,2,128,128]{3,2,1,0:T(8,128)(2,1)S(1)} %pad_maximum_fusion.4.refs_4_), channel_id=1, source_target_pairs={{0,0},{1,1},{2,2},{3,3},{4,8},{5,9},{6,10},{7,11},{8,4},{9,5},{10,... | collective-permute-start | bytes 786440 | tf_op jit(solution)/shard_map/ppermute | solution.py:169
  16.5 25.5 %collective-permute-start.6 = (bf16[4,2,128,128]{3,2,1,0:T(8,128)(2,1)S(1)}, bf16[4,2,128,128]{3,2,1,0:T(8,128)(2,1)S(1)}, u32[]{:S(2)}, u32[]{:S(2)}) collective-permute-start(bf16[4,2,128,128]{3,2,1,0:T(8,128)(2,1)S(1)} %pad_maximum_fusion.4.refs_4_), channel_id=1, source_target_pairs={{0,4},{1,5},{2,6},{3,7},{4,0},{5,1},{6,2},{7,3},{8,12},{9,13},{10,... | collective-permute-start | bytes 786440 | tf_op jit(solution)/shard_map/ppermute | solution.py:169
  19.5 23.2 %collective-permute-start.3 = (bf16[2,128,1024]{2,1,0:T(8,128)(2,1)}, bf16[2,128,1024]{2,1,0:T(8,128)(2,1)S(1)}, u32[]{:S(2)}, u32[]{:S(2)}) collective-permute-start(bf16[2,128,1024]{2,1,0:T(8,128)(2,1)} %pad_maximum_fusion.3), channel_id=1, source_target_pairs={{0,2},{1,3},{2,0},{3,1},{4,6},{5,7},{6,4},{7,5},{8,10},{9,11},{10,... | collective-permute-start | bytes 1572872 | tf_op jit(solution)/shard_map/ppermute | solution.py:169
  28.2 8.2 %collective-permute-start.9 = (bf16[4,2,128,128]{3,2,1,0:T(8,128)(2,1)S(1)}, bf16[4,2,128,128]{3,2,1,0:T(8,128)(2,1)}, u32[]{:S(2)}, u32[]{:S(2)}) collective-permute-start(bf16[4,2,128,128]{3,2,1,0:T(8,128)(2,1)S(1)} %collective-permute-done.7.refs_6_), channel_id=1, source_target_pairs={{0,4},{1,5},{2,6},{3,7},{4,0},{5,1},{6,2},{7,3},{8,12},{9,13},{10,... | collective-permute-start | bytes 786440 | tf_op jit(solution)/shard_map/ppermute | solution.py:169
  28.7 19.7 %collective-permute-start.2 = (bf16[2,128,1024]{2,1,0:T(8,128)(2,1)S(1)}, bf16[2,128,1024]{2,1,0:T(8,128)(2,1)S(1)}, u32[]{:S(2)}, u32[]{:S(2)}) collective-permute-start(bf16[2,128,1024]{2,1,0:T(8,128)(2,1)S(1)} %pad_maximum_fusion.1), channel_id=1, source_target_pairs={{0,1},{1,0},{2,3},{3,2},{4,5},{5,4},{6,7},{7,6},{8,9},{9,8},{10,11... | collective-permute-start | bytes 1572872 | tf_op jit(solution)/shard_map/ppermute | solution.py:169
  36.3 23.5 %collective-permute-start.10 = (bf16[4,2,128,128]{3,2,1,0:T(8,128)(2,1)S(1)}, bf16[4,2,128,128]{3,2,1,0:T(8,128)(2,1)S(1)}, u32[]{:S(2)}, u32[]{:S(2)}) collective-permute-start(bf16[4,2,128,128]{3,2,1,0:T(8,128)(2,1)S(1)} %pad_maximum_fusion.5.refs_4_), channel_id=1, source_target_pairs={{0,12},{1,13},{2,14},{3,15},{4,4},{5,5},{6,6},{7,7},{8,8},{9,9},{1... | collective-permute-start | bytes 786440 | tf_op jit(solution)/shard_map/ppermute | solution.py:169
  41.9 23.7 %collective-permute-start.16 = (bf16[4,2,128,128]{3,2,1,0:T(8,128)(2,1)S(1)}, bf16[4,2,128,128]{3,2,1,0:T(8,128)(2,1)S(1)}, u32[]{:S(2)}, u32[]{:S(2)}) collective-permute-start(bf16[4,2,128,128]{3,2,1,0:T(8,128)(2,1)S(1)} %pad_maximum_fusion.5.refs_4_), channel_id=1, source_target_pairs={{0,8},{1,9},{2,10},{3,11},{4,12},{5,13},{6,14},{7,15},{8,0},{9,1},... | collective-permute-start | bytes 786440 | tf_op jit(solution)/shard_map/ppermute | solution.py:169
  42.0 18.7 %collective-permute-start.17 = (bf16[4,2,128,128]{3,2,1,0:T(8,128)(2,1)S(1)}, bf16[4,2,128,128]{3,2,1,0:T(8,128)(2,1)S(1)}, u32[]{:S(2)}, u32[]{:S(2)}) collective-permute-start(bf16[4,2,128,128]{3,2,1,0:T(8,128)(2,1)S(1)} %pad_maximum_fusion.5.refs_4_), channel_id=1, source_target_pairs={{0,0},{1,1},{2,2},{3,3},{4,8},{5,9},{6,10},{7,11},{8,4},{9,5},{10,... | collective-permute-start | bytes 786440 | tf_op jit(solution)/shard_map/ppermute | solution.py:169
  42.7 17.9 %collective-permute-start.13 = (bf16[4,2,128,128]{3,2,1,0:T(8,128)(2,1)S(1)}, bf16[4,2,128,128]{3,2,1,0:T(8,128)(2,1)S(1)}, u32[]{:S(2)}, u32[]{:S(2)}) collective-permute-start(bf16[4,2,128,128]{3,2,1,0:T(8,128)(2,1)S(1)} %pad_maximum_fusion.5.refs_4_), channel_id=1, source_target_pairs={{0,4},{1,5},{2,6},{3,7},{4,0},{5,1},{6,2},{7,3},{8,12},{9,13},{10,... | collective-permute-start | bytes 786440 | tf_op jit(solution)/shard_map/ppermute | solution.py:169
  59.8 7.4 %collective-permute-start.18 = (bf16[4,2,128,128]{3,2,1,0:T(8,128)(2,1)S(1)}, bf16[4,2,128,128]{3,2,1,0:T(8,128)(2,1)S(1)}, u32[]{:S(2)}, u32[]{:S(2)}) collective-permute-start(bf16[4,2,128,128]{3,2,1,0:T(8,128)(2,1)S(1)} %get-tuple-element.63), channel_id=1, source_target_pairs={{0,4},{1,5},{2,6},{3,7},{4,0},{5,1},{6,2},{7,3},{8,12},{9,13},{10,... | collective-permute-start | bytes 786440 | tf_op jit(solution)/shard_map/ppermute | solution.py:169
  59.9 26.8 %collective-permute-start.20 = (bf16[4,2,128,128]{3,2,1,0:T(8,128)(2,1)S(1)}, bf16[4,2,128,128]{3,2,1,0:T(8,128)(2,1)S(1)}, u32[]{:S(2)}, u32[]{:S(2)}) collective-permute-start(bf16[4,2,128,128]{3,2,1,0:T(8,128)(2,1)S(1)} %get-tuple-element.63), channel_id=1, source_target_pairs={{0,0},{1,1},{2,2},{3,3},{4,8},{5,9},{6,10},{7,11},{8,4},{9,5},{10,... | collective-permute-start | bytes 786440 | tf_op jit(solution)/shard_map/ppermute | solution.py:169
  60.6 26.1 %collective-permute-start.15 = (bf16[2,128,512]{2,1,0:T(8,128)(2,1)S(1)}, bf16[2,128,512]{2,1,0:T(8,128)(2,1)S(1)}, u32[]{:S(2)}, u32[]{:S(2)}) collective-permute-start(bf16[2,128,512]{2,1,0:T(8,128)(2,1)S(1)} %get-tuple-element.59), channel_id=1, source_target_pairs={{0,3},{1,2},{2,1},{3,0},{4,7},{5,6},{6,5},{7,4},{8,11},{9,10},{10,... | collective-permute-start | bytes 786440 | tf_op jit(solution)/shard_map/ppermute | solution.py:169
  60.7 15.2 %collective-permute-start.11 = (bf16[4,2,128,128]{3,2,1,0:T(8,128)(2,1)S(1)}, bf16[4,2,128,128]{3,2,1,0:T(8,128)(2,1)S(1)}, u32[]{:S(2)}, u32[]{:S(2)}) collective-permute-start(bf16[4,2,128,128]{3,2,1,0:T(8,128)(2,1)S(1)} %get-tuple-element.53), channel_id=1, source_target_pairs={{0,4},{1,5},{2,6},{3,7},{4,0},{5,1},{6,2},{7,3},{8,12},{9,13},{10,... | collective-permute-start | bytes 786440 | tf_op jit(solution)/shard_map/ppermute | solution.py:169
  65.6 21.1 %collective-permute-start.14 = (bf16[2,128,512]{2,1,0:T(8,128)(2,1)S(1)}, bf16[2,128,512]{2,1,0:T(8,128)(2,1)S(1)}, u32[]{:S(2)}, u32[]{:S(2)}) collective-permute-start(bf16[2,128,512]{2,1,0:T(8,128)(2,1)S(1)} %get-tuple-element.57), channel_id=1, source_target_pairs={{0,2},{1,3},{2,0},{3,1},{4,6},{5,7},{6,4},{7,5},{8,10},{9,11},{10,... | collective-permute-start | bytes 786440 | tf_op jit(solution)/shard_map/ppermute | solution.py:169
  67.2 19.5 %collective-permute-start.19 = (bf16[4,2,128,128]{3,2,1,0:T(8,128)(2,1)S(1)}, bf16[4,2,128,128]{3,2,1,0:T(8,128)(2,1)S(1)}, u32[]{:S(2)}, u32[]{:S(2)}) collective-permute-start(bf16[4,2,128,128]{3,2,1,0:T(8,128)(2,1)S(1)} %add_convert_fusion.3), channel_id=1, source_target_pairs={{0,8},{1,9},{2,10},{3,11},{4,12},{5,13},{6,14},{7,15},{8,0},{9,1},... | collective-permute-start | bytes 786440 | tf_op jit(solution)/shard_map/ppermute | solution.py:169
  75.9 13.7 %collective-permute-start.12 = (bf16[2,128,512]{2,1,0:T(8,128)(2,1)S(1)}, bf16[2,128,512]{2,1,0:T(8,128)(2,1)S(1)}, u32[]{:S(2)}, u32[]{:S(2)}) collective-permute-start(bf16[2,128,512]{2,1,0:T(8,128)(2,1)S(1)} %get-tuple-element.54), channel_id=1, source_target_pairs={{0,1},{1,0},{2,3},{3,2},{4,5},{5,4},{6,7},{7,6},{8,9},{9,8},{10,11... | collective-permute-start | bytes 786440 | tf_op jit(solution)/shard_map/ppermute | solution.py:169
  86.7 8.8 %collective-permute-start.27 = (bf16[4,2,128,128]{3,2,1,0:T(8,128)(2,1)S(1)}, bf16[4,2,128,128]{3,2,1,0:T(8,128)(2,1)S(1)}, u32[]{:S(2)}, u32[]{:S(2)}) collective-permute-start(bf16[4,2,128,128]{3,2,1,0:T(8,128)(2,1)S(1)} %get-tuple-element.86), channel_id=1, source_target_pairs={{0,4},{1,5},{2,6},{3,7},{4,0},{5,1},{6,2},{7,3},{8,12},{9,13},{10,... | collective-permute-start | bytes 786440 | tf_op jit(solution)/shard_map/ppermute | solution.py:169
  86.8 20.8 %collective-permute-start.30 = (bf16[4,2,128,128]{3,2,1,0:T(8,128)(2,1)S(1)}, bf16[4,2,128,128]{3,2,1,0:T(8,128)(2,1)S(1)}, u32[]{:S(2)}, u32[]{:S(2)}) collective-permute-start(bf16[4,2,128,128]{3,2,1,0:T(8,128)(2,1)S(1)} %get-tuple-element.86), channel_id=1, source_target_pairs={{0,0},{1,1},{2,2},{3,3},{4,8},{5,9},{6,10},{7,11},{8,4},{9,5},{10,... | collective-permute-start | bytes 786440 | tf_op jit(solution)/shard_map/ppermute | solution.py:169
  87.5 9.8 %collective-permute-start.21 = (bf16[2,128,512]{2,1,0:T(8,128)(2,1)S(1)}, bf16[2,128,512]{2,1,0:T(8,128)(2,1)S(1)}, u32[]{:S(2)}, u32[]{:S(2)}) collective-permute-start(bf16[2,128,512]{2,1,0:T(8,128)(2,1)S(1)} %get-tuple-element.79), channel_id=1, source_target_pairs={{0,2},{1,3},{2,0},{3,1},{4,6},{5,7},{6,4},{7,5},{8,10},{9,11},{10,... | collective-permute-start | bytes 786440 | tf_op jit(solution)/shard_map/ppermute | solution.py:169
  88.4 23.8 %collective-permute-start.23 = (bf16[2,128,512]{2,1,0:T(8,128)(2,1)S(1)}, bf16[2,128,512]{2,1,0:T(8,128)(2,1)S(1)}, u32[]{:S(2)}, u32[]{:S(2)}) collective-permute-start(bf16[2,128,512]{2,1,0:T(8,128)(2,1)S(1)} %get-tuple-element.81), channel_id=1, source_target_pairs={{0,3},{1,2},{2,1},{3,0},{4,7},{5,6},{6,5},{7,4},{8,11},{9,10},{10,... | collective-permute-start | bytes 786440 | tf_op jit(solution)/shard_map/ppermute | solution.py:169
  95.6 14.4 %collective-permute-start.29 = (bf16[4,2,128,128]{3,2,1,0:T(8,128)(2,1)S(1)}, bf16[4,2,128,128]{3,2,1,0:T(8,128)(2,1)S(1)}, u32[]{:S(2)}, u32[]{:S(2)}) collective-permute-start(bf16[4,2,128,128]{3,2,1,0:T(8,128)(2,1)S(1)} %add_convert_fusion.1), channel_id=1, source_target_pairs={{0,8},{1,9},{2,10},{3,11},{4,12},{5,13},{6,14},{7,15},{8,0},{9,1},... | collective-permute-start | bytes 786440 | tf_op jit(solution)/shard_map/ppermute | solution.py:169
  96.2 11.4 %collective-permute-start.28 = (bf16[4,2,128,128]{3,2,1,0:T(8,128)(2,1)S(1)}, bf16[4,2,128,128]{3,2,1,0:T(8,128)(2,1)S(1)}, u32[]{:S(2)}, u32[]{:S(2)}) collective-permute-start(bf16[4,2,128,128]{3,2,1,0:T(8,128)(2,1)S(1)} %get-tuple-element.87), channel_id=1, source_target_pairs={{0,4},{1,5},{2,6},{3,7},{4,0},{5,1},{6,2},{7,3},{8,12},{9,13},{10,... | collective-permute-start | bytes 786440 | tf_op jit(solution)/shard_map/ppermute | solution.py:169
  98.7 4.6 %collective-permute-start.25 = (bf16[2,128,128]{2,1,0:T(8,128)(2,1)S(1)}, bf16[2,128,128]{2,1,0:T(8,128)(2,1)S(1)}, u32[]{:S(2)}, u32[]{:S(2)}) collective-permute-start(bf16[2,128,128]{2,1,0:T(8,128)(2,1)S(1)} %get-tuple-element.102), channel_id=1, source_target_pairs={{0,2},{1,3},{2,0},{3,1},{4,6},{5,7},{6,4},{7,5},{8,10},{9,11},{10,... | collective-permute-start | bytes 196616 | tf_op jit(solution)/shard_map/ppermute | solution.py:169
  103.3 4.3 %collective-permute-start.26 = (bf16[2,128,128]{2,1,0:T(8,128)(2,1)S(1)}, bf16[2,128,128]{2,1,0:T(8,128)(2,1)S(1)}, u32[]{:S(2)}, u32[]{:S(2)}) collective-permute-start(bf16[2,128,128]{2,1,0:T(8,128)(2,1)S(1)} %get-tuple-element.101), channel_id=1, source_target_pairs={{0,3},{1,2},{2,1},{3,0},{4,7},{5,6},{6,5},{7,4},{8,11},{9,10},{10,... | collective-permute-start | bytes 196616 | tf_op jit(solution)/shard_map/ppermute | solution.py:169
  107.6 4.5 %collective-permute-start.22 = (bf16[2,128,512]{2,1,0:T(8,128)(2,1)S(1)}, bf16[2,128,512]{2,1,0:T(8,128)(2,1)S(1)}, u32[]{:S(2)}, u32[]{:S(2)}) collective-permute-start(bf16[2,128,512]{2,1,0:T(8,128)(2,1)S(1)} %get-tuple-element.80), channel_id=1, source_target_pairs={{0,1},{1,0},{2,3},{3,2},{4,5},{5,4},{6,7},{7,6},{8,9},{9,8},{10,11... | collective-permute-start | bytes 786440 | tf_op jit(solution)/shard_map/ppermute | solution.py:169
  110.3 5.0 %collective-permute-start.32 = (bf16[2,128,128]{2,1,0:T(8,128)(2,1)S(1)}, bf16[2,128,128]{2,1,0:T(8,128)(2,1)S(1)}, u32[]{:S(2)}, u32[]{:S(2)}) collective-permute-start(bf16[2,128,128]{2,1,0:T(8,128)(2,1)S(1)} %get-tuple-element.99), channel_id=1, source_target_pairs={{0,2},{1,3},{2,0},{3,1},{4,6},{5,7},{6,4},{7,5},{8,10},{9,11},{10,... | collective-permute-start | bytes 196616 | tf_op jit(solution)/shard_map/ppermute | solution.py:169
  111.2 4.5 %collective-permute-start.33 = (bf16[2,128,128]{2,1,0:T(8,128)(2,1)S(1)}, bf16[2,128,128]{2,1,0:T(8,128)(2,1)S(1)}, u32[]{:S(2)}, u32[]{:S(2)}) collective-permute-start(bf16[2,128,128]{2,1,0:T(8,128)(2,1)S(1)} %get-tuple-element.98), channel_id=1, source_target_pairs={{0,3},{1,2},{2,1},{3,0},{4,7},{5,6},{6,5},{7,4},{8,11},{9,10},{10,... | collective-permute-start | bytes 196616 | tf_op jit(solution)/shard_map/ppermute | solution.py:169
  (11 other events, 64.0 us)
